TPU v7x, 32 devices: a whole 2x2x4 slice. The times are simulated.
32 devices in a mesh: replica: 8 (over z, y), shard: 4 (over x, core).
Axes of the slice: x: 2, y: 2, z: 4, core: 2. Of those that a mesh axis runs over, the one named last changes fastest.
Arguments:
- block_input: bfloat16 [16, 256, 2048], P('replica', 'shard'), may hold values from -6 to 6
- segment_ids: int32 [16, 256], P('replica'), may hold values from 0 to 3, never falling along the last dimension, each value on 1 to 192 neighbouring positions
- norm_gain: bfloat16 [2048], P('shard'), may hold values from 0.5 to 1.5
- w_in: bfloat16 [2048, 8192], P(None, 'shard'), may hold values from -0.125 to 0.125
- conv_weight: bfloat16 [4, 4096], P(None, 'shard'), may hold values from -3 to 3
- conv_bias: bfloat16 [4096], P('shard'), may hold values from -1.5 to 1.5
- x_proj: bfloat16 [160, 4096], P(None, 'shard'), may hold values from -1 to 1
- dt_proj: bfloat16 [128, 4096], P(None, 'shard'), may hold values from -0.5 to 0.5
- dt_bias: bfloat16 [4096], P('shard'), may hold values from -4 to 1
- d_skip: bfloat16 [4096], P('shard'), may hold values from 0.5 to 1.5
- out_proj: bfloat16 [4096, 2048], P(None, 'shard'), may hold values from -0.1875 to 0.1875
- out_grad: bfloat16 [16, 256, 2048], P('replica', 'shard'), may hold values from -6 to 6
Outputs:
- block_output: bfloat16 [16, 256, 2048], P('replica', 'shard')
- input_grad: bfloat16 [16, 256, 2048], P('replica', 'shard')
- grad_norm_gain: float32 [2048], P('shard')
- grad_w_in: float32 [2048, 8192], P('replica', 'shard')
- grad_conv_weight: float32 [4, 4096], P(None, 'shard')
- grad_conv_bias: float32 [4096], P('shard')
- grad_x_proj: float32 [160, 4096], P(None, 'shard')
- grad_dt_proj: float32 [128, 4096], P(None, 'shard')
- grad_dt_bias: float32 [4096], P('shard')
- grad_d_skip: float32 [4096], P('shard')
- grad_out_proj: float32 [4096, 2048], P('replica', 'shard')
Inputs may be any that keep to these rules, and one draw needn't show every extreme that they name: `segment_ids`: within each sequence the ids never fall; each of the 4 documents holds 1 to 192 tokens and one holds exactly 192.
All inputs are finite; a program needn't handle non-finite values.
Results may differ from a plain program's by a relative error of at most 0.012.
The roundings to bfloat16 on the way count: a program that leaves them out, or rounds other values in their place, can miss the bound.
Values may be sent and summed in bfloat16 or wider, within the bound.
A program may use at most 240 MiB of HBM per device.

v0:
```python
import jax
import jax.numpy as jnp
from jax import lax
from jax.sharding import PartitionSpec as P

KW = 4


EPS = 1e-05
block_len = 16


def passed_along(block, axis, distance):
    devices = range(lax.axis_size(axis))
    route = [(i - distance, i) for i in devices if i - distance in devices]
    return lax.ppermute(block, axis, route)


def carried_in(value, axis, join, neutral):
    count, mine = (lax.axis_size(axis), lax.axis_index(axis))
    pieces = jax.tree.map(lambda part: lax.all_gather(part, axis), value)
    total = jax.tree.map(
        lambda part, zero: jnp.full_like(part, 0) + jnp.asarray(zero, part.dtype), value, neutral
    )

    def hop(position, total):
        longer = join(total, jax.tree.map(lambda part: part[position], pieces))
        return jax.tree.map(lambda new, old: jnp.where(position < mine, new, old), longer, total)

    return lax.fori_loop(0, count - 1, hop, total)


def entering(shard, axis, join, neutral):
    count = lax.axis_size(axis)
    place = lax.axis_index(axis)
    ahead = count - 1 - place
    gathered = jax.tree.map(
        lambda a, kind: lax.all_gather(a.astype(kind), axis), shard, (jnp.bfloat16, jnp.bfloat16)
    )
    state = jax.tree.map(lambda a, e: jnp.zeros_like(a) + jnp.asarray(e, a.dtype), shard, neutral)

    def one(hop, state):
        source = count - 1 - hop
        return join(
            state,
            jax.tree.map(
                lambda a, own: lax.dynamic_index_in_dim(a, source, 0, False).astype(own.dtype),
                gathered,
                shard,
            ),
        )

    return lax.fori_loop(0, ahead, one, state)


def rows_dot(first_op, second_op):
    return jnp.dot(first_op, second_op, preferred_element_type=jnp.float32)


def inner_dot(first_op, second_op):
    return lax.dot_general(
        first_op, second_op, (((0,), (0,)), ((), ())), preferred_element_type=jnp.float32
    )


def outer_dot(first_op, second_op):
    return lax.dot_general(
        first_op, second_op, (((1,), (1,)), ((), ())), preferred_element_type=jnp.float32
    )


def silu_slope(values):
    sig_val = jax.nn.sigmoid(values)
    return sig_val + values * sig_val * (1.0 - sig_val)


def decay_of(rate_row, key_row, keep_val):
    return (1.0 - rate_row[:, None] * (key_row * key_row)[None, :]) * keep_val


def block_forward(carried, pieces):
    rate_blk, conv_blk, key_blk, query_blk, keep_blk = pieces
    outputs = []
    for t in range(rate_blk.shape[0]):
        decay_now = decay_of(rate_blk[t], key_blk[t], keep_blk[t])
        carried = decay_now * carried + (rate_blk[t] * conv_blk[t])[:, None] * key_blk[t][None, :]
        outputs.append(jnp.sum(carried * query_blk[t][None, :], axis=1))
    return (carried, jnp.stack(outputs))


def block_product(carried, pieces):
    total_decay, local_state = carried
    rate_blk, conv_blk, key_blk, query_blk, keep_blk = pieces
    for t in range(rate_blk.shape[0]):
        decay_now = decay_of(rate_blk[t], key_blk[t], keep_blk[t])
        total_decay = decay_now * total_decay
        local_state = (
            decay_now * local_state + (rate_blk[t] * conv_blk[t])[:, None] * key_blk[t][None, :]
        )
    return ((total_decay, local_state), None)


def block_record(carried, pieces):
    end_state, outputs = block_forward(carried, pieces)
    return (end_state, (carried, outputs))


def block_adjoint(adjoint, pieces):
    rate_blk, key_blk, query_blk, keep_blk, dout_blk = pieces
    for t in reversed(range(rate_blk.shape[0])):
        adjoint = adjoint + dout_blk[t][:, None] * query_blk[t][None, :]
        adjoint = decay_of(rate_blk[t], key_blk[t], keep_blk[t]) * adjoint
    return (adjoint, None)


def block_backward(grad_state, inputs):
    start_state = inputs[0]
    pieces = inputs[1:6]
    dout_blk = inputs[6]
    pullback = jax.vjp(block_forward, start_state, pieces)[1]
    grad_start, grad_pieces = pullback((grad_state, dout_blk))
    return (grad_start, grad_pieces[:4])


def chain_combine(earlier, later):
    return (earlier[0] * later[0], later[0] * earlier[1] + later[1])


def conv_apply(extended, conv_w, conv_b, tap_masks):
    tok_local = extended.shape[0] - (KW - 1)
    conv_sum = conv_b + conv_w[KW - 1] * extended[KW - 1 :]
    for j in range(KW - 1):
        conv_sum = (
            conv_sum + conv_w[j] * extended[j : j + tok_local] * tap_masks[KW - 2 - j][:, None]
        )
    return conv_sum


def one_batch(weights, x_rows, cot_rows, seg_window):
    norm_gain, w_in, conv_weight, conv_bias, x_proj, dt_proj, dt_bias, d_skip, out_proj = weights
    tok_local = x_rows.shape[0]
    width = d_skip.shape[0]
    rank = dt_proj.shape[0]
    state_dim = (x_proj.shape[0] - rank) // 2
    count_blocks = tok_local // block_len
    x_vals = x_rows.astype(jnp.float32)
    inv_rms = lax.rsqrt(jnp.mean(x_vals * x_vals, axis=1, keepdims=True) + EPS)
    gain_vals = norm_gain.astype(jnp.float32)
    normed = (x_vals * inv_rms * gain_vals).astype(jnp.bfloat16)
    mixed = rows_dot(normed, w_in).astype(jnp.bfloat16)
    x_part = mixed[:, :width]
    z_vals = mixed[:, width:].astype(jnp.float32)
    edge_rows = passed_along(x_part[tok_local - (KW - 1) :], "shard", 1)
    extended = jnp.concatenate([edge_rows, x_part], axis=0).astype(jnp.float32)
    tap_masks = [
        (seg_window[KW - 1 - d : KW - 1 - d + tok_local] == seg_window[KW - 1 :]).astype(
            jnp.float32
        )
        for d in range(1, KW)
    ]
    keep_rows = tap_masks[0]
    conv_w = conv_weight.astype(jnp.float32)
    conv_b = conv_bias.astype(jnp.float32)
    conv_pre = conv_apply(extended, conv_w, conv_b, tap_masks)
    conv_out = jax.nn.silu(conv_pre).astype(jnp.bfloat16)
    conv_vals = conv_out.astype(jnp.float32)
    proj_vals = outer_dot(conv_out, x_proj)
    dt_low = proj_vals[:, :rank].astype(jnp.bfloat16)
    key_rows = proj_vals[:, rank : rank + state_dim]
    query_rows = proj_vals[:, rank + state_dim :]
    beta_vals = jax.nn.sigmoid(rows_dot(dt_low, dt_proj) + dt_bias.astype(jnp.float32))
    key_square = jnp.sum(key_rows * key_rows, axis=1, keepdims=True)
    denom_inv = 1.0 / (1.0 + beta_vals * key_square)
    step_rate = beta_vals * denom_inv

    def blocked(values):
        return values.reshape((count_blocks, block_len) + values.shape[1:])

    pieces = (
        blocked(step_rate),
        blocked(conv_vals),
        blocked(key_rows),
        blocked(query_rows),
        blocked(keep_rows),
    )
    unit_state = jnp.ones((width, state_dim), jnp.float32)
    zero_state = jnp.zeros((width, state_dim), jnp.float32)
    total_decay, local_state = lax.scan(block_product, (unit_state, zero_state), pieces)[0]
    state_in = carried_in(
        (total_decay, local_state), "shard", chain_combine, (unit_state, zero_state)
    )[1]
    starts, rec_blocks = lax.scan(block_record, state_in, pieces)[1]
    recurrent = rec_blocks.reshape(tok_local, width)
    skip_vals = d_skip.astype(jnp.float32)
    y_total = recurrent + skip_vals * conv_vals
    gate_act = jax.nn.silu(z_vals)
    gated = (y_total * gate_act).astype(jnp.bfloat16)
    out_val = (x_vals + rows_dot(gated, out_proj)).astype(jnp.bfloat16)
    grad_out_proj = inner_dot(gated, cot_rows)
    grad_gated = outer_dot(cot_rows, out_proj)
    grad_y = grad_gated * gate_act
    grad_z = grad_gated * y_total * silu_slope(z_vals)
    grad_d_skip = jnp.sum(grad_y * conv_vals, axis=0)
    dout_blocks = blocked(grad_y)
    adj_pieces = (pieces[0], pieces[2], pieces[3], pieces[4], dout_blocks)
    grad_local = lax.scan(block_adjoint, zero_state, adj_pieces, reverse=True)[0]
    grad_end = entering(
        (total_decay, grad_local), "shard", chain_combine, (unit_state, zero_state)
    )[1]
    back_pieces = (starts,) + pieces + (dout_blocks,)
    rate_back, conv_back, key_back, query_back = lax.scan(
        block_backward, grad_end, back_pieces, reverse=True
    )[1]
    grad_rate = rate_back.reshape(tok_local, width)
    grad_keys = key_back.reshape(tok_local, state_dim)
    grad_queries = query_back.reshape(tok_local, state_dim)
    grad_conv = grad_y * skip_vals + conv_back.reshape(tok_local, width)
    grad_keys = grad_keys - 2.0 * key_rows * jnp.sum(
        grad_rate * step_rate * step_rate, axis=1, keepdims=True
    )
    grad_dt = grad_rate * denom_inv * denom_inv * beta_vals * (1.0 - beta_vals)
    grad_dt_bias = jnp.sum(grad_dt, axis=0)
    grad_dt_low = grad_dt.astype(jnp.bfloat16)
    grad_dt_proj = inner_dot(dt_low, grad_dt_low)
    grad_dt_in = outer_dot(grad_dt_low, dt_proj)
    grad_proj = jnp.concatenate([grad_dt_in, grad_keys, grad_queries], axis=1).astype(jnp.bfloat16)
    grad_x_proj = inner_dot(grad_proj, conv_out)
    grad_conv = grad_conv + rows_dot(grad_proj, x_proj)
    grad_pre = grad_conv * silu_slope(conv_pre)

    def conv_local(ext_vals, tap_wts, bias_vals):
        return conv_apply(ext_vals, tap_wts, bias_vals, tap_masks)

    conv_pull = jax.vjp(conv_local, extended, conv_w, conv_b)[1]
    grad_ext, grad_conv_weight, grad_conv_bias = conv_pull(grad_pre)
    back_rows = passed_along(grad_ext[: KW - 1].astype(jnp.bfloat16), "shard", -1).astype(
        jnp.float32
    )
    grad_x_part = jnp.concatenate(
        [grad_ext[KW - 1 : tok_local], grad_ext[tok_local:] + back_rows], axis=0
    )
    grad_mixed = jnp.concatenate([grad_x_part, grad_z], axis=1).astype(jnp.bfloat16)
    grad_w_in = inner_dot(normed, grad_mixed)
    grad_normed = outer_dot(grad_mixed, w_in)
    grad_norm_gain = jnp.sum(grad_normed * x_vals * inv_rms, axis=0)
    scaled = grad_normed * gain_vals
    grad_x = inv_rms * (
        scaled - x_vals * inv_rms * inv_rms * jnp.mean(scaled * x_vals, axis=1, keepdims=True)
    )
    dx_val = (cot_rows.astype(jnp.float32) + grad_x).astype(jnp.bfloat16)
    grad_list = (
        grad_norm_gain,
        grad_w_in,
        grad_conv_weight,
        grad_conv_bias,
        grad_x_proj,
        grad_dt_proj,
        grad_dt_bias,
        grad_d_skip,
        grad_out_proj,
    )
    return (out_val, dx_val, grad_list)


def body(
    block_input,
    segment_ids,
    norm_gain,
    w_in,
    conv_weight,
    conv_bias,
    x_proj,
    dt_proj,
    dt_bias,
    d_skip,
    out_proj,
    out_grad,
):
    micro_count = block_input.shape[0]
    tok_local = block_input.shape[1]
    shard_pos = lax.axis_index("shard")
    seg_padded = jnp.pad(segment_ids, ((0, 0), (KW - 1, 0)), constant_values=-1)
    seg_windows = lax.dynamic_slice_in_dim(seg_padded, shard_pos * tok_local, tok_local + KW - 1, 1)
    full_sums = None
    shard_sums = None
    out_rows = []
    grad_rows = []
    for m in range(micro_count):
        gathered = (
            lax.all_gather(norm_gain, "shard", axis=0, tiled=True),
            lax.all_gather(w_in, "shard", axis=1, tiled=True),
            lax.all_gather(conv_weight, "shard", axis=1, tiled=True),
            lax.all_gather(conv_bias, "shard", axis=0, tiled=True),
            lax.all_gather(x_proj, "shard", axis=1, tiled=True),
            lax.all_gather(dt_proj, "shard", axis=1, tiled=True),
            lax.all_gather(dt_bias, "shard", axis=0, tiled=True),
            lax.all_gather(d_skip, "shard", axis=0, tiled=True),
            lax.all_gather(out_proj, "shard", axis=1, tiled=True),
        )
        out_val, dx_val, grad_list = one_batch(
            gathered, block_input[m], out_grad[m], seg_windows[m]
        )
        out_rows.append(out_val)
        grad_rows.append(dx_val)
        full_sums = (
            grad_list if full_sums is None else tuple((a + b for a, b in zip(full_sums, grad_list)))
        )
    shard_sums = (
        lax.psum_scatter(
            full_sums[0].astype(jnp.bfloat16), "shard", scatter_dimension=0, tiled=True
        ).astype(jnp.float32),
        lax.psum_scatter(
            full_sums[1].astype(jnp.bfloat16), "shard", scatter_dimension=1, tiled=True
        ).astype(jnp.float32),
        lax.psum_scatter(
            full_sums[2].astype(jnp.bfloat16), "shard", scatter_dimension=1, tiled=True
        ).astype(jnp.float32),
        lax.psum_scatter(
            full_sums[3].astype(jnp.bfloat16), "shard", scatter_dimension=0, tiled=True
        ).astype(jnp.float32),
        lax.psum_scatter(
            full_sums[4].astype(jnp.bfloat16), "shard", scatter_dimension=1, tiled=True
        ).astype(jnp.float32),
        lax.psum_scatter(
            full_sums[5].astype(jnp.bfloat16), "shard", scatter_dimension=1, tiled=True
        ).astype(jnp.float32),
        lax.psum_scatter(
            full_sums[6].astype(jnp.bfloat16), "shard", scatter_dimension=0, tiled=True
        ).astype(jnp.float32),
        lax.psum_scatter(
            full_sums[7].astype(jnp.bfloat16), "shard", scatter_dimension=0, tiled=True
        ).astype(jnp.float32),
        lax.psum_scatter(
            full_sums[8].astype(jnp.bfloat16), "shard", scatter_dimension=1, tiled=True
        ).astype(jnp.float32),
    )
    large_sums = (
        lax.psum_scatter(shard_sums[1], "replica", scatter_dimension=0, tiled=True),
        lax.psum_scatter(shard_sums[8], "replica", scatter_dimension=0, tiled=True),
    )
    small_sums = lax.psum(
        (
            shard_sums[0],
            shard_sums[2],
            shard_sums[3],
            shard_sums[4],
            shard_sums[5],
            shard_sums[6],
            shard_sums[7],
        ),
        "replica",
    )
    return (
        jnp.stack(out_rows),
        jnp.stack(grad_rows),
        small_sums[0],
        large_sums[0],
        small_sums[1],
        small_sums[2],
        small_sums[3],
        small_sums[4],
        small_sums[5],
        small_sums[6],
        large_sums[1],
    )


def solution(mesh):
    return jax.shard_map(
        body,
        mesh=mesh,
        in_specs=(
            P("replica", "shard", None),
            P("replica", None),
            P("shard"),
            P(None, "shard"),
            P(None, "shard"),
            P("shard"),
            P(None, "shard"),
            P(None, "shard"),
            P("shard"),
            P("shard"),
            P(None, "shard"),
            P("replica", "shard", None),
        ),
        out_specs=(
            P("replica", "shard", None),
            P("replica", "shard", None),
            P("shard"),
            P("replica", "shard"),
            P(None, "shard"),
            P("shard"),
            P(None, "shard"),
            P(None, "shard"),
            P("shard"),
            P("shard"),
            P("replica", "shard"),
        ),
        check_vma=False,
    )
```

profile of v0, /device:TPU:0, one launch (start us, length us, event | category | flops | bytes accessed | tf_op | source)
XLA Modules:
  0.0 2360.5 jit_solution(17861980219472843263)
XLA Ops:
  42.2 171.9 %all-gather.18.cloned.1.call-done = bf16[2048,8192]{1,0:T(8,128)(2,1)} async-done(((bf16[2048,2048]{1,0:T(8,128)(2,1)}), bf16[2048,8192]{1,0:T(8,128)(2,1)}) %all-gather.18.cloned.1.call-update) | async-done | bytes 33554448 | tf_op jit(solution)/shard_map/all_gather | solution.py:291
  214.1 15.5 convolution_convert_fusion.1
  231.8 14.6 convolution_convert_fusion
  252.0 69.6 %all-gather.24.cloned.1.call-done = bf16[4096,2048]{1,0:T(8,128)(2,1)} async-done(((bf16[4096,512]{1,0:T(8,128)(2,1)}), bf16[4096,2048]{1,0:T(8,128)(2,1)}) %all-gather.24.cloned.1.call-update) | async-done | bytes 16777232 | tf_op jit(solution)/shard_map/all_gather | solution.py:298
  321.6 15.2 multiply_reduce_fusion.193
  345.4 14.9 all-gather.22.cloned.1.call-done
  363.1 102.7 %while.190 = (s32[]{:T(128)}, f32[4096,16]{0,1:T(8,128)S(1)}, f32[4096,16]{0,1:T(8,128)}, f32[4,16,4096]{2,1,0:T(8,128)S(1)}, f32[4,16,16]{2,1,0:T(8,128)}, /*in...) while((s32[]{:T(128)}, f32[4096,16]{0,1:T(8,128)S(1)}, ...), condition=%wide.region_3.4_spmd.clone, body=%wide.region_2.3_spmd.clone.sunk | while | flops 10682642 | bytes 5774296 | solution.py:188
  366.7 11.3 multiply_add_fusion.148
  378.0 10.8 fusion.699
  392.3 11.3 multiply_add_fusion.148
  403.6 10.8 fusion.699
  418.0 11.3 multiply_add_fusion.148
  429.3 10.8 fusion.699
  443.7 11.3 multiply_add_fusion.148
  455.0 10.8 fusion.699
  468.5 15.7 multiply_reduce_fusion.192
  489.1 102.7 %while.192 = (s32[]{:T(128)}, f32[4096,16]{0,1:T(8,128)S(1)}, f32[4096,16]{0,1:T(8,128)S(1)}, f32[4,16,4096]{2,1,0:T(8,128)S(1)}, f32[4,16,16]{2,1,0:T(8,128)S(1...) while((s32[]{:T(128)}, f32[4096,16]{0,1:T(8,128)S(1)}, ...), condition=%wide.region_27.28_spmd.clone, body=%wide.region_26.27_spmd.clone.sunk | while | flops 10682642 | bytes 3677088 | solution.py:188
  493.0 11.2 multiply_add_fusion.149
  504.2 10.7 fusion.703
  518.8 11.2 multiply_add_fusion.149
  544.5 11.2 multiply_add_fusion.149
  570.0 11.2 multiply_add_fusion.149
  592.6 65.8 %while.194 = (s32[]{:T(128)}, f32[4096,16]{0,1:T(8,128)S(1)}, f32[4,16,4096]{2,1,0:T(8,128)S(1)}, f32[4,16,16]{2,1,0:T(8,128)}, f32[4,16]{1,0:T(4,128)}, /*index...) while((s32[]{:T(128)}, f32[4096,16]{0,1:T(8,128)S(1)}, ...), condition=%wide.region_49.50_spmd.clone, body=%wide.region_48.49_spmd.clone.sunk | while | flops 6357267 | bytes 2104179 | solution.py:206
  597.8 11.2 add_multiply_fusion.4
  614.3 11.2 add_multiply_fusion.4
  630.8 11.2 add_multiply_fusion.4
  647.2 11.2 add_multiply_fusion.4
  679.0 60.7 %while.195 = (s32[]{:T(128)}, f32[4096,16]{0,1:T(8,128)S(1)}, f32[4,16,4096]{2,1,0:T(8,128)S(1)}, f32[4,16,16]{2,1,0:T(8,128)S(1)}, f32[4,16]{1,0:T(4,128)S(1)},...) while((s32[]{:T(128)}, f32[4096,16]{0,1:T(8,128)S(1)}, ...), condition=%wide.region_137.138_spmd.clone, body=%wide.region_136.137_spmd.clone.sunk | while | flops 6357267 | bytes 2104179 | solution.py:206
  682.6 11.4 add_multiply_fusion.5
  698.1 11.4 add_multiply_fusion.5
  713.2 11.4 add_multiply_fusion.5
  728.2 11.4 add_multiply_fusion.5
  774.1 119.0 %while.184 = (s32[]{:T(128)}, f32[4096,16]{0,1:T(8,128)S(1)}, f32[4,4096,16]{1,2,0:T(8,128)}, f32[4,16,4096]{2,1,0:T(8,128)}, f32[4,16,4096]{2,1,0:T(8,128)S(1)}...) while((s32[]{:T(128)}, f32[4096,16]{0,1:T(8,128)S(1)}, ...), condition=%wide.region_23.24_spmd, body=%wide.region_6.23_spmd.sunk | while | flops 11534609 | bytes 8923085 | solution.py:192
  782.2 11.6 multiply_reduce_fusion.240
  811.8 11.6 multiply_reduce_fusion.240
  841.5 11.6 multiply_reduce_fusion.240
  871.4 11.6 multiply_reduce_fusion.240
  895.3 203.1 %while.187 = (s32[]{:T(128)}, f32[4096,16]{0,1:T(8,128)S(1)}, f32[4,16,4096]{2,1,0:T(8,128)}, f32[4,16,4096]{2,1,0:T(8,128)}, f32[4,16,16]{2,1,0:T(8,128)S(1)}, ...) while((s32[]{:T(128)}, f32[4096,16]{0,1:T(8,128)S(1)}, ...), condition=%wide.region_133.134_spmd, body=%wide.region_52.133_spmd.sunk | while | flops 34942480 | bytes 17066536 | solution.py:211
  903.1 11.3 multiply_add_fusion.146
  953.7 11.3 multiply_add_fusion.146
  1004.6 11.3 multiply_add_fusion.146
  1055.1 11.3 multiply_add_fusion.146
  1113.8 98.0 %while.185 = (s32[]{:T(128)}, f32[4096,16]{0,1:T(8,128)S(1)}, f32[4,4096,16]{1,2,0:T(8,128)}, f32[4,16,4096]{2,1,0:T(8,128)}, f32[4,16,4096]{2,1,0:T(8,128)S(1)}...) while((s32[]{:T(128)}, f32[4096,16]{0,1:T(8,128)S(1)}, ...), condition=%wide.region_47.48_spmd, body=%wide.region_30.47_spmd.sunk | while | flops 11534609 | bytes 8923085 | solution.py:192
  1119.4 12.0 multiply_reduce_fusion.249
  1143.9 12.0 multiply_reduce_fusion.249
  1168.4 12.0 multiply_reduce_fusion.249
  1192.7 12.0 multiply_reduce_fusion.249
  1213.9 195.1 %while.189 = (s32[]{:T(128)}, f32[4096,16]{0,1:T(8,128)S(1)}, f32[4,16,4096]{2,1,0:T(8,128)}, f32[4,16,4096]{2,1,0:T(8,128)}, f32[4,16,16]{2,1,0:T(8,128)S(1)}, ...) while((s32[]{:T(128)}, f32[4096,16]{0,1:T(8,128)S(1)}, ...), condition=%wide.region_221.222_spmd, body=%wide.region_140.221_spmd.sunk | while | flops 34942480 | bytes 17066536 | solution.py:211
  1218.9 11.7 multiply_add_fusion.147
  1268.0 11.7 multiply_add_fusion.147
  1316.7 11.7 multiply_add_fusion.147
  1365.4 11.7 multiply_add_fusion.147
  1415.6 13.6 fusion.432
  1429.1 18.9 add_convert_fusion.1
  1465.5 26.1 %fusion.425 = f32[2048,8192]{1,0:T(8,128)} fusion(bf16[64,4096]{1,0:T(8,128)(2,1)S(1)} %copy-done.18, bf16[3,4096]{1,0:T(4,128)(2,1)S(1)} %fusion.446, bf16[61,4096]{1,0:T(8,128)(2,1)S(1)} %slice.5298, f32[2048]{0:T(1024)S(1)} %bitcast.3490, f32[64]{0:T(128)S(1)} %copy-done.54, bf16[2,64,2048]{2,1,0:T(8,128)(2,1)S(1)} %copy-done.2), kind=kOutput, calls=%fused_computation.1561 | convolution fusion | flops 2151153664 | bytes 68461056 | tf_op jit(solution)/shard_map/dot_general | solution.py:61
  1491.6 33.7 %add_convert_fusion = bf16[2048,8192]{1,0:T(8,128)(2,1)} fusion(f32[2048,8192]{1,0:T(8,128)} %fusion.425, bf16[64,4096]{1,0:T(8,128)(2,1)S(1)} %copy-done.19, bf16[3,4096]{1,0:T(4,128)(2,1)S(1)} %fusion.445, bf16[61,4096]{1,0:T(8,128)(2,1)} %slice.5301, f32[64]{0:T(128)S(1)} %copy-done.52, f32[2048]{0:T(1024)S(1)} %bitcast.3491, ...), kind=kOutput, calls=%fused_computation.1428 | convolution fusion | flops 2184708096 | bytes 101990912 | tf_op jit(solution)/shard_map/dot_general | solution.py:61
  1536.4 38.0 %reduce-scatter.18.cloned.1.call-done = bf16[4096,512]{1,0:T(8,128)(2,1)} async-done(((bf16[4096,2048]{1,0:T(8,128)(2,1)}), bf16[4096,512]{1,0:T(8,128)(2,1)}) %reduce-scatter.18.cloned.1.call-update) | async-done | bytes 4194320 | tf_op jit(solution)/shard_map/reduce_scatter | solution.py:333
  1581.3 230.6 %reduce-scatter.10.cloned.1.call-done = bf16[2048,2048]{1,0:T(8,128)(2,1)} async-done(((bf16[2048,8192]{1,0:T(8,128)(2,1)}), bf16[2048,2048]{1,0:T(8,128)(2,1)}) %reduce-scatter.10.cloned.1.call-update) | async-done | bytes 8388624 | tf_op jit(solution)/shard_map/reduce_scatter | solution.py:312
  1811.9 11.6 convert_element_type.346
  1845.0 15.8 fusion.424
  1860.8 15.9 fusion.419
  1896.1 98.4 %all-reduce.216 = (f32[512]{0:T(512)}, f32[4,1024]{1,0:T(4,128)}, f32[1024]{0:T(1024)}, f32[160,1024]{1,0:T(8,128)}, f32[128,1024]{1,0:T(8,128)}, /*index=5*/f32[1024]{0:T(1024)}, f32[1024]{0:T(1024)}) all-reduce(f32[512]{0:T(512)S(1)} %dynamic-slice_convert_fusion.3, ...), channel_id=1, replica_groups=mesh['replica'=8,'shard'=4] {'replica'}, use_global_device_ids=true, to_apply=%region_227.228 | all-reduce | flops 302592 | bytes 1822720 | tf_op jit(solution)/shard_map/psum | solution.py:341
  1994.5 73.0 %reduce-scatter.20.cloned.1.call-done = f32[512,512]{1,0:T(8,128)} async-done(((f32[4096,512]{1,0:T(8,128)}), f32[512,512]{1,0:T(8,128)}) %reduce-scatter.20.cloned.1.call-update) | async-done | bytes 1048592 | tf_op jit(solution)/shard_map/reduce_scatter | solution.py:339
  2067.5 286.3 %reduce-scatter.12.cloned.1.call-done = f32[256,2048]{1,0:T(8,128)} async-done(((f32[2048,2048]{1,0:T(8,128)}), f32[256,2048]{1,0:T(8,128)}) %reduce-scatter.12.cloned.1.call-update) | async-done | bytes 2097168 | tf_op jit(solution)/shard_map/reduce_scatter | solution.py:338
  (1373 shorter events, 757.6 us)
Async XLA Ops:
  7.2 206.9 %all-gather.18.cloned.1.call-start = ((), (), s32[]{:S(2)}) async-start(), calls=%async_computation.7 | async-start | bytes 41943040 | tf_op jit(solution)/shard_map/all_gather | solution.py:291
  7.9 5.2 copy-start.82
  7.9 11.3 copy-start.75
  8.0 17.4 copy-start.76
  8.0 22.5 copy-start.77
  8.0 28.3 %copy-start.71 = (bf16[4,1024]{1,0:T(4,128)(2,1)S(1)}, bf16[4,1024]{1,0:T(4,128)(2,1)}, u32[]{:S(2)}) copy-start(bf16[4,1024]{1,0:T(4,128)(2,1)} %param.40) | copy-start | bytes 24580
  8.0 313.6 %all-gather.24.cloned.1.call-start = ((), (), s32[]{:S(2)}) async-start(), calls=%async_computation.10 | async-start | bytes 20971520 | tf_op jit(solution)/shard_map/all_gather | solution.py:298
  8.7 333.4 %all-gather.20.cloned.1.call-start = ((), (), s32[]{:S(2)}) async-start(), calls=%async_computation.8 | async-start | bytes 1638400 | tf_op jit(solution)/shard_map/all_gather | solution.py:294
  9.5 350.8 %all-gather.22.cloned.1.call-start = ((), (), s32[]{:S(2)}) async-start(), calls=%async_computation.9 | async-start | bytes 1310720 | tf_op jit(solution)/shard_map/all_gather | solution.py:295
  10.0 748.7 %all-gather.28.cloned.1.call-start = ((), (), s32[]{:S(2)}) async-start(), calls=%async_computation.18 | async-start | bytes 1310720 | tf_op jit(solution)/shard_map/all_gather | solution.py:21
  11.8 217.8 %copy-start.53 = (f32[64]{0:T(128)}, f32[64]{0:T(128)S(1)}, u32[]{:S(2)}) copy-start(f32[64]{0:T(128)S(1)} %add_rsqrt_fusion.1) | copy-start | bytes 772
  11.8 220.0 %copy-start.51 = (f32[64]{0:T(128)}, f32[64]{0:T(128)S(1)}, u32[]{:S(2)}) copy-start(f32[64]{0:T(128)S(1)} %add_rsqrt_fusion) | copy-start | bytes 772
  19.3 212.5 %copy-start.33 = (f32[4,1,512]{2,1,0:T(1,128)}, f32[4,1,512]{2,1,0:T(1,128)S(1)}, u32[]{:S(2)}) copy-start(f32[4,1,512]{2,1,0:T(1,128)S(1)} %convert_element_type.375) | copy-start | bytes 24580
  229.6 92.0 %copy-start.26 = (bf16[64,8192]{1,0:T(8,128)(2,1)}, bf16[64,8192]{1,0:T(8,128)(2,1)S(1)}, u32[]{:S(2)}) copy-start(bf16[64,8192]{1,0:T(8,128)(2,1)S(1)} %convolution_convert_fusion.1) | copy-start | bytes 3145732
  229.7 21.2 collective-permute-start
  246.5 75.2 %copy-start.30 = (bf16[2,64,2048]{2,1,0:T(8,128)(2,1)S(1)}, bf16[2,64,2048]{2,1,0:T(8,128)(2,1)}, u32[]{:S(2)}) copy-start(bf16[2,64,2048]{2,1,0:T(8,128)(2,1)} %param.47) | copy-start | bytes 1572868
  248.4 217.7 %collective-permute-start.1 = (bf16[3,4096]{1,0:T(4,128)(2,1)S(1)}, bf16[3,4096]{1,0:T(4,128)(2,1)S(1)}, u32[]{:S(2)}, u32[]{:S(2)}) collective-permute-start(bf16[3,4096]{1,0:T(4,128)(2,1)S(1)} %slice.5288), channel_id=1, source_target_pairs={{0,1},{1,2},{2,3},{4,5},{5,6},{6,7},{8,9},{9,10},{10,11},{12,13},{... | collective-permute-start | bytes 73736 | tf_op jit(solution)/shard_map/ppermute | solution.py:16
  336.9 23.4 copy-start.11
  344.0 19.1 copy-start.45
  363.1 105.4 %copy-start.59 = (f32[4096]{0:T(1024)S(1)}, f32[4096]{0:T(1024)}, u32[]{:S(2)}) copy-start(f32[4096]{0:T(1024)} %convert_element_type.292) | copy-start | bytes 49156
  363.1 105.4 %copy-start.64 = (f32[1,4096]{1,0:T(1,128)S(1)}, f32[1,4096]{1,0:T(1,128)}, u32[]{:S(2)}) copy-start(f32[1,4096]{1,0:T(1,128)} %get-tuple-element.3206) | copy-start | bytes 49156
  363.1 105.4 %copy-start.66 = (f32[1,4096]{1,0:T(1,128)S(1)}, f32[1,4096]{1,0:T(1,128)}, u32[]{:S(2)}) copy-start(f32[1,4096]{1,0:T(1,128)} %get-tuple-element.3207) | copy-start | bytes 49156
  363.1 105.4 %copy-start.68 = (f32[1,4096]{1,0:T(1,128)S(1)}, f32[1,4096]{1,0:T(1,128)}, u32[]{:S(2)}) copy-start(f32[1,4096]{1,0:T(1,128)} %get-tuple-element.3208) | copy-start | bytes 49156
  378.0 10.8 copy-start.10
  403.6 10.8 copy-start.10
  429.3 10.8 copy-start.10
  455.0 10.8 copy-start.10
  465.8 18.4 copy-start
  465.8 18.3 copy-start.4
  465.8 295.8 %all-gather.26.cloned.1.call-start = ((), (), s32[]{:S(2)}) async-start(), calls=%async_computation.17 | async-start | bytes 1310720 | tf_op jit(solution)/shard_map/all_gather | solution.py:21
  591.9 86.1 %copy-start.3 = (f32[4096,16]{0,1:T(8,128)}, f32[4096,16]{0,1:T(8,128)S(1)}, u32[]{:S(2)}) copy-start(f32[4096,16]{0,1:T(8,128)S(1)} %get-tuple-element.1341) | copy-start | bytes 786436
  591.9 506.5 %all-gather.32.cloned.1.call-start = ((), (), s32[]{:S(2)}) async-start(), calls=%async_computation.20 | async-start | bytes 1310720 | tf_op jit(solution)/shard_map/all_gather | solution.py:21
  592.6 65.8 %copy-start.5 = (f32[4096,16]{0,1:T(8,128)S(1)}, f32[4096,16]{0,1:T(8,128)}, u32[]{:S(2)}) copy-start(f32[4096,16]{0,1:T(8,128)} %copy-done.4) | copy-start | bytes 786436
  674.6 426.8 %all-gather.30.cloned.1.call-start = ((), (), s32[]{:S(2)}) async-start(), calls=%async_computation.19 | async-start | bytes 1310720 | tf_op jit(solution)/shard_map/all_gather | solution.py:21
  674.7 4.3 copy-start.6
  678.7 895.7 %reduce-scatter.18.cloned.1.call-start = ((), (), s32[]{:S(2)}) async-start(), calls=%async_computation.15 | async-start | bytes 20971520 | tf_op jit(solution)/shard_map/reduce_scatter | solution.py:333
  739.6 15.7 copy-start.35
  739.7 15.7 copy-start.41
  739.7 15.7 copy-start.80
  1213.9 195.1 %copy-start.12 = (bf16[64,4096]{1,0:T(8,128)(2,1)S(1)}, bf16[64,4096]{1,0:T(8,128)(2,1)}, u32[]{:S(2)}) copy-start(bf16[64,4096]{1,0:T(8,128)(2,1)} %copy-done.11) | copy-start | bytes 1572868
  1213.9 195.1 %copy-start.50 = (f32[4096]{0:T(1024)S(1)}, f32[4096]{0:T(1024)}, u32[]{:S(2)}) copy-start(f32[4096]{0:T(1024)} %convert_element_type.309) | copy-start | bytes 49156
  1409.1 6.5 copy-start.31
  1415.6 13.6 copy-start.15
  1448.1 363.8 %reduce-scatter.10.cloned.1.call-start = ((), (), s32[]{:S(2)}) async-start(), calls=%async_computation.11 | async-start | bytes 41943040 | tf_op jit(solution)/shard_map/reduce_scatter | solution.py:312
  1448.7 4.2 copy-start.37
  1452.3 5.1 copy-start.23
  1455.7 7.4 collective-permute-start.2
  1460.7 4.8 copy-start.2
  1460.7 4.8 copy-start.18
  1460.7 4.7 copy-start.34
  1460.7 4.7 copy-start.54
  1460.9 30.8 %copy-start.20 = (bf16[61,4096]{1,0:T(8,128)(2,1)}, bf16[61,4096]{1,0:T(8,128)(2,1)S(1)}, u32[]{:S(2)}) copy-start(bf16[61,4096]{1,0:T(8,128)(2,1)S(1)} %slice.5298) | copy-start | bytes 1499140
  1461.8 3.6 collective-permute-start.3
  1465.5 26.1 %copy-start.19 = (bf16[64,4096]{1,0:T(8,128)(2,1)S(1)}, bf16[64,4096]{1,0:T(8,128)(2,1)}, u32[]{:S(2)}) copy-start(bf16[64,4096]{1,0:T(8,128)(2,1)} %get-tuple-element.3213) | copy-start | bytes 1572868
  1465.5 26.1 %copy-start.52 = (f32[64]{0:T(128)S(1)}, f32[64]{0:T(128)}, u32[]{:S(2)}) copy-start(f32[64]{0:T(128)} %copy-done.51) | copy-start | bytes 772
  1525.4 363.1 %reduce-scatter.22.cloned.1.call-start = ((), (), s32[]{:S(2)}) async-start(), calls=%async_computation.21 | async-start | bytes 1310720
  1530.6 359.0 %reduce-scatter.16.cloned.1.call-start = ((), (), s32[]{:S(2)}) async-start(), calls=%async_computation.14 | async-start | bytes 1310720 | tf_op jit(solution)/shard_map/reduce_scatter | solution.py:324
  1533.7 362.4 %reduce-scatter.14.cloned.1.call-start = ((), (), s32[]{:S(2)}) async-start(), calls=%async_computation.13 | async-start | bytes 1638400 | tf_op jit(solution)/shard_map/reduce_scatter | solution.py:321
  1536.4 531.2 %reduce-scatter.20.cloned.1.call-start = ((), (), s32[]{:S(2)}) async-start(), calls=%async_computation.16 | async-start | bytes 9437184 | tf_op jit(solution)/shard_map/reduce_scatter | solution.py:339
  1581.1 772.8 %reduce-scatter.12.cloned.1.call-start = ((), (), s32[]{:S(2)}) async-start(), calls=%async_computation.12 | async-start | bytes 18874368 | tf_op jit(solution)/shard_map/reduce_scatter | solution.py:338
  1826.1 9.1 copy-start.16
  1835.2 9.8 copy-start.22
  1845.0 15.8 copy-start.21
  1860.8 26.4 %copy-start.32 = (bf16[2,64,2048]{2,1,0:T(8,128)(2,1)S(1)}, bf16[2,64,2048]{2,1,0:T(8,128)(2,1)}, u32[]{:S(2)}) copy-start(bf16[2,64,2048]{2,1,0:T(8,128)(2,1)} %param.47) | copy-start | bytes 1572868
  (53 other events, 137.8 us)
Sparse Core Ops, SparseCore 0:
  9.6 204.4 all-gather.17
  215.7 105.9 all-gather.23
  323.2 18.8 all-gather.19
  343.5 16.7 all-gather.21
  466.0 16.7 all-gather.27
  592.0 16.7 all-gather.25
  674.7 16.7 all-gather.31
  693.1 16.7 all-gather.29
  1448.2 126.1 reduce-scatter.17
  1577.0 234.8 reduce-scatter.9
  1814.6 24.8 reduce-scatter.21
  1841.9 24.8 reduce-scatter.15
  1869.5 26.5 reduce-scatter.13
  1900.2 167.2 reduce-scatter.19
  2072.2 281.5 reduce-scatter.11
where the time goes:
time: 2380 us; the launch traced here: 2360 us
  waiting for transfers between devices  901 us (38%)
  other arithmetic  841 us (35%)
  matrix products  225 us (9%)
  local copies, waits for them, and re-layouts  197 us (8%)
  blocking collectives  164 us (7%)
    reduce_scatter x1, waiting for transfers between devices, body(): lax.psum_scatter(shard_sums[1], 'replica', scatter_dimension=0, tiled=True)  286 us
    reduce_scatter x1, waiting for transfers between devices, body(): lax.psum_scatter(full_sums[1].astype(jnp.bfloat16), 'shard', scatter_dime...  231 us
    reduce_sum x72, other arithmetic, decay_of(): return (1.0 - rate_row[:, None] * (key_row * key_row)[None, :]) * keep_val  219 us
    all_gather x1, waiting for transfers between devices, body(): lax.all_gather(w_in, 'shard', axis=1, tiled=True)  172 us
    reduce_sum x72, other arithmetic, block_forward(): outputs.append(jnp.sum(carried * query_blk[t][None, :], axis=1))  157 us
    dot_general x8, matrix products, inner_dot(): lax.dot_general(first_op, second_op, (((0,), (0,)), ((), ())), preferred_...  100 us
    psum x1, blocking collectives, body(): lax.psum((shard_sums[0], shard_sums[2], shard_sums[3], shard_sums[4], sha...  98.4 us
    add x8, other arithmetic, block_forward(): decay_now * carried  92.3 us
  transfers between devices with their start and end apart: 19, of which 10 were waited for; matrix products, arithmetic and copies ran while one was open for 39% of the time, Pallas kernels for 0%

commit v1 on v0

v1 whole, which is shorter than its diff:
```python
import functools

import jax
import jax.numpy as jnp
from jax import lax
from jax.experimental import pallas as pl
from jax.experimental.pallas import tpu as pltpu
from jax.sharding import PartitionSpec as P

KW = 4
EPS = 1e-05
CHUNK = 16
LANES = 128
f32 = jnp.float32
bf16 = jnp.bfloat16


def rows_dot(a, b):
    return jnp.dot(a, b, preferred_element_type=f32)


def inner_dot(a, b):
    return lax.dot_general(a, b, (((0,), (0,)), ((), ())), preferred_element_type=f32)


def outer_dot(a, b):
    return lax.dot_general(a, b, (((1,), (1,)), ((), ())), preferred_element_type=f32)


def silu_slope(values):
    sig_val = jax.nn.sigmoid(values)
    return sig_val + values * sig_val * (1.0 - sig_val)


def recurrence_kernel(
    rate_ref, conv_ref, dy_ref, keyc_ref, queryc_ref, key_ref, keep_ref, qd_ref, kd_ref, k2d_ref,
    y_ref, grate_ref, gconv_ref, gkey_ref, gquery_ref,
    state, rk, u, dys, kept, adj, adj_state, diag1, diag2, diag3,
):
    length, width = rate_ref.shape[1:]
    n = keyc_ref.shape[2]
    groups = width // LANES
    span = CHUNK * n
    chunks = length // CHUNK

    def lane(g):
        return slice(g * LANES, (g + 1) * LANES)

    def prepare(base):
        rows = pl.ds(base, CHUNK)
        rate = rate_ref[0, rows, :]
        keep = keep_ref[0, rows, :]
        conv = conv_ref[0, rows, :].astype(f32)
        for g in range(groups):
            rk[:, lane(g)] = rate[:, lane(g)] * keep
        u[...] = rate * conv
        kept[...] = keep
        return rate, conv, keep

    def column(block, t):
        return jnp.broadcast_to(block[:, t : t + 1], (n, LANES))

    def row(ref, t, g):
        return jnp.broadcast_to(ref[t : t + 1, lane(g)], (n, LANES))

    state[0:n, :] = jnp.zeros((n, width), state.dtype)

    def forward(j, held):
        base = pl.multiple_of(j * CHUNK, CHUNK)
        prepare(base)
        keys = keyc_ref[0, j]
        held = list(held)
        for t in range(CHUNK):
            key = column(keys, t)
            key2 = key * key
            keep = jnp.broadcast_to(kept[t : t + 1, :], (n, LANES))
            at = pl.ds(pl.multiple_of((base + t + 1) * n, n), n)
            for g in range(groups):
                decay = keep - row(rk, t, g) * key2
                held[g] = decay * held[g] + row(u, t, g) * key
                state[at, lane(g)] = held[g].astype(bf16)
        block = state[pl.ds(pl.multiple_of(base * n + n, n), span), :]
        y_ref[0, pl.ds(base, CHUNK), :] = rows_dot(qd_ref[0, pl.ds(base, CHUNK), :], block)
        return tuple(held)

    zero = tuple(jnp.zeros((n, LANES), f32) for _ in range(groups))
    lax.fori_loop(0, chunks, forward, zero)

    mask = (
        lax.broadcasted_iota(jnp.int32, (CHUNK, span), 1) // n
        == lax.broadcasted_iota(jnp.int32, (CHUNK, span), 0)
    )

    def backward(step, held):
        j = chunks - 1 - step
        base = pl.multiple_of(j * CHUNK, CHUNK)
        rows = pl.ds(base, CHUNK)
        rate, conv, keeps = prepare(base)
        dys[...] = dy_ref[0, rows, :]
        keys = keyc_ref[0, j]
        queries = queryc_ref[0, j]
        held = list(held)
        for t in reversed(range(CHUNK)):
            key = column(keys, t)
            key2 = key * key
            query = column(queries, t)
            keep = jnp.broadcast_to(kept[t : t + 1, :], (n, LANES))
            at = pl.ds(pl.multiple_of((base + t) * n, n), n)
            for g in range(groups):
                grad = held[g] + row(dys, t, g) * query
                decay = keep - row(rk, t, g) * key2
                held[g] = decay * grad
                adj[t * n : (t + 1) * n, lane(g)] = grad.astype(bf16)
                before = state[at, lane(g)].astype(f32)
                adj_state[t * n : (t + 1) * n, lane(g)] = (grad * before).astype(bf16)
        block = state[pl.ds(pl.multiple_of(base * n + n, n), span), :]
        w1 = rows_dot(kd_ref[0, rows, :], adj[...])
        w2 = rows_dot(k2d_ref[0, rows, :], adj_state[...])
        a1 = outer_dot(u[...].astype(bf16), adj[...])
        a2 = outer_dot(rk[...].astype(bf16), adj_state[...])
        a3 = outer_dot(dys[...].astype(bf16), block)
        diag1[rows, :] = jnp.where(mask, a1, 0.0)
        diag2[rows, :] = jnp.where(mask, a2, 0.0)
        diag3[rows, :] = jnp.where(mask, a3, 0.0)
        keep_all = jnp.concatenate([keeps] * groups, axis=1)
        grate = conv * w1 - keep_all * w2
        grate_ref[0, rows, :] = grate
        gconv_ref[0, rows, :] = rate * w1
        return tuple(held)

    lax.fori_loop(0, chunks, backward, zero)

    pick = (
        lax.broadcasted_iota(jnp.int32, (span, n), 0) % n
        == lax.broadcasted_iota(jnp.int32, (span, n), 1)
    ).astype(bf16)

    def picked(ref):
        value = ref[...]
        high = value.astype(bf16)
        low = (value - high.astype(f32)).astype(bf16)
        return rows_dot(high, pick) + rows_dot(low, pick)

    rate = rate_ref[0]
    self_term = jnp.sum(grate_ref[0] * rate * rate, axis=1, keepdims=True)
    gkey_ref[0] = picked(diag1) - 2.0 * key_ref[0] * (picked(diag2) + self_term)
    gquery_ref[0] = picked(diag3)


def recurrence(rate, conv, dy, keys, queries, keep):
    seqs, length, width = rate.shape
    n = keys.shape[2]
    span = CHUNK * n
    chunks = length // CHUNK

    def chunked(values):
        return values.reshape(seqs, chunks, CHUNK, n).transpose(0, 1, 3, 2)

    spot = (jnp.arange(length)[:, None] % CHUNK == jnp.arange(span)[None, :] // n)

    def diagonal(values):
        return jnp.where(spot, jnp.tile(values, (1, 1, CHUNK)), 0.0).astype(bf16)

    keep_lanes = jnp.broadcast_to(keep[:, :, None], (seqs, length, LANES))

    def spec(*shape):
        return pl.BlockSpec((1,) + shape, lambda s: (s,) + (0,) * len(shape))

    wide = spec(length, width)
    small = spec(length, n)
    square = spec(length, span)
    chunk_spec = spec(chunks, n, CHUNK)
    return pl.pallas_call(
        recurrence_kernel,
        grid=(seqs,),
        in_specs=[wide, wide, wide, chunk_spec, chunk_spec, small, spec(length, LANES), square, square, square],
        out_specs=[wide, wide, wide, small, small],
        out_shape=[jax.ShapeDtypeStruct((seqs, length, width), f32)] * 3
        + [jax.ShapeDtypeStruct((seqs, length, n), f32)] * 2,
        scratch_shapes=[
            pltpu.VMEM(((length + 1) * n, width), bf16),
            pltpu.VMEM((CHUNK, width), f32),
            pltpu.VMEM((CHUNK, width), f32),
            pltpu.VMEM((CHUNK, width), f32),
            pltpu.VMEM((CHUNK, LANES), f32),
            pltpu.VMEM((span, width), bf16),
            pltpu.VMEM((span, width), bf16),
            pltpu.VMEM((length, span), f32),
            pltpu.VMEM((length, span), f32),
            pltpu.VMEM((length, span), f32),
        ],
        compiler_params=pltpu.CompilerParams(vmem_limit_bytes=56 << 20),
        name="recurrence",
    )(rate, conv, dy, chunked(keys), chunked(queries), keys, keep_lanes, diagonal(queries), diagonal(keys), diagonal(keys * keys))


def to_channels(cols):
    half = cols.shape[1] // 2
    me = lax.axis_index("shard")
    first, second = cols[:, :half], cols[:, half:]
    low = me < 2
    one = lax.ppermute(jnp.where(low, first, second), "shard", [(0, 0), (1, 2), (2, 1), (3, 3)])
    two = lax.ppermute(jnp.where(low, second, first), "shard", [(0, 1), (1, 3), (2, 0), (3, 2)])
    even = me % 2 == 0
    return jnp.where(even, one, two), jnp.where(even, two, one)


def to_columns(x_part, z_part):
    me = lax.axis_index("shard")
    even = me % 2 == 0
    one = lax.ppermute(jnp.where(even, x_part, z_part), "shard", [(0, 0), (2, 1), (1, 2), (3, 3)])
    two = lax.ppermute(jnp.where(even, z_part, x_part), "shard", [(1, 0), (3, 1), (0, 2), (2, 3)])
    low = me < 2
    return jnp.concatenate([jnp.where(low, one, two), jnp.where(low, two, one)], axis=1)


def body(
    block_input, segment_ids, norm_gain, w_in, conv_weight, conv_bias, x_proj, dt_proj, dt_bias,
    d_skip, out_proj, out_grad,
):
    seqs, local, model = block_input.shape
    length = segment_ids.shape[1]
    tokens = seqs * length
    width = d_skip.shape[0]
    rank = dt_proj.shape[0]
    n = (x_proj.shape[0] - rank) // 2
    me = lax.axis_index("shard")

    x_all = lax.all_gather(block_input, "shard", axis=1, tiled=True).reshape(tokens, model)
    cot = lax.all_to_all(out_grad, "shard", split_axis=2, concat_axis=1, tiled=True).reshape(tokens, -1)
    gain = lax.all_gather(norm_gain, "shard", axis=0, tiled=True).astype(f32)

    def normalise(rows):
        vals = rows.astype(f32)
        inv = lax.rsqrt(jnp.mean(vals * vals, axis=-1, keepdims=True) + EPS)
        return vals, inv

    x_vals, inv_rms = normalise(x_all)
    normed = (x_vals * inv_rms * gain).astype(bf16)
    mixed = rows_dot(normed, w_in).astype(bf16)
    x_part, z_part = to_channels(mixed)
    grad_gated = lax.psum_scatter(outer_dot(cot, out_proj).astype(bf16), "shard", scatter_dimension=1, tiled=True).astype(f32)

    def split(values):
        return values.reshape(seqs, length, -1)

    seg_padded = jnp.pad(segment_ids, ((0, 0), (KW - 1, 0)), constant_values=-1)
    taps = [
        (seg_padded[:, KW - 1 - d : KW - 1 - d + length] == segment_ids).astype(f32) for d in range(KW)
    ]
    conv_w = conv_weight.astype(f32)
    xs = split(x_part).astype(f32)
    x_padded = jnp.pad(xs, ((0, 0), (KW - 1, 0), (0, 0)))
    conv_pre = conv_bias.astype(f32) + conv_w[KW - 1] * xs
    for j in range(KW - 1):
        d = KW - 1 - j
        conv_pre = conv_pre + conv_w[j] * x_padded[:, j : j + length] * taps[d][:, :, None]
    conv_out = jax.nn.silu(conv_pre).astype(bf16)
    conv_vals = conv_out.astype(f32)
    conv_flat = conv_out.reshape(tokens, width)
    proj = lax.psum(outer_dot(conv_flat, x_proj), "shard")
    dt_low = proj[:, :rank].astype(bf16)
    keys = split(proj[:, rank : rank + n])
    queries = split(proj[:, rank + n :])
    beta = split(jax.nn.sigmoid(rows_dot(dt_low, dt_proj) + dt_bias.astype(f32)))
    key_square = jnp.sum(keys * keys, axis=2, keepdims=True)
    denom_inv = 1.0 / (1.0 + beta * key_square)
    rate = beta * denom_inv

    z_vals = split(z_part).astype(f32)
    gate = jax.nn.silu(z_vals)
    grad_gated = split(grad_gated)
    dy = grad_gated * gate
    recurrent, grad_rate, grad_conv_rec, grad_keys, grad_queries = recurrence(
        rate, conv_out, dy, keys, queries, taps[1]
    )
    skip = d_skip.astype(f32)
    y_total = recurrent + skip * conv_vals
    gated = (y_total * gate).astype(bf16).reshape(tokens, width)
    gated_all = lax.all_gather(gated, "shard", axis=1, tiled=True)
    cols = model // 4
    x_cols = lax.dynamic_slice_in_dim(x_all, me * cols, cols, 1).astype(f32)
    out_cols = (x_cols + rows_dot(gated_all, out_proj)).astype(bf16).reshape(seqs, length, cols)
    block_output = lax.all_to_all(out_cols, "shard", split_axis=1, concat_axis=2, tiled=True)
    grad_out_proj = lax.psum_scatter(
        inner_dot(gated_all, cot).astype(bf16), "replica", scatter_dimension=0, tiled=True
    ).astype(f32)

    grad_z = (grad_gated * y_total * silu_slope(z_vals)).astype(bf16)
    grad_d_skip = jnp.sum(dy * conv_vals, axis=(0, 1))
    grad_dt = grad_rate * denom_inv * denom_inv * beta * (1.0 - beta)
    grad_dt_bias = jnp.sum(grad_dt, axis=(0, 1))
    grad_dt_low = grad_dt.astype(bf16).reshape(tokens, width)
    grad_dt_proj = inner_dot(dt_low, grad_dt_low)
    grad_proj = jnp.concatenate(
        [outer_dot(grad_dt_low, dt_proj), grad_keys.reshape(tokens, n), grad_queries.reshape(tokens, n)], axis=1
    )
    grad_proj = lax.psum(grad_proj, "shard").astype(bf16)
    grad_x_proj = inner_dot(grad_proj, conv_flat)
    grad_conv = dy * skip + grad_conv_rec + split(rows_dot(grad_proj, x_proj))
    grad_pre = grad_conv * silu_slope(conv_pre)
    grad_conv_bias = jnp.sum(grad_pre, axis=(0, 1))
    grad_conv_weight = jnp.stack(
        [
            jnp.sum(grad_pre * x_padded[:, j : j + length] * taps[KW - 1 - j][:, :, None], axis=(0, 1))
            for j in range(KW)
        ]
    )
    grad_x = conv_w[KW - 1] * grad_pre
    for j in range(KW - 1):
        d = KW - 1 - j
        ahead = jnp.pad(grad_pre * taps[d][:, :, None], ((0, 0), (0, d), (0, 0)))[:, d:]
        grad_x = grad_x + conv_w[j] * ahead
    grad_mixed = to_columns(grad_x.astype(bf16).reshape(tokens, width), grad_z.reshape(tokens, width))
    grad_w_in = lax.psum_scatter(
        inner_dot(normed, grad_mixed).astype(bf16), "replica", scatter_dimension=0, tiled=True
    ).astype(f32)
    grad_normed = lax.psum_scatter(
        split(outer_dot(grad_mixed, w_in)).astype(bf16), "shard", scatter_dimension=1, tiled=True
    ).astype(f32)
    x_own, inv_own = normalise(block_input)
    grad_gain = jnp.sum(grad_normed * x_own * inv_own, axis=(0, 1))
    scaled = grad_normed * gain
    grad_in = inv_own * (
        scaled - x_own * inv_own * inv_own * jnp.mean(scaled * x_own, axis=-1, keepdims=True)
    )
    input_grad = (out_grad.astype(f32) + grad_in).astype(bf16)

    small = jnp.concatenate(
        [
            grad_x_proj, grad_dt_proj, grad_conv_weight, grad_conv_bias[None], grad_dt_bias[None],
            grad_d_skip[None],
        ]
    )
    small = lax.psum(small.astype(bf16), "replica").astype(f32)
    grad_gain = lax.psum_scatter(lax.psum(grad_gain, "replica"), "shard", scatter_dimension=0, tiled=True)
    top = x_proj.shape[0]
    return (
        block_output, input_grad, grad_gain, grad_w_in,
        small[top + rank : top + rank + KW], small[top + rank + KW], small[:top], small[top : top + rank],
        small[top + rank + KW + 1], small[top + rank + KW + 2], grad_out_proj,
    )


def solution(mesh):
    return jax.shard_map(
        body,
        mesh=mesh,
        in_specs=(
            P("replica", "shard", None), P("replica", None), P("shard"), P(None, "shard"), P(None, "shard"),
            P("shard"), P(None, "shard"), P(None, "shard"), P("shard"), P("shard"), P(None, "shard"),
            P("replica", "shard", None),
        ),
        out_specs=(
            P("replica", "shard", None), P("replica", "shard", None), P("shard"), P("replica", "shard"),
            P(None, "shard"), P("shard"), P(None, "shard"), P(None, "shard"), P("shard"), P("shard"),
            P("replica", "shard"),
        ),
        check_vma=False,
    )
```

time: 2380 us -> 665 us (0.28)
  other arithmetic: 841 us -> 43.4 us
  waiting for transfers between devices: 901 us -> 397 us
  matrix products: 225 us -> 52 us
  local copies, waits for them, and re-layouts: 197 us -> 28.7 us
  blocking collectives: 164 us -> 64.4 us
  Pallas kernels: 0 us -> 53.7 us
    reduce_scatter x6 -> x4, waiting for transfers between devices: 635 us -> 218 us  [the longest x1 150 us: body(): lax.psum_scatter(inner_dot(normed, grad_mixed).astype(bf16), 'replica', s...]
    reduce_sum x146 -> x6, other arithmetic: 380 us -> 21.4 us  [the longest x1 8.44 us: body(): grad_conv_bias = jnp.sum(grad_pre, axis=(0, 1))]
    all_gather x8 -> x2, waiting for transfers between devices: 262 us -> 0.04 us  [the longest x1 0.02 us: body(): lax.all_gather(block_input, 'shard', axis=1, tiled=True)]
    mul x570 -> x3, other arithmetic: 209 us -> 3.95 us  [the longest x1 2.22 us: body(): grad_pre * taps[d][:, :, None]]
    add x22 -> x0, other arithmetic: 189 us -> none  [the longest x8 92.3 us: block_forward(): decay_now * carried]
    dot_general x24 -> x12, matrix products: 225 us -> 52 us  [the longest x4 18.9 us: outer_dot(): lax.dot_general(a, b, (((1,), (1,)), ((), ())), preferred_element_type=f32)]
    slice x81 -> x6, local copies, waits for them, and re-layouts: 113 us -> 6.56 us  [the longest x1 1.87 us: body(): small[:top]]
    ppermute x4, waiting for transfers between devices: 2.29 us -> 87.8 us  [the longest x1 47.4 us: to_channels(): lax.ppermute(jnp.where(low, second, first), 'shard', [(0, 1), (1, 3), (2,...]
  transfers between devices with their start and end apart: 19 -> 13, of which waited for: 10 -> 8; matrix products, arithmetic and copies ran while one was open for 39% -> 12% of each run, Pallas kernels for 0% -> 0%
where the time goes in v1:
time: 665 us; the launch traced here: 663 us
  waiting for transfers between devices  397 us (60%)
  blocking collectives  64.4 us (10%)
  Pallas kernels  53.7 us (8%)
  matrix products  52 us (8%)
  other arithmetic  43.4 us (7%)
  local copies, waits for them, and re-layouts  28.7 us (4%)
  between operations  15.6 us (2%)
  starting transfers between devices  8.53 us (1%)
    reduce_scatter x1, waiting for transfers between devices, body(): lax.psum_scatter(inner_dot(normed, grad_mixed).astype(bf16), 'replica', s...  150 us
    pallas_call x1, Pallas kernels, recurrence(): pl.pallas_call(recurrence_kernel, grid=(seqs,), in_specs=[wide, wide, wid...  53.7 us
    psum x1, waiting for transfers between devices, body(): small = lax.psum(small.astype(bf16), 'replica').astype(f32)  49.4 us
    ppermute x1, waiting for transfers between devices, to_channels(): lax.ppermute(jnp.where(low, second, first), 'shard', [(0, 1), (1, 3), (2,...  47.4 us
    reduce_scatter x1, waiting for transfers between devices, body(): lax.psum_scatter(inner_dot(gated_all, cot).astype(bf16), 'replica', scatt...  40.8 us
    ppermute x1, waiting for transfers between devices, to_columns(): lax.ppermute(jnp.where(even, z_part, x_part), 'shard', [(1, 0), (3, 1), (...  40.4 us
    psum x1, waiting for transfers between devices, body(): proj = lax.psum(outer_dot(conv_flat, x_proj), 'shard')  33 us
    reduce_scatter x1, waiting for transfers between devices, body(): lax.psum_scatter(split(outer_dot(grad_mixed, w_in)).astype(bf16), 'shard'...  27.3 us
  transfers between devices with their start and end apart: 13, of which 8 were waited for; matrix products, arithmetic and copies ran while one was open for 12% of the time, Pallas kernels for 0%

profile of v1, /device:TPU:0, one launch (start us, length us, event | category | flops | bytes accessed | tf_op | source)
XLA Modules:
  0.0 663.5 jit_solution(17002286347579974088)
XLA Ops:
  8.0 2.4 copy.53
  10.3 0.9 reshape.209
  11.2 15.1 %all_to_all.33 = bf16[4,2,32768]{2,1,0:T(2,128)(2,1)S(1)} all-to-all(bf16[4,2,32768]{2,1,0:T(2,128)(2,1)S(1)} %reshape.209), channel_id=1, replica_groups=mesh['replica'=8,'shard'=4] {'shard'}, dimensions={0} | all-to-all | bytes 1048576 | tf_op jit(solution)/shard_map/all_to_all | solution.py:230
  26.3 0.7 reshape.210
  27.0 0.9 copy.69
  28.0 0.8 copy-done.23
  28.8 6.6 %convolution_convert_fusion.2 = bf16[512,4096]{1,0:T(8,128)(2,1)} fusion(bf16[512,512]{1,0:T(8,128)(2,1)S(1)} %bitcast.103, bf16[4096,512]{1,0:T(8,128)(2,1)} %param.22), kind=kOutput, calls=%fused_computation.2 | convolution fusion | flops 2149580800 | bytes 8912896 | tf_op jit(solution)/shard_map/dot_general | solution.py:27
  36.1 5.1 all-gather
  41.3 2.2 multiply_reduce_fusion
  43.6 9.1 %convolution_convert_fusion.4 = bf16[512,2048]{1,0:T(8,128)(2,1)S(1)} fusion(bf16[2048,2048]{1,0:T(8,128)(2,1)} %param.15, bf16[512,2048]{1,0:T(8,128)(2,1)S(1)} %bitcast.94, f32[2048]{0:T(1024)S(1)} %bitcast.109, f32[512]{0:T(512)S(1)} %bitcast.125), kind=kOutput, calls=%fused_computation.7 | convolution fusion | flops 4300210176 | bytes 12593152 | tf_op jit(solution)/shard_map/dot_general | solution.py:19
  53.0 0.7 collective-permute-start
  53.7 1.7 collective-permute-start.1
  56.2 47.4 %collective-permute-done.1 = bf16[512,1024]{1,0:T(8,128)(2,1)} collective-permute-done((bf16[512,1024]{1,0:T(8,128)(2,1)S(1)}, bf16[512,1024]{1,0:T(8,128)(2,1)}, u32[]{:S(2)}, u32[]{:S(2)}) %collective-permute-start.1) | collective-permute-done | bytes 1048608 | tf_op jit(solution)/shard_map/ppermute | solution.py:203
  103.6 2.4 bitcast_convert_fusion
  106.0 6.3 fusion.8
  112.3 1.2 fusion.45
  113.9 33.0 %all-reduce.10.cloned.1.call-done = f32[512,160]{0,1:T(8,128)} async-done(((f32[512,160]{0,1:T(8,128)}), f32[512,160]{0,1:T(8,128)}) %all-reduce.10.cloned.1.call-update) | async-done | bytes 327696 | tf_op jit(solution)/shard_map/psum | solution.py:261
  147.0 0.8 fusion.43
  148.9 1.1 copy_bitcast_fusion
  150.0 0.7 add_divide_fusion.1
  150.7 1.7 fusion.16.rate_ref
  152.5 1.0 select_convert_fusion
  153.4 0.8 broadcast_in_dim.27.keep_ref
  154.2 53.7 %recurrence.1 = (f32[2,256,1024]{2,1,0:T(8,128)}, f32[2,256,1024]{2,1,0:T(8,128)}, f32[2,256,1024]{2,1,0:T(8,128)}, f32[2,256,16]{2,1,0:T(8,128)}, f32[2,256,16]{2,1,0:T(8,128)}) custom-call(f32[2,256,1024]{2,1,0:T(8,128)} %fusion.16.rate_ref, bf16[2,256,1024]{2,1,0:T(8,128)(2,1)} %copy-done.2, f32[2,256,1024]{2,1,0:T(8,128)} %get-tuple-element.32.dy_ref, ...), custom_call_target="tpu_custom_call" | custom-call | tf_op jit(solution)/shard_map/recurrence/pallas_call | solution.py:173
  207.9 2.9 fusion.38
  210.8 1.2 fusion.46
  212.0 1.2 copy.67
  213.2 1.1 copy.68
  214.3 1.7 pad_maximum_fusion.3
  216.0 15.3 %all-reduce.13 = bf16[512,160]{0,1:T(8,128)(2,1)} all-reduce(f32[512,160]{0,1:T(8,128)} %pad_maximum_fusion.3), channel_id=1, replica_groups=mesh['replica'=8,'shard'=4] {'shard'}, use_global_device_ids=true, to_apply=%region_5.6 | all-reduce | flops 81920 | bytes 491520 | tf_op jit(solution)/shard_map/psum | solution.py:298
  231.3 1.5 fusion.47
  232.9 8.4 %fusion.36 = (bf16[1024]{0:T(1024)(128)(2,1)S(1)}, bf16[1024]{0:T(1024)(128)(2,1)S(1)}, bf16[1024]{0:T(1024)(128)(2,1)S(1)}, bf16[1024]{0:T(1024)(128)(2,1)S(1)}...) fusion(bf16[512,1024]{1,0:T(8,128)(2,1)} %copy-done.15, ...), kind=kLoop, calls=%fused_computation.110 | loop fusion | flops 18344960 | bytes 19943424 | tf_op jit(solution)/shard_map/reduce_sum | solution.py:302
  241.5 2.2 broadcast_multiply_fusion.2
  243.9 0.7 copy-done.12
  244.8 2.3 broadcast_select_fusion.1
  247.2 1.1 broadcast_select_fusion
  248.6 1.6 collective-permute-start.2
  251.0 2.8 concatenate.12
  254.1 40.4 %collective-permute-done.3 = bf16[512,1024]{1,0:T(8,128)(2,1)} collective-permute-done((bf16[512,1024]{1,0:T(8,128)(2,1)}, bf16[512,1024]{1,0:T(8,128)(2,1)}, u32[]{:S(2)}, u32[]{:S(2)}) %collective-permute-start.3) | collective-permute-done | bytes 1048608 | tf_op jit(solution)/shard_map/ppermute | solution.py:212
  294.5 1.7 broadcast_select_fusion.3
  296.2 9.8 %convolution_convert_fusion.3 = bf16[512,2048]{1,0:T(8,128)(2,1)} fusion(bf16[2048,2048]{1,0:T(8,128)(2,1)} %param.15, bf16[512,1024]{1,0:T(8,128)(2,1)S(1)} %get-tuple-element.42, bf16[512,1024]{1,0:T(8,128)(2,1)S(1)} %get-tuple-element.41), kind=kOutput, calls=%fused_computation.6 | convolution fusion | flops 4300210176 | bytes 12582912 | tf_op jit(solution)/shard_map/dot_general | solution.py:27
  306.2 0.9 copy-done.24
  307.1 6.5 convolution_convert_fusion.1
  313.8 1.5 copy-done.19
  315.3 8.6 %convolution_convert_fusion = bf16[2048,2048]{1,0:T(8,128)(2,1)} fusion(bf16[512,1024]{1,0:T(8,128)(2,1)} %copy-done.22, bf16[512,1024]{1,0:T(8,128)(2,1)} %copy-done.21, bf16[512,2048]{1,0:T(8,128)(2,1)S(1)} %bitcast.95, f32[2048]{0:T(1024)S(1)} %bitcast.110, f32[512]{0:T(512)S(1)} %bitcast.126), kind=kOutput, calls=%fused_computation | convolution fusion | flops 4307550208 | bytes 12593152 | tf_op jit(solution)/shard_map/dot_general | solution.py:23
  326.0 49.4 %all-reduce.12.cloned.1.call-done = bf16[295,1024]{1,0:T(8,128)(2,1)} async-done(((bf16[295,1024]{1,0:T(8,128)(2,1)}), bf16[295,1024]{1,0:T(8,128)(2,1)}) %all-reduce.12.cloned.1.call-update) | async-done | bytes 604176 | tf_op jit(solution)/shard_map/psum | solution.py:335
  375.3 1.9 slice.117
  377.2 1.8 slice.118
  379.0 1.3 slice.115
  380.3 1.4 fusion.42
  381.7 27.3 %reduce-scatter.7.cloned.1.call-done = bf16[2,64,2048]{2,1,0:T(8,128)(2,1)} async-done(((bf16[2,256,2048]{2,1,0:T(8,128)(2,1)}), bf16[2,64,2048]{2,1,0:T(8,128)(2,1)}) %reduce-scatter.7.cloned.1.call-update) | async-done | bytes 524304 | tf_op jit(solution)/shard_map/reduce_scatter | solution.py:318
  409.1 1.4 fusion.29
  410.4 5.9 all-reduce.5
  416.4 23.0 %psum.32 = f32[512]{0:T(512)} all-reduce(f32[512]{0:T(512)S(1)} %dynamic-slice.1), channel_id=1, replica_groups=mesh['replica'=8,'shard'=4] {'replica'}, use_global_device_ids=true, to_apply=%region_9.10 | all-reduce | flops 512 | bytes 4096 | tf_op jit(solution)/shard_map/psum | solution.py:336
  439.4 6.0 fusion.19
  445.4 1.3 copy.65
  446.7 3.5 all-to-all-start.1
  450.2 1.2 fusion.23
  451.4 7.6 %all-to-all-done.1 = bf16[2,256,512]{2,0,1:T(2,128)(2,1)S(1)} async-done(((bf16[2,256,512]{2,0,1:T(2,128)(2,1)}), bf16[2,256,512]{2,0,1:T(2,128)(2,1)S(1)}, u32[]{:S(2)}, u32[]{:S(2)}) %all-to-all-start.1) | async-done | bytes 524320 | tf_op jit(solution)/shard_map/all_to_all | solution.py:284
  459.4 1.2 all_to_all.30
  460.6 40.8 %reduce-scatter.11.cloned.1.call-done = bf16[512,512]{1,0:T(8,128)(2,1)} async-done(((bf16[4096,512]{1,0:T(8,128)(2,1)}), bf16[512,512]{1,0:T(8,128)(2,1)}) %reduce-scatter.11.cloned.1.call-update) | async-done | bytes 524304 | tf_op jit(solution)/shard_map/reduce_scatter | solution.py:285
  501.4 2.1 convert_element_type.173
  503.6 150.3 %reduce-scatter.9.cloned.1.call-done = bf16[256,2048]{1,0:T(8,128)(2,1)} async-done(((bf16[2048,2048]{1,0:T(8,128)(2,1)}), bf16[256,2048]{1,0:T(8,128)(2,1)}) %reduce-scatter.9.cloned.1.call-update) | async-done | bytes 1048592 | tf_op jit(solution)/shard_map/reduce_scatter | solution.py:315
  653.9 2.8 convert_element_type.170
  (160 shorter events, 7.8 us)
Async XLA Ops:
  7.2 105.2 %copy-start = (bf16[160,1024]{1,0:T(8,128)(2,1)S(1)}, bf16[160,1024]{1,0:T(8,128)(2,1)}, u32[]{:S(2)}) copy-start(bf16[160,1024]{1,0:T(8,128)(2,1)} %param.18) | copy-start | bytes 983044
  7.2 34.1 %all-gather.4.cloned.1.call-start = ((), (), s32[]{:S(2)}) async-start(), calls=%async_computation.6 | async-start | bytes 2621440 | tf_op jit(solution)/shard_map/all_gather | solution.py:229
  7.9 98.0 %reduce-scatter.5.cloned.1.call-start = ((), (), s32[]{:S(2)}) async-start(), calls=%async_computation.8 | async-start | bytes 5242880 | tf_op jit(solution)/shard_map/reduce_scatter | solution.py:242
  28.0 0.8 copy-start.23
  35.5 0.7 copy-start.48
  35.5 111.5 %all-reduce.10.cloned.1.call-start = ((), (), s32[]{:S(2)}) async-start(), calls=%async_computation.7 | async-start | bytes 655360 | tf_op jit(solution)/shard_map/psum | solution.py:261
  41.3 2.3 copy-start.18
  43.6 9.2 %copy-start.45 = (f32[1,2,2,128]{3,1,2,0:T(2,128)}, f32[1,2,2,128]{3,1,2,0:T(2,128)S(1)}, u32[]{:S(2)}) copy-start(f32[1,2,2,128]{3,1,2,0:T(2,128)S(1)} %copy.71) | copy-start | bytes 6148
  52.8 2.6 copy-start.42
  52.8 2.6 copy-start.43
  52.8 2.6 copy-start.44
  52.8 3.2 copy-start.47
  52.8 3.3 copy-start.39
  53.0 3.2 collective-permute-start
  53.7 49.8 %collective-permute-start.1 = (bf16[512,1024]{1,0:T(8,128)(2,1)S(1)}, bf16[512,1024]{1,0:T(8,128)(2,1)}, u32[]{:S(2)}, u32[]{:S(2)}) collective-permute-start(bf16[512,1024]{1,0:T(8,128)(2,1)S(1)} %get-tuple-element.49), channel_id=1, source_target_pairs={{0,1},{1,3},{2,0},{3,2},{4,5},{5,7},{6,4},{7,6},{8,9},{9,11},{10,8... | collective-permute-start | bytes 3145736 | tf_op jit(solution)/shard_map/ppermute | solution.py:203
  56.1 49.9 %copy-start.35 = (f32[2,256]{1,0:T(2,128)}, f32[2,256]{1,0:T(2,128)S(1)}, u32[]{:S(2)}) copy-start(f32[2,256]{1,0:T(2,128)S(1)} %get-tuple-element.64) | copy-start | bytes 6148
  56.1 49.9 %copy-start.37 = (f32[2,256]{1,0:T(2,128)}, f32[2,256]{1,0:T(2,128)S(1)}, u32[]{:S(2)}) copy-start(f32[2,256]{1,0:T(2,128)S(1)} %get-tuple-element.66) | copy-start | bytes 6148
  56.1 49.8 %copy-start.28 = (f32[1,1024]{1,0:T(1,128)}, f32[1,1024]{1,0:T(1,128)S(1)}, u32[]{:S(2)}) copy-start(f32[1,1024]{1,0:T(1,128)S(1)} %get-tuple-element.60) | copy-start | bytes 12292
  56.2 49.8 %copy-start.30 = (f32[1,1024]{1,0:T(1,128)}, f32[1,1024]{1,0:T(1,128)S(1)}, u32[]{:S(2)}) copy-start(f32[1,1024]{1,0:T(1,128)S(1)} %get-tuple-element.61) | copy-start | bytes 12292
  56.2 49.8 %copy-start.32 = (f32[1,1024]{1,0:T(1,128)}, f32[1,1024]{1,0:T(1,128)S(1)}, u32[]{:S(2)}) copy-start(f32[1,1024]{1,0:T(1,128)S(1)} %get-tuple-element.62) | copy-start | bytes 12292
  56.2 49.8 %copy-start.15 = (bf16[512,1024]{1,0:T(8,128)(2,1)}, bf16[512,1024]{1,0:T(8,128)(2,1)S(1)}, u32[]{:S(2)}) copy-start(bf16[512,1024]{1,0:T(8,128)(2,1)S(1)} %collective-permute-done) | copy-start | bytes 3145732
  106.0 6.4 copy-start.5
  112.3 35.9 %copy-start.2 = (bf16[2,256,1024]{2,1,0:T(8,128)(2,1)}, bf16[2,256,1024]{2,1,0:T(8,128)(2,1)S(1)}, u32[]{:S(2)}) copy-start(bf16[2,256,1024]{2,1,0:T(8,128)(2,1)S(1)} %get-tuple-element.33.conv_ref) | copy-start | bytes 3145732
  113.6 192.6 %all-gather.6.cloned.1.call-start = ((), (), s32[]{:S(2)}) async-start(), calls=%async_computation.9 | async-start | bytes 5242880 | tf_op jit(solution)/shard_map/all_gather | solution.py:280
  147.9 2.1 copy-start.13
  148.0 2.0 copy-start.25
  148.0 2.0 copy-start.27
  210.8 1.2 copy-start.9
  212.0 20.8 %copy-start.3 = (bf16[2,256,1024]{2,1,0:T(8,128)(2,1)S(1)}, bf16[2,256,1024]{2,1,0:T(8,128)(2,1)}, u32[]{:S(2)}) copy-start(bf16[2,256,1024]{2,1,0:T(8,128)(2,1)} %copy-done.2) | copy-start | bytes 3145732
  212.0 20.8 %copy-start.4 = (f32[2,256,1024]{2,1,0:T(8,128)S(1)}, f32[2,256,1024]{2,1,0:T(8,128)}, u32[]{:S(2)}) copy-start(f32[2,256,1024]{2,1,0:T(8,128)} %get-tuple-element.32.dy_ref) | copy-start | bytes 6291460
  216.0 16.8 %copy-start.34 = (f32[1024]{0:T(1024)S(1)}, f32[1024]{0:T(1024)}, u32[]{:S(2)}) copy-start(f32[1024]{0:T(1024)} %convert_element_type.155) | copy-start | bytes 12292
  231.3 1.5 copy-start.7
  232.8 8.5 %copy-start.36 = (f32[2,256]{1,0:T(2,128)S(1)}, f32[2,256]{1,0:T(2,128)}, u32[]{:S(2)}) copy-start(f32[2,256]{1,0:T(2,128)} %copy-done.35) | copy-start | bytes 6148
  232.9 8.5 %copy-start.38 = (f32[2,256]{1,0:T(2,128)S(1)}, f32[2,256]{1,0:T(2,128)}, u32[]{:S(2)}) copy-start(f32[2,256]{1,0:T(2,128)} %copy-done.37) | copy-start | bytes 6148
  241.3 134.0 %all-reduce.12.cloned.1.call-start = ((), (), s32[]{:S(2)}) async-start(), calls=%async_computation.12 | async-start | bytes 1212416 | tf_op jit(solution)/shard_map/psum | solution.py:335
  241.4 2.3 copy-start.6
  241.4 2.5 copy-start.8
  241.4 3.2 copy-start.12
  241.4 3.4 copy-start.14
  241.4 3.4 copy-start.29
  241.4 3.4 copy-start.31
  241.5 3.4 copy-start.33
  247.2 3.1 copy-start.40
  247.2 3.1 copy-start.41
  247.2 3.1 copy-start.20
  247.2 3.5 copy-start.10
  247.2 3.5 copy-start.26
  248.3 46.2 %collective-permute-start.3 = (bf16[512,1024]{1,0:T(8,128)(2,1)}, bf16[512,1024]{1,0:T(8,128)(2,1)}, u32[]{:S(2)}, u32[]{:S(2)}) collective-permute-start(bf16[512,1024]{1,0:T(8,128)(2,1)} %bitcast.32), channel_id=1, source_target_pairs={{1,0},{3,1},{0,2},{2,3},{5,4},{7,5},{4,6},{6,7},{9,8},{11,9},{8,10... | collective-permute-start | bytes 3145736 | tf_op jit(solution)/shard_map/ppermute | solution.py:212
  248.6 45.9 %collective-permute-start.2 = (bf16[512,1024]{1,0:T(8,128)(2,1)S(1)}, bf16[512,1024]{1,0:T(8,128)(2,1)}, u32[]{:S(2)}, u32[]{:S(2)}) collective-permute-start(bf16[512,1024]{1,0:T(8,128)(2,1)S(1)} %bitcast.99), channel_id=1, source_target_pairs={{0,0},{2,1},{1,2},{3,3},{4,4},{6,5},{5,6},{7,7},{8,8},{10,9},{9,10... | collective-permute-start | bytes 3145736 | tf_op jit(solution)/shard_map/ppermute | solution.py:211
  253.8 155.3 %reduce-scatter.7.cloned.1.call-start = ((), (), s32[]{:S(2)}) async-start(), calls=%async_computation.10 | async-start | bytes 2621440 | tf_op jit(solution)/shard_map/reduce_scatter | solution.py:318
  296.2 9.9 %copy-start.21 = (bf16[512,1024]{1,0:T(8,128)(2,1)}, bf16[512,1024]{1,0:T(8,128)(2,1)S(1)}, u32[]{:S(2)}) copy-start(bf16[512,1024]{1,0:T(8,128)(2,1)S(1)} %get-tuple-element.41) | copy-start | bytes 3145732
  296.2 9.9 %copy-start.22 = (bf16[512,1024]{1,0:T(8,128)(2,1)}, bf16[512,1024]{1,0:T(8,128)(2,1)S(1)}, u32[]{:S(2)}) copy-start(bf16[512,1024]{1,0:T(8,128)(2,1)S(1)} %get-tuple-element.42) | copy-start | bytes 3145732
  306.1 1.0 copy-start.24
  306.1 195.3 %reduce-scatter.11.cloned.1.call-start = ((), (), s32[]{:S(2)}) async-start(), calls=%async_computation.13 | async-start | bytes 4718592 | tf_op jit(solution)/shard_map/reduce_scatter | solution.py:285
  313.7 1.6 copy-start.19
  313.7 1.6 copy-start.46
  313.7 340.1 %reduce-scatter.9.cloned.1.call-start = ((), (), s32[]{:S(2)}) async-start(), calls=%async_computation.11 | async-start | bytes 9437184 | tf_op jit(solution)/shard_map/reduce_scatter | solution.py:315
  323.9 0.7 copy-start.49
  323.9 1.9 copy-start.11
  445.3 4.8 copy-start.16
  445.4 4.8 copy-start.17
  446.7 12.3 %all-to-all-start.1 = ((bf16[2,256,512]{2,0,1:T(2,128)(2,1)}), bf16[2,256,512]{2,0,1:T(2,128)(2,1)S(1)}, u32[]{:S(2)}, u32[]{:S(2)}) async-start(bf16[2,256,512]{2,0,1:T(2,128)(2,1)} %copy.65), calls=%async_computation.2 | async-start | bytes 1048576 | tf_op jit(solution)/shard_map/all_to_all | solution.py:284
  459.4 197.2 %copy-start.1 = (bf16[160,1024]{1,0:T(8,128)(2,1)S(1)}, bf16[160,1024]{1,0:T(8,128)(2,1)}, u32[]{:S(2)}) copy-start(bf16[160,1024]{1,0:T(8,128)(2,1)} %param.18) | copy-start | bytes 983044
Sparse Core Ops, SparseCore 0:
  9.6 27.1 all-gather.3
  39.3 56.1 reduce-scatter.4
  113.7 33.2 all-reduce.9
  241.4 54.2 all-gather.5
  300.0 75.2 all-reduce.11
  378.3 30.7 reduce-scatter.6
  413.1 88.2 reduce-scatter.10
  505.0 148.7 reduce-scatter.8

commit v2 on v1

v2 whole, which is shorter than its diff:
```python
import functools

import jax
import jax.numpy as jnp
from jax import lax
from jax.experimental import pallas as pl
from jax.experimental.pallas import tpu as pltpu
from jax.sharding import PartitionSpec as P

KW = 4
EPS = 1e-05
CHUNK = 16
LANES = 128
f32 = jnp.float32
bf16 = jnp.bfloat16


def rows_dot(a, b):
    return jnp.dot(a, b, preferred_element_type=f32)


def inner_dot(a, b):
    return lax.dot_general(a, b, (((0,), (0,)), ((), ())), preferred_element_type=f32)


def outer_dot(a, b):
    return lax.dot_general(a, b, (((1,), (1,)), ((), ())), preferred_element_type=f32)


def silu_slope(values):
    sig_val = jax.nn.sigmoid(values)
    return sig_val + values * sig_val * (1.0 - sig_val)

MESH = pl.DeviceIdType.MESH
BLOCK = 64


def lane(g):
    return slice(g * LANES, (g + 1) * LANES)


def column(block, t):
    return jnp.broadcast_to(block[:, t : t + 1], (block.shape[0], LANES))


def row(ref, t, g, n):
    return jnp.broadcast_to(ref[t : t + 1, lane(g)], (n, LANES))


def prepare(base, rate_ref, conv_ref, keep_ref, rk, u, kept):
    rows = pl.ds(base, CHUNK)
    rate = rate_ref[0, rows, :]
    keep = keep_ref[0, rows, :]
    conv = conv_ref[0, rows, :].astype(f32)
    for g in range(rate.shape[1] // LANES):
        rk[:, lane(g)] = rate[:, lane(g)] * keep
    u[...] = rate * conv
    kept[...] = keep
    return rate, conv, keep


def forward_kernel(rate_ref, conv_ref, keyc_ref, keep_ref, qd_ref, y_ref, state_ref, held_ref, rk, u, kept):
    width = rate_ref.shape[2]
    n = keyc_ref.shape[2]
    groups = width // LANES
    span = CHUNK * n

    @pl.when(pl.program_id(1) == 0)
    def _():
        held_ref[...] = jnp.zeros_like(held_ref)

    def chunk(j, held):
        base = pl.multiple_of(j * CHUNK, CHUNK)
        prepare(base, rate_ref, conv_ref, keep_ref, rk, u, kept)
        keys = keyc_ref[0, j]
        held = list(held)
        for t in range(CHUNK):
            key = column(keys, t)
            key2 = key * key
            keep = jnp.broadcast_to(kept[t : t + 1, :], (n, LANES))
            at = pl.ds(pl.multiple_of((base + t) * n, n), n)
            for g in range(groups):
                decay = keep - row(rk, t, g, n) * key2
                held[g] = decay * held[g] + row(u, t, g, n) * key
                state_ref[0, at, lane(g)] = held[g].astype(bf16)
        block = state_ref[0, pl.ds(pl.multiple_of(base * n, span), span), :]
        y_ref[0, pl.ds(base, CHUNK), :] = rows_dot(qd_ref[0, pl.ds(base, CHUNK), :], block)
        return tuple(held)

    start = tuple(held_ref[:, lane(g)] for g in range(groups))
    end = lax.fori_loop(0, rate_ref.shape[1] // CHUNK, chunk, start)
    for g in range(groups):
        held_ref[:, lane(g)] = end[g]


def backward_kernel(
    rate_ref, conv_ref, dy_ref, keyc_ref, queryc_ref, key_ref, keep_ref, kd_ref, k2d_ref, state_ref, last_ref,
    grate_ref, gconv_ref, gkey_ref, gquery_ref,
    held_ref, rk, u, dys, kept, adj, adj_state, diag1, diag2, diag3,
):
    block_rows, width = rate_ref.shape[1:]
    n = keyc_ref.shape[2]
    groups = width // LANES
    span = CHUNK * n
    chunks = block_rows // CHUNK

    @pl.when(pl.program_id(1) == 0)
    def _():
        held_ref[...] = jnp.zeros_like(held_ref)

    mask = (
        lax.broadcasted_iota(jnp.int32, (CHUNK, span), 1) // n
        == lax.broadcasted_iota(jnp.int32, (CHUNK, span), 0)
    )

    def chunk(step, held):
        j = chunks - 1 - step
        base = pl.multiple_of(j * CHUNK, CHUNK)
        rows = pl.ds(base, CHUNK)
        rate, conv, keeps = prepare(base, rate_ref, conv_ref, keep_ref, rk, u, kept)
        dys[...] = dy_ref[0, rows, :]
        keys = keyc_ref[0, j]
        queries = queryc_ref[0, j]
        held = list(held)
        for t in reversed(range(CHUNK)):
            key = column(keys, t)
            key2 = key * key
            query = column(queries, t)
            keep = jnp.broadcast_to(kept[t : t + 1, :], (n, LANES))
            prior = jnp.maximum(base + t - 1, 0)
            at = pl.ds(pl.multiple_of(prior * n, n), n)
            for g in range(groups):
                grad = held[g] + row(dys, t, g, n) * query
                decay = keep - row(rk, t, g, n) * key2
                held[g] = decay * grad
                adj[t * n : (t + 1) * n, lane(g)] = grad.astype(bf16)
                before = state_ref[0, at, lane(g)].astype(f32)
                if t == 0:
                    before = jnp.where(j == 0, last_ref[0, :, lane(g)].astype(f32), before)
                adj_state[t * n : (t + 1) * n, lane(g)] = (grad * before).astype(bf16)
        block = state_ref[0, pl.ds(pl.multiple_of(base * n, span), span), :]
        w1 = rows_dot(kd_ref[0, rows, :], adj[...])
        w2 = rows_dot(k2d_ref[0, rows, :], adj_state[...])
        a1 = outer_dot(u[...].astype(bf16), adj[...])
        a2 = outer_dot(rk[...].astype(bf16), adj_state[...])
        a3 = outer_dot(dys[...].astype(bf16), block)
        diag1[rows, :] = jnp.where(mask, a1, 0.0)
        diag2[rows, :] = jnp.where(mask, a2, 0.0)
        diag3[rows, :] = jnp.where(mask, a3, 0.0)
        for g in range(groups):
            grate_ref[0, rows, lane(g)] = conv[:, lane(g)] * w1[:, lane(g)] - keeps * w2[:, lane(g)]
        gconv_ref[0, rows, :] = rate * w1
        return tuple(held)

    start = tuple(held_ref[:, lane(g)] for g in range(groups))
    end = lax.fori_loop(0, chunks, chunk, start)
    for g in range(groups):
        held_ref[:, lane(g)] = end[g]

    pick = (
        lax.broadcasted_iota(jnp.int32, (span, n), 0) % n
        == lax.broadcasted_iota(jnp.int32, (span, n), 1)
    ).astype(bf16)

    def picked(ref):
        value = ref[...]
        high = value.astype(bf16)
        low = (value - high.astype(f32)).astype(bf16)
        return rows_dot(high, pick) + rows_dot(low, pick)

    rate = rate_ref[0]
    self_term = jnp.sum(grate_ref[0] * rate * rate, axis=1, keepdims=True)
    gkey_ref[0] = picked(diag1) - 2.0 * key_ref[0] * (picked(diag2) + self_term)
    gquery_ref[0] = picked(diag3)


def chunked(values, seqs):
    n = values.shape[0]
    return values.reshape(n, seqs, -1, CHUNK).transpose(1, 2, 0, 3)


def diagonal(values):
    length, n = values.shape[1:]
    spot = jnp.arange(length)[:, None] % CHUNK == jnp.arange(CHUNK * n)[None, :] // n
    return jnp.where(spot, jnp.tile(values, (1, 1, CHUNK)), 0.0).astype(bf16)


def specs_for(length, reverse):
    blocks = length // BLOCK

    def place(b):
        return blocks - 1 - b if reverse else b

    def spec(*shape):
        return pl.BlockSpec((1,) + shape, lambda s, b: (s, place(b)) + (0,) * (len(shape) - 1))

    return blocks, spec


def recurrence_forward(rate, conv, keyc, keep_lanes, qd):
    seqs, length, width = rate.shape
    n = keyc.shape[2]
    span = CHUNK * n
    blocks, spec = specs_for(length, False)
    wide = spec(BLOCK, width)
    return pl.pallas_call(
        forward_kernel,
        grid=(seqs, blocks),
        in_specs=[wide, wide, spec(BLOCK // CHUNK, n, CHUNK), spec(BLOCK, LANES), spec(BLOCK, span)],
        out_specs=[wide, spec(BLOCK * n, width)],
        out_shape=[
            jax.ShapeDtypeStruct((seqs, length, width), f32),
            jax.ShapeDtypeStruct((seqs, length * n, width), bf16),
        ],
        scratch_shapes=[
            pltpu.VMEM((n, width), f32),
            pltpu.VMEM((CHUNK, width), f32),
            pltpu.VMEM((CHUNK, width), f32),
            pltpu.VMEM((CHUNK, LANES), f32),
        ],
        compiler_params=pltpu.CompilerParams(vmem_limit_bytes=24 << 20),
        cost_estimate=pl.CostEstimate(flops=16_000_000_000, bytes_accessed=24 << 20, transcendentals=0),
        name="recurrence_forward",
    )(rate, conv, keyc, keep_lanes, qd)


def recurrence_backward(rate, conv, dy, keyc, queryc, keys, keep_lanes, kd, k2d, states):
    seqs, length, width = rate.shape
    n = keyc.shape[2]
    span = CHUNK * n
    blocks, spec = specs_for(length, True)
    wide = spec(BLOCK, width)
    small = spec(BLOCK, n)
    square = spec(BLOCK, span)
    chunk_spec = spec(BLOCK // CHUNK, n, CHUNK)
    before = pl.BlockSpec((1, n, width), lambda s, b: (s, jnp.maximum((blocks - 1 - b) * BLOCK - 1, 0), 0))
    return pl.pallas_call(
        backward_kernel,
        grid=(seqs, blocks),
        in_specs=[
            wide, wide, wide, chunk_spec, chunk_spec, small, spec(BLOCK, LANES), square, square,
            spec(BLOCK * n, width), before,
        ],
        out_specs=[wide, wide, small, small],
        out_shape=[jax.ShapeDtypeStruct((seqs, length, width), f32)] * 2
        + [jax.ShapeDtypeStruct((seqs, length, n), f32)] * 2,
        scratch_shapes=[
            pltpu.VMEM((n, width), f32),
            pltpu.VMEM((CHUNK, width), f32),
            pltpu.VMEM((CHUNK, width), f32),
            pltpu.VMEM((CHUNK, width), f32),
            pltpu.VMEM((CHUNK, LANES), f32),
            pltpu.VMEM((span, width), bf16),
            pltpu.VMEM((span, width), bf16),
            pltpu.VMEM((BLOCK, span), f32),
            pltpu.VMEM((BLOCK, span), f32),
            pltpu.VMEM((BLOCK, span), f32),
        ],
        compiler_params=pltpu.CompilerParams(vmem_limit_bytes=28 << 20),
        cost_estimate=pl.CostEstimate(flops=30_000_000_000, bytes_accessed=28 << 20, transcendentals=0),
        name="recurrence_backward",
    )(rate, conv, dy, keyc, queryc, keys, keep_lanes, kd, k2d, states, states)


def peer(hop):
    me = lax.axis_index("shard")
    core = lax.rem(me, 2)
    chip = me // 2
    if hop & 1:
        core = 1 - core
    if hop & 2:
        chip = 1 - chip
    return chip * 2 + core


def meet_group():
    barrier = pltpu.get_barrier_semaphore()
    for hop in (1, 2, 3):
        pl.semaphore_signal(barrier, inc=1, device_id={"shard": peer(hop)}, device_id_type=MESH)
    pl.semaphore_wait(barrier, 3)


def remote(src, dst, sends, recvs, at, hop):
    return pltpu.make_async_remote_copy(
        src_ref=src, dst_ref=dst, send_sem=sends.at[at], recv_sem=recvs.at[at],
        device_id={"shard": peer(hop)}, device_id_type=MESH,
    )


def group_params(collective_id, limit):
    return pltpu.CompilerParams(collective_id=collective_id, has_side_effects=True, vmem_limit_bytes=limit)


VMEM_SPEC = pl.BlockSpec(memory_space=pltpu.VMEM)


def gather_kernel(x_ref, cot_ref, gain_ref, xs_ref, cots_ref, gains_ref, sends, recvs, local):
    me = lax.axis_index("shard")
    rows = x_ref.shape[1]
    cols = cots_ref.shape[2]
    lift = gain_ref.shape[0]
    meet_group()

    def mine(ref, owner):
        return ref.at[:, pl.ds(pl.multiple_of(owner * rows, 16), rows), :]

    def part(owner):
        return cot_ref.at[:, :, pl.ds(pl.multiple_of(owner * cols, 128), cols)]

    def gain_rows(owner):
        return gains_ref.at[pl.ds(pl.multiple_of(owner * lift, 8), lift), :]

    x_core = remote(x_ref, mine(xs_ref, me), sends, recvs, 0, 1)
    x_chip = remote(x_ref, mine(xs_ref, me), sends, recvs, 1, 2)
    x_chip.start()
    x_core.start()
    rest = [remote(part(peer(hop)), mine(cots_ref, me), sends, recvs, 2 + hop, hop) for hop in (1, 2, 3)]
    rest += [remote(gain_ref, gain_rows(me), sends, recvs, 5 + hop, hop) for hop in (1, 2, 3)]
    for copy in rest:
        copy.start()
    own = [
        pltpu.make_async_copy(x_ref, mine(xs_ref, me), local.at[0]),
        pltpu.make_async_copy(part(me), mine(cots_ref, me), local.at[1]),
        pltpu.make_async_copy(gain_ref, gain_rows(me), local.at[2]),
    ]
    for copy in own:
        copy.start()
    x_chip.wait_recv()
    onward = remote(mine(xs_ref, peer(2)), mine(xs_ref, peer(2)), sends, recvs, 2, 1)
    onward.start()
    for copy in own + rest:
        copy.wait()
    x_chip.wait_send()
    x_core.wait()
    onward.wait()


def gather_inputs(x, cot, gain):
    seqs, rows, model = x.shape
    group = lax.axis_size("shard")
    lifted = jnp.broadcast_to(gain.astype(f32)[None], (8, gain.shape[0]))
    xs, cots, gains = pl.pallas_call(
        gather_kernel,
        in_specs=[VMEM_SPEC] * 3,
        out_specs=[VMEM_SPEC] * 3,
        out_shape=[
            jax.ShapeDtypeStruct((seqs, rows * group, model), x.dtype),
            jax.ShapeDtypeStruct((seqs, rows * group, model // group), x.dtype),
            jax.ShapeDtypeStruct((8 * group, gain.shape[0]), f32),
        ],
        scratch_shapes=[
            pltpu.SemaphoreType.DMA((9,)), pltpu.SemaphoreType.DMA((9,)), pltpu.SemaphoreType.DMA((3,)),
        ],
        compiler_params=group_params(1, 16 << 20),
        name="gather_inputs",
    )(x, cot, lifted)
    return xs, cots, gains[::8].reshape(-1)


def split_kernel(mixed_ref, parts_ref, sends, recvs, local):
    me = lax.axis_index("shard")
    width = parts_ref.shape[2]
    slot = me // 2
    meet_group()

    def send(i):
        return pltpu.make_async_remote_copy(
            src_ref=mixed_ref.at[:, pl.ds(i * width, width)],
            dst_ref=parts_ref.at[slot],
            send_sem=sends.at[i],
            recv_sem=recvs.at[slot],
            device_id={"shard": lax.rem(2 * me + i, 4)},
            device_id_type=MESH,
        )

    def keep(i):
        return pltpu.make_async_copy(mixed_ref.at[:, pl.ds(i * width, width)], parts_ref.at[slot], local.at[0])

    for i in range(2):
        away = lax.rem(2 * me + i, 4) != me

        @pl.when(away)
        def _(i=i):
            send(i).start()

        @pl.when(jnp.logical_not(away))
        def _(i=i):
            keep(i).start()

    for i in range(2):
        away = lax.rem(2 * me + i, 4) != me

        @pl.when(away)
        def _(i=i):
            send(i).wait_send()

        @pl.when(jnp.logical_not(away))
        def _(i=i):
            keep(i).wait()

    for at in range(2):

        @pl.when(2 * at + me // 2 != me)
        def _(at=at):
            pltpu.make_async_remote_copy(
                src_ref=parts_ref.at[at], dst_ref=parts_ref.at[at], send_sem=sends.at[at], recv_sem=recvs.at[at],
                device_id={"shard": peer(1)}, device_id_type=MESH,
            ).wait_recv()


def to_channels(mixed):
    tokens, cols = mixed.shape
    return pl.pallas_call(
        split_kernel,
        in_specs=[VMEM_SPEC],
        out_specs=VMEM_SPEC,
        out_shape=jax.ShapeDtypeStruct((2, tokens, cols // 2), mixed.dtype),
        scratch_shapes=[
            pltpu.SemaphoreType.DMA((2,)), pltpu.SemaphoreType.DMA((2,)), pltpu.SemaphoreType.DMA((1,)),
        ],
        compiler_params=group_params(2, 16 << 20),
        name="to_channels",
    )(mixed)


def total_kernel(part_ref, out_ref, near, chip_sum, far, sends, recvs):
    me = lax.axis_index("shard")
    half = part_ref.shape[1] // 2
    mine = pl.ds(pl.multiple_of(lax.rem(me, 2) * half, 128), half)
    other = pl.ds(pl.multiple_of((1 - lax.rem(me, 2)) * half, 128), half)
    meet_group()
    first = remote(part_ref.at[:, other], near, sends, recvs, 0, 1)
    first.start()
    first.wait()
    chip_sum[...] = part_ref[:, mine] + near[...]
    second = remote(chip_sum, far, sends, recvs, 1, 2)
    second.start()
    second.wait()
    out_ref[:, mine] = chip_sum[...] + far[...]
    third = remote(out_ref.at[:, mine], out_ref.at[:, mine], sends, recvs, 2, 1)
    third.start()
    third.wait()


def group_total(part, collective_id):
    rows, cols = part.shape
    half = pltpu.VMEM((rows, cols // 2), f32)
    return pl.pallas_call(
        total_kernel,
        in_specs=[VMEM_SPEC],
        out_specs=VMEM_SPEC,
        out_shape=jax.ShapeDtypeStruct((rows, cols), f32),
        scratch_shapes=[half, half, half, pltpu.SemaphoreType.DMA((3,)), pltpu.SemaphoreType.DMA((3,))],
        compiler_params=group_params(collective_id, 16 << 20),
        name="group_total",
    )(part)


def gain_kernel(part_ref, out_ref, near, mine, far, sends, recvs, far_sends, far_recvs):
    me = lax.axis_index("shard")
    home = lax.axis_index("replica")
    count = far.shape[0]
    barrier = pltpu.get_barrier_semaphore()
    for hop in (1, 2, 3):
        pl.semaphore_signal(barrier, inc=1, device_id={"shard": peer(hop)}, device_id_type=MESH)
    for step in range(1, count):
        pl.semaphore_signal(
            barrier, inc=1, device_id={"replica": lax.rem(home + step, count)}, device_id_type=MESH
        )
    pl.semaphore_wait(barrier, count + 2)
    copies = [remote(part_ref.at[peer(hop)], near.at[hop - 1], sends, recvs, hop - 1, hop) for hop in (1, 2, 3)]
    for copy in copies:
        copy.start()
    for copy in copies:
        copy.wait()
    mine[...] = part_ref[me] + near[0] + near[1] + near[2]
    far[0] = mine[...]
    copies = [
        pltpu.make_async_remote_copy(
            src_ref=mine, dst_ref=far.at[step], send_sem=far_sends.at[step], recv_sem=far_recvs.at[step],
            device_id={"replica": lax.rem(home + step, count)}, device_id_type=MESH,
        )
        for step in range(1, count)
    ]
    for copy in copies:
        copy.start()
    for copy in copies:
        copy.wait()
    out_ref[...] = jnp.sum(far[...], axis=0)


def gain_total(part):
    group, count = lax.axis_size("shard"), lax.axis_size("replica")
    tile = (part.shape[0] // group // 128, 128)
    return pl.pallas_call(
        gain_kernel,
        in_specs=[VMEM_SPEC],
        out_specs=VMEM_SPEC,
        out_shape=jax.ShapeDtypeStruct(tile, f32),
        scratch_shapes=[
            pltpu.VMEM((3,) + tile, f32), pltpu.VMEM(tile, f32), pltpu.VMEM((count,) + tile, f32),
            pltpu.SemaphoreType.DMA((3,)), pltpu.SemaphoreType.DMA((3,)),
            pltpu.SemaphoreType.DMA((count,)), pltpu.SemaphoreType.DMA((count,)),
        ],
        compiler_params=group_params(5, 16 << 20),
        name="gain_total",
    )(part.reshape((group,) + tile)).reshape(-1)


def by_hop(value, hop):
    return lax.ppermute(value, "shard", [(i, i ^ hop) for i in range(4)])


def pair(value):
    return lax.ppermute(value, "replica", [(i, i ^ 1) for i in range(lax.axis_size("replica"))])


def far_sum(blocks):
    count = lax.axis_size("replica")
    height = count // 2
    mine = lax.axis_index("replica") // 2

    def pick(at):
        return lax.dynamic_index_in_dim(blocks, at, 0, False)

    total = pick(mine)
    for step in range(1, height):
        out = pick(lax.rem(mine + step, height)).astype(bf16)
        total = total + lax.ppermute(out, "replica", [(i, (i + 2 * step) % count) for i in range(count)]).astype(f32)
    return total


def far_gather(block):
    count = lax.axis_size("replica")
    height = count // 2
    mine = lax.axis_index("replica") // 2
    full = jnp.zeros((height,) + block.shape, block.dtype)
    full = lax.dynamic_update_index_in_dim(full, block, mine, 0)
    for step in range(1, height):
        got = lax.ppermute(block, "replica", [(i, (i + 2 * step) % count) for i in range(count)])
        full = lax.dynamic_update_index_in_dim(full, got, lax.rem(mine + height - step, height), 0)
    return full


def x_home(x_own):
    one = lax.ppermute(x_own, "shard", [(1, 0), (2, 1)])
    two = lax.ppermute(x_own, "shard", [(3, 1)])
    return one, two


def z_home(z_own):
    one = lax.ppermute(z_own, "shard", [(0, 2), (2, 3)])
    two = lax.ppermute(z_own, "shard", [(1, 2)])
    return one, two


def columns_home(x_own, x_got, z_own, z_got):
    me = lax.axis_index("shard")
    first = jnp.where(me == 0, x_own, jnp.where(me == 1, x_got[0], z_got[0]))
    second = jnp.where(me == 3, z_own, jnp.where(me == 2, z_got[1], jnp.where(me == 1, x_got[1], x_got[0])))
    return jnp.concatenate([first, second], axis=1)


def after(value, *others):
    return lax.optimization_barrier((value,) + others)[0]


def body(
    block_input, segment_ids, norm_gain, w_in, conv_weight, conv_bias, x_proj, dt_proj, dt_bias,
    d_skip, out_proj, out_grad,
):
    seqs, local, model = block_input.shape
    length = segment_ids.shape[1]
    tokens = seqs * length
    width = d_skip.shape[0]
    rank = dt_proj.shape[0]
    n = (x_proj.shape[0] - rank) // 2
    me = lax.axis_index("shard")
    count = lax.axis_size("replica")
    height = count // 2
    side = lax.rem(lax.axis_index("replica"), 2)

    def split(values):
        return values.reshape(seqs, length, -1)

    def halves(values, blocks):
        parts = values.reshape(values.shape[0], blocks, 2, -1)
        keep = lax.dynamic_index_in_dim(parts, side, 2, False)
        give = lax.dynamic_index_in_dim(parts, 1 - side, 2, False)
        return keep.reshape(values.shape[0], -1), give.reshape(values.shape[0], -1)

    def both(keep, got):
        return jnp.concatenate([keep, got], axis=0)

    xs, cots, gain = gather_inputs(block_input, out_grad, norm_gain)
    x_all = xs.reshape(tokens, model)
    cot = cots.reshape(tokens, -1)

    def normalise(rows):
        vals = rows.astype(f32)
        inv = lax.rsqrt(jnp.mean(vals * vals, axis=-1, keepdims=True) + EPS)
        return vals, inv

    x_vals, inv_rms = normalise(x_all)
    scaled_x = x_vals * inv_rms
    normed = (scaled_x * gain).astype(bf16)
    mixed = rows_dot(normed, w_in).astype(bf16)
    parts = to_channels(mixed)
    x_part, z_part = parts[0], parts[1]

    cot_late = after(cot, parts)
    partial = outer_dot(cot_late, out_proj).astype(bf16).reshape(tokens, 2, 2, width)
    core = lax.rem(me, 2)
    chip = me // 2
    near = by_hop(lax.dynamic_index_in_dim(partial, 1 - core, 2, False), 1)
    chip_part = lax.dynamic_index_in_dim(partial, core, 2, False).astype(f32) + near.astype(f32)
    grad_gated = lax.dynamic_index_in_dim(chip_part, chip, 1, False) + by_hop(
        lax.dynamic_index_in_dim(chip_part, 1 - chip, 1, False).astype(bf16), 2
    ).astype(f32)
    grad_gated = split(grad_gated)

    normed_late = after(normed, parts)
    normed_keep, normed_give = halves(normed_late, height)
    normed_pair = both(normed_keep, pair(normed_give))
    cot_pair = both(cot, pair(cot_late))

    seg_padded = jnp.pad(segment_ids, ((0, 0), (KW - 1, 0)), constant_values=-1)
    taps = [
        (seg_padded[:, KW - 1 - d : KW - 1 - d + length] == segment_ids).astype(f32) for d in range(KW)
    ]
    conv_w = conv_weight.astype(f32)
    xv = split(x_part).astype(f32)
    x_padded = jnp.pad(xv, ((0, 0), (KW - 1, 0), (0, 0)))
    conv_pre = conv_bias.astype(f32) + conv_w[KW - 1] * xv
    for j in range(KW - 1):
        d = KW - 1 - j
        conv_pre = conv_pre + conv_w[j] * x_padded[:, j : j + length] * taps[d][:, :, None]
    conv_out = jax.nn.silu(conv_pre).astype(bf16)
    conv_vals = conv_out.astype(f32)
    conv_flat = conv_out.reshape(tokens, width)
    proj = group_total(outer_dot(x_proj, conv_flat), 3)
    dt_low = proj[:rank].astype(bf16)
    key_cols = proj[rank : rank + n]
    query_cols = proj[rank + n :]
    keys = split(key_cols.T)
    queries = split(query_cols.T)
    beta = split(jax.nn.sigmoid(inner_dot(dt_low, dt_proj) + dt_bias.astype(f32)))
    key_square = jnp.sum(keys * keys, axis=2, keepdims=True)
    denom_inv = 1.0 / (1.0 + beta * key_square)
    rate = beta * denom_inv
    keep_lanes = jnp.broadcast_to(taps[1][:, :, None], (seqs, length, LANES))
    keyc = chunked(key_cols, seqs)
    recurrent, states = recurrence_forward(rate, conv_out, keyc, keep_lanes, diagonal(queries))

    z_vals = split(z_part).astype(f32)
    gate = jax.nn.silu(z_vals)
    dy = grad_gated * gate
    skip = d_skip.astype(f32)
    y_total = recurrent + skip * conv_vals
    gated = (y_total * gate).astype(bf16).reshape(tokens, width)
    grad_z = (grad_gated * y_total * silu_slope(z_vals)).astype(bf16).reshape(tokens, width)

    def group_gather(value):
        across = by_hop(value, 2)
        near_two = by_hop(jnp.concatenate([value], axis=1), 1)
        near_far = by_hop(across, 1)
        stacked = jnp.stack([value, near_two, across, near_far])
        order = jnp.stack([jnp.bitwise_xor(me, i) for i in range(4)])
        return [lax.dynamic_index_in_dim(stacked, order[i], 0, False) for i in range(4)]

    gated_keep, gated_give = halves(gated, height // 4 if height >= 4 else 1)
    gated_got = pair(gated_give)
    gated_parts = group_gather(gated)
    gated_all = jnp.concatenate(gated_parts, axis=1)
    got_all = jnp.concatenate(group_gather(gated_got), axis=1)
    keep_all, _ = halves(gated_all, height)
    cols = model // 4
    x_cols = lax.dynamic_slice_in_dim(x_all, me * cols, cols, 1).astype(f32)
    out_cols = (x_cols + rows_dot(gated_all, out_proj)).astype(bf16).reshape(seqs, 4, local, cols)

    def rows_for(hop):
        return lax.dynamic_index_in_dim(out_cols, jnp.bitwise_xor(me, hop), 1, False)

    out_stack = jnp.stack([rows_for(0)] + [by_hop(rows_for(hop), hop) for hop in (1, 2, 3)])
    block_output = jnp.concatenate(
        [lax.dynamic_index_in_dim(out_stack, jnp.bitwise_xor(me, i), 0, False) for i in range(4)], axis=2
    )
    grad_out_proj = far_sum(
        inner_dot(both(keep_all, got_all), cot_pair).reshape(height, -1, cols)
    )
    z_got = z_home(grad_z)
    grad_w_z = far_sum(
        inner_dot(normed_pair, both(grad_z, pair(grad_z))).reshape(height, -1, width)
    ).astype(bf16)

    grad_rate, grad_conv_rec, grad_keys, grad_queries = recurrence_backward(
        rate, conv_out, dy, keyc, chunked(query_cols, seqs), keys, keep_lanes, diagonal(keys),
        diagonal(keys * keys), states,
    )
    grad_d_skip = jnp.sum(dy * conv_vals, axis=(0, 1))
    grad_dt = grad_rate * denom_inv * denom_inv * beta * (1.0 - beta)
    grad_dt_bias = jnp.sum(grad_dt, axis=(0, 1))
    grad_dt_low = grad_dt.astype(bf16).reshape(tokens, width)
    grad_proj = jnp.concatenate(
        [outer_dot(dt_proj, grad_dt_low), grad_keys.reshape(tokens, n).T, grad_queries.reshape(tokens, n).T]
    )
    grad_proj = group_total(grad_proj, 4).astype(bf16)
    grad_dt_proj = rows_dot(dt_low, grad_dt_low)
    grad_x_proj = rows_dot(grad_proj, conv_flat)
    grad_conv = dy * skip + grad_conv_rec + split(inner_dot(grad_proj, x_proj))
    grad_pre = grad_conv * silu_slope(conv_pre)
    grad_conv_bias = jnp.sum(grad_pre, axis=(0, 1))
    grad_conv_weight = jnp.stack(
        [
            jnp.sum(grad_pre * x_padded[:, j : j + length] * taps[KW - 1 - j][:, :, None], axis=(0, 1))
            for j in range(KW)
        ]
    )
    grad_x = conv_w[KW - 1] * grad_pre
    for j in range(KW - 1):
        d = KW - 1 - j
        ahead = jnp.pad(grad_pre * taps[d][:, :, None], ((0, 0), (0, d), (0, 0)))[:, d:]
        grad_x = grad_x + conv_w[j] * ahead
    grad_x = grad_x.astype(bf16).reshape(tokens, width)
    x_rows = inner_dot(normed_pair, both(grad_x, pair(grad_x))).reshape(height, -1, width)

    small = jnp.concatenate(
        [
            grad_x_proj, grad_dt_proj, grad_conv_weight, grad_conv_bias[None], grad_dt_bias[None],
            grad_d_skip[None],
        ]
    )
    unit = 16 * count
    padded = -(-small.shape[0] // unit) * unit
    small = jnp.pad(small, ((0, padded - small.shape[0]), (0, 0))).reshape(height, 2, -1, width)
    small_keep = lax.dynamic_index_in_dim(small, side, 1, False)
    small_got = pair(lax.dynamic_index_in_dim(small, 1 - side, 1, False).astype(bf16))
    small_rows = small_keep + small_got.astype(f32)
    summed = far_sum(jnp.concatenate([x_rows, small_rows], axis=1))
    per = x_rows.shape[1]
    grad_w_x = summed[:per].astype(bf16)
    small_side = far_gather(summed[per:].astype(bf16))
    other_side = pair(small_side)
    small = jnp.stack(
        [jnp.where(side == 0, small_side, other_side), jnp.where(side == 0, other_side, small_side)], axis=1
    ).reshape(padded, width).astype(f32)

    grad_cols = columns_home(grad_x, x_home(grad_x), grad_z, z_got)
    grad_w_in = columns_home(grad_w_x, x_home(grad_w_x), grad_w_z, z_home(grad_w_z)).astype(f32)
    grad_normed = outer_dot(grad_cols, w_in)
    grad_gain = gain_total(jnp.sum(grad_normed * scaled_x, axis=0))
    by_owner = grad_normed.astype(bf16).reshape(seqs, 2, 2, local, model)
    near = by_hop(lax.dynamic_index_in_dim(by_owner, 1 - core, 2, False), 1)
    chip_rows = lax.dynamic_index_in_dim(by_owner, core, 2, False).astype(f32) + near.astype(f32)
    grad_normed = lax.dynamic_index_in_dim(chip_rows, chip, 1, False) + by_hop(
        lax.dynamic_index_in_dim(chip_rows, 1 - chip, 1, False).astype(bf16), 2
    ).astype(f32)
    x_own, inv_own = normalise(block_input)
    scaled = grad_normed * gain
    grad_in = inv_own * (
        scaled - x_own * inv_own * inv_own * jnp.mean(scaled * x_own, axis=-1, keepdims=True)
    )
    input_grad = (out_grad.astype(f32) + grad_in).astype(bf16)

    top = x_proj.shape[0]
    return (
        block_output, input_grad, grad_gain, grad_w_in,
        small[top + rank : top + rank + KW], small[top + rank + KW], small[:top], small[top : top + rank],
        small[top + rank + KW + 1], small[top + rank + KW + 2], grad_out_proj,
    )


def solution(mesh):
    return jax.shard_map(
        body,
        mesh=mesh,
        in_specs=(
            P("replica", "shard", None), P("replica", None), P("shard"), P(None, "shard"), P(None, "shard"),
            P("shard"), P(None, "shard"), P(None, "shard"), P("shard"), P("shard"), P(None, "shard"),
            P("replica", "shard", None),
        ),
        out_specs=(
            P("replica", "shard", None), P("replica", "shard", None), P("shard"), P("replica", "shard"),
            P(None, "shard"), P("shard"), P(None, "shard"), P(None, "shard"), P("shard"), P("shard"),
            P("replica", "shard"),
        ),
        check_vma=False,
    )
```

time: 665 us -> 574 us (0.86)
  waiting for transfers between devices: 397 us -> 147 us
  local copies, waits for them, and re-layouts: 28.7 us -> 113 us
  Pallas kernels: 53.7 us -> 134 us
  starting transfers between devices: 8.53 us -> 73.9 us
  blocking collectives: 64.4 us -> 0 us
  between operations: 15.6 us -> 2.16 us
  other arithmetic: 43.4 us -> 50.1 us
    reduce_scatter x4 -> x0, waiting for transfers between devices: 218 us -> none  [the longest x1 150 us: body(): lax.psum_scatter(inner_dot(normed, grad_mixed).astype(bf16), 'replica', s...]
    psum x2 -> x0, waiting for transfers between devices: 82.4 us -> none  [the longest x1 49.4 us: body(): small = lax.psum(small.astype(bf16), 'replica').astype(f32)]
    pallas_call x1 -> x7, Pallas kernels: 53.7 us -> 134 us  [the longest x1 37.6 us: recurrence_backward(): pl.pallas_call(backward_kernel, grid=(seqs, blocks), in_specs=[wide, wide...]
    ppermute x4 -> x40, starting transfers between devices: 4.33 us -> 73.9 us  [the longest x13 19.2 us: by_hop(): return lax.ppermute(value, 'shard', [(i, i ^ hop) for i in range(4)])]
    ppermute x4 -> x40, waiting for transfers between devices: 87.8 us -> 147 us  [the longest x9 65.4 us: far_sum(): lax.ppermute(out, 'replica', [(i, (i + 2 * step) % count) for i in range(...]
    psum x2 -> x0, blocking collectives: 38.3 us -> none  [the longest x1 23 us: body(): lax.psum(grad_gain, 'replica')]
    dynamic_slice x0 -> x7, local copies, waits for them, and re-layouts: none -> 27 us  [the longest x1 11.1 us: body(): lax.dynamic_index_in_dim(partial, core, 2, False).astype(f32)]
    unnamed x107 -> x180, local copies, waits for them, and re-layouts: 10.4 us -> 31.1 us
  transfers between devices with their start and end apart: 13 -> 40, of which waited for: 8 -> 14; matrix products, arithmetic and copies ran while one was open for 12% -> 27% of each run, Pallas kernels for 0% -> 17%
where the time goes in v2:
time: 574 us; the launch traced here: 567 us
  waiting for transfers between devices  147 us (26%)
  Pallas kernels  134 us (23%)
  local copies, waits for them, and re-layouts  113 us (20%)
  starting transfers between devices  73.9 us (13%)
  other arithmetic  50.1 us (9%)
  matrix products  47.1 us (8%)
    ppermute x9, waiting for transfers between devices, far_sum(): lax.ppermute(out, 'replica', [(i, (i + 2 * step) % count) for i in range(...  65.4 us
    pallas_call x1, Pallas kernels, recurrence_backward(): pl.pallas_call(backward_kernel, grid=(seqs, blocks), in_specs=[wide, wide...  37.6 us
    ppermute x7, waiting for transfers between devices, pair(): lax.ppermute(value, 'replica', [(i, i ^ 1) for i in range(lax.axis_size('...  37.3 us
    ppermute x13, waiting for transfers between devices, by_hop(): return lax.ppermute(value, 'shard', [(i, i ^ hop) for i in range(4)])  32.2 us
    unnamed x180, local copies, waits for them, and re-layouts  31.1 us
    pallas_call x1, Pallas kernels, gain_total(): pl.pallas_call(gain_kernel, in_specs=[VMEM_SPEC], out_specs=VMEM_SPEC, ou...  25.7 us
    pallas_call x1, Pallas kernels, gather_inputs(): pl.pallas_call(gather_kernel, in_specs=[VMEM_SPEC] * 3, out_specs=[VMEM_S...  21.9 us
    ppermute x13, starting transfers between devices, by_hop(): return lax.ppermute(value, 'shard', [(i, i ^ hop) for i in range(4)])  19.2 us
  transfers between devices with their start and end apart: 40, of which 14 were waited for; matrix products, arithmetic and copies ran while one was open for 27% of the time, Pallas kernels for 17%

profile of v2, /device:TPU:0, one launch (start us, length us, event | category | flops | bytes accessed | tf_op | source)
XLA Modules:
  0.0 567.5 jit_solution(5077763095850284015)
XLA Ops:
  3.5 21.9 %gather_inputs.1 = (bf16[2,256,2048]{2,1,0:T(8,128)(2,1)S(1)}, bf16[2,256,512]{2,1,0:T(8,128)(2,1)S(1)}, f32[32,512]{1,0:T(8,128)S(1)}) custom-call(bf16[2,64,2048]{2,1,0:T(8,128)(2,1)S(1)} %copy-done.6, bf16[2,64,2048]{2,1,0:T(8,128)(2,1)S(1)} %copy-done.13, f32[8,512]{1,0:T(8,128)S(1)} %broadcast_in_dim.41.gain_ref), custom_call_target="tpu_custom_call" | custom-call | tf_op jit(solution)/shard_map/gather_inputs/pallas_call | solution.py:342
  27.0 8.9 %convolution_convert_fusion.1.mixed_ref = bf16[512,2048]{1,0:T(8,128)(2,1)S(1)} fusion(bf16[512,2048]{1,0:T(8,128)(2,1)S(1)} %multiply_convert_fusion, bf16[2048,2048]{1,0:T(8,128)(2,1)} %param.15), kind=kOutput, calls=%fused_computation.38 | convolution fusion | flops 4296015872 | bytes 12582912 | tf_op jit(solution)/shard_map/dot_general | solution.py:19
  36.0 14.9 %to_channels.1 = bf16[2,512,1024]{2,1,0:T(8,128)(2,1)S(1)} custom-call(bf16[512,2048]{1,0:T(8,128)(2,1)S(1)} %convolution_convert_fusion.1.mixed_ref), custom_call_target="tpu_custom_call" | custom-call | tf_op jit(solution)/shard_map/to_channels/pallas_call | solution.py:413
  52.2 4.5 convolution_convert_fusion
  56.7 8.0 %reshape.266 = bf16[512,2,2,1024]{3,2,1,0:T(2,128)(2,1)} reshape(bf16[512,4096]{1,0:T(8,128)(2,1)} %convolution_convert_fusion) | data formatting | bytes 8388608 | tf_op jit(solution)/shard_map/reshape | solution.py:612
  64.7 11.1 %constant_dynamic-slice_fusion.6 = (bf16[512,2,1,1024]{3,2,1,0:T(2,128)(2,1)}, bf16[512,2,1,1024]{3,2,1,0:T(2,128)(2,1)S(1)}) fusion(bf16[512,2,2,1024]{3,2,1,0:T(2,128)(2,1)} %reshape.266, s32[]{:T(128)S(6)} %select_n.230, s32[]{:T(128)S(6)} %select_n.231), kind=kLoop, calls=%fused_computation.213 | loop fusion | bytes 8388616 | tf_op jit(solution)/shard_map/jit(dynamic_index_in_dim)/dynamic_slice | solution.py:616
  75.7 2.5 copy.101
  78.3 11.1 %collective-permute-start.6 = (bf16[512,2,1024]{2,0,1:T(8,128)(2,1)}, bf16[512,2,1024]{2,0,1:T(8,128)(2,1)}, u32[]{:S(2)}, u32[]{:S(2)}) collective-permute-start(bf16[512,2,1024]{2,0,1:T(8,128)(2,1)} %bitcast.230), channel_id=1, source_target_pairs={{0,1},{1,0},{2,3},{3,2},{4,5},{5,4},{6,7},{7,6},{8,9},{9,8},{10,11... | collective-permute-start | bytes 6291464 | tf_op jit(solution)/shard_map/ppermute | solution.py:511
  89.3 4.5 reshape.279
  93.8 8.5 %constant_dynamic-slice_fusion.2 = (bf16[512,4,1,256]{3,2,1,0:T(2,128)(2,1)}, bf16[512,4,1,256]{3,2,1,0:T(2,128)(2,1)}) fusion(bf16[512,4,2,256]{3,2,1,0:T(2,128)(2,1)} %reshape.279, s32[]{:T(128)S(6)} %select_n.246, s32[]{:T(128)S(6)} %select_n.247), kind=kLoop, calls=%fused_computation.209 | loop fusion | bytes 4194312 | tf_op jit(solution)/shard_map/jit(dynamic_index_in_dim)/dynamic_slice | solution.py:588
  102.3 5.9 %copy.83 = bf16[512,4,1,256]{0,3,1,2:T(8,128)(2,1)} copy(bf16[512,4,1,256]{3,2,1,0:T(2,128)(2,1)} %get-tuple-element.74) | data formatting | bytes 2097152
  111.0 4.3 convert_add_fusion
  116.5 1.9 copy-done.5
  123.0 17.4 %collective-permute-done.7 = bf16[512,1024]{1,0:T(8,128)(2,1)} collective-permute-done((bf16[512,1024]{1,0:T(8,128)(2,1)S(1)}, bf16[512,1024]{1,0:T(8,128)(2,1)}, u32[]{:S(2)}, u32[]{:S(2)}) %collective-permute-start.7) | collective-permute-done | bytes 1048608 | tf_op jit(solution)/shard_map/ppermute | solution.py:511
  140.5 2.4 bitcast_add_fusion
  142.9 4.5 fusion.26
  147.9 8.9 %group_total.2 = f32[160,512]{1,0:T(8,128)S(1)} custom-call(f32[160,512]{1,0:T(8,128)S(1)} %convolution_bitcast_fusion.part_ref), custom_call_target="tpu_custom_call" | custom-call | tf_op jit(solution)/shard_map/group_total/pallas_call | solution.py:448
  167.0 1.8 copy.67
  169.5 1.8 copy.65
  172.7 1.8 copy.56
  176.7 1.8 add_divide_fusion.1
  179.9 15.8 %recurrence_forward.1 = (f32[2,256,1024]{2,1,0:T(8,128)S(1)}, bf16[2,4096,1024]{2,1,0:T(8,128)(2,1)S(1)}) custom-call(f32[2,256,1024]{2,1,0:T(8,128)S(1)} %fusion.47.rate_ref, bf16[2,256,1024]{2,1,0:T(8,128)(2,1)S(1)} %get-tuple-element.45.conv_ref, f32[2,16,16,16]{3,2,1,0:T(8,128)S(1)} %get-tuple-element.118.keyc_ref, ...), custom_call_target="tpu_custom_call" | custom-call | flops 16000000000 | bytes 25165824 | tf_op jit(solution)/shard_map/recurrence_forward/pallas_call | solution.py:206
  197.0 5.8 %copy-done.21 = bf16[2,4096,1024]{2,1,0:T(8,128)(2,1)} copy-done((bf16[2,4096,1024]{2,1,0:T(8,128)(2,1)}, bf16[2,4096,1024]{2,1,0:T(8,128)(2,1)S(1)}, u32[]{:S(2)}) %copy-start.21) | copy-done | bytes 16777240
  202.8 37.6 %recurrence_backward.1 = (f32[2,256,1024]{2,1,0:T(8,128)S(1)}, f32[2,256,1024]{2,1,0:T(8,128)S(1)}, f32[2,256,16]{2,1,0:T(8,128)S(1)}, f32[2,256,16]{2,1,0:T(8,128)S(1)}) custom-call(f32[2,256,1024]{2,1,0:T(8,128)S(1)} %fusion.47.rate_ref, bf16[2,256,1024]{2,1,0:T(8,128)(2,1)S(1)} %get-tuple-element.45.conv_ref, f32[2,256,1024]{2,1,0:T(8,128)S(1)} %copy-done.2, ...), custom_call_target="tpu_custom_call" | custom-call | flops 30000001024 | bytes 29360128 | tf_op jit(solution)/shard_map/recurrence_backward/pallas_call | solution.py:237
  240.5 1.8 fusion.112
  244.4 1.9 convolution_bitcast_fusion.1
  246.3 8.9 %group_total.3 = f32[160,512]{1,0:T(8,128)S(1)} custom-call(f32[160,512]{1,0:T(8,128)S(1)} %pad_maximum_fusion.8.part_ref), custom_call_target="tpu_custom_call" | custom-call | tf_op jit(solution)/shard_map/group_total/pallas_call | solution.py:448
  257.8 8.6 %fusion.109 = (f32[1024]{0:T(1024)S(1)}, f32[1024]{0:T(1024)S(1)}, f32[1024]{0:T(1024)S(1)}, f32[1024]{0:T(1024)S(1)}, f32[1024]{0:T(1024)S(1)}, /*index=5*/f32[...) fusion(bf16[2,256,1024]{2,1,0:T(8,128)(2,1)S(1)} %bitcast.253, ...), kind=kLoop, calls=%fused_computation.239 | loop fusion | flops 20966400 | bytes 22050816 | tf_op jit(solution)/shard_map/reduce_sum | solution.py:712
  269.4 4.4 concatenate.56
  280.6 2.5 constant_dynamic-slice_fusion
  284.3 2.1 fusion.22
  286.3 3.7 collective-permute-start.9
  290.1 12.1 %collective-permute-done.16 = bf16[4,48,1024]{2,1,0:T(8,128)(2,1)} collective-permute-done((bf16[4,48,1024]{2,1,0:T(8,128)(2,1)}, bf16[4,48,1024]{2,1,0:T(8,128)(2,1)}, u32[]{:S(2)}, u32[]{:S(2)}) %collective-permute-start.16) | collective-permute-done | bytes 393248 | tf_op jit(solution)/shard_map/ppermute | solution.py:515
  303.9 8.9 %collective-permute-done.32 = bf16[512,512]{1,0:T(8,128)(2,1)S(1)} collective-permute-done((bf16[512,512]{1,0:T(8,128)(2,1)S(1)}, bf16[512,512]{1,0:T(8,128)(2,1)S(1)}, u32[]{:S(2)}, u32[]{:S(2)}) %collective-permute-start.32) | collective-permute-done | bytes 524320 | tf_op jit(solution)/shard_map/ppermute | solution.py:515
  314.9 5.8 %copy.82 = bf16[512,4,1,256]{0,3,1,2:T(8,128)(2,1)} copy(bf16[512,4,1,256]{3,2,1,0:T(2,128)(2,1)} %get-tuple-element.73) | data formatting | bytes 2097152
  323.4 2.7 collective-permute-start.34
  327.4 4.5 fusion.43
  332.2 8.7 %collective-permute-done.34 = bf16[512,512]{1,0:T(8,128)(2,1)} collective-permute-done((bf16[512,512]{1,0:T(8,128)(2,1)}, bf16[512,512]{1,0:T(8,128)(2,1)}, u32[]{:S(2)}, u32[]{:S(2)}) %collective-permute-start.34) | collective-permute-done | bytes 524320 | tf_op jit(solution)/shard_map/ppermute | solution.py:511
  341.9 1.8 collective-permute-start.22
  343.7 2.4 select_select_fusion.1
  346.1 8.6 %multiply_reduce_fusion = (f32[2048]{0:T(1024)S(1)}, bf16[512,2048]{1,0:T(8,128)(2,1)S(1)}) fusion(f32[512]{0:T(512)S(1)} %bitcast.312, bf16[2,256,2048]{2,1,0:T(8,128)(2,1)S(1)} %get-tuple-element.22, bf16[2048,2048]{1,0:T(8,128)(2,1)} %param.15, bf16[512,1024]{1,0:T(8,128)(2,1)S(1)} %get-tuple-element.86, bf16[512,1024]{1,0:T(8,128)(2,1)S(1)} %get-tuple-element.85), kind=kOutput, calls=%fused_computation.33 | convolution fusion | flops 4304402432 | bytes 14690304 | tf_op jit(solution)/shard_map/dot_general | solution.py:27
  354.8 9.4 %collective-permute-done.15 = bf16[512,1024]{1,0:T(8,128)(2,1)} collective-permute-done((bf16[512,1024]{1,0:T(8,128)(2,1)}, bf16[512,1024]{1,0:T(8,128)(2,1)}, u32[]{:S(2)}, u32[]{:S(2)}) %collective-permute-start.15) | collective-permute-done | bytes 1048608 | tf_op jit(solution)/shard_map/ppermute | solution.py:515
  364.2 3.8 collective-permute-start.24
  368.0 4.2 fusion.39
  373.4 25.7 %gain_total.1 = f32[4,128]{1,0:T(4,128)S(1)} custom-call(f32[4,4,128]{2,1,0:T(4,128)S(1)} %bitcast.243), custom_call_target="tpu_custom_call" | custom-call | tf_op jit(solution)/shard_map/gain_total/pallas_call | solution.py:495
  402.2 3.4 collective-permute-start.18
  413.0 7.0 %collective-permute-done.17 = bf16[304,1024]{1,0:T(8,128)(2,1)S(1)} collective-permute-done((bf16[304,1024]{1,0:T(8,128)(2,1)S(1)}, bf16[304,1024]{1,0:T(8,128)(2,1)S(1)}, u32[]{:S(2)}, u32[]{:S(2)}) %collective-permute-start.17) | collective-permute-done | bytes 622624 | tf_op jit(solution)/shard_map/ppermute | solution.py:529
  420.0 26.0 %collective-permute-done.18 = bf16[304,1024]{1,0:T(8,128)(2,1)S(1)} collective-permute-done((bf16[304,1024]{1,0:T(8,128)(2,1)S(1)}, bf16[304,1024]{1,0:T(8,128)(2,1)S(1)}, u32[]{:S(2)}, u32[]{:S(2)}) %collective-permute-start.18) | collective-permute-done | bytes 622624 | tf_op jit(solution)/shard_map/ppermute | solution.py:529
  446.5 13.9 %collective-permute-start.28 = (bf16[48,1024]{1,0:T(8,128)(2,1)S(1)}, bf16[48,1024]{1,0:T(8,128)(2,1)S(1)}, u32[]{:S(2)}, u32[]{:S(2)}) collective-permute-start(bf16[48,1024]{1,0:T(8,128)(2,1)S(1)} %slice.126), channel_id=1, source_target_pairs={{0,8},{4,12},{8,16},{12,20},{16,24},{20,28},{24,0},{28,4},{1,9},{5... | collective-permute-start | bytes 294920 | tf_op jit(solution)/shard_map/ppermute | solution.py:540
  461.3 3.6 collective-permute-done.28
  464.9 6.6 %collective-permute-done.29 = bf16[48,1024]{1,0:T(8,128)(2,1)S(1)} collective-permute-done((bf16[48,1024]{1,0:T(8,128)(2,1)S(1)}, bf16[48,1024]{1,0:T(8,128)(2,1)S(1)}, u32[]{:S(2)}, u32[]{:S(2)}) %collective-permute-start.29) | collective-permute-done | bytes 98336 | tf_op jit(solution)/shard_map/ppermute | solution.py:540
  471.5 2.2 collective-permute-start.30
  473.7 2.4 collective-permute-done.30
  477.6 2.1 collective-permute-start.25
  482.1 1.8 fusion.34
  484.8 4.0 copy.77
  488.8 5.9 %fusion.53 = bf16[512,512]{1,0:T(8,128)(2,1)S(1)} fusion(bf16[4096,512]{1,0:T(8,128)(2,1)} %param.22, bf16[512,1024]{0,1:T(8,128)(2,1)} %bitcast.264, bf16[512,1024]{0,1:T(8,128)(2,1)} %bitcast.266, bf16[512,1024]{0,1:T(8,128)(2,1)} %bitcast.268, bf16[512,1024]{0,1:T(8,128)(2,1)} %bitcast.262, bf16[512,2048]{1,0:T(8,128)(2,1)S(1)} %bitcast.236, ...), kind=kOutput, calls=%fused_computation.102 | convolution fusion | flops 2165047296 | bytes 9437188 | tf_op jit(solution)/shard_map/dot_general | solution.py:19
  499.1 3.5 fusion.8
  502.9 6.8 %collective-permute-done.31 = bf16[4,48,1024]{2,1,0:T(8,128)(2,1)S(1)} collective-permute-done((bf16[4,48,1024]{2,1,0:T(8,128)(2,1)S(1)}, bf16[4,48,1024]{2,1,0:T(8,128)(2,1)S(1)}, u32[]{:S(2)}, u32[]{:S(2)}) %collective-permute-start.31) | collective-permute-done | bytes 393248 | tf_op jit(solution)/shard_map/ppermute | solution.py:515
  515.1 1.7 collective-permute-start.13
  519.7 4.1 collective-permute-start.39
  525.4 6.0 %collective-permute-done.13 = bf16[2,64,2048]{2,1,0:T(8,128)(2,1)S(1)} collective-permute-done((bf16[2,64,2048]{2,1,0:T(8,128)(2,1)S(1)}, bf16[2,64,2048]{2,1,0:T(8,128)(2,1)S(1)}, u32[]{:S(2)}, u32[]{:S(2)}) %collective-permute-start.13) | collective-permute-done | bytes 524320 | tf_op jit(solution)/shard_map/ppermute | solution.py:511
  533.1 9.8 %collective-permute-done.39 = bf16[512,512]{1,0:T(8,128)(2,1)S(1)} collective-permute-done((bf16[512,512]{1,0:T(8,128)(2,1)S(1)}, bf16[512,512]{1,0:T(8,128)(2,1)S(1)}, u32[]{:S(2)}, u32[]{:S(2)}) %collective-permute-start.39) | collective-permute-done | bytes 524320 | tf_op jit(solution)/shard_map/ppermute | solution.py:529
  542.9 22.5 %collective-permute-done.38 = bf16[512,512]{1,0:T(8,128)(2,1)S(1)} collective-permute-done((bf16[512,512]{1,0:T(8,128)(2,1)S(1)}, bf16[512,512]{1,0:T(8,128)(2,1)S(1)}, u32[]{:S(2)}, u32[]{:S(2)}) %collective-permute-start.38) | collective-permute-done | bytes 524320 | tf_op jit(solution)/shard_map/ppermute | solution.py:529
  (315 shorter events, 92.1 us)
Async XLA Ops:
  0.6 146.8 %copy-start = (bf16[160,1024]{1,0:T(8,128)(2,1)S(1)}, bf16[160,1024]{1,0:T(8,128)(2,1)}, u32[]{:S(2)}) copy-start(bf16[160,1024]{1,0:T(8,128)(2,1)} %param.18) | copy-start | bytes 983044
  25.4 26.8 %copy-start.19 = (bf16[2,256,512]{2,1,0:T(8,128)(2,1)}, bf16[2,256,512]{2,1,0:T(8,128)(2,1)S(1)}, u32[]{:S(2)}) copy-start(bf16[2,256,512]{2,1,0:T(8,128)(2,1)S(1)} %get-tuple-element.25) | copy-start | bytes 1572868
  36.0 16.2 %copy-start.86 = (bf16[4096,512]{1,0:T(8,128)(2,1)S(1)}, bf16[4096,512]{1,0:T(8,128)(2,1)}, u32[]{:S(2)}) copy-start(bf16[4096,512]{1,0:T(8,128)(2,1)} %param.22) | copy-start | bytes 12582916
  78.3 32.8 %collective-permute-start.6 = (bf16[512,2,1024]{2,0,1:T(8,128)(2,1)}, bf16[512,2,1024]{2,0,1:T(8,128)(2,1)}, u32[]{:S(2)}, u32[]{:S(2)}) collective-permute-start(bf16[512,2,1024]{2,0,1:T(8,128)(2,1)} %bitcast.230), channel_id=1, source_target_pairs={{0,1},{1,0},{2,3},{3,2},{4,5},{5,4},{6,7},{7,6},{8,9},{9,8},{10,11... | collective-permute-start | bytes 6291464 | tf_op jit(solution)/shard_map/ppermute | solution.py:511
  108.1 178.2 %collective-permute-start.14 = (bf16[512,1024]{0,1:T(8,128)(2,1)}, bf16[512,1024]{0,1:T(8,128)(2,1)}, u32[]{:S(2)}, u32[]{:S(2)}) collective-permute-start(bf16[512,1024]{0,1:T(8,128)(2,1)} %bitcast.64), channel_id=1, source_target_pairs={{0,4},{4,0},{8,12},{12,8},{16,20},{20,16},{24,28},{28,24},{1,5},{5... | collective-permute-start | bytes 3145736 | tf_op jit(solution)/shard_map/ppermute | solution.py:515
  115.5 25.0 %collective-permute-start.7 = (bf16[512,1024]{1,0:T(8,128)(2,1)S(1)}, bf16[512,1024]{1,0:T(8,128)(2,1)}, u32[]{:S(2)}, u32[]{:S(2)}) collective-permute-start(bf16[512,1024]{1,0:T(8,128)(2,1)S(1)} %fusion.76), channel_id=1, source_target_pairs={{0,2},{1,3},{2,0},{3,1},{4,6},{5,7},{6,4},{7,5},{8,10},{9,11},{10,... | collective-permute-start | bytes 3145736 | tf_op jit(solution)/shard_map/ppermute | solution.py:511
  122.2 20.6 %copy-start.61 = (f32[2,256]{1,0:T(2,128)}, f32[2,256]{1,0:T(2,128)S(1)}, u32[]{:S(2)}) copy-start(f32[2,256]{1,0:T(2,128)S(1)} %get-tuple-element.112) | copy-start | bytes 6148
  122.2 20.6 %copy-start.71 = (f32[2,256]{1,0:T(2,128)}, f32[2,256]{1,0:T(2,128)S(1)}, u32[]{:S(2)}) copy-start(f32[2,256]{1,0:T(2,128)S(1)} %get-tuple-element.111) | copy-start | bytes 6148
  122.2 20.6 %copy-start.73 = (f32[2,256]{1,0:T(2,128)}, f32[2,256]{1,0:T(2,128)S(1)}, u32[]{:S(2)}) copy-start(f32[2,256]{1,0:T(2,128)S(1)} %get-tuple-element.113) | copy-start | bytes 6148
  122.3 20.6 %copy-start.63 = (f32[1,1024]{1,0:T(1,128)}, f32[1,1024]{1,0:T(1,128)S(1)}, u32[]{:S(2)}) copy-start(f32[1,1024]{1,0:T(1,128)S(1)} %get-tuple-element.105) | copy-start | bytes 12292
  122.3 20.6 %copy-start.65 = (f32[1,1024]{1,0:T(1,128)}, f32[1,1024]{1,0:T(1,128)S(1)}, u32[]{:S(2)}) copy-start(f32[1,1024]{1,0:T(1,128)S(1)} %get-tuple-element.106) | copy-start | bytes 12292
  122.3 20.6 %copy-start.67 = (f32[1,1024]{1,0:T(1,128)}, f32[1,1024]{1,0:T(1,128)S(1)}, u32[]{:S(2)}) copy-start(f32[1,1024]{1,0:T(1,128)S(1)} %get-tuple-element.107) | copy-start | bytes 12292
  122.3 20.6 %copy-start.69 = (f32[1,1024]{1,0:T(1,128)}, f32[1,1024]{1,0:T(1,128)S(1)}, u32[]{:S(2)}) copy-start(f32[1,1024]{1,0:T(1,128)S(1)} %get-tuple-element.108) | copy-start | bytes 12292
  123.0 19.9 %copy-start.22 = (f32[2,256,1024]{2,1,0:T(8,128)S(1)}, f32[2,256,1024]{2,1,0:T(8,128)}, u32[]{:S(2)}) copy-start(f32[2,256,1024]{2,1,0:T(8,128)} %convert.14) | copy-start | bytes 6291460
  123.0 19.9 %copy-start.29 = (bf16[1,512,1024]{2,1,0:T(8,128)(2,1)S(1)}, bf16[1,512,1024]{2,1,0:T(8,128)(2,1)}, u32[]{:S(2)}) copy-start(bf16[1,512,1024]{2,1,0:T(8,128)(2,1)} %get-tuple-element.81) | copy-start | bytes 3145732
  165.2 11.4 %copy-start.81 = (f32[1024]{0:T(1024)S(1)}, f32[1024]{0:T(1024)}, u32[]{:S(2)}) copy-start(f32[1024]{0:T(1024)} %convert_element_type.267) | copy-start | bytes 12292
  179.9 22.9 %copy-start.2 = (f32[2,256,1024]{2,1,0:T(8,128)S(1)}, f32[2,256,1024]{2,1,0:T(8,128)}, u32[]{:S(2)}) copy-start(f32[2,256,1024]{2,1,0:T(8,128)} %get-tuple-element.44.dy_ref) | copy-start | bytes 6291460
  179.9 22.9 %copy-start.8 = (f32[512,16]{1,0:T(8,128)S(1)}, f32[512,16]{1,0:T(8,128)}, u32[]{:S(2)}) copy-start(f32[512,16]{1,0:T(8,128)} %copy.63) | copy-start | bytes 98308
  244.4 12.6 %copy-start.12 = (f32[2,256,1024]{2,1,0:T(8,128)S(1)}, f32[2,256,1024]{2,1,0:T(8,128)}, u32[]{:S(2)}) copy-start(f32[2,256,1024]{2,1,0:T(8,128)} %copy-done.11) | copy-start | bytes 6291460
  246.3 10.7 %copy-start.28 = (bf16[1,512,1024]{2,1,0:T(8,128)(2,1)S(1)}, bf16[1,512,1024]{2,1,0:T(8,128)(2,1)}, u32[]{:S(2)}) copy-start(bf16[1,512,1024]{2,1,0:T(8,128)(2,1)} %copy-done.27) | copy-start | bytes 3145732
  257.8 11.7 %copy-start.77 = (f32[1024]{0:T(1024)S(1)}, f32[1024]{0:T(1024)}, u32[]{:S(2)}) copy-start(f32[1024]{0:T(1024)} %get-tuple-element.43) | copy-start | bytes 12292
  267.5 55.9 %collective-permute-start.21 = (bf16[512,1024]{1,0:T(8,128)(2,1)}, bf16[512,1024]{1,0:T(8,128)(2,1)}, u32[]{:S(2)}, u32[]{:S(2)}) collective-permute-start(bf16[512,1024]{1,0:T(8,128)(2,1)} %bitcast.55), channel_id=1, source_target_pairs={{0,4},{4,0},{8,12},{12,8},{16,20},{20,16},{24,28},{28,24},{1,5},{5... | collective-permute-start | bytes 3145736 | tf_op jit(solution)/shard_map/ppermute | solution.py:515
  267.8 73.5 %collective-permute-start.10 = (bf16[512,1024]{1,0:T(8,128)(2,1)}, bf16[512,1024]{1,0:T(8,128)(2,1)}, u32[]{:S(2)}, u32[]{:S(2)}) collective-permute-start(bf16[512,1024]{1,0:T(8,128)(2,1)} %bitcast.55), channel_id=1, source_target_pairs={{1,2},{5,6},{9,10},{13,14},{17,18},{21,22},{25,26},{29,30}} | collective-permute-start | bytes 3145736 | tf_op jit(solution)/shard_map/ppermute | solution.py:553
  277.3 24.9 %collective-permute-start.16 = (bf16[4,48,1024]{2,1,0:T(8,128)(2,1)}, bf16[4,48,1024]{2,1,0:T(8,128)(2,1)}, u32[]{:S(2)}, u32[]{:S(2)}) collective-permute-start(bf16[4,48,1024]{2,1,0:T(8,128)(2,1)} %fusion.96), channel_id=1, source_target_pairs={{0,4},{4,0},{8,12},{12,8},{16,20},{20,16},{24,28},{28,24},{1,5},{5... | collective-permute-start | bytes 1179656 | tf_op jit(solution)/shard_map/ppermute | solution.py:515
  283.2 29.6 %collective-permute-start.32 = (bf16[512,512]{1,0:T(8,128)(2,1)S(1)}, bf16[512,512]{1,0:T(8,128)(2,1)S(1)}, u32[]{:S(2)}, u32[]{:S(2)}) collective-permute-start(bf16[512,512]{1,0:T(8,128)(2,1)S(1)} %bitcast.282), channel_id=1, source_target_pairs={{0,4},{4,0},{8,12},{12,8},{16,20},{20,16},{24,28},{28,24},{1,5},{5... | collective-permute-start | bytes 1572872 | tf_op jit(solution)/shard_map/ppermute | solution.py:515
  286.3 55.0 %collective-permute-start.9 = (bf16[512,1024]{1,0:T(8,128)(2,1)}, bf16[512,1024]{1,0:T(8,128)(2,1)}, u32[]{:S(2)}, u32[]{:S(2)}) collective-permute-start(bf16[512,1024]{1,0:T(8,128)(2,1)} %bitcast.55), channel_id=1, source_target_pairs={{0,2},{2,3},{4,6},{6,7},{8,10},{10,11},{12,14},{14,15},{16,18},{18... | collective-permute-start | bytes 3145736 | tf_op jit(solution)/shard_map/ppermute | solution.py:552
  302.2 39.2 %collective-permute-start.11 = (bf16[512,1024]{1,0:T(8,128)(2,1)}, bf16[512,1024]{1,0:T(8,128)(2,1)}, u32[]{:S(2)}, u32[]{:S(2)}) collective-permute-start(bf16[512,1024]{1,0:T(8,128)(2,1)} %bitcast.54), channel_id=1, source_target_pairs={{3,1},{7,5},{11,9},{15,13},{19,17},{23,21},{27,25},{31,29}} | collective-permute-start | bytes 3145736 | tf_op jit(solution)/shard_map/ppermute | solution.py:547
  313.6 28.3 %collective-permute-start.8 = (bf16[512,1024]{1,0:T(8,128)(2,1)}, bf16[512,1024]{1,0:T(8,128)(2,1)}, u32[]{:S(2)}, u32[]{:S(2)}) collective-permute-start(bf16[512,1024]{1,0:T(8,128)(2,1)} %bitcast.54), channel_id=1, source_target_pairs={{1,0},{2,1},{5,4},{6,5},{9,8},{10,9},{13,12},{14,13},{17,16},{18,1... | collective-permute-start | bytes 3145736 | tf_op jit(solution)/shard_map/ppermute | solution.py:546
  323.4 17.6 %collective-permute-start.34 = (bf16[512,512]{1,0:T(8,128)(2,1)}, bf16[512,512]{1,0:T(8,128)(2,1)}, u32[]{:S(2)}, u32[]{:S(2)}) collective-permute-start(bf16[512,512]{1,0:T(8,128)(2,1)} %copy-done.51), channel_id=1, source_target_pairs={{0,2},{1,3},{2,0},{3,1},{4,6},{5,7},{6,4},{7,5},{8,10},{9,11},{10,... | collective-permute-start | bytes 1572872 | tf_op jit(solution)/shard_map/ppermute | solution.py:511
  341.0 23.3 %collective-permute-start.15 = (bf16[512,1024]{1,0:T(8,128)(2,1)}, bf16[512,1024]{1,0:T(8,128)(2,1)}, u32[]{:S(2)}, u32[]{:S(2)}) collective-permute-start(bf16[512,1024]{1,0:T(8,128)(2,1)} %bitcast.54), channel_id=1, source_target_pairs={{0,4},{4,0},{8,12},{12,8},{16,20},{20,16},{24,28},{28,24},{1,5},{5... | collective-permute-start | bytes 3145736 | tf_op jit(solution)/shard_map/ppermute | solution.py:515
  341.3 71.6 %collective-permute-start.1 = (bf16[512,1024]{0,1:T(8,128)(2,1)S(1)}, bf16[512,1024]{0,1:T(8,128)(2,1)S(1)}, u32[]{:S(2)}, u32[]{:S(2)}) collective-permute-start(bf16[512,1024]{0,1:T(8,128)(2,1)S(1)} %copy-done.49), channel_id=1, source_target_pairs={{0,2},{1,3},{2,0},{3,1},{4,6},{5,7},{6,4},{7,5},{8,10},{9,11},{10,... | collective-permute-start | bytes 3145736 | tf_op jit(solution)/shard_map/ppermute | solution.py:511
  341.3 30.9 %collective-permute-start.33 = (bf16[512,512]{1,0:T(8,128)(2,1)S(1)}, bf16[512,512]{1,0:T(8,128)(2,1)}, u32[]{:S(2)}, u32[]{:S(2)}) collective-permute-start(bf16[512,512]{1,0:T(8,128)(2,1)S(1)} %copy-done.52), channel_id=1, source_target_pairs={{0,1},{1,0},{2,3},{3,2},{4,5},{5,4},{6,7},{7,6},{8,9},{9,8},{10,11... | collective-permute-start | bytes 1572872 | tf_op jit(solution)/shard_map/ppermute | solution.py:511
  341.4 59.1 %collective-permute-start.35 = (bf16[512,512]{1,0:T(8,128)(2,1)}, bf16[512,512]{1,0:T(8,128)(2,1)}, u32[]{:S(2)}, u32[]{:S(2)}) collective-permute-start(bf16[512,512]{1,0:T(8,128)(2,1)} %collective-permute-done.34), channel_id=1, source_target_pairs={{0,1},{1,0},{2,3},{3,2},{4,5},{5,4},{6,7},{7,6},{8,9},{9,8},{10,11... | collective-permute-start | bytes 1572872 | tf_op jit(solution)/shard_map/ppermute | solution.py:511
  341.9 60.3 %collective-permute-start.22 = (bf16[256,1024]{1,0:T(8,128)(2,1)S(1)}, bf16[256,1024]{1,0:T(8,128)(2,1)S(1)}, u32[]{:S(2)}, u32[]{:S(2)}) collective-permute-start(bf16[256,1024]{1,0:T(8,128)(2,1)S(1)} %get-tuple-element.58), channel_id=1, source_target_pairs={{0,8},{4,12},{8,16},{12,20},{16,24},{20,28},{24,0},{28,4},{1,9},{5... | collective-permute-start | bytes 1572872 | tf_op jit(solution)/shard_map/ppermute | solution.py:529
  346.1 21.9 %copy-start.45 = (bf16[512,4,1,256]{0,3,1,2:T(8,128)(2,1)S(1)}, bf16[512,4,1,256]{0,3,1,2:T(8,128)(2,1)}, u32[]{:S(2)}) copy-start(bf16[512,4,1,256]{0,3,1,2:T(8,128)(2,1)} %copy.82) | copy-start | bytes 3145732
  364.2 41.4 %collective-permute-start.24 = (bf16[256,1024]{1,0:T(8,128)(2,1)S(1)}, bf16[256,1024]{1,0:T(8,128)(2,1)S(1)}, u32[]{:S(2)}, u32[]{:S(2)}) collective-permute-start(bf16[256,1024]{1,0:T(8,128)(2,1)S(1)} %get-tuple-element.59), channel_id=1, source_target_pairs={{0,24},{4,28},{8,0},{12,4},{16,8},{20,12},{24,16},{28,20},{1,25},{... | collective-permute-start | bytes 1572872 | tf_op jit(solution)/shard_map/ppermute | solution.py:529
  372.2 37.8 %collective-permute-start.23 = (bf16[256,1024]{1,0:T(8,128)(2,1)S(1)}, bf16[256,1024]{1,0:T(8,128)(2,1)S(1)}, u32[]{:S(2)}, u32[]{:S(2)}) collective-permute-start(bf16[256,1024]{1,0:T(8,128)(2,1)S(1)} %get-tuple-element.60), channel_id=1, source_target_pairs={{0,16},{4,20},{8,24},{12,28},{16,0},{20,4},{24,8},{28,12},{1,17},{... | collective-permute-start | bytes 1572872 | tf_op jit(solution)/shard_map/ppermute | solution.py:529
  400.5 19.5 %collective-permute-start.17 = (bf16[304,1024]{1,0:T(8,128)(2,1)S(1)}, bf16[304,1024]{1,0:T(8,128)(2,1)S(1)}, u32[]{:S(2)}, u32[]{:S(2)}) collective-permute-start(bf16[304,1024]{1,0:T(8,128)(2,1)S(1)} %get-tuple-element.50), channel_id=1, source_target_pairs={{0,8},{4,12},{8,16},{12,20},{16,24},{20,28},{24,0},{28,4},{1,9},{5... | collective-permute-start | bytes 1867784 | tf_op jit(solution)/shard_map/ppermute | solution.py:529
  402.2 43.8 %collective-permute-start.18 = (bf16[304,1024]{1,0:T(8,128)(2,1)S(1)}, bf16[304,1024]{1,0:T(8,128)(2,1)S(1)}, u32[]{:S(2)}, u32[]{:S(2)}) collective-permute-start(bf16[304,1024]{1,0:T(8,128)(2,1)S(1)} %get-tuple-element.51), channel_id=1, source_target_pairs={{0,16},{4,20},{8,24},{12,28},{16,0},{20,4},{24,8},{28,12},{1,17},{... | collective-permute-start | bytes 1867784 | tf_op jit(solution)/shard_map/ppermute | solution.py:529
  405.6 40.4 %collective-permute-start.19 = (bf16[304,1024]{1,0:T(8,128)(2,1)S(1)}, bf16[304,1024]{1,0:T(8,128)(2,1)S(1)}, u32[]{:S(2)}, u32[]{:S(2)}) collective-permute-start(bf16[304,1024]{1,0:T(8,128)(2,1)S(1)} %get-tuple-element.52), channel_id=1, source_target_pairs={{0,24},{4,28},{8,0},{12,4},{16,8},{20,12},{24,16},{28,20},{1,25},{... | collective-permute-start | bytes 1867784 | tf_op jit(solution)/shard_map/ppermute | solution.py:529
  410.0 87.8 %collective-permute-start.36 = (bf16[512,512]{1,0:T(8,128)(2,1)S(1)}, bf16[512,512]{1,0:T(8,128)(2,1)}, u32[]{:S(2)}, u32[]{:S(2)}) collective-permute-start(bf16[512,512]{1,0:T(8,128)(2,1)S(1)} %bitcast.246), channel_id=1, source_target_pairs={{0,4},{4,0},{8,12},{12,8},{16,20},{20,16},{24,28},{28,24},{1,5},{5... | collective-permute-start | bytes 1572872 | tf_op jit(solution)/shard_map/ppermute | solution.py:515
  412.9 64.7 %collective-permute-start = (bf16[512,1024]{0,1:T(8,128)(2,1)S(1)}, bf16[512,1024]{0,1:T(8,128)(2,1)S(1)}, u32[]{:S(2)}, u32[]{:S(2)}) collective-permute-start(bf16[512,1024]{0,1:T(8,128)(2,1)S(1)} %copy-done.49), channel_id=1, source_target_pairs={{0,1},{1,0},{2,3},{3,2},{4,5},{5,4},{6,7},{7,6},{8,9},{9,8},{10,11... | collective-permute-start | bytes 3145736 | tf_op jit(solution)/shard_map/ppermute | solution.py:511
  420.0 74.7 %collective-permute-start.12 = (bf16[2,2,64,2048]{3,2,0,1:T(8,128)(2,1)}, bf16[2,2,64,2048]{3,2,0,1:T(8,128)(2,1)}, u32[]{:S(2)}, u32[]{:S(2)}) collective-permute-start(bf16[2,2,64,2048]{3,2,0,1:T(8,128)(2,1)} %bitcast.231), channel_id=1, source_target_pairs={{0,1},{1,0},{2,3},{3,2},{4,5},{5,4},{6,7},{7,6},{8,9},{9,8},{10,11... | collective-permute-start | bytes 3145736 | tf_op jit(solution)/shard_map/ppermute | solution.py:511
  446.0 33.7 %collective-permute-start.2 = (bf16[512,1024]{0,1:T(8,128)(2,1)S(1)}, bf16[512,1024]{0,1:T(8,128)(2,1)S(1)}, u32[]{:S(2)}, u32[]{:S(2)}) collective-permute-start(bf16[512,1024]{0,1:T(8,128)(2,1)S(1)} %collective-permute-done.1), channel_id=1, source_target_pairs={{0,1},{1,0},{2,3},{3,2},{4,5},{5,4},{6,7},{7,6},{8,9},{9,8},{10,11... | collective-permute-start | bytes 3145736 | tf_op jit(solution)/shard_map/ppermute | solution.py:511
  446.5 34.7 %copy-start.32 = (bf16[304,1024]{1,0:T(8,128)(2,1)}, bf16[304,1024]{1,0:T(8,128)(2,1)S(1)}, u32[]{:S(2)}) copy-start(bf16[304,1024]{1,0:T(8,128)(2,1)S(1)} %fusion.63) | copy-start | bytes 1867780
  446.5 34.7 %copy-start.40 = (bf16[1,512,1024]{1,2,0:T(8,128)(2,1)S(1)}, bf16[1,512,1024]{1,2,0:T(8,128)(2,1)}, u32[]{:S(2)}) copy-start(bf16[1,512,1024]{1,2,0:T(8,128)(2,1)} %copy.59) | copy-start | bytes 3145732
  446.5 18.4 %collective-permute-start.28 = (bf16[48,1024]{1,0:T(8,128)(2,1)S(1)}, bf16[48,1024]{1,0:T(8,128)(2,1)S(1)}, u32[]{:S(2)}, u32[]{:S(2)}) collective-permute-start(bf16[48,1024]{1,0:T(8,128)(2,1)S(1)} %slice.126), channel_id=1, source_target_pairs={{0,8},{4,12},{8,16},{12,20},{16,24},{20,28},{24,0},{28,4},{1,9},{5... | collective-permute-start | bytes 294920 | tf_op jit(solution)/shard_map/ppermute | solution.py:540
  464.9 6.6 %collective-permute-start.29 = (bf16[48,1024]{1,0:T(8,128)(2,1)S(1)}, bf16[48,1024]{1,0:T(8,128)(2,1)S(1)}, u32[]{:S(2)}, u32[]{:S(2)}) collective-permute-start(bf16[48,1024]{1,0:T(8,128)(2,1)S(1)} %slice.126), channel_id=1, source_target_pairs={{0,16},{4,20},{8,24},{12,28},{16,0},{20,4},{24,8},{28,12},{1,17},{... | collective-permute-start | bytes 294920 | tf_op jit(solution)/shard_map/ppermute | solution.py:540
  471.5 4.6 collective-permute-start.30
  476.1 37.8 %collective-permute-start.26 = (bf16[256,1024]{1,0:T(8,128)(2,1)S(1)}, bf16[256,1024]{1,0:T(8,128)(2,1)}, u32[]{:S(2)}, u32[]{:S(2)}) collective-permute-start(bf16[256,1024]{1,0:T(8,128)(2,1)S(1)} %fusion.84), channel_id=1, source_target_pairs={{1,2},{5,6},{9,10},{13,14},{17,18},{21,22},{25,26},{29,30}} | collective-permute-start | bytes 1572872 | tf_op jit(solution)/shard_map/ppermute | solution.py:553
  477.6 37.3 %collective-permute-start.25 = (bf16[256,1024]{1,0:T(8,128)(2,1)S(1)}, bf16[256,1024]{1,0:T(8,128)(2,1)}, u32[]{:S(2)}, u32[]{:S(2)}) collective-permute-start(bf16[256,1024]{1,0:T(8,128)(2,1)S(1)} %fusion.84), channel_id=1, source_target_pairs={{0,2},{2,3},{4,6},{6,7},{8,10},{10,11},{12,14},{14,15},{16,18},{18... | collective-permute-start | bytes 1572872 | tf_op jit(solution)/shard_map/ppermute | solution.py:552
  479.8 35.3 %collective-permute-start.27 = (bf16[256,1024]{1,0:T(8,128)(2,1)}, bf16[256,1024]{1,0:T(8,128)(2,1)}, u32[]{:S(2)}, u32[]{:S(2)}) collective-permute-start(bf16[256,1024]{1,0:T(8,128)(2,1)} %slice.125), channel_id=1, source_target_pairs={{3,1},{7,5},{11,9},{15,13},{19,17},{23,21},{27,25},{31,29}} | collective-permute-start | bytes 1572872 | tf_op jit(solution)/shard_map/ppermute | solution.py:547
  494.7 20.4 %collective-permute-start.20 = (bf16[256,1024]{1,0:T(8,128)(2,1)}, bf16[256,1024]{1,0:T(8,128)(2,1)S(1)}, u32[]{:S(2)}, u32[]{:S(2)}) collective-permute-start(bf16[256,1024]{1,0:T(8,128)(2,1)} %slice.125), channel_id=1, source_target_pairs={{1,0},{2,1},{5,4},{6,5},{9,8},{10,9},{13,12},{14,13},{17,16},{18,1... | collective-permute-start | bytes 1572872 | tf_op jit(solution)/shard_map/ppermute | solution.py:546
  497.8 11.9 %collective-permute-start.31 = (bf16[4,48,1024]{2,1,0:T(8,128)(2,1)S(1)}, bf16[4,48,1024]{2,1,0:T(8,128)(2,1)S(1)}, u32[]{:S(2)}, u32[]{:S(2)}) collective-permute-start(bf16[4,48,1024]{2,1,0:T(8,128)(2,1)S(1)} %copy-done.44), channel_id=1, source_target_pairs={{0,4},{4,0},{8,12},{12,8},{16,20},{20,16},{24,28},{28,24},{1,5},{5... | collective-permute-start | bytes 1179656 | tf_op jit(solution)/shard_map/ppermute | solution.py:515
  509.7 9.9 %collective-permute-start.5 = (bf16[2,64,512]{2,1,0:T(8,128)(2,1)S(1)}, bf16[2,64,512]{2,1,0:T(8,128)(2,1)S(1)}, u32[]{:S(2)}, u32[]{:S(2)}) collective-permute-start(bf16[2,64,512]{2,1,0:T(8,128)(2,1)S(1)} %get-tuple-element.96), channel_id=1, source_target_pairs={{0,3},{1,2},{2,1},{3,0},{4,7},{5,6},{6,5},{7,4},{8,11},{9,10},{10,... | collective-permute-start | bytes 393224 | tf_op jit(solution)/shard_map/ppermute | solution.py:511
  513.9 9.9 %collective-permute-start.4 = (bf16[2,64,512]{2,1,0:T(8,128)(2,1)S(1)}, bf16[2,64,512]{2,1,0:T(8,128)(2,1)S(1)}, u32[]{:S(2)}, u32[]{:S(2)}) collective-permute-start(bf16[2,64,512]{2,1,0:T(8,128)(2,1)S(1)} %get-tuple-element.97), channel_id=1, source_target_pairs={{0,2},{1,3},{2,0},{3,1},{4,6},{5,7},{6,4},{7,5},{8,10},{9,11},{10,... | collective-permute-start | bytes 393224 | tf_op jit(solution)/shard_map/ppermute | solution.py:511
  514.9 9.5 %collective-permute-start.3 = (bf16[2,64,512]{2,1,0:T(8,128)(2,1)S(1)}, bf16[2,64,512]{2,1,0:T(8,128)(2,1)S(1)}, u32[]{:S(2)}, u32[]{:S(2)}) collective-permute-start(bf16[2,64,512]{2,1,0:T(8,128)(2,1)S(1)} %get-tuple-element.98), channel_id=1, source_target_pairs={{0,1},{1,0},{2,3},{3,2},{4,5},{5,4},{6,7},{7,6},{8,9},{9,8},{10,11... | collective-permute-start | bytes 393224 | tf_op jit(solution)/shard_map/ppermute | solution.py:511
  515.1 18.0 %collective-permute-start.37 = (bf16[512,512]{1,0:T(8,128)(2,1)S(1)}, bf16[512,512]{1,0:T(8,128)(2,1)S(1)}, u32[]{:S(2)}, u32[]{:S(2)}) collective-permute-start(bf16[512,512]{1,0:T(8,128)(2,1)S(1)} %get-tuple-element.55), channel_id=1, source_target_pairs={{0,8},{4,12},{8,16},{12,20},{16,24},{20,28},{24,0},{28,4},{1,9},{5... | collective-permute-start | bytes 1572872 | tf_op jit(solution)/shard_map/ppermute | solution.py:529
  515.1 16.3 %collective-permute-start.13 = (bf16[2,64,2048]{2,1,0:T(8,128)(2,1)S(1)}, bf16[2,64,2048]{2,1,0:T(8,128)(2,1)S(1)}, u32[]{:S(2)}, u32[]{:S(2)}) collective-permute-start(bf16[2,64,2048]{2,1,0:T(8,128)(2,1)S(1)} %fusion.89), channel_id=1, source_target_pairs={{0,2},{1,3},{2,0},{3,1},{4,6},{5,7},{6,4},{7,5},{8,10},{9,11},{10,... | collective-permute-start | bytes 1572872 | tf_op jit(solution)/shard_map/ppermute | solution.py:511
  519.6 11.7 %copy-start.7 = (bf16[2,64,2048]{2,1,0:T(8,128)(2,1)S(1)}, bf16[2,64,2048]{2,1,0:T(8,128)(2,1)}, u32[]{:S(2)}) copy-start(bf16[2,64,2048]{2,1,0:T(8,128)(2,1)} %x_ref.1) | copy-start | bytes 1572868
  519.6 11.7 %copy-start.60 = (f32[1,4,4,128]{3,1,2,0:T(4,128)S(1)}, f32[1,4,4,128]{3,1,2,0:T(4,128)}, u32[]{:S(2)}) copy-start(f32[1,4,4,128]{3,1,2,0:T(4,128)} %copy-done.59) | copy-start | bytes 24580
  519.7 23.2 %collective-permute-start.39 = (bf16[512,512]{1,0:T(8,128)(2,1)S(1)}, bf16[512,512]{1,0:T(8,128)(2,1)S(1)}, u32[]{:S(2)}, u32[]{:S(2)}) collective-permute-start(bf16[512,512]{1,0:T(8,128)(2,1)S(1)} %get-tuple-element.56), channel_id=1, source_target_pairs={{0,24},{4,28},{8,0},{12,4},{16,8},{20,12},{24,16},{28,20},{1,25},{... | collective-permute-start | bytes 1572872 | tf_op jit(solution)/shard_map/ppermute | solution.py:529
  523.8 41.6 %collective-permute-start.38 = (bf16[512,512]{1,0:T(8,128)(2,1)S(1)}, bf16[512,512]{1,0:T(8,128)(2,1)S(1)}, u32[]{:S(2)}, u32[]{:S(2)}) collective-permute-start(bf16[512,512]{1,0:T(8,128)(2,1)S(1)} %get-tuple-element.57), channel_id=1, source_target_pairs={{0,16},{4,20},{8,24},{12,28},{16,0},{20,4},{24,8},{28,12},{1,17},{... | collective-permute-start | bytes 1572872 | tf_op jit(solution)/shard_map/ppermute | solution.py:529
  531.8 35.5 %copy-start.1 = (bf16[160,1024]{1,0:T(8,128)(2,1)S(1)}, bf16[160,1024]{1,0:T(8,128)(2,1)}, u32[]{:S(2)}) copy-start(bf16[160,1024]{1,0:T(8,128)(2,1)} %param.18) | copy-start | bytes 983044
  (63 other events, 215.0 us)

commit v3 on v2

v3 whole, which is shorter than its diff:
```python
import functools

import jax
import jax.numpy as jnp
from jax import lax
from jax.experimental import pallas as pl
from jax.experimental.pallas import tpu as pltpu
from jax.sharding import PartitionSpec as P

KW = 4
EPS = 1e-05
CHUNK = 16
LANES = 128
f32 = jnp.float32
bf16 = jnp.bfloat16


def rows_dot(a, b):
    return jnp.dot(a, b, preferred_element_type=f32)


def inner_dot(a, b):
    return lax.dot_general(a, b, (((0,), (0,)), ((), ())), preferred_element_type=f32)


def outer_dot(a, b):
    return lax.dot_general(a, b, (((1,), (1,)), ((), ())), preferred_element_type=f32)


def silu_slope(values):
    sig_val = jax.nn.sigmoid(values)
    return sig_val + values * sig_val * (1.0 - sig_val)

MESH = pl.DeviceIdType.MESH
BLOCK = 128


def lane(g):
    return slice(g * LANES, (g + 1) * LANES)


def column(block, t):
    return jnp.broadcast_to(block[:, t : t + 1], (block.shape[0], LANES))


def row(ref, t, g, n):
    return jnp.broadcast_to(ref[t : t + 1, lane(g)], (n, LANES))


def prepare(base, rate_ref, conv_ref, keep_ref, rk, u, kept):
    rows = pl.ds(base, CHUNK)
    rate = rate_ref[0, rows, :]
    keep = keep_ref[0, rows, :]
    conv = conv_ref[0, rows, :].astype(f32)
    for g in range(rate.shape[1] // LANES):
        rk[:, lane(g)] = rate[:, lane(g)] * keep
    u[...] = rate * conv
    kept[...] = keep
    return rate, conv, keep


def shifted(cols, j):
    size = cols.shape[1]
    return pltpu.roll(cols, lax.rem(size - j * CHUNK, size), 1)


def spread_mask(n):
    shape = (CHUNK, CHUNK * n)
    return lax.broadcasted_iota(jnp.int32, shape, 1) // n == lax.broadcasted_iota(jnp.int32, shape, 0)


def picker(n):
    shape = (n, CHUNK * n)
    return (lax.broadcasted_iota(jnp.int32, shape, 1) % n == lax.broadcasted_iota(jnp.int32, shape, 0)).astype(bf16)


def diagonal(rows, mask, pick):
    return jnp.where(mask, rows_dot(rows.astype(bf16), pick), 0.0).astype(bf16)


def forward_kernel(
    conv_ref, z_ref, proj_ref, keep_ref, dt_proj_ref, dt_bias_ref, skip_ref,
    y_ref, gated_ref, rate_ref, beta_ref, state_ref,
    held_ref, rk, u, kept, query_rows,
):
    width = conv_ref.shape[2]
    rank = dt_proj_ref.shape[0]
    n = (proj_ref.shape[0] - rank) // 2
    groups = width // LANES
    span = CHUNK * n

    @pl.when(pl.program_id(1) == 0)
    def _():
        held_ref[...] = jnp.zeros_like(held_ref)

    dt_low = proj_ref[0:rank, :].astype(bf16)
    keys = proj_ref[rank : rank + n, :]
    query_rows[...] = proj_ref[rank + n :, :].T
    key_square = jnp.sum(keys.T * keys.T, axis=1, keepdims=True)
    beta = jax.nn.sigmoid(inner_dot(dt_low, dt_proj_ref[...]) + dt_bias_ref[...])
    beta_ref[0] = beta
    rate_ref[0] = beta / (1.0 + beta * key_square)
    mask, pick = spread_mask(n), picker(n)

    def chunk(j, held):
        base = pl.multiple_of(j * CHUNK, CHUNK)
        rows = pl.ds(base, CHUNK)
        _, conv, _ = prepare(base, rate_ref, conv_ref, keep_ref, rk, u, kept)
        near_keys = shifted(keys, j)
        held = list(held)
        for t in range(CHUNK):
            key = column(near_keys, t)
            key2 = key * key
            keep = jnp.broadcast_to(kept[t : t + 1, :], (n, LANES))
            at = pl.ds(pl.multiple_of((base + t) * n, n), n)
            for g in range(groups):
                decay = keep - row(rk, t, g, n) * key2
                held[g] = decay * held[g] + row(u, t, g, n) * key
                state_ref[0, at, lane(g)] = held[g].astype(bf16)
        block = state_ref[0, pl.ds(pl.multiple_of(base * n, span), span), :]
        total = rows_dot(diagonal(query_rows[rows, :], mask, pick), block) + skip_ref[...] * conv
        y_ref[0, rows, :] = total
        z = z_ref[0, rows, :].astype(f32)
        gated_ref[0, rows, :] = (total * (z * jax.nn.sigmoid(z))).astype(bf16)
        return tuple(held)

    start = tuple(held_ref[:, lane(g)] for g in range(groups))
    end = lax.fori_loop(0, conv_ref.shape[1] // CHUNK, chunk, start)
    for g in range(groups):
        held_ref[:, lane(g)] = end[g]


def backward_kernel(
    rate_ref, beta_ref, conv_ref, dy_ref, proj_ref, keep_ref, dt_proj_ref, state_ref, last_ref,
    gconv_ref, gdt_ref, gproj_ref, gdt_proj_ref, gdt_bias_ref, gskip_ref,
    held_ref, grate, rk, u, dys, kept, key_rows, adj, adj_state, diag1, diag2, diag3,
):
    block_rows, width = rate_ref.shape[1:]
    rank = dt_proj_ref.shape[0]
    n = (proj_ref.shape[0] - rank) // 2
    groups = width // LANES
    span = CHUNK * n
    chunks = block_rows // CHUNK

    @pl.when(pl.program_id(1) == 0)
    def _():
        held_ref[...] = jnp.zeros_like(held_ref)

    @pl.when((pl.program_id(0) == 0) & (pl.program_id(1) == 0))
    def _():
        gdt_proj_ref[...] = jnp.zeros_like(gdt_proj_ref)
        gdt_bias_ref[...] = jnp.zeros_like(gdt_bias_ref)
        gskip_ref[...] = jnp.zeros_like(gskip_ref)

    keys = proj_ref[rank : rank + n, :]
    queries = proj_ref[rank + n :, :]
    key_rows[...] = keys.T
    mask, pick = spread_mask(n), picker(n)

    def chunk(step, held):
        j = chunks - 1 - step
        base = pl.multiple_of(j * CHUNK, CHUNK)
        rows = pl.ds(base, CHUNK)
        rate, conv, keeps = prepare(base, rate_ref, conv_ref, keep_ref, rk, u, kept)
        dys[...] = dy_ref[0, rows, :]
        near_keys = shifted(keys, j)
        near_queries = shifted(queries, j)
        held = list(held)
        for t in reversed(range(CHUNK)):
            key = column(near_keys, t)
            key2 = key * key
            query = column(near_queries, t)
            keep = jnp.broadcast_to(kept[t : t + 1, :], (n, LANES))
            prior = jnp.maximum(base + t - 1, 0)
            at = pl.ds(pl.multiple_of(prior * n, n), n)
            for g in range(groups):
                grad = held[g] + row(dys, t, g, n) * query
                decay = keep - row(rk, t, g, n) * key2
                held[g] = decay * grad
                adj[t * n : (t + 1) * n, lane(g)] = grad.astype(bf16)
                before = state_ref[0, at, lane(g)].astype(f32)
                if t == 0:
                    before = jnp.where(j == 0, last_ref[0, :, lane(g)].astype(f32), before)
                adj_state[t * n : (t + 1) * n, lane(g)] = (grad * before).astype(bf16)
        block = state_ref[0, pl.ds(pl.multiple_of(base * n, span), span), :]
        key_block = key_rows[rows, :]
        w1 = rows_dot(diagonal(key_block, mask, pick), adj[...])
        w2 = rows_dot(diagonal(key_block * key_block, mask, pick), adj_state[...])
        a1 = outer_dot(u[...].astype(bf16), adj[...])
        a2 = outer_dot(rk[...].astype(bf16), adj_state[...])
        a3 = outer_dot(dys[...].astype(bf16), block)
        diag1[rows, :] = jnp.where(mask, a1, 0.0)
        diag2[rows, :] = jnp.where(mask, a2, 0.0)
        diag3[rows, :] = jnp.where(mask, a3, 0.0)
        for g in range(groups):
            grate[rows, lane(g)] = conv[:, lane(g)] * w1[:, lane(g)] - keeps * w2[:, lane(g)]
        gconv_ref[0, rows, :] = rate * w1
        return tuple(held)

    start = tuple(held_ref[:, lane(g)] for g in range(groups))
    end = lax.fori_loop(0, chunks, chunk, start)
    for g in range(groups):
        held_ref[:, lane(g)] = end[g]

    def picked(left, value):
        high = value.astype(bf16)
        low = (value - high.astype(f32)).astype(bf16)
        return outer_dot(left, high) + outer_dot(left, low)

    rate = rate_ref[0]
    beta = beta_ref[0]
    grad_rate = grate[...]
    self_term = picked(jnp.ones((n, width), bf16), grad_rate * rate * rate)
    key_square = jnp.sum(key_rows[...] * key_rows[...], axis=1, keepdims=True)
    denom_inv = 1.0 / (1.0 + beta * key_square)
    grad_dt = grad_rate * denom_inv * denom_inv * beta * (1.0 - beta)
    low = grad_dt.astype(bf16)
    gdt_ref[0] = low
    gdt_bias_ref[...] += jnp.sum(grad_dt, axis=0, keepdims=True)
    gskip_ref[...] += jnp.sum(dy_ref[0] * conv_ref[0].astype(f32), axis=0, keepdims=True)
    gdt_proj_ref[...] += rows_dot(proj_ref[0:rank, :].astype(bf16), low)
    gproj_ref[0:rank, :] = outer_dot(dt_proj_ref[...], low)
    gproj_ref[rank : rank + n, :] = picked(pick, diag1[...]) - 2.0 * keys * (picked(pick, diag2[...]) + self_term)
    gproj_ref[rank + n :, :] = picked(pick, diag3[...])


def specs_for(length, reverse):
    blocks = length // BLOCK

    def place(b):
        return blocks - 1 - b if reverse else b

    def spec(*shape):
        return pl.BlockSpec((1,) + shape, lambda s, b: (s, place(b)) + (0,) * (len(shape) - 1))

    def across_spec(rows):
        return pl.BlockSpec((rows, BLOCK), lambda s, b: (0, s * blocks + place(b)))

    def whole(*shape):
        return pl.BlockSpec(shape, lambda s, b: (0,) * len(shape))

    return blocks, spec, across_spec, whole


def recurrence_forward(conv, z, proj, keep_lanes, dt_proj, dt_bias, skip):
    seqs, length, width = conv.shape
    rank = dt_proj.shape[0]
    n = (proj.shape[0] - rank) // 2
    blocks, spec, across_spec, whole = specs_for(length, False)
    wide = spec(BLOCK, width)
    full = jax.ShapeDtypeStruct((seqs, length, width), f32)
    return pl.pallas_call(
        forward_kernel,
        grid=(seqs, blocks),
        in_specs=[
            wide, wide, across_spec(proj.shape[0]), spec(BLOCK, LANES), whole(rank, width), whole(1, width),
            whole(1, width),
        ],
        out_specs=[wide, wide, wide, wide, spec(BLOCK * n, width)],
        out_shape=[
            full, jax.ShapeDtypeStruct((seqs, length, width), bf16), full, full,
            jax.ShapeDtypeStruct((seqs, length * n, width), bf16),
        ],
        scratch_shapes=[
            pltpu.VMEM((n, width), f32),
            pltpu.VMEM((CHUNK, width), f32),
            pltpu.VMEM((CHUNK, width), f32),
            pltpu.VMEM((CHUNK, LANES), f32),
            pltpu.VMEM((BLOCK, n), f32),
        ],
        compiler_params=pltpu.CompilerParams(vmem_limit_bytes=24 << 20),
        cost_estimate=pl.CostEstimate(flops=16_000_000_000, bytes_accessed=24 << 20, transcendentals=0),
        name="recurrence_forward",
    )(conv, z, proj, keep_lanes, dt_proj, dt_bias, skip)


def recurrence_backward(rate, beta, conv, dy, proj, keep_lanes, dt_proj, states):
    seqs, length, width = rate.shape
    rank = dt_proj.shape[0]
    n = (proj.shape[0] - rank) // 2
    span = CHUNK * n
    blocks, spec, across_spec, whole = specs_for(length, True)
    wide = spec(BLOCK, width)
    before = pl.BlockSpec((1, n, width), lambda s, b: (s, jnp.maximum((blocks - 1 - b) * BLOCK - 1, 0), 0))
    lined = pltpu.VMEM((BLOCK, span), f32)
    return pl.pallas_call(
        backward_kernel,
        grid=(seqs, blocks),
        in_specs=[
            wide, wide, wide, wide, across_spec(proj.shape[0]), spec(BLOCK, LANES), whole(rank, width),
            spec(BLOCK * n, width), before,
        ],
        out_specs=[wide, wide, across_spec(proj.shape[0]), whole(rank, width), whole(1, width), whole(1, width)],
        out_shape=[
            jax.ShapeDtypeStruct((seqs, length, width), f32),
            jax.ShapeDtypeStruct((seqs, length, width), bf16),
            jax.ShapeDtypeStruct(proj.shape, f32),
            jax.ShapeDtypeStruct((rank, width), f32),
            jax.ShapeDtypeStruct((1, width), f32),
            jax.ShapeDtypeStruct((1, width), f32),
        ],
        scratch_shapes=[
            pltpu.VMEM((n, width), f32),
            pltpu.VMEM((BLOCK, width), f32),
            pltpu.VMEM((CHUNK, width), f32),
            pltpu.VMEM((CHUNK, width), f32),
            pltpu.VMEM((CHUNK, width), f32),
            pltpu.VMEM((CHUNK, LANES), f32),
            pltpu.VMEM((BLOCK, n), f32),
            pltpu.VMEM((span, width), bf16),
            pltpu.VMEM((span, width), bf16),
            lined, lined, lined,
        ],
        compiler_params=pltpu.CompilerParams(vmem_limit_bytes=28 << 20),
        cost_estimate=pl.CostEstimate(flops=30_000_000_000, bytes_accessed=28 << 20, transcendentals=0),
        name="recurrence_backward",
    )(rate, beta, conv, dy, proj, keep_lanes, dt_proj, states, states)


def peer(hop):
    me = lax.axis_index("shard")
    core = lax.rem(me, 2)
    chip = me // 2
    if hop & 1:
        core = 1 - core
    if hop & 2:
        chip = 1 - chip
    return chip * 2 + core


def meet_group():
    barrier = pltpu.get_barrier_semaphore()
    for hop in (1, 2, 3):
        pl.semaphore_signal(barrier, inc=1, device_id={"shard": peer(hop)}, device_id_type=MESH)
    pl.semaphore_wait(barrier, 3)


def remote(src, dst, sends, recvs, at, hop):
    return pltpu.make_async_remote_copy(
        src_ref=src, dst_ref=dst, send_sem=sends.at[at], recv_sem=recvs.at[at],
        device_id={"shard": peer(hop)}, device_id_type=MESH,
    )


def group_params(collective_id, limit):
    return pltpu.CompilerParams(collective_id=collective_id, has_side_effects=True, vmem_limit_bytes=limit)


VMEM_SPEC = pl.BlockSpec(memory_space=pltpu.VMEM)


ANY_SPEC = pl.BlockSpec(memory_space=pl.ANY)


def part_copy(src, dst, send, recv, shard):
    return pltpu.make_async_remote_copy(
        src_ref=src, dst_ref=dst, send_sem=send, recv_sem=recv, device_id={"shard": shard}, device_id_type=MESH
    )


def front_kernel(
    x_ref, cot_ref, gain_ref, w_hbm, o_hbm,
    xs_ref, all_cots_ref, gains_ref, normed_ref, pair_ref, parts_ref, own_ref, send_ref,
    w_ref, o_ref, lhs, mixed, pairs, near, sends, recvs, local, part_sends, part_recvs, part_local,
    pair_sends, pair_recvs, pair_local,
):
    me = lax.axis_index("shard")
    chip = me // 2
    slot = me // 2
    seqs, rows, model = x_ref.shape
    cots_ref = all_cots_ref.at[0]
    cols = all_cots_ref.shape[3]
    side = lax.rem(lax.axis_index("replica"), 2)
    height = lax.axis_size("replica") // 2
    block = model // 2 // height
    aligned = block % LANES == 0
    width = parts_ref.shape[3]
    lift = gain_ref.shape[0]
    span = 2 * rows
    tile = 256
    loads = [
        pltpu.make_async_copy(w_hbm, w_ref, local.at[3]),
        pltpu.make_async_copy(o_hbm, o_ref, local.at[4]),
    ]
    for copy in loads:
        copy.start()
    other = meet_group_and_pair()

    def mine(ref, owner):
        return ref.at[:, pl.ds(pl.multiple_of(owner * rows, 16), rows), :]

    def part(owner):
        return cot_ref.at[:, :, pl.ds(pl.multiple_of(owner * cols, 128), cols)]

    def gain_rows(owner):
        return gains_ref.at[pl.ds(pl.multiple_of(owner * lift, 8), lift), :]

    gain_sends = [remote(gain_ref, gain_rows(me), sends, recvs, 5 + hop, hop) for hop in (1, 2, 3)]
    x_core = remote(x_ref, mine(xs_ref, me), sends, recvs, 0, 1)
    x_chip = remote(x_ref, mine(xs_ref, me), sends, recvs, 1, 2)
    cot_sends = [remote(part(peer(hop)), mine(cots_ref, me), sends, recvs, 2 + hop, hop) for hop in (1, 2, 3)]
    for copy in gain_sends + [x_core, x_chip] + cot_sends:
        copy.start()
    own = [
        pltpu.make_async_copy(x_ref, mine(xs_ref, me), local.at[0]),
        pltpu.make_async_copy(part(me), mine(cots_ref, me), local.at[1]),
        pltpu.make_async_copy(gain_ref, gain_rows(me), local.at[2]),
    ]
    for copy in own:
        copy.start()
    for copy in own:
        copy.wait()
    for copy in gain_sends:
        copy.wait()
    x_core.wait()
    gain = jnp.concatenate([gains_ref[lift * d : lift * d + 1, :] for d in range(4)], axis=1)
    loads[0].wait()

    def piece(half, i):
        where = jnp.bitwise_xor(chip, half)
        return parts_ref.at[slot, :, pl.ds(pl.multiple_of(where * span, 16), span), :]

    def away(i):
        return lax.rem(2 * me + i, 4) != me

    def send(half, i):
        return part_copy(
            mixed.at[half, i], piece(half, i), part_sends.at[2 * half + i], part_recvs.at[2 * slot + half],
            lax.rem(2 * me + i, 4),
        )

    def keep(half, i):
        return pltpu.make_async_copy(mixed.at[half, i], piece(half, i), part_local.at[half])

    def either(i, yes, no):
        pl.when(away(i))(yes)
        pl.when(jnp.logical_not(away(i)))(no)

    def run_half(half):
        where = jnp.bitwise_xor(chip, half) * span

        for seq in range(seqs):

            def norm(r, carry, seq=seq):
                at = pl.ds(pl.multiple_of(where + r * 16, 16), 16)
                vals = xs_ref[seq, at, :].astype(f32)
                inv = lax.rsqrt(jnp.mean(vals * vals, axis=1, keepdims=True) + EPS)
                out = (vals * inv * gain).astype(bf16)
                normed_ref[seq, at, :] = out
                lhs[pl.ds(pl.multiple_of(seq * span + r * 16, 16), 16), :] = out
                return carry

            lax.fori_loop(0, span // 16, norm, 0)
        for copy in normed_copies(half):
            copy.start()
        for i in range(2):

            def product(t, carry, i=i):
                value = rows_dot(lhs[...], w_ref[:, pl.ds(pl.multiple_of(i * width + t * tile, tile), tile)])
                for seq in range(seqs):
                    mixed[half, i, seq, :, pl.ds(pl.multiple_of(t * tile, tile), tile)] = value[
                        seq * span : (seq + 1) * span
                    ].astype(bf16)
                return carry

            lax.fori_loop(0, width // tile, product, 0)
            either(i, lambda i=i: send(half, i).start(), lambda i=i: keep(half, i).start())

    def normed_copies(half):
        where = pl.ds(pl.multiple_of(jnp.bitwise_xor(chip, half) * span, 16), span)
        copies = []
        for b in range(height if aligned else 0):
            def cut(which, b=b):
                return normed_ref.at[:, where, pl.ds(pl.multiple_of((2 * b + which) * block, LANES), block)]

            goal = (slice(None), where, slice(b * block, (b + 1) * block))
            at = half * height + b
            copies.append(pltpu.make_async_copy(cut(side), pair_ref.at[(0,) + goal], pair_local.at[at]))
            copies.append(across(cut(1 - side), pair_ref.at[(1,) + goal], pair_sends, pair_recvs, at, other))
        return copies

    run_half(0)
    x_chip.wait_recv()
    onward = remote(mine(xs_ref, peer(2)), mine(xs_ref, peer(2)), sends, recvs, 2, 1)
    onward.start()
    onward.wait()
    run_half(1)

    for copy in cot_sends:
        copy.wait()
    cot_pair = across(all_cots_ref.at[0], all_cots_ref.at[1], sends, recvs, 11, other)
    cot_pair.start()
    loads[1].wait()

    def partial(block, t):
        return outer_dot(
            cots_ref[...].reshape(seqs * 4 * rows, cols),
            o_ref[pl.ds(pl.multiple_of(block * width + t * tile, tile), tile), :],
        )

    def lanes(t):
        return pl.ds(pl.multiple_of(t * tile, tile), tile)

    near_sends = []
    for at, hop in enumerate((3, 1)):

        def fill(t, carry, at=at, hop=hop):
            pairs[at, :, lanes(t)] = partial(peer(hop), t).astype(bf16)
            return carry

        lax.fori_loop(0, width // tile, fill, 0)
        copy = remote(pairs.at[at], near.at[at], sends, recvs, 9 + at, 1)
        copy.start()
        near_sends.append(copy)
    near_sends[0].wait()

    def to_send(t, carry):
        send_ref[:, lanes(t)] = (partial(peer(2), t) + near[0, :, lanes(t)].astype(f32)).astype(bf16)
        return carry

    lax.fori_loop(0, width // tile, to_send, 0)
    near_sends[1].wait()

    def to_own(t, carry):
        own_ref[:, lanes(t)] = partial(me, t) + near[1, :, lanes(t)].astype(f32)
        return carry

    lax.fori_loop(0, width // tile, to_own, 0)

    x_chip.wait_send()
    cot_pair.wait()
    for copy in normed_copies(0) + normed_copies(1):
        copy.wait()
    for half in range(2):
        for i in range(2):
            either(i, lambda half=half, i=i: send(half, i).wait_send(), lambda half=half, i=i: keep(half, i).wait())
        for at in range(2):

            @pl.when(2 * at + me // 2 != me)
            def _(at=at, half=half):
                part_copy(
                    mixed.at[0, 0], mixed.at[0, 0], part_sends.at[0], part_recvs.at[2 * at + half], peer(1)
                ).wait_recv()


def front(x, cot, gain, w_in, out_proj):
    seqs, rows, model = x.shape
    group = lax.axis_size("shard")
    length = rows * group
    cols = model // group
    width = w_in.shape[1] // 2
    tokens = seqs * length
    lifted = jnp.broadcast_to(gain.astype(f32)[None], (8, gain.shape[0]))
    far_sems = pltpu.SemaphoreType.DMA((lax.axis_size("replica"),))
    return pl.pallas_call(
        front_kernel,
        in_specs=[VMEM_SPEC] * 3 + [ANY_SPEC] * 2,
        out_specs=[VMEM_SPEC] * 8,
        out_shape=[
            jax.ShapeDtypeStruct((seqs, length, model), bf16),
            jax.ShapeDtypeStruct((2, seqs, length, cols), bf16),
            jax.ShapeDtypeStruct((8 * group, gain.shape[0]), f32),
            jax.ShapeDtypeStruct((seqs, length, model), bf16),
            jax.ShapeDtypeStruct((2, seqs, length, model // 2), bf16),
            jax.ShapeDtypeStruct((2, seqs, length, width), bf16),
            jax.ShapeDtypeStruct((tokens, width), f32),
            jax.ShapeDtypeStruct((tokens, width), bf16),
        ],
        scratch_shapes=[
            pltpu.VMEM(w_in.shape, bf16),
            pltpu.VMEM(out_proj.shape, bf16),
            pltpu.VMEM((tokens // 2, model), bf16),
            pltpu.VMEM((2, 2, seqs, 2 * rows, width), bf16),
            pltpu.VMEM((2, tokens, width), bf16),
            pltpu.VMEM((2, tokens, width), bf16),
            pltpu.SemaphoreType.DMA((12,)), pltpu.SemaphoreType.DMA((12,)), pltpu.SemaphoreType.DMA((5,)),
            pltpu.SemaphoreType.DMA((4,)), pltpu.SemaphoreType.DMA((4,)), pltpu.SemaphoreType.DMA((2,)),
            far_sems, far_sems, far_sems,
        ],
        compiler_params=group_params(1, 48 << 20),
        name="front",
    )(x, cot, lifted, w_in, out_proj)


def pair_signal(barrier):
    home = lax.axis_index("replica")
    other = home + 1 - 2 * lax.rem(home, 2)
    pl.semaphore_signal(barrier, inc=1, device_id={"replica": other}, device_id_type=MESH)
    return other


def across(src, dst, sends, recvs, at, other):
    return pltpu.make_async_remote_copy(
        src_ref=src, dst_ref=dst, send_sem=sends.at[at], recv_sem=recvs.at[at],
        device_id={"replica": other}, device_id_type=MESH,
    )


def meet_group_and_pair():
    barrier = pltpu.get_barrier_semaphore()
    for hop in (1, 2, 3):
        pl.semaphore_signal(barrier, inc=1, device_id={"shard": peer(hop)}, device_id_type=MESH)
    other = pair_signal(barrier)
    pl.semaphore_wait(barrier, 4)
    return other


def middle_kernel(
    keep_ref, give_ref, gz_ref, x_hbm, o_hbm,
    both_ref, gz_got_ref, out_ref,
    o_ref, gives, xcol, acc, outs, sends, recvs, local, o_local,
):
    me = lax.axis_index("shard")
    side = lax.rem(lax.axis_index("replica"), 2)
    tokens, half = keep_ref.shape
    keeps_ref, gots_ref = both_ref.at[0], both_ref.at[1]
    seqs, rows, _ = out_ref.shape
    cols = acc.shape[1]
    piece = o_hbm.shape[0] // lax.axis_size("replica")
    per = half // piece
    loads = []
    for d in range(4):
        for q in range(2):
            for j in range(per):
                at = d * 2 * half + (2 * j) * piece + (side if q == 0 else 1 - side) * piece
                loads.append(
                    pltpu.make_async_copy(
                        o_hbm.at[pl.ds(pl.multiple_of(at, piece), piece), :],
                        o_ref.at[q, pl.ds(d * half + j * piece, piece), :],
                        o_local.at[len(loads)],
                    )
                )
    for copy in loads:
        copy.start()
    fetch = pltpu.make_async_copy(
        x_hbm.at[:, pl.ds(pl.multiple_of(me * cols, 128), cols)], xcol, local.at[0]
    )
    fetch.start()
    other = meet_group_and_pair()

    def spot(ref, owner):
        return ref.at[:, pl.ds(pl.multiple_of(owner * half, 128), half)]

    give_pair = across(give_ref, spot(gots_ref, me), sends, recvs, 0, other)
    gz_pair = across(gz_ref, gz_got_ref, sends, recvs, 1, other)
    k_chip = remote(keep_ref, spot(keeps_ref, me), sends, recvs, 2, 2)
    v_chip = remote(give_ref, spot(gives, me), sends, recvs, 3, 2)
    k_core = remote(keep_ref, spot(keeps_ref, me), sends, recvs, 4, 1)
    v_core = remote(give_ref, spot(gives, me), sends, recvs, 5, 1)
    k_own = pltpu.make_async_copy(keep_ref, spot(keeps_ref, me), local.at[1])
    v_own = pltpu.make_async_copy(give_ref, spot(gives, me), local.at[2])
    for copy in (k_core, v_core, k_chip, give_pair, v_chip, gz_pair, k_own, v_own):
        copy.start()

    def gated_rows(q, owner):
        where = pl.ds(pl.multiple_of(owner * half, 128), half)
        left = keeps_ref if q == 0 else gives
        return rows_dot(left[:, where], o_ref[q, where, :])

    k_own.wait()
    v_own.wait()
    for copy in loads:
        copy.wait()
    fetch.wait()
    acc[...] = xcol[...].astype(f32) + gated_rows(0, me)
    acc[...] += gated_rows(1, me)
    k_core.wait()
    acc[...] += gated_rows(0, peer(1))
    v_core.wait()
    acc[...] += gated_rows(1, peer(1))
    k_chip.wait_recv()
    k_on = remote(spot(keeps_ref, peer(2)), spot(keeps_ref, peer(2)), sends, recvs, 6, 1)
    k_on.start()
    give_pair.wait_recv()
    g_chip = remote(spot(gots_ref, me), spot(gots_ref, me), sends, recvs, 7, 2)
    g_core = remote(spot(gots_ref, me), spot(gots_ref, me), sends, recvs, 8, 1)
    g_core.start()
    acc[...] += gated_rows(0, peer(2))
    k_on.wait()
    acc[...] += gated_rows(0, peer(3))
    v_chip.wait_recv()
    v_on = remote(spot(gives, peer(2)), spot(gives, peer(2)), sends, recvs, 9, 1)
    v_on.start()
    acc[...] += gated_rows(1, peer(2))
    v_on.wait()
    outs[...] = (acc[...] + gated_rows(1, peer(3))).astype(bf16).reshape(outs.shape)

    def out_rows(owner):
        return outs.at[:, pl.ds(pl.multiple_of(owner * rows, 16), rows), :]

    home = out_ref.at[:, :, pl.ds(pl.multiple_of(me * cols, 128), cols)]
    out_own = pltpu.make_async_copy(out_rows(me), home, local.at[3])
    out_own.start()
    out_sends = [remote(out_rows(peer(hop)), home, sends, recvs, 9 + hop, hop) for hop in (2, 3, 1)]
    for copy in out_sends:
        copy.start()
    g_chip.start()
    g_chip.wait_recv()
    g_on = remote(spot(gots_ref, peer(2)), spot(gots_ref, peer(2)), sends, recvs, 13, 1)
    g_on.start()
    for copy in out_sends + [g_on, g_core, gz_pair]:
        copy.wait()
    for copy in (g_chip, give_pair, k_chip, v_chip):
        copy.wait_send()
    out_own.wait()


def middle(keep, give, grad_z, x_all, out_proj, seqs):
    tokens, half = keep.shape
    group = lax.axis_size("shard")
    model = x_all.shape[1]
    cols = model // group
    return pl.pallas_call(
        middle_kernel,
        in_specs=[VMEM_SPEC] * 3 + [ANY_SPEC] * 2,
        out_specs=[VMEM_SPEC] * 3,
        out_shape=[
            jax.ShapeDtypeStruct((2, tokens, half * group), bf16),
            jax.ShapeDtypeStruct(grad_z.shape, bf16),
            jax.ShapeDtypeStruct((seqs, tokens // seqs // group, model), bf16),
        ],
        scratch_shapes=[
            pltpu.VMEM((2, half * group, cols), bf16),
            pltpu.VMEM((tokens, half * group), bf16),
            pltpu.VMEM((tokens, cols), bf16),
            pltpu.VMEM((tokens, cols), f32),
            pltpu.VMEM((seqs, tokens // seqs, cols), bf16),
            pltpu.SemaphoreType.DMA((14,)), pltpu.SemaphoreType.DMA((14,)), pltpu.SemaphoreType.DMA((4,)),
            pltpu.SemaphoreType.DMA((8 * max(1, half * group // 4 // (out_proj.shape[0] // lax.axis_size("replica"))),)),
        ],
        compiler_params=group_params(6, 20 << 20),
        name="middle",
    )(keep, give, grad_z, x_all, out_proj)


def home_kernel(gx_ref, gz_ref, small_ref, got_ref, cols_ref, small_got_ref, sends, recvs, local):
    me = lax.axis_index("shard")
    width = gx_ref.shape[1]
    other = meet_group_and_pair()
    pair_copy = across(gx_ref, got_ref, sends, recvs, 0, other)
    pair_copy.start()
    small_copy = across(small_ref, small_got_ref, sends, recvs, 3, other)
    small_copy.start()

    def goal(slot):
        return (4 * slot + me) // 2

    spot = cols_ref.at[:, pl.ds(pl.multiple_of(lax.rem(me, 2) * width, 128), width)]

    def send(slot, ref):
        return part_copy(ref, spot, sends.at[1 + slot], recvs.at[1 + lax.rem(me, 2)], goal(slot))

    def keep(ref):
        return pltpu.make_async_copy(ref, spot, local.at[0])

    refs = (gx_ref, gz_ref)
    for slot in (0, 1):
        pl.when(goal(slot) != me)(lambda slot=slot: send(slot, refs[slot]).start())
        pl.when(goal(slot) == me)(lambda slot=slot: keep(refs[slot]).start())
    for slot in (0, 1):
        pl.when(goal(slot) != me)(lambda slot=slot: send(slot, refs[slot]).wait_send())
        pl.when(goal(slot) == me)(lambda slot=slot: keep(refs[slot]).wait())
    for at in range(2):

        @pl.when(lax.rem(2 * me + at, 4) != me)
        def _(at=at):
            part_copy(gx_ref, gx_ref, sends.at[0], recvs.at[1 + at], peer(1)).wait_recv()

    pair_copy.wait()
    small_copy.wait()


def to_home(gx, gz, small):
    tokens, width = gx.shape
    return pl.pallas_call(
        home_kernel,
        in_specs=[VMEM_SPEC] * 3,
        out_specs=[VMEM_SPEC] * 3,
        out_shape=[
            jax.ShapeDtypeStruct(gx.shape, bf16),
            jax.ShapeDtypeStruct((tokens, 2 * width), bf16),
            jax.ShapeDtypeStruct(small.shape, bf16),
        ],
        scratch_shapes=[
            pltpu.SemaphoreType.DMA((4,)), pltpu.SemaphoreType.DMA((4,)), pltpu.SemaphoreType.DMA((1,)),
        ],
        compiler_params=group_params(7, 16 << 20),
        name="to_home",
    )(gx, gz, small)


def finish_kernel(
    xb_ref, sb_ref, wz_ref, cols_ref, w_hbm, x_ref, cot_ref, gain_ref,
    gw_ref, small_ref, dx_ref, ggain_ref,
    w_ref, x_in, s_in, lhs, pairs, near, g_own, g_send, g_far, h_send, h_cols, s_own, gains, gain_near, gain_sum,
    gain_pair, gain_two, gain_in,
    sends, recvs, far_sends, far_recvs, local,
):
    me = lax.axis_index("shard")
    home = lax.axis_index("replica")
    count = lax.axis_size("replica")
    height = count // 2
    mine = home // 2
    side = lax.rem(home, 2)
    seqs, rows, model = x_ref.shape
    tokens = cols_ref.shape[0]
    length = tokens // seqs
    deep, width = wz_ref.shape
    half = deep // 2
    tile = 256
    span = seqs * rows
    load = pltpu.make_async_copy(w_hbm, w_ref, local.at[0])
    load.start()
    barrier = pltpu.get_barrier_semaphore()
    for hop in (1, 2, 3):
        pl.semaphore_signal(barrier, inc=1, device_id={"shard": peer(hop)}, device_id_type=MESH)
    other = pair_signal(barrier)

    def far(step):
        return lax.rem(home + 2 * step, count)

    for step in range(1, height):
        pl.semaphore_signal(barrier, inc=1, device_id={"replica": far(step)}, device_id_type=MESH)
    pl.semaphore_wait(barrier, 3 + height)

    def far_copy(src, dst, kind, step):
        at = kind * height + step
        return across(src, dst, far_sends, far_recvs, at, far(step))

    def block(step):
        return lax.rem(mine + step, height)

    order = range(1, height)
    s_sends = [far_copy(sb_ref.at[block(step)], s_in.at[step - 1], 0, step) for step in order]

    def x_sends(part):
        cut = slice(part * half, (part + 1) * half)
        return [
            far_copy(xb_ref.at[block(step), cut], x_in.at[step - 1, cut], 1 + part, step) for step in order
        ]

    for copy in s_sends + x_sends(0):
        copy.start()

    spot = pl.ds(pl.multiple_of(lax.rem(me, 2) * width, LANES), width)

    def goal(slot):
        return (4 * slot + me) // 2

    def home_pieces(at):
        if at == 2:
            return 1, wz_ref, h_cols.at[:, spot]
        cut = slice(at * half, (at + 1) * half)
        return 0, h_send.at[cut], h_cols.at[cut, spot]

    def home_send(at):
        slot, src, dst = home_pieces(at)
        return part_copy(src, dst, sends.at[at], recvs.at[at * 2 + lax.rem(me, 2)], goal(slot))

    def home_keep(at):
        _, src, dst = home_pieces(at)
        return pltpu.make_async_copy(src, dst, local.at[1 + at])

    def home_start(at):
        slot = home_pieces(at)[0]
        pl.when(goal(slot) != me)(lambda: home_send(at).start())
        pl.when(goal(slot) == me)(lambda: home_keep(at).start())

    home_start(2)

    def stage(owners):
        for i, owner in enumerate(owners):
            for seq in range(seqs):
                at = pl.ds(pl.multiple_of(seq * length + owner * rows, 16), rows)
                lhs[i * span + seq * rows : i * span + (seq + 1) * rows, :] = cols_ref[at, :]

    def lanes(t):
        return pl.ds(pl.multiple_of(t * tile, tile), tile)

    def product(t):
        return outer_dot(lhs[...], w_ref[lanes(t), :])

    stage((peer(3), peer(1)))
    load.wait()

    def first(t, carry):
        value = product(t)
        pairs[0, :, lanes(t)] = value[:span].astype(bf16)
        pairs[1, :, lanes(t)] = value[span:].astype(bf16)
        return carry

    lax.fori_loop(0, model // tile, first, 0)
    near_send = remote(pairs, near, sends, recvs, 6, 1)
    near_send.start()

    for copy in s_sends:
        copy.wait_recv()
    total = sb_ref[mine].astype(f32)
    for step in order:
        total = total + s_in[step - 1].astype(f32)
    s_own[...] = total.astype(bf16)
    small_ref[side, mine] = s_own[...]
    spread = [far_copy(s_own, small_ref.at[side, mine], 3, step) for step in order]
    for copy in spread + x_sends(1):
        copy.start()

    stage((peer(2), me))
    near_send.wait()

    def second(t, carry):
        value = product(t)
        g_send[:, lanes(t)] = (value[:span] + near[0, :, lanes(t)].astype(f32)).astype(bf16)
        g_own[:, lanes(t)] = value[span:] + near[1, :, lanes(t)].astype(f32)
        return carry

    lax.fori_loop(0, model // tile, second, 0)
    chip_send = remote(g_send, g_far, sends, recvs, 7, 2)
    chip_send.start()
    chip_send.wait()

    gains[...] = jnp.zeros_like(gains)
    for seq in range(seqs):

        def last(r, carry, seq=seq):
            at = pl.ds(pl.multiple_of(r * 16, 16), 16)
            flat = pl.ds(pl.multiple_of(seq * rows + r * 16, 16), 16)
            grad = g_own[flat, :] + g_far[flat, :].astype(f32)
            vals = x_ref[seq, at, :].astype(f32)
            inv = lax.rsqrt(jnp.mean(vals * vals, axis=1, keepdims=True) + EPS)
            scaled = grad * gain_ref[...]
            mean = jnp.mean(scaled * vals, axis=1, keepdims=True)
            out = inv * (scaled - vals * (inv * inv * mean))
            dx_ref[seq, at, :] = (cot_ref[seq, at, :].astype(f32) + out).astype(bf16)
            terms = grad * (vals * inv)
            gains[...] += terms[:8] + terms[8:]
            return carry

        lax.fori_loop(0, rows // 16, last, 0)
    gains[...] = jnp.broadcast_to(jnp.sum(gains[...], axis=0, keepdims=True), gains.shape)
    wide = model // 4

    def gain_part(owner):
        return gains.at[:, pl.ds(pl.multiple_of(owner * wide, LANES), wide)]

    gain_sends = [remote(gain_part(peer(hop)), gain_near.at[hop - 1], sends, recvs, 7 + hop, hop) for hop in (1, 2, 3)]
    for copy in gain_sends:
        copy.start()

    def home_sum(part):
        for copy in x_sends(part):
            copy.wait_recv()
        cut = slice(part * half, (part + 1) * half)
        total = xb_ref[mine, cut].astype(f32)
        for step in order:
            total = total + x_in[step - 1, cut].astype(f32)
        h_send[cut] = total.astype(bf16)
        home_start(part)

    for copy in gain_sends:
        copy.wait()
    gain_sum[...] = gains[:, pl.ds(pl.multiple_of(me * wide, LANES), wide)] + gain_near[0] + gain_near[1] + gain_near[2]
    gain_copy = across(gain_sum, gain_pair, sends, recvs, 11, other)
    gain_copy.start()
    home_sum(0)
    gain_copy.wait()
    gain_two[...] = gain_sum[...] + gain_pair[...]
    gain_far = [far_copy(gain_two, gain_in.at[step - 1], 4, step) for step in order]
    for copy in gain_far:
        copy.start()
    for copy in spread:
        copy.wait_recv()
    small_pair = across(small_ref.at[side], small_ref.at[side], sends, recvs, 12, other)
    small_pair.start()
    home_sum(1)
    for copy in gain_far:
        copy.wait()
    total = gain_two[...]
    for step in order:
        total = total + gain_in[step - 1]
    ggain_ref[...] = total

    for at in (2, 0, 1):
        slot = home_pieces(at)[0]
        pl.when(goal(slot) != me)(lambda at=at: home_send(at).wait_send())
        pl.when(goal(slot) == me)(lambda at=at: home_keep(at).wait())

        for place in range(2):
            source = lax.rem(2 * me + place, 4)
            wanted = (me // 2 == slot) & (source != me)

            @pl.when(wanted)
            def _(at=at, place=place):
                _, src, _ = home_pieces(at)
                part_copy(src, src, sends.at[at], recvs.at[at * 2 + place], peer(1)).wait_recv()

    for r in range(0, deep, 32):
        gw_ref[r : r + 32, :] = h_cols[r : r + 32, :].astype(f32)
    small_pair.wait()
    for copy in s_sends + spread + x_sends(0) + x_sends(1):
        copy.wait_send()


def finish(x_blocks, small_blocks, wz, cols, w_in, x, cot, gain):
    height, deep, width = x_blocks.shape
    seqs, rows, model = x.shape
    span = seqs * rows
    lines = small_blocks.shape[1]
    wide = model // 4
    gain_tile = pltpu.VMEM((8, wide), f32)
    other = max(height - 1, 1)
    return pl.pallas_call(
        finish_kernel,
        in_specs=[VMEM_SPEC] * 4 + [ANY_SPEC] + [VMEM_SPEC] * 3,
        out_specs=[VMEM_SPEC] * 4,
        out_shape=[
            jax.ShapeDtypeStruct((deep, 2 * width), f32),
            jax.ShapeDtypeStruct((2, height, lines, width), bf16),
            jax.ShapeDtypeStruct(x.shape, bf16),
            jax.ShapeDtypeStruct((8, wide), f32),
        ],
        scratch_shapes=[
            pltpu.VMEM(w_in.shape, bf16),
            pltpu.VMEM((other, deep, width), bf16),
            pltpu.VMEM((other, lines, width), bf16),
            pltpu.VMEM((2 * span, cols.shape[1]), bf16),
            pltpu.VMEM((2, span, model), bf16),
            pltpu.VMEM((2, span, model), bf16),
            pltpu.VMEM((span, model), f32),
            pltpu.VMEM((span, model), bf16),
            pltpu.VMEM((span, model), bf16),
            pltpu.VMEM((deep, width), bf16),
            pltpu.VMEM((deep, 2 * width), bf16),
            pltpu.VMEM((lines, width), bf16),
            pltpu.VMEM((8, model), f32),
            pltpu.VMEM((3, 8, wide), f32),
            gain_tile, gain_tile, gain_tile,
            pltpu.VMEM((other, 8, wide), f32),
            pltpu.SemaphoreType.DMA((13,)), pltpu.SemaphoreType.DMA((13,)),
            pltpu.SemaphoreType.DMA((5 * height,)), pltpu.SemaphoreType.DMA((5 * height,)),
            pltpu.SemaphoreType.DMA((4,)),
        ],
        compiler_params=group_params(8, 48 << 20),
        name="finish",
    )(x_blocks, small_blocks, wz, cols, w_in, x, cot, gain)


def total_kernel(part_ref, out_ref, near, chip_sum, far, sends, recvs):
    me = lax.axis_index("shard")
    half = part_ref.shape[1] // 2
    mine = pl.ds(pl.multiple_of(lax.rem(me, 2) * half, 128), half)
    other = pl.ds(pl.multiple_of((1 - lax.rem(me, 2)) * half, 128), half)
    meet_group()
    first = remote(part_ref.at[:, other], near, sends, recvs, 0, 1)
    first.start()
    first.wait()
    chip_sum[...] = part_ref[:, mine] + near[...]
    second = remote(chip_sum, far, sends, recvs, 1, 2)
    second.start()
    second.wait()
    out_ref[:, mine] = chip_sum[...] + far[...]
    third = remote(out_ref.at[:, mine], out_ref.at[:, mine], sends, recvs, 2, 1)
    third.start()
    third.wait()


def group_total(part, collective_id):
    rows, cols = part.shape
    half = pltpu.VMEM((rows, cols // 2), f32)
    return pl.pallas_call(
        total_kernel,
        in_specs=[VMEM_SPEC],
        out_specs=VMEM_SPEC,
        out_shape=jax.ShapeDtypeStruct((rows, cols), f32),
        scratch_shapes=[half, half, half, pltpu.SemaphoreType.DMA((3,)), pltpu.SemaphoreType.DMA((3,))],
        compiler_params=group_params(collective_id, 16 << 20),
        name="group_total",
    )(part)


def by_hop(value, hop):
    return lax.ppermute(value, "shard", [(i, i ^ hop) for i in range(4)])


def pair(value):
    return lax.ppermute(value, "replica", [(i, i ^ 1) for i in range(lax.axis_size("replica"))])


def far_send(blocks):
    count = lax.axis_size("replica")
    height = count // 2
    mine = lax.axis_index("replica") // 2

    def pick(at):
        return lax.dynamic_index_in_dim(blocks, at, 0, False)

    sent = []
    for step in range(1, height):
        out = pick(lax.rem(mine + step, height)).astype(bf16)
        sent.append(lax.ppermute(out, "replica", [(i, (i + 2 * step) % count) for i in range(count)]))
    return pick(mine), tuple(sent)


def far_total(own, sent):
    total = own
    for value in sent:
        total = total + value.astype(f32)
    return total


def after(value, *others):
    return lax.optimization_barrier((value,) + others)[0]


def body(
    block_input, segment_ids, norm_gain, w_in, conv_weight, conv_bias, x_proj, dt_proj, dt_bias,
    d_skip, out_proj, out_grad,
):
    seqs, local, model = block_input.shape
    length = segment_ids.shape[1]
    tokens = seqs * length
    width = d_skip.shape[0]
    rank = dt_proj.shape[0]
    n = (x_proj.shape[0] - rank) // 2
    me = lax.axis_index("shard")
    count = lax.axis_size("replica")
    height = count // 2
    side = lax.rem(lax.axis_index("replica"), 2)

    def split(values):
        return values.reshape(seqs, length, -1)

    def halves(values, blocks):
        piece = values.shape[1] // blocks // 2
        cuts = [values[:, b * piece : (b + 1) * piece] for b in range(2 * blocks)]
        even = jnp.concatenate(cuts[0::2], axis=1)
        odd = jnp.concatenate(cuts[1::2], axis=1)
        return jnp.where(side == 0, even, odd), jnp.where(side == 0, odd, even)

    def both(keep, got):
        return jnp.concatenate([keep, got], axis=0)

    xs, cots, gains, normed, normed_pair, parts, gated_own, gated_send = front(
        block_input, out_grad, norm_gain, w_in, out_proj
    )
    gain = gains[::8].reshape(1, -1)
    x_all = xs.reshape(tokens, model)
    cot_pair = cots.reshape(2 * tokens, -1)
    if model // count % LANES == 0:
        normed_pair = normed_pair.reshape(2 * tokens, -1)
    else:
        normed_keep, normed_give = halves(normed.reshape(tokens, model), height)
        normed_pair = jnp.concatenate([normed_keep, pair(normed_give)], axis=0)
    x_part, z_part = parts[0], parts[1]

    seg_padded = jnp.pad(segment_ids, ((0, 0), (KW - 1, 0)), constant_values=-1)
    taps = [
        (seg_padded[:, KW - 1 - d : KW - 1 - d + length] == segment_ids).astype(f32) for d in range(KW)
    ]
    conv_w = conv_weight.astype(f32)
    xv = x_part.astype(f32)
    x_padded = jnp.pad(xv, ((0, 0), (KW - 1, 0), (0, 0)))
    conv_pre = conv_bias.astype(f32) + conv_w[KW - 1] * xv
    for j in range(KW - 1):
        d = KW - 1 - j
        conv_pre = conv_pre + conv_w[j] * x_padded[:, j : j + length] * taps[d][:, :, None]
    conv_out = jax.nn.silu(conv_pre).astype(bf16)
    conv_flat = conv_out.reshape(tokens, width)
    proj = group_total(outer_dot(x_proj, conv_flat), 3)
    gated_far = by_hop(after(gated_send, proj), 2)
    keep_lanes = jnp.broadcast_to(taps[1][:, :, None], (seqs, length, LANES))
    skip = d_skip.astype(f32)
    y_total, gated, rate, beta, states = recurrence_forward(
        conv_out, z_part, proj, keep_lanes, dt_proj, dt_bias.astype(f32)[None], skip[None]
    )
    y_total, gated, gated_far = lax.optimization_barrier((y_total, gated, gated_far))
    grad_gated = split(gated_own + gated_far.astype(f32))
    z_vals = z_part.astype(f32)
    dy = grad_gated * jax.nn.silu(z_vals)
    grad_z = (grad_gated * y_total * silu_slope(z_vals)).astype(bf16).reshape(tokens, width)

    gated_keep, gated_give = halves(gated.reshape(tokens, width), height // 4)
    cols = model // 4
    gated_both, grad_z_got, block_output = middle(gated_keep, gated_give, grad_z, x_all, out_proj, seqs)
    out_blocks = inner_dot(gated_both.reshape(2 * tokens, -1), cot_pair).astype(bf16).reshape(height, -1, cols)
    z_blocks = inner_dot(normed_pair, both(grad_z, grad_z_got)).astype(bf16).reshape(height, -1, width)
    out_own, out_sent = far_send(out_blocks)
    z_own, z_sent = far_send(z_blocks)
    rate, out_own, z_own = lax.optimization_barrier((rate, out_own, z_own))

    grad_conv_rec, grad_dt_low, grad_proj, grad_dt_proj, grad_dt_bias, grad_d_skip = recurrence_backward(
        rate, beta, conv_out, dy, proj, keep_lanes, dt_proj, states
    )
    grad_proj, out_sent = lax.optimization_barrier((grad_proj, out_sent))
    grad_proj = group_total(grad_proj, 4).astype(bf16)
    grad_x_proj = rows_dot(grad_proj, conv_flat)
    grad_conv = dy * skip + grad_conv_rec + split(inner_dot(grad_proj, x_proj))
    grad_pre = grad_conv * silu_slope(conv_pre)
    grad_conv_bias = jnp.sum(grad_pre, axis=(0, 1))
    grad_conv_weight = jnp.stack(
        [
            jnp.sum(grad_pre * x_padded[:, j : j + length] * taps[KW - 1 - j][:, :, None], axis=(0, 1))
            for j in range(KW)
        ]
    )
    grad_x = conv_w[KW - 1] * grad_pre
    for j in range(KW - 1):
        d = KW - 1 - j
        ahead = jnp.pad(grad_pre * taps[d][:, :, None], ((0, 0), (0, d), (0, 0)))[:, d:]
        grad_x = grad_x + conv_w[j] * ahead
    grad_x = grad_x.astype(bf16).reshape(tokens, width)

    small = jnp.concatenate(
        [grad_x_proj, grad_dt_proj, grad_conv_weight, grad_conv_bias[None], grad_dt_bias, grad_d_skip]
    )
    unit = 16 * count
    padded = -(-small.shape[0] // unit) * unit
    small = jnp.pad(small, ((0, padded - small.shape[0]), (0, 0))).reshape(height, 2, -1, width)
    small_keep = jnp.where(side == 0, small[:, 0], small[:, 1])
    small_give = jnp.where(side == 0, small[:, 1], small[:, 0]).astype(bf16).reshape(-1, width)
    grad_x_got, grad_cols, small_got = to_home(grad_x, grad_z, small_give)
    small_blocks = (small_keep + small_got.reshape(small_keep.shape).astype(f32)).astype(bf16)
    x_blocks = inner_dot(normed_pair, both(grad_x, grad_x_got)).astype(bf16).reshape(height, -1, width)
    x_blocks, z_sent = lax.optimization_barrier((x_blocks, z_sent))
    grad_w_z = far_total(z_own.astype(f32), z_sent).astype(bf16)
    grad_out_proj = far_total(out_own.astype(f32), out_sent)
    grad_w_in, small, input_grad, grad_gain = finish(
        x_blocks, small_blocks, grad_w_z, grad_cols, w_in, block_input, out_grad, gain
    )
    small = small.transpose(1, 0, 2, 3).reshape(padded, width).astype(f32)

    top = x_proj.shape[0]
    return (
        block_output, input_grad, grad_gain[0], grad_w_in,
        small[top + rank : top + rank + KW], small[top + rank + KW], small[:top], small[top : top + rank],
        small[top + rank + KW + 1], small[top + rank + KW + 2], grad_out_proj,
    )


def solution(mesh):
    return jax.shard_map(
        body,
        mesh=mesh,
        in_specs=(
            P("replica", "shard", None), P("replica", None), P("shard"), P(None, "shard"), P(None, "shard"),
            P("shard"), P(None, "shard"), P(None, "shard"), P("shard"), P("shard"), P(None, "shard"),
            P("replica", "shard", None),
        ),
        out_specs=(
            P("replica", "shard", None), P("replica", "shard", None), P("shard"), P("replica", "shard"),
            P(None, "shard"), P("shard"), P(None, "shard"), P(None, "shard"), P("shard"), P("shard"),
            P("replica", "shard"),
        ),
        check_vma=False,
    )
```

time: 574 us -> 373 us (0.65)
  Pallas kernels: 134 us -> 299 us
  waiting for transfers between devices: 147 us -> 0.02 us
  local copies, waits for them, and re-layouts: 113 us -> 27.6 us
  starting transfers between devices: 73.9 us -> 10.2 us
  matrix products: 47.1 us -> 10.8 us
  other arithmetic: 50.1 us -> 18.7 us
    pallas_call x3 -> x4, Pallas kernels: 62.5 us -> 217 us  [the longest x1 84.4 us: finish(): pl.pallas_call(finish_kernel, in_specs=[VMEM_SPEC] * 4 + [ANY_SPEC] + [VM...]
    ppermute x27 -> x6, waiting for transfers between devices: 115 us -> 0.02 us  [far_send(): lax.ppermute(out, 'replica', [(i, (i + 2 * step) % count) for i in range(...]
    ppermute x27 -> x6, starting transfers between devices: 54.7 us -> 8.62 us  [far_send(): lax.ppermute(out, 'replica', [(i, (i + 2 * step) % count) for i in range(...]
    ppermute x13 -> x1, waiting for transfers between devices: 32.2 us -> 0.01 us  [by_hop(): return lax.ppermute(value, 'shard', [(i, i ^ hop) for i in range(4)])]
    dynamic_slice x7 -> x0, local copies, waits for them, and re-layouts: 27 us -> none  [the longest x1 11.1 us: body(): lax.dynamic_index_in_dim(partial, core, 2, False).astype(f32)]
    reshape x9 -> x0, local copies, waits for them, and re-layouts: 22.5 us -> none  [the longest x1 7.99 us: body(): outer_dot(cot_late, out_proj).astype(bf16).reshape(tokens, 2, 2, width)]
    ppermute x13 -> x1, starting transfers between devices: 19.2 us -> 1.57 us  [by_hop(): return lax.ppermute(value, 'shard', [(i, i ^ hop) for i in range(4)])]
    dot_general x4 -> x1, matrix products: 17.2 us -> 1.18 us  [rows_dot(): return jnp.dot(a, b, preferred_element_type=f32)]
  transfers between devices with their start and end apart: 40 -> 7, of which waited for: 14 -> 0; matrix products, arithmetic and copies ran while one was open for 27% -> 5% of each run, Pallas kernels for 17% -> 29%
where the time goes in v3:
time: 373 us; the launch traced here: 368 us
  Pallas kernels  299 us (80%)
  local copies, waits for them, and re-layouts  27.6 us (7%)
  other arithmetic  18.7 us (5%)
  matrix products  10.8 us (3%)
  starting transfers between devices  10.2 us (3%)
    pallas_call x1, Pallas kernels, finish(): pl.pallas_call(finish_kernel, in_specs=[VMEM_SPEC] * 4 + [ANY_SPEC] + [VM...  84.4 us
    pallas_call x1, Pallas kernels, front(): pl.pallas_call(front_kernel, in_specs=[VMEM_SPEC] * 3 + [ANY_SPEC] * 2, o...  49.7 us
    pallas_call x1, Pallas kernels, middle(): pl.pallas_call(middle_kernel, in_specs=[VMEM_SPEC] * 3 + [ANY_SPEC] * 2,...  48.4 us
    pallas_call x1, Pallas kernels, recurrence_backward(): pl.pallas_call(backward_kernel, grid=(seqs, blocks), in_specs=[wide, wide...  45.7 us
    pallas_call x1, Pallas kernels, to_home(): pl.pallas_call(home_kernel, in_specs=[VMEM_SPEC] * 3, out_specs=[VMEM_SPE...  34.1 us
    pallas_call x1, Pallas kernels, recurrence_forward(): pl.pallas_call(forward_kernel, grid=(seqs, blocks), in_specs=[wide, wide,...  19.3 us
    pallas_call x2, Pallas kernels, group_total(): pl.pallas_call(total_kernel, in_specs=[VMEM_SPEC], out_specs=VMEM_SPEC, o...  17.9 us
    unnamed x74, local copies, waits for them, and re-layouts  15.2 us
  transfers between devices with their start and end apart: 7, of which 0 were waited for; matrix products, arithmetic and copies ran while one was open for 5% of the time, Pallas kernels for 29%

profile of v3, /device:TPU:0, one launch (start us, length us, event | category | flops | bytes accessed | tf_op | source)
XLA Modules:
  0.0 367.9 jit_solution(14131648510842563116)
XLA Ops:
  0.6 0.0 copy-start
  0.7 0.7 convert_element_type.120
  1.4 0.9 compare_convert_fusion.2
  2.3 0.9 fusion.36
  3.2 0.7 broadcast_in_dim.12.gain_ref
  3.8 1.0 copy-done.5
  4.9 1.0 copy-done.7
  5.9 49.7 %front.1 = (bf16[2,256,2048]{2,1,0:T(8,128)(2,1)S(1)}, bf16[2,2,256,512]{3,2,1,0:T(8,128)(2,1)S(1)}, f32[32,512]{1,0:T(8,128)S(1)}, bf16[2,256,2048]{2,1,0:T(8,1...) custom-call(bf16[2,64,2048]{2,1,0:T(8,128)(2,1)S(1)} %copy-done.5, ...), custom_call_target="tpu_custom_call" | custom-call | tf_op jit(solution)/shard_map/front/pallas_call | solution.py:555
  55.7 0.0 copy-start.11
  55.7 3.0 slice_bitcast_fusion
  58.7 2.7 fusion.26
  61.4 0.5 convolution_bitcast_fusion.part_ref
  61.9 8.9 %group_total.2.proj_ref = f32[160,512]{1,0:T(8,128)S(1)} custom-call(f32[160,512]{1,0:T(8,128)S(1)} %convolution_bitcast_fusion.part_ref), custom_call_target="tpu_custom_call" | custom-call | tf_op jit(solution)/shard_map/group_total/pallas_call | solution.py:1069
  70.9 1.6 collective-permute-start
  72.5 0.1 broadcast_in_dim.13.keep_ref
  72.7 19.3 %recurrence_forward.1 = (f32[2,256,1024]{2,1,0:T(8,128)S(1)}, bf16[2,256,1024]{2,1,0:T(8,128)(2,1)S(1)}, f32[2,256,1024]{2,1,0:T(8,128)S(1)}, f32[2,256,1024]{2,1,0:T(8,128)S(1)}, bf16[2,4096,1024]{2,1,0:T(8,128)(2,1)S(1)}) custom-call(bf16[2,256,1024]{2,1,0:T(8,128)(2,1)S(1)} %get-tuple-element.104.conv_ref, ...), custom_call_target="tpu_custom_call" | custom-call | flops 16000000000 | bytes 25165824 | tf_op jit(solution)/shard_map/recurrence_forward/pallas_call | solution.py:252
  92.0 5.8 %copy-done.15 = bf16[2,4096,1024]{2,1,0:T(8,128)(2,1)} copy-done((bf16[2,4096,1024]{2,1,0:T(8,128)(2,1)}, bf16[2,4096,1024]{2,1,0:T(8,128)(2,1)S(1)}, u32[]{:S(2)}) %copy-start.15) | copy-done | bytes 16777240
  97.8 1.8 convert_add_fusion
  99.6 0.1 copy-done.19
  99.7 1.1 fusion.25
  100.8 0.1 broadcast_select_fusion
  100.9 1.0 copy-done.1
  101.9 0.9 copy-done.4
  102.8 48.4 %middle.1 = (bf16[2,512,2048]{2,1,0:T(8,128)(2,1)S(1)}, bf16[512,1024]{1,0:T(8,128)(2,1)S(1)}, bf16[2,64,2048]{2,1,0:T(8,128)(2,1)S(1)}) custom-call(bf16[512,512]{1,0:T(8,128)(2,1)S(1)} %get-tuple-element.125.keep_ref, bf16[512,512]{1,0:T(8,128)(2,1)S(1)} %get-tuple-element.124.give_ref, bf16[512,1024]{1,0:T(8,128)(2,1)S(1)} %bitcast.92, ...), custom_call_target="tpu_custom_call" | custom-call | tf_op jit(solution)/shard_map/middle/pallas_call | solution.py:713
  151.2 2.4 convolution_convert_fusion
  153.6 0.9 dynamic-slice_bitcast_fusion.3
  154.6 3.6 collective-permute-start.3
  158.2 1.0 collective-permute-start.1
  159.2 2.4 fusion.21
  161.6 0.0 copy-start.14
  161.7 1.4 dynamic-slice_bitcast_fusion
  163.1 2.8 collective-permute-start.6
  165.9 1.1 collective-permute-start.5
  167.0 45.7 %recurrence_backward.1 = (f32[2,256,1024]{2,1,0:T(8,128)S(1)}, bf16[2,256,1024]{2,1,0:T(8,128)(2,1)}, f32[160,512]{1,0:T(8,128)S(1)}, f32[128,1024]{1,0:T(8,128)...) custom-call(f32[2,256,1024]{2,1,0:T(8,128)S(1)} %get-tuple-element.69.rate_ref, ...), custom_call_target="tpu_custom_call" | custom-call | flops 30000001024 | bytes 29360128 | tf_op jit(solution)/shard_map/recurrence_backward/pallas_call | solution.py:286
  212.7 0.1 collective-permute-start.4
  212.8 8.9 %group_total.3 = f32[160,512]{1,0:T(8,128)S(1)} custom-call(f32[160,512]{1,0:T(8,128)S(1)} %get-tuple-element.74.part_ref), custom_call_target="tpu_custom_call" | custom-call | tf_op jit(solution)/shard_map/group_total/pallas_call | solution.py:1069
  221.8 1.2 fusion.28
  223.0 0.5 fusion.30
  223.4 0.1 copy-done.17
  223.6 0.6 copy-done.20
  224.2 3.3 fusion.34
  227.6 3.0 concatenate.10
  230.6 1.6 pad.29
  232.2 0.1 select_convert_fusion
  232.3 0.3 copy-done.18
  232.5 0.5 broadcast_multiply_fusion
  233.0 1.1 fusion.4
  234.1 34.1 %to_home.1 = (bf16[512,1024]{1,0:T(8,128)(2,1)S(1)}, bf16[512,2048]{1,0:T(8,128)(2,1)S(1)}, bf16[192,1024]{1,0:T(8,128)(2,1)S(1)}) custom-call(bf16[512,1024]{1,0:T(8,128)(2,1)S(1)} %bitcast.95, bf16[512,1024]{1,0:T(8,128)(2,1)S(1)} %bitcast.94, bf16[192,1024]{1,0:T(8,128)(2,1)S(1)} %bitcast.98), custom_call_target="tpu_custom_call" | custom-call | tf_op jit(solution)/shard_map/to_home/pallas_call | solution.py:775
  268.2 1.3 copy-done.2
  269.6 0.2 fusion.27.sb_ref
  269.8 3.8 %fusion.18 = bf16[1024,1024]{1,0:T(8,128)(2,1)} fusion(bf16[1024,1024]{1,0:T(8,128)(2,1)S(1)} %bitcast.135, bf16[512,1024]{1,0:T(8,128)(2,1)S(1)} %get-tuple-element.78, bf16[512,1024]{1,0:T(8,128)(2,1)S(1)} %bitcast.96), kind=kOutput, calls=%fused_computation.35 | convolution fusion | flops 2152726528 | bytes 6291456 | tf_op jit(solution)/shard_map/dot_general | solution.py:23
  273.6 1.8 add_convert_fusion.wz_ref
  275.4 84.4 %finish.1 = (f32[256,2048]{1,0:T(8,128)S(1)}, bf16[2,4,48,1024]{3,2,1,0:T(8,128)(2,1)S(1)}, bf16[2,64,2048]{2,1,0:T(8,128)(2,1)S(1)}, f32[8,512]{1,0:T(8,128)S(1)}) custom-call(bf16[4,256,1024]{2,1,0:T(8,128)(2,1)} %bitcast.113, bf16[4,48,1024]{2,1,0:T(8,128)(2,1)S(1)} %fusion.27.sb_ref, bf16[256,1024]{1,0:T(8,128)(2,1)S(1)} %add_convert_fusion.wz_ref, ...), custom_call_target="tpu_custom_call" | custom-call | tf_op jit(solution)/shard_map/finish/pallas_call | solution.py:1011
  359.8 0.2 convert_bitcast_fusion
  360.0 0.2 copy.25
  360.2 0.6 fusion.35
  360.8 0.6 slice.127
  361.4 0.8 slice.130
  362.2 0.9 slice.129
  363.1 0.6 slice.112
  363.7 1.2 convert_add_fusion.1
  365.0 0.8 copy.32
  365.7 0.8 copy.33
  366.5 1.3 copy.34
  (69 shorter events, 0.2 us)
Async XLA Ops:
  0.6 60.8 %copy-start = (bf16[160,1024]{1,0:T(8,128)(2,1)S(1)}, bf16[160,1024]{1,0:T(8,128)(2,1)}, u32[]{:S(2)}) copy-start(bf16[160,1024]{1,0:T(8,128)(2,1)} %param.18) | copy-start | bytes 983044
  3.8 1.0 copy-start.5
  4.9 1.0 copy-start.7
  55.6 3.0 copy-start.3
  55.7 3.0 copy-start.11
  58.7 2.7 copy-start.16
  61.4 11.0 %copy-start.31 = (bf16[1024]{0:T(1024)(128)(2,1)S(1)}, bf16[1024]{0:T(1024)(128)(2,1)}, u32[]{:S(2)}) copy-start(bf16[1024]{0:T(1024)(128)(2,1)} %param.21) | copy-start | bytes 6148
  61.4 11.0 %copy-start.32 = (bf16[1024]{0:T(1024)(128)(2,1)S(1)}, bf16[1024]{0:T(1024)(128)(2,1)}, u32[]{:S(2)}) copy-start(bf16[1024]{0:T(1024)(128)(2,1)} %param.20) | copy-start | bytes 6148
  61.4 11.2 %copy-start.13 = (bf16[128,1024]{1,0:T(8,128)(2,1)S(1)}, bf16[128,1024]{1,0:T(8,128)(2,1)}, u32[]{:S(2)}) copy-start(bf16[128,1024]{1,0:T(8,128)(2,1)} %dt_proj_ref.3) | copy-start | bytes 786436
  70.8 21.2 %copy-start.9 = (f32[160,512]{1,0:T(8,128)}, f32[160,512]{1,0:T(8,128)S(1)}, u32[]{:S(2)}) copy-start(f32[160,512]{1,0:T(8,128)S(1)} %group_total.2.proj_ref) | copy-start | bytes 983044
  70.9 26.9 %collective-permute-start = (bf16[512,1024]{1,0:T(8,128)(2,1)}, bf16[512,1024]{1,0:T(8,128)(2,1)}, u32[]{:S(2)}, u32[]{:S(2)}) collective-permute-start(bf16[512,1024]{1,0:T(8,128)(2,1)} %get-tuple-element.57), channel_id=1, source_target_pairs={{0,2},{1,3},{2,0},{3,1},{4,6},{5,7},{6,4},{7,5},{8,10},{9,11},{10,... | collective-permute-start | bytes 3145736 | tf_op jit(solution)/shard_map/ppermute | solution.py:1081
  72.6 25.1 %copy-start.22 = (f32[512,1024]{1,0:T(8,128)S(1)}, f32[512,1024]{1,0:T(8,128)}, u32[]{:S(2)}) copy-start(f32[512,1024]{1,0:T(8,128)} %get-tuple-element.59) | copy-start | bytes 6291460
  92.0 5.8 %copy-start.15 = (bf16[2,4096,1024]{2,1,0:T(8,128)(2,1)}, bf16[2,4096,1024]{2,1,0:T(8,128)(2,1)S(1)}, u32[]{:S(2)}) copy-start(bf16[2,4096,1024]{2,1,0:T(8,128)(2,1)S(1)} %get-tuple-element.71.state_ref.last_ref) | copy-start | bytes 50331652
  97.8 1.9 copy-start.19
  99.7 2.2 copy-start.1
  100.8 2.0 copy-start.4
  102.8 48.4 %copy-start.12 = (bf16[2,2,256,512]{3,2,1,0:T(8,128)(2,1)S(1)}, bf16[2,2,256,512]{3,2,1,0:T(8,128)(2,1)}, u32[]{:S(2)}) copy-start(bf16[2,2,256,512]{3,2,1,0:T(8,128)(2,1)} %copy-done.11) | copy-start | bytes 3145732
  153.6 5.6 %copy-start.33 = (bf16[2,2,256,1024]{3,2,1,0:T(8,128)(2,1)S(1)}, bf16[2,2,256,1024]{3,2,1,0:T(8,128)(2,1)}, u32[]{:S(2)}) copy-start(bf16[2,2,256,1024]{3,2,1,0:T(8,128)(2,1)} %get-tuple-element.64) | copy-start | bytes 6291460
  154.6 58.1 %collective-permute-start.3 = (bf16[512,512]{1,0:T(8,128)(2,1)S(1)}, bf16[512,512]{1,0:T(8,128)(2,1)S(1)}, u32[]{:S(2)}, u32[]{:S(2)}) collective-permute-start(bf16[512,512]{1,0:T(8,128)(2,1)S(1)} %get-tuple-element.115), channel_id=1, source_target_pairs={{0,24},{4,28},{8,0},{12,4},{16,8},{20,12},{24,16},{28,20},{1,25},{... | collective-permute-start | bytes 1572872 | tf_op jit(solution)/shard_map/ppermute | solution.py:1099
  158.2 54.6 %collective-permute-start.2 = (bf16[512,512]{1,0:T(8,128)(2,1)S(1)}, bf16[512,512]{1,0:T(8,128)(2,1)S(1)}, u32[]{:S(2)}, u32[]{:S(2)}) collective-permute-start(bf16[512,512]{1,0:T(8,128)(2,1)S(1)} %get-tuple-element.116), channel_id=1, source_target_pairs={{0,16},{4,20},{8,24},{12,28},{16,0},{20,4},{24,8},{28,12},{1,17},{... | collective-permute-start | bytes 1572872 | tf_op jit(solution)/shard_map/ppermute | solution.py:1099
  158.2 54.6 %collective-permute-start.1 = (bf16[512,512]{1,0:T(8,128)(2,1)S(1)}, bf16[512,512]{1,0:T(8,128)(2,1)S(1)}, u32[]{:S(2)}, u32[]{:S(2)}) collective-permute-start(bf16[512,512]{1,0:T(8,128)(2,1)S(1)} %get-tuple-element.117), channel_id=1, source_target_pairs={{0,8},{4,12},{8,16},{12,20},{16,24},{20,28},{24,0},{28,4},{1,9},{5... | collective-permute-start | bytes 1572872 | tf_op jit(solution)/shard_map/ppermute | solution.py:1099
  161.6 5.4 %copy-start.10 = (f32[160,512]{1,0:T(8,128)S(1)}, f32[160,512]{1,0:T(8,128)}, u32[]{:S(2)}) copy-start(f32[160,512]{1,0:T(8,128)} %copy-done.9) | copy-start | bytes 983044
  161.6 5.4 %copy-start.14 = (bf16[128,1024]{1,0:T(8,128)(2,1)S(1)}, bf16[128,1024]{1,0:T(8,128)(2,1)}, u32[]{:S(2)}) copy-start(bf16[128,1024]{1,0:T(8,128)(2,1)} %dt_proj_ref.3) | copy-start | bytes 786436
  163.1 110.5 %collective-permute-start.6 = (bf16[256,1024]{1,0:T(8,128)(2,1)}, bf16[256,1024]{1,0:T(8,128)(2,1)}, u32[]{:S(2)}, u32[]{:S(2)}) collective-permute-start(bf16[256,1024]{1,0:T(8,128)(2,1)} %get-tuple-element.108), channel_id=1, source_target_pairs={{0,24},{4,28},{8,0},{12,4},{16,8},{20,12},{24,16},{28,20},{1,25},{... | collective-permute-start | bytes 1572872 | tf_op jit(solution)/shard_map/ppermute | solution.py:1099
  165.9 107.7 %collective-permute-start.5 = (bf16[256,1024]{1,0:T(8,128)(2,1)}, bf16[256,1024]{1,0:T(8,128)(2,1)}, u32[]{:S(2)}, u32[]{:S(2)}) collective-permute-start(bf16[256,1024]{1,0:T(8,128)(2,1)} %get-tuple-element.109), channel_id=1, source_target_pairs={{0,16},{4,20},{8,24},{12,28},{16,0},{20,4},{24,8},{28,12},{1,17},{... | collective-permute-start | bytes 1572872 | tf_op jit(solution)/shard_map/ppermute | solution.py:1099
  212.7 9.0 %copy-start.25 = (bf16[512,512]{1,0:T(8,128)(2,1)}, bf16[512,512]{1,0:T(8,128)(2,1)S(1)}, u32[]{:S(2)}) copy-start(bf16[512,512]{1,0:T(8,128)(2,1)S(1)} %collective-permute-done.3) | copy-start | bytes 1572868
  212.7 60.9 %collective-permute-start.4 = (bf16[256,1024]{1,0:T(8,128)(2,1)}, bf16[256,1024]{1,0:T(8,128)(2,1)}, u32[]{:S(2)}, u32[]{:S(2)}) collective-permute-start(bf16[256,1024]{1,0:T(8,128)(2,1)} %get-tuple-element.110), channel_id=1, source_target_pairs={{0,8},{4,12},{8,16},{12,20},{16,24},{20,28},{24,0},{28,4},{1,9},{5... | collective-permute-start | bytes 1572872 | tf_op jit(solution)/shard_map/ppermute | solution.py:1099
  212.8 10.7 %copy-start.27 = (bf16[512,512]{1,0:T(8,128)(2,1)}, bf16[512,512]{1,0:T(8,128)(2,1)S(1)}, u32[]{:S(2)}) copy-start(bf16[512,512]{1,0:T(8,128)(2,1)S(1)} %collective-permute-done.2) | copy-start | bytes 1572868
  212.8 10.6 %copy-start.29 = (bf16[512,512]{1,0:T(8,128)(2,1)}, bf16[512,512]{1,0:T(8,128)(2,1)S(1)}, u32[]{:S(2)}) copy-start(bf16[512,512]{1,0:T(8,128)(2,1)S(1)} %collective-permute-done.1) | copy-start | bytes 1572868
  221.7 1.8 copy-start.17
  221.8 2.5 copy-start.20
  224.2 3.3 copy-start.21
  230.6 2.0 copy-start.18
  234.1 35.6 %copy-start.34 = (bf16[2,2,256,1024]{3,2,1,0:T(8,128)(2,1)S(1)}, bf16[2,2,256,1024]{3,2,1,0:T(8,128)(2,1)}, u32[]{:S(2)}) copy-start(bf16[2,2,256,1024]{3,2,1,0:T(8,128)(2,1)} %get-tuple-element.64) | copy-start | bytes 6291460
  268.2 1.4 copy-start.2
  269.8 3.8 %copy-start.23 = (bf16[256,1024]{1,0:T(8,128)(2,1)S(1)}, bf16[256,1024]{1,0:T(8,128)(2,1)}, u32[]{:S(2)}) copy-start(bf16[256,1024]{1,0:T(8,128)(2,1)} %get-tuple-element.81) | copy-start | bytes 1572868
  273.6 1.8 copy-start.6
  273.6 1.8 copy-start.8
  360.0 3.7 %copy-start.24 = (bf16[512,512]{1,0:T(8,128)(2,1)S(1)}, bf16[512,512]{1,0:T(8,128)(2,1)}, u32[]{:S(2)}) copy-start(bf16[512,512]{1,0:T(8,128)(2,1)} %get-tuple-element.91) | copy-start | bytes 1572868
  360.0 3.7 %copy-start.26 = (bf16[512,512]{1,0:T(8,128)(2,1)S(1)}, bf16[512,512]{1,0:T(8,128)(2,1)}, u32[]{:S(2)}) copy-start(bf16[512,512]{1,0:T(8,128)(2,1)} %copy-done.25) | copy-start | bytes 1572868
  360.0 3.7 %copy-start.28 = (bf16[512,512]{1,0:T(8,128)(2,1)S(1)}, bf16[512,512]{1,0:T(8,128)(2,1)}, u32[]{:S(2)}) copy-start(bf16[512,512]{1,0:T(8,128)(2,1)} %copy-done.27) | copy-start | bytes 1572868
  360.0 3.7 %copy-start.30 = (bf16[512,512]{1,0:T(8,128)(2,1)S(1)}, bf16[512,512]{1,0:T(8,128)(2,1)}, u32[]{:S(2)}) copy-start(bf16[512,512]{1,0:T(8,128)(2,1)} %copy-done.29) | copy-start | bytes 1572868

commit v4 on v3

--- a/solution.py
+++ b/solution.py
@@ -33,6 +33,7 @@
 
 MESH = pl.DeviceIdType.MESH
 BLOCK = 128
+PIECES = 1
 
 
 def lane(g):
@@ -64,13 +65,13 @@
     return pltpu.roll(cols, lax.rem(size - j * CHUNK, size), 1)
 
 
-def spread_mask(n):
-    shape = (CHUNK, CHUNK * n)
+def spread_mask(n, size=CHUNK):
+    shape = (size, size * n)
     return lax.broadcasted_iota(jnp.int32, shape, 1) // n == lax.broadcasted_iota(jnp.int32, shape, 0)
 
 
-def picker(n):
-    shape = (n, CHUNK * n)
+def picker(n, size=CHUNK):
+    shape = (n, size * n)
     return (lax.broadcasted_iota(jnp.int32, shape, 1) % n == lax.broadcasted_iota(jnp.int32, shape, 0)).astype(bf16)
 
 
@@ -133,13 +134,12 @@
 def backward_kernel(
     rate_ref, beta_ref, conv_ref, dy_ref, proj_ref, keep_ref, dt_proj_ref, state_ref, last_ref,
     gconv_ref, gdt_ref, gproj_ref, gdt_proj_ref, gdt_bias_ref, gskip_ref,
-    held_ref, grate, rk, u, dys, kept, key_rows, adj, adj_state, diag1, diag2, diag3,
+    held_ref, grate, rk, u, dys, kept, key_rows, adj, adj_state, sums,
 ):
     block_rows, width = rate_ref.shape[1:]
     rank = dt_proj_ref.shape[0]
     n = (proj_ref.shape[0] - rank) // 2
     groups = width // LANES
-    span = CHUNK * n
     chunks = block_rows // CHUNK
 
     @pl.when(pl.program_id(1) == 0)
@@ -155,7 +155,10 @@
     keys = proj_ref[rank : rank + n, :]
     queries = proj_ref[rank + n :, :]
     key_rows[...] = keys.T
-    mask, pick = spread_mask(n), picker(n)
+    mask, pick = spread_mask(n, CHUNK // PIECES), picker(n, CHUNK // PIECES)
+
+    spot = lax.broadcasted_iota(jnp.int32, (n, LANES), 1)
+    sums[...] = jnp.zeros_like(sums)
 
     def chunk(step, held):
         j = chunks - 1 - step
@@ -166,35 +169,50 @@
         near_keys = shifted(keys, j)
         near_queries = shifted(queries, j)
         held = list(held)
+        after = [state_ref[0, pl.ds(pl.multiple_of((base + CHUNK - 1) * n, n), n), lane(g)] for g in range(groups)]
+        found = [jnp.zeros((n, LANES), f32) for _ in range(3)]
+        def settle(p):
+            size = CHUNK // PIECES
+            part = slice(p * size, (p + 1) * size)
+            some = pl.ds(base + p * size, size)
+            key_block = key_rows[some, :]
+            w1 = rows_dot(diagonal(key_block, mask, pick), adj[p][...].astype(bf16))
+            w2 = rows_dot(diagonal(key_block * key_block, mask, pick), adj_state[p][...].astype(bf16))
+            for g in range(groups):
+                grate[some, lane(g)] = conv[part, lane(g)] * w1[:, lane(g)] - keeps[part] * w2[:, lane(g)]
+            gconv_ref[0, some, :] = rate[part] * w1
+
         for t in reversed(range(CHUNK)):
+            piece, place = t // (CHUNK // PIECES), t % (CHUNK // PIECES)
+            own = slice(place * n, (place + 1) * n)
             key = column(near_keys, t)
             key2 = key * key
             query = column(near_queries, t)
             keep = jnp.broadcast_to(kept[t : t + 1, :], (n, LANES))
             prior = jnp.maximum(base + t - 1, 0)
             at = pl.ds(pl.multiple_of(prior * n, n), n)
+            parts = [None] * 3
             for g in range(groups):
-                grad = held[g] + row(dys, t, g, n) * query
-                decay = keep - row(rk, t, g, n) * key2
+                slope = row(dys, t, g, n)
+                pace = row(rk, t, g, n)
+                grad = held[g] + slope * query
+                decay = keep - pace * key2
                 held[g] = decay * grad
-                adj[t * n : (t + 1) * n, lane(g)] = grad.astype(bf16)
-                before = state_ref[0, at, lane(g)].astype(f32)
+                before = state_ref[0, at, lane(g)]
                 if t == 0:
-                    before = jnp.where(j == 0, last_ref[0, :, lane(g)].astype(f32), before)
-                adj_state[t * n : (t + 1) * n, lane(g)] = (grad * before).astype(bf16)
-        block = state_ref[0, pl.ds(pl.multiple_of(base * n, span), span), :]
-        key_block = key_rows[rows, :]
-        w1 = rows_dot(diagonal(key_block, mask, pick), adj[...])
-        w2 = rows_dot(diagonal(key_block * key_block, mask, pick), adj_state[...])
-        a1 = outer_dot(u[...].astype(bf16), adj[...])
-        a2 = outer_dot(rk[...].astype(bf16), adj_state[...])
-        a3 = outer_dot(dys[...].astype(bf16), block)
-        diag1[rows, :] = jnp.where(mask, a1, 0.0)
-        diag2[rows, :] = jnp.where(mask, a2, 0.0)
-        diag3[rows, :] = jnp.where(mask, a3, 0.0)
-        for g in range(groups):
-            grate[rows, lane(g)] = conv[:, lane(g)] * w1[:, lane(g)] - keeps * w2[:, lane(g)]
-        gconv_ref[0, rows, :] = rate * w1
+                    before = jnp.where(j == 0, last_ref[0, :, lane(g)], before)
+                cross = grad * before.astype(f32)
+                adj[piece][own, lane(g)] = grad
+                adj_state[piece][own, lane(g)] = cross
+                terms = (grad * row(u, t, g, n), cross * pace, after[g].astype(f32) * slope)
+                parts = [v if p is None else p + v for p, v in zip(parts, terms)]
+                after[g] = before
+            if place == 0:
+                settle(piece)
+            here = spot == base + t
+            found = [jnp.where(here, jnp.sum(p, axis=1, keepdims=True), f) for p, f in zip(parts, found)]
+        for i in range(3):
+            sums[i] += found[i]
         return tuple(held)
 
     start = tuple(held_ref[:, lane(g)] for g in range(groups))
@@ -220,8 +238,8 @@
     gskip_ref[...] += jnp.sum(dy_ref[0] * conv_ref[0].astype(f32), axis=0, keepdims=True)
     gdt_proj_ref[...] += rows_dot(proj_ref[0:rank, :].astype(bf16), low)
     gproj_ref[0:rank, :] = outer_dot(dt_proj_ref[...], low)
-    gproj_ref[rank : rank + n, :] = picked(pick, diag1[...]) - 2.0 * keys * (picked(pick, diag2[...]) + self_term)
-    gproj_ref[rank + n :, :] = picked(pick, diag3[...])
+    gproj_ref[rank : rank + n, :] = sums[0] - 2.0 * keys * (sums[1] + self_term)
+    gproj_ref[rank + n :, :] = sums[2]
 
 
 def specs_for(length, reverse):
@@ -282,7 +300,6 @@
     blocks, spec, across_spec, whole = specs_for(length, True)
     wide = spec(BLOCK, width)
     before = pl.BlockSpec((1, n, width), lambda s, b: (s, jnp.maximum((blocks - 1 - b) * BLOCK - 1, 0), 0))
-    lined = pltpu.VMEM((BLOCK, span), f32)
     return pl.pallas_call(
         backward_kernel,
         grid=(seqs, blocks),
@@ -307,9 +324,9 @@
             pltpu.VMEM((CHUNK, width), f32),
             pltpu.VMEM((CHUNK, LANES), f32),
             pltpu.VMEM((BLOCK, n), f32),
-            pltpu.VMEM((span, width), bf16),
-            pltpu.VMEM((span, width), bf16),
-            lined, lined, lined,
+            [pltpu.VMEM((span // PIECES, width), f32)] * PIECES,
+            [pltpu.VMEM((span // PIECES, width), f32)] * PIECES,
+            pltpu.VMEM((3, n, BLOCK), f32),
         ],
         compiler_params=pltpu.CompilerParams(vmem_limit_bytes=28 << 20),
         cost_estimate=pl.CostEstimate(flops=30_000_000_000, bytes_accessed=28 << 20, transcendentals=0),
@@ -360,7 +377,7 @@
 
 def front_kernel(
     x_ref, cot_ref, gain_ref, w_hbm, o_hbm,
-    xs_ref, all_cots_ref, gains_ref, normed_ref, pair_ref, parts_ref, own_ref, send_ref,
+    xs_ref, cots_ref, gains_ref, normed_ref, pair_ref, parts_ref, own_ref, send_ref,
     w_ref, o_ref, lhs, mixed, pairs, near, sends, recvs, local, part_sends, part_recvs, part_local,
     pair_sends, pair_recvs, pair_local,
 ):
@@ -368,8 +385,7 @@
     chip = me // 2
     slot = me // 2
     seqs, rows, model = x_ref.shape
-    cots_ref = all_cots_ref.at[0]
-    cols = all_cots_ref.shape[3]
+    cols = cots_ref.shape[2]
     side = lax.rem(lax.axis_index("replica"), 2)
     height = lax.axis_size("replica") // 2
     block = model // 2 // height
@@ -488,8 +504,6 @@
 
     for copy in cot_sends:
         copy.wait()
-    cot_pair = across(all_cots_ref.at[0], all_cots_ref.at[1], sends, recvs, 11, other)
-    cot_pair.start()
     loads[1].wait()
 
     def partial(block, t):
@@ -528,7 +542,6 @@
     lax.fori_loop(0, width // tile, to_own, 0)
 
     x_chip.wait_send()
-    cot_pair.wait()
     for copy in normed_copies(0) + normed_copies(1):
         copy.wait()
     for half in range(2):
@@ -558,7 +571,7 @@
         out_specs=[VMEM_SPEC] * 8,
         out_shape=[
             jax.ShapeDtypeStruct((seqs, length, model), bf16),
-            jax.ShapeDtypeStruct((2, seqs, length, cols), bf16),
+            jax.ShapeDtypeStruct((seqs, length, cols), bf16),
             jax.ShapeDtypeStruct((8 * group, gain.shape[0]), f32),
             jax.ShapeDtypeStruct((seqs, length, model), bf16),
             jax.ShapeDtypeStruct((2, seqs, length, model // 2), bf16),
@@ -573,7 +586,7 @@
             pltpu.VMEM((2, 2, seqs, 2 * rows, width), bf16),
             pltpu.VMEM((2, tokens, width), bf16),
             pltpu.VMEM((2, tokens, width), bf16),
-            pltpu.SemaphoreType.DMA((12,)), pltpu.SemaphoreType.DMA((12,)), pltpu.SemaphoreType.DMA((5,)),
+            pltpu.SemaphoreType.DMA((11,)), pltpu.SemaphoreType.DMA((11,)), pltpu.SemaphoreType.DMA((5,)),
             pltpu.SemaphoreType.DMA((4,)), pltpu.SemaphoreType.DMA((4,)), pltpu.SemaphoreType.DMA((2,)),
             far_sems, far_sems, far_sems,
         ],
@@ -605,17 +618,71 @@
     return other
 
 
+def collect_kernel(keep_ref, give_ref, gz_ref, keeps_ref, gives_ref, gz_both_ref, sends, recvs, local):
+    me = lax.axis_index("shard")
+    half = keep_ref.shape[1]
+    other = meet_group_and_pair()
+
+    def spot(ref, owner):
+        return ref.at[:, pl.ds(pl.multiple_of(owner * half, 128), half)]
+
+    k_chip = remote(keep_ref, spot(keeps_ref, me), sends, recvs, 0, 2)
+    v_chip = remote(give_ref, spot(gives_ref, me), sends, recvs, 1, 2)
+    k_core = remote(keep_ref, spot(keeps_ref, me), sends, recvs, 2, 1)
+    v_core = remote(give_ref, spot(gives_ref, me), sends, recvs, 3, 1)
+    gz_pair = across(gz_ref, gz_both_ref.at[1], sends, recvs, 4, other)
+    own = [
+        pltpu.make_async_copy(keep_ref, spot(keeps_ref, me), local.at[0]),
+        pltpu.make_async_copy(give_ref, spot(gives_ref, me), local.at[1]),
+        pltpu.make_async_copy(gz_ref, gz_both_ref.at[0], local.at[2]),
+    ]
+    for copy in [k_chip, v_chip, gz_pair, k_core, v_core] + own:
+        copy.start()
+    k_chip.wait_recv()
+    k_on = remote(spot(keeps_ref, peer(2)), spot(keeps_ref, peer(2)), sends, recvs, 5, 1)
+    k_on.start()
+    v_chip.wait_recv()
+    v_on = remote(spot(gives_ref, peer(2)), spot(gives_ref, peer(2)), sends, recvs, 6, 1)
+    v_on.start()
+    for copy in own + [k_core, v_core, gz_pair, k_on, v_on]:
+        copy.wait()
+    k_chip.wait_send()
+    v_chip.wait_send()
+
+
+def cost(microseconds):
+    return pl.CostEstimate(flops=int(microseconds * 1e9), bytes_accessed=1 << 20, transcendentals=0)
+
+
+def collect(keep, give, grad_z):
+    tokens, half = keep.shape
+    group = lax.axis_size("shard")
+    wide = jax.ShapeDtypeStruct((tokens, half * group), bf16)
+    return pl.pallas_call(
+        collect_kernel,
+        in_specs=[VMEM_SPEC] * 3,
+        out_specs=[VMEM_SPEC] * 3,
+        out_shape=[wide, wide, jax.ShapeDtypeStruct((2,) + grad_z.shape, bf16)],
+        scratch_shapes=[
+            pltpu.SemaphoreType.DMA((7,)), pltpu.SemaphoreType.DMA((7,)), pltpu.SemaphoreType.DMA((3,)),
+        ],
+        compiler_params=group_params(6, 16 << 20),
+        cost_estimate=cost(25),
+        name="collect",
+    )(keep, give, grad_z)
+
+
 def middle_kernel(
-    keep_ref, give_ref, gz_ref, x_hbm, o_hbm,
-    both_ref, gz_got_ref, out_ref,
-    o_ref, gives, xcol, acc, outs, sends, recvs, local, o_local,
+    keeps_ref, gives_ref, give_ref, cot_ref, x_hbm, o_hbm,
+    both_ref, cots_ref, out_ref,
+    o_ref, xcol, outs, sends, recvs, local, o_local,
 ):
     me = lax.axis_index("shard")
     side = lax.rem(lax.axis_index("replica"), 2)
-    tokens, half = keep_ref.shape
-    keeps_ref, gots_ref = both_ref.at[0], both_ref.at[1]
+    tokens, half = give_ref.shape
+    gots_ref = both_ref.at[1]
     seqs, rows, _ = out_ref.shape
-    cols = acc.shape[1]
+    cols = xcol.shape[1]
     piece = o_hbm.shape[0] // lax.axis_size("replica")
     per = half // piece
     loads = []
@@ -638,163 +705,101 @@
     fetch.start()
     other = meet_group_and_pair()
 
-    def spot(ref, owner):
-        return ref.at[:, pl.ds(pl.multiple_of(owner * half, 128), half)]
-
-    give_pair = across(give_ref, spot(gots_ref, me), sends, recvs, 0, other)
-    gz_pair = across(gz_ref, gz_got_ref, sends, recvs, 1, other)
-    k_chip = remote(keep_ref, spot(keeps_ref, me), sends, recvs, 2, 2)
-    v_chip = remote(give_ref, spot(gives, me), sends, recvs, 3, 2)
-    k_core = remote(keep_ref, spot(keeps_ref, me), sends, recvs, 4, 1)
-    v_core = remote(give_ref, spot(gives, me), sends, recvs, 5, 1)
-    k_own = pltpu.make_async_copy(keep_ref, spot(keeps_ref, me), local.at[1])
-    v_own = pltpu.make_async_copy(give_ref, spot(gives, me), local.at[2])
-    for copy in (k_core, v_core, k_chip, give_pair, v_chip, gz_pair, k_own, v_own):
+    def spot(owner):
+        return gots_ref.at[:, pl.ds(pl.multiple_of(owner * half, 128), half)]
+
+    give_pair = across(give_ref, spot(me), sends, recvs, 0, other)
+    cot_pair = across(cot_ref, cots_ref.at[1], sends, recvs, 1, other)
+    own = [
+        pltpu.make_async_copy(keeps_ref, both_ref.at[0], local.at[1]),
+        pltpu.make_async_copy(cot_ref, cots_ref.at[0], local.at[2]),
+    ]
+    for copy in [give_pair, cot_pair] + own:
         copy.start()
-
-    def gated_rows(q, owner):
-        where = pl.ds(pl.multiple_of(owner * half, 128), half)
-        left = keeps_ref if q == 0 else gives
-        return rows_dot(left[:, where], o_ref[q, where, :])
-
-    k_own.wait()
-    v_own.wait()
-    for copy in loads:
+    for copy in loads + [fetch]:
         copy.wait()
-    fetch.wait()
-    acc[...] = xcol[...].astype(f32) + gated_rows(0, me)
-    acc[...] += gated_rows(1, me)
-    k_core.wait()
-    acc[...] += gated_rows(0, peer(1))
-    v_core.wait()
-    acc[...] += gated_rows(1, peer(1))
-    k_chip.wait_recv()
-    k_on = remote(spot(keeps_ref, peer(2)), spot(keeps_ref, peer(2)), sends, recvs, 6, 1)
-    k_on.start()
-    give_pair.wait_recv()
-    g_chip = remote(spot(gots_ref, me), spot(gots_ref, me), sends, recvs, 7, 2)
-    g_core = remote(spot(gots_ref, me), spot(gots_ref, me), sends, recvs, 8, 1)
-    g_core.start()
-    acc[...] += gated_rows(0, peer(2))
-    k_on.wait()
-    acc[...] += gated_rows(0, peer(3))
-    v_chip.wait_recv()
-    v_on = remote(spot(gives, peer(2)), spot(gives, peer(2)), sends, recvs, 9, 1)
-    v_on.start()
-    acc[...] += gated_rows(1, peer(2))
-    v_on.wait()
-    outs[...] = (acc[...] + gated_rows(1, peer(3))).astype(bf16).reshape(outs.shape)
-
-    def out_rows(owner):
-        return outs.at[:, pl.ds(pl.multiple_of(owner * rows, 16), rows), :]
-
-    home = out_ref.at[:, :, pl.ds(pl.multiple_of(me * cols, 128), cols)]
-    out_own = pltpu.make_async_copy(out_rows(me), home, local.at[3])
-    out_own.start()
-    out_sends = [remote(out_rows(peer(hop)), home, sends, recvs, 9 + hop, hop) for hop in (2, 3, 1)]
+    tile = 256
+
+    def product(t, carry):
+        rows_at = pl.ds(pl.multiple_of(t * tile, tile), tile)
+        value = (
+            xcol[rows_at, :].astype(f32)
+            + rows_dot(keeps_ref[rows_at, :], o_ref[0])
+            + rows_dot(gives_ref[rows_at, :], o_ref[1])
+        )
+        outs[rows_at, :] = value.astype(bf16)
+        return carry
+
+    lax.fori_loop(0, tokens // tile, product, 0)
+    length = tokens // seqs
+    out_sends = []
+    for seq in range(seqs):
+        for n_hop, hop in enumerate((2, 3, 1)):
+            src = outs.at[pl.ds(pl.multiple_of(seq * length + peer(hop) * rows, 16), rows), :]
+            dst = out_ref.at[seq, :, pl.ds(pl.multiple_of(me * cols, 128), cols)]
+            out_sends.append(remote(src, dst, sends, recvs, 2 + seq * 3 + n_hop, hop))
+        own.append(
+            pltpu.make_async_copy(
+                outs.at[pl.ds(pl.multiple_of(seq * length + me * rows, 16), rows), :],
+                out_ref.at[seq, :, pl.ds(pl.multiple_of(me * cols, 128), cols)],
+                local.at[3 + seq],
+            )
+        )
+        own[-1].start()
     for copy in out_sends:
         copy.start()
+    base = 2 + seqs * 3
+    give_pair.wait_recv()
+    g_chip = remote(spot(me), spot(me), sends, recvs, base, 2)
+    g_core = remote(spot(me), spot(me), sends, recvs, base + 1, 1)
     g_chip.start()
+    g_core.start()
     g_chip.wait_recv()
-    g_on = remote(spot(gots_ref, peer(2)), spot(gots_ref, peer(2)), sends, recvs, 13, 1)
+    g_on = remote(spot(peer(2)), spot(peer(2)), sends, recvs, base + 2, 1)
     g_on.start()
-    for copy in out_sends + [g_on, g_core, gz_pair]:
+    for copy in out_sends + [g_on, g_core, cot_pair] + own:
         copy.wait()
-    for copy in (g_chip, give_pair, k_chip, v_chip):
-        copy.wait_send()
-    out_own.wait()
-
-
-def middle(keep, give, grad_z, x_all, out_proj, seqs):
-    tokens, half = keep.shape
+    g_chip.wait_send()
+    give_pair.wait_send()
+
+
+def middle(keeps, gives, give, cot, x_all, out_proj, seqs):
+    tokens, half = give.shape
     group = lax.axis_size("shard")
     model = x_all.shape[1]
     cols = model // group
+    pieces = 8 * max(1, half * lax.axis_size("replica") // out_proj.shape[0])
     return pl.pallas_call(
         middle_kernel,
-        in_specs=[VMEM_SPEC] * 3 + [ANY_SPEC] * 2,
+        in_specs=[VMEM_SPEC] * 4 + [ANY_SPEC] * 2,
         out_specs=[VMEM_SPEC] * 3,
         out_shape=[
             jax.ShapeDtypeStruct((2, tokens, half * group), bf16),
-            jax.ShapeDtypeStruct(grad_z.shape, bf16),
+            jax.ShapeDtypeStruct((2, tokens, cols), bf16),
             jax.ShapeDtypeStruct((seqs, tokens // seqs // group, model), bf16),
         ],
         scratch_shapes=[
             pltpu.VMEM((2, half * group, cols), bf16),
-            pltpu.VMEM((tokens, half * group), bf16),
             pltpu.VMEM((tokens, cols), bf16),
-            pltpu.VMEM((tokens, cols), f32),
-            pltpu.VMEM((seqs, tokens // seqs, cols), bf16),
-            pltpu.SemaphoreType.DMA((14,)), pltpu.SemaphoreType.DMA((14,)), pltpu.SemaphoreType.DMA((4,)),
-            pltpu.SemaphoreType.DMA((8 * max(1, half * group // 4 // (out_proj.shape[0] // lax.axis_size("replica"))),)),
+            pltpu.VMEM((tokens, cols), bf16),
+            pltpu.SemaphoreType.DMA((5 + 3 * seqs,)), pltpu.SemaphoreType.DMA((5 + 3 * seqs,)),
+            pltpu.SemaphoreType.DMA((3 + seqs,)), pltpu.SemaphoreType.DMA((pieces,)),
         ],
-        compiler_params=group_params(6, 20 << 20),
+        compiler_params=group_params(7, 20 << 20),
+        cost_estimate=cost(25),
         name="middle",
-    )(keep, give, grad_z, x_all, out_proj)
-
-
-def home_kernel(gx_ref, gz_ref, small_ref, got_ref, cols_ref, small_got_ref, sends, recvs, local):
-    me = lax.axis_index("shard")
-    width = gx_ref.shape[1]
-    other = meet_group_and_pair()
-    pair_copy = across(gx_ref, got_ref, sends, recvs, 0, other)
-    pair_copy.start()
-    small_copy = across(small_ref, small_got_ref, sends, recvs, 3, other)
-    small_copy.start()
-
-    def goal(slot):
-        return (4 * slot + me) // 2
-
-    spot = cols_ref.at[:, pl.ds(pl.multiple_of(lax.rem(me, 2) * width, 128), width)]
-
-    def send(slot, ref):
-        return part_copy(ref, spot, sends.at[1 + slot], recvs.at[1 + lax.rem(me, 2)], goal(slot))
-
-    def keep(ref):
-        return pltpu.make_async_copy(ref, spot, local.at[0])
-
-    refs = (gx_ref, gz_ref)
-    for slot in (0, 1):
-        pl.when(goal(slot) != me)(lambda slot=slot: send(slot, refs[slot]).start())
-        pl.when(goal(slot) == me)(lambda slot=slot: keep(refs[slot]).start())
-    for slot in (0, 1):
-        pl.when(goal(slot) != me)(lambda slot=slot: send(slot, refs[slot]).wait_send())
-        pl.when(goal(slot) == me)(lambda slot=slot: keep(refs[slot]).wait())
-    for at in range(2):
-
-        @pl.when(lax.rem(2 * me + at, 4) != me)
-        def _(at=at):
-            part_copy(gx_ref, gx_ref, sends.at[0], recvs.at[1 + at], peer(1)).wait_recv()
-
-    pair_copy.wait()
-    small_copy.wait()
-
-
-def to_home(gx, gz, small):
-    tokens, width = gx.shape
-    return pl.pallas_call(
-        home_kernel,
-        in_specs=[VMEM_SPEC] * 3,
-        out_specs=[VMEM_SPEC] * 3,
-        out_shape=[
-            jax.ShapeDtypeStruct(gx.shape, bf16),
-            jax.ShapeDtypeStruct((tokens, 2 * width), bf16),
-            jax.ShapeDtypeStruct(small.shape, bf16),
-        ],
-        scratch_shapes=[
-            pltpu.SemaphoreType.DMA((4,)), pltpu.SemaphoreType.DMA((4,)), pltpu.SemaphoreType.DMA((1,)),
-        ],
-        compiler_params=group_params(7, 16 << 20),
-        name="to_home",
-    )(gx, gz, small)
+    )(keeps, gives, give, cot, x_all, out_proj)
+
+
+PARTS = 4
 
 
 def finish_kernel(
-    xb_ref, sb_ref, wz_ref, cols_ref, w_hbm, x_ref, cot_ref, gain_ref,
+    gx_ref, gz_ref, small_keep_ref, small_give_ref, wz_ref, norm_ref, w_hbm, x_ref, cot_ref, gain_ref,
     gw_ref, small_ref, dx_ref, ggain_ref,
-    w_ref, x_in, s_in, lhs, pairs, near, g_own, g_send, g_far, h_send, h_cols, s_own, gains, gain_near, gain_sum,
-    gain_pair, gain_two, gain_in,
-    sends, recvs, far_sends, far_recvs, local,
+    w_ref, got, cols_ref, turned, xb_ref, sb_ref, small_got, x_in, s_in, lhs, pairs, near, g_own, g_send, g_far,
+    h_send, h_cols, s_own, gains, gain_near, gain_sum, gain_pair, gain_two, gain_in,
+    sends, recvs, far_sends, far_recvs, home_sends, home_recvs, local,
 ):
     me = lax.axis_index("shard")
     home = lax.axis_index("replica")
@@ -803,10 +808,10 @@
     mine = home // 2
     side = lax.rem(home, 2)
     seqs, rows, model = x_ref.shape
-    tokens = cols_ref.shape[0]
+    tokens, width = gx_ref.shape
     length = tokens // seqs
-    deep, width = wz_ref.shape
-    half = deep // 2
+    deep = wz_ref.shape[0]
+    part = width // PARTS
     tile = 256
     span = seqs * rows
     load = pltpu.make_async_copy(w_hbm, w_ref, local.at[0])
@@ -823,39 +828,34 @@
         pl.semaphore_signal(barrier, inc=1, device_id={"replica": far(step)}, device_id_type=MESH)
     pl.semaphore_wait(barrier, 3 + height)
 
-    def far_copy(src, dst, kind, step):
-        at = kind * height + step
-        return across(src, dst, far_sends, far_recvs, at, far(step))
-
-    def block(step):
-        return lax.rem(mine + step, height)
-
-    order = range(1, height)
-    s_sends = [far_copy(sb_ref.at[block(step)], s_in.at[step - 1], 0, step) for step in order]
-
-    def x_sends(part):
-        cut = slice(part * half, (part + 1) * half)
-        return [
-            far_copy(xb_ref.at[block(step), cut], x_in.at[step - 1, cut], 1 + part, step) for step in order
-        ]
-
-    for copy in s_sends + x_sends(0):
+    def cut(p):
+        return slice(p * part, (p + 1) * part)
+
+    y_sends = [across(gx_ref.at[:, cut(p)], got.at[:, cut(p)], sends, recvs, p, other) for p in range(PARTS)]
+    small_send = across(small_give_ref, small_got, sends, recvs, PARTS, other)
+    y_sends[0].start()
+    small_send.start()
+    for copy in y_sends[1:]:
         copy.start()
-
-    spot = pl.ds(pl.multiple_of(lax.rem(me, 2) * width, LANES), width)
 
     def goal(slot):
         return (4 * slot + me) // 2
 
+    spot = pl.ds(pl.multiple_of(lax.rem(me, 2) * width, LANES), width)
+
     def home_pieces(at):
-        if at == 2:
+        if at == PARTS:
             return 1, wz_ref, h_cols.at[:, spot]
-        cut = slice(at * half, (at + 1) * half)
-        return 0, h_send.at[cut], h_cols.at[cut, spot]
+        if at == PARTS + 1:
+            return 0, gx_ref, cols_ref.at[:, spot]
+        if at == PARTS + 2:
+            return 1, gz_ref, cols_ref.at[:, spot]
+        place = pl.ds(pl.multiple_of(lax.rem(me, 2) * width + at * part, LANES), part)
+        return 0, h_send.at[:, cut(at)], h_cols.at[:, place]
 
     def home_send(at):
         slot, src, dst = home_pieces(at)
-        return part_copy(src, dst, sends.at[at], recvs.at[at * 2 + lax.rem(me, 2)], goal(slot))
+        return part_copy(src, dst, home_sends.at[at], home_recvs.at[at * 2 + lax.rem(me, 2)], goal(slot))
 
     def home_keep(at):
         _, src, dst = home_pieces(at)
@@ -866,7 +866,64 @@
         pl.when(goal(slot) != me)(lambda: home_send(at).start())
         pl.when(goal(slot) == me)(lambda: home_keep(at).start())
 
-    home_start(2)
+    def home_wait(at):
+        slot = home_pieces(at)[0]
+        pl.when(goal(slot) != me)(lambda: home_send(at).wait_send())
+        pl.when(goal(slot) == me)(lambda: home_keep(at).wait())
+        for place in range(2):
+            source = lax.rem(2 * me + place, 4)
+
+            @pl.when((me // 2 == slot) & (source != me))
+            def _(place=place):
+                src = home_pieces(at)[1]
+                part_copy(src, src, home_sends.at[at], home_recvs.at[at * 2 + place], peer(1)).wait_recv()
+
+    for at in (PARTS + 1, PARTS + 2, PARTS):
+        home_start(at)
+
+    for i in range(2 * tokens // tile):
+        for j in range(norm_ref.shape[1] // tile):
+            turned[j * tile : (j + 1) * tile, i * tile : (i + 1) * tile] = norm_ref[
+                i * tile : (i + 1) * tile, j * tile : (j + 1) * tile
+            ].T
+
+    def far_copy(src, dst, kind, step):
+        return across(src, dst, far_sends, far_recvs, kind * height + step, far(step))
+
+    def block(step):
+        return lax.rem(mine + step, height)
+
+    order = range(1, height)
+
+    def lines(at):
+        return pl.ds(pl.multiple_of(at * deep, 16), deep)
+
+    def x_sends(p):
+        return [
+            far_copy(xb_ref.at[lines(block(step)), cut(p)], x_in.at[step - 1, :, cut(p)], p, step) for step in order
+        ]
+
+    def x_part(p):
+        y_sends[p].wait_recv()
+
+        def rows_of(t, carry):
+            at = pl.ds(pl.multiple_of(t * tile, tile), tile)
+            value = rows_dot(turned[at, :tokens], gx_ref[:, cut(p)]) + rows_dot(turned[at, tokens:], got[:, cut(p)])
+            xb_ref[at, cut(p)] = value.astype(bf16)
+            return carry
+
+        lax.fori_loop(0, xb_ref.shape[0] // tile, rows_of, 0)
+        for copy in x_sends(p):
+            copy.start()
+
+    x_part(0)
+    small_send.wait_recv()
+    for at in range(height):
+        sb_ref[at] = (small_keep_ref[at] + small_got[at].astype(f32)).astype(bf16)
+    s_sends = [far_copy(sb_ref.at[block(step)], s_in.at[step - 1], PARTS, step) for step in order]
+    for copy in s_sends:
+        copy.start()
+    x_part(1)
 
     def stage(owners):
         for i, owner in enumerate(owners):
@@ -880,6 +937,8 @@
     def product(t):
         return outer_dot(lhs[...], w_ref[lanes(t), :])
 
+    home_wait(PARTS + 1)
+    home_wait(PARTS + 2)
     stage((peer(3), peer(1)))
     load.wait()
 
@@ -890,8 +949,9 @@
         return carry
 
     lax.fori_loop(0, model // tile, first, 0)
-    near_send = remote(pairs, near, sends, recvs, 6, 1)
+    near_send = remote(pairs, near, sends, recvs, PARTS + 1, 1)
     near_send.start()
+    x_part(2)
 
     for copy in s_sends:
         copy.wait_recv()
@@ -900,9 +960,10 @@
         total = total + s_in[step - 1].astype(f32)
     s_own[...] = total.astype(bf16)
     small_ref[side, mine] = s_own[...]
-    spread = [far_copy(s_own, small_ref.at[side, mine], 3, step) for step in order]
-    for copy in spread + x_sends(1):
+    spread = [far_copy(s_own, small_ref.at[side, mine], PARTS + 1, step) for step in order]
+    for copy in spread:
         copy.start()
+    x_part(3)
 
     stage((peer(2), me))
     near_send.wait()
@@ -914,8 +975,19 @@
         return carry
 
     lax.fori_loop(0, model // tile, second, 0)
-    chip_send = remote(g_send, g_far, sends, recvs, 7, 2)
+    chip_send = remote(g_send, g_far, sends, recvs, PARTS + 2, 2)
     chip_send.start()
+
+    def home_sum(p):
+        for copy in x_sends(p):
+            copy.wait_recv()
+        total = xb_ref[lines(mine), cut(p)].astype(f32)
+        for step in order:
+            total = total + x_in[step - 1, :, cut(p)].astype(f32)
+        h_send[:, cut(p)] = total.astype(bf16)
+        home_start(p)
+
+    home_sum(0)
     chip_send.wait()
 
     gains[...] = jnp.zeros_like(gains)
@@ -942,36 +1014,28 @@
     def gain_part(owner):
         return gains.at[:, pl.ds(pl.multiple_of(owner * wide, LANES), wide)]
 
-    gain_sends = [remote(gain_part(peer(hop)), gain_near.at[hop - 1], sends, recvs, 7 + hop, hop) for hop in (1, 2, 3)]
+    gain_sends = [
+        remote(gain_part(peer(hop)), gain_near.at[hop - 1], sends, recvs, PARTS + 2 + hop, hop) for hop in (1, 2, 3)
+    ]
     for copy in gain_sends:
         copy.start()
-
-    def home_sum(part):
-        for copy in x_sends(part):
-            copy.wait_recv()
-        cut = slice(part * half, (part + 1) * half)
-        total = xb_ref[mine, cut].astype(f32)
-        for step in order:
-            total = total + x_in[step - 1, cut].astype(f32)
-        h_send[cut] = total.astype(bf16)
-        home_start(part)
-
     for copy in gain_sends:
         copy.wait()
     gain_sum[...] = gains[:, pl.ds(pl.multiple_of(me * wide, LANES), wide)] + gain_near[0] + gain_near[1] + gain_near[2]
-    gain_copy = across(gain_sum, gain_pair, sends, recvs, 11, other)
+    gain_copy = across(gain_sum, gain_pair, sends, recvs, PARTS + 6, other)
     gain_copy.start()
-    home_sum(0)
+    home_sum(1)
     gain_copy.wait()
     gain_two[...] = gain_sum[...] + gain_pair[...]
-    gain_far = [far_copy(gain_two, gain_in.at[step - 1], 4, step) for step in order]
+    gain_far = [far_copy(gain_two, gain_in.at[step - 1], PARTS + 2, step) for step in order]
     for copy in gain_far:
         copy.start()
+    home_sum(2)
     for copy in spread:
         copy.wait_recv()
-    small_pair = across(small_ref.at[side], small_ref.at[side], sends, recvs, 12, other)
+    small_pair = across(small_ref.at[side], small_ref.at[side], sends, recvs, PARTS + 7, other)
     small_pair.start()
-    home_sum(1)
+    home_sum(3)
     for copy in gain_far:
         copy.wait()
     total = gain_two[...]
@@ -979,38 +1043,33 @@
         total = total + gain_in[step - 1]
     ggain_ref[...] = total
 
-    for at in (2, 0, 1):
-        slot = home_pieces(at)[0]
-        pl.when(goal(slot) != me)(lambda at=at: home_send(at).wait_send())
-        pl.when(goal(slot) == me)(lambda at=at: home_keep(at).wait())
-
-        for place in range(2):
-            source = lax.rem(2 * me + place, 4)
-            wanted = (me // 2 == slot) & (source != me)
-
-            @pl.when(wanted)
-            def _(at=at, place=place):
-                _, src, _ = home_pieces(at)
-                part_copy(src, src, sends.at[at], recvs.at[at * 2 + place], peer(1)).wait_recv()
-
+    for at in (PARTS, 0, 1, 2, 3):
+        home_wait(at)
     for r in range(0, deep, 32):
         gw_ref[r : r + 32, :] = h_cols[r : r + 32, :].astype(f32)
     small_pair.wait()
-    for copy in s_sends + spread + x_sends(0) + x_sends(1):
+    small_send.wait_send()
+    for p in range(PARTS):
+        y_sends[p].wait_send()
+        for copy in x_sends(p):
+            copy.wait_send()
+    for copy in s_sends + spread:
         copy.wait_send()
 
 
-def finish(x_blocks, small_blocks, wz, cols, w_in, x, cot, gain):
-    height, deep, width = x_blocks.shape
+def finish(gx, gz, small_keep, small_give, wz, norm, w_in, x, cot, gain):
+    tokens, width = gx.shape
+    height, lines, _ = small_keep.shape
+    deep = wz.shape[0]
     seqs, rows, model = x.shape
     span = seqs * rows
-    lines = small_blocks.shape[1]
     wide = model // 4
     gain_tile = pltpu.VMEM((8, wide), f32)
     other = max(height - 1, 1)
+    kinds = (PARTS + 3) * height
     return pl.pallas_call(
         finish_kernel,
-        in_specs=[VMEM_SPEC] * 4 + [ANY_SPEC] + [VMEM_SPEC] * 3,
+        in_specs=[VMEM_SPEC] * 6 + [ANY_SPEC] + [VMEM_SPEC] * 3,
         out_specs=[VMEM_SPEC] * 4,
         out_shape=[
             jax.ShapeDtypeStruct((deep, 2 * width), f32),
@@ -1020,9 +1079,15 @@
         ],
         scratch_shapes=[
             pltpu.VMEM(w_in.shape, bf16),
+            pltpu.VMEM((tokens, width), bf16),
+            pltpu.VMEM((tokens, 2 * width), bf16),
+            pltpu.VMEM((height * deep, 2 * tokens), bf16),
+            pltpu.VMEM((height * deep, width), bf16),
+            pltpu.VMEM((height, lines, width), bf16),
+            pltpu.VMEM((height, lines, width), bf16),
             pltpu.VMEM((other, deep, width), bf16),
             pltpu.VMEM((other, lines, width), bf16),
-            pltpu.VMEM((2 * span, cols.shape[1]), bf16),
+            pltpu.VMEM((2 * span, 2 * width), bf16),
             pltpu.VMEM((2, span, model), bf16),
             pltpu.VMEM((2, span, model), bf16),
             pltpu.VMEM((span, model), f32),
@@ -1035,13 +1100,15 @@
             pltpu.VMEM((3, 8, wide), f32),
             gain_tile, gain_tile, gain_tile,
             pltpu.VMEM((other, 8, wide), f32),
-            pltpu.SemaphoreType.DMA((13,)), pltpu.SemaphoreType.DMA((13,)),
-            pltpu.SemaphoreType.DMA((5 * height,)), pltpu.SemaphoreType.DMA((5 * height,)),
-            pltpu.SemaphoreType.DMA((4,)),
+            pltpu.SemaphoreType.DMA((PARTS + 8,)), pltpu.SemaphoreType.DMA((PARTS + 8,)),
+            pltpu.SemaphoreType.DMA((kinds,)), pltpu.SemaphoreType.DMA((kinds,)),
+            pltpu.SemaphoreType.DMA((PARTS + 3,)), pltpu.SemaphoreType.DMA((2 * PARTS + 6,)),
+            pltpu.SemaphoreType.DMA((PARTS + 4,)),
         ],
-        compiler_params=group_params(8, 48 << 20),
+        compiler_params=group_params(8, 56 << 20),
+        cost_estimate=cost(80),
         name="finish",
-    )(x_blocks, small_blocks, wz, cols, w_in, x, cot, gain)
+    )(gx, gz, small_keep, small_give, wz, norm, w_in, x, cot, gain)
 
 
 def total_kernel(part_ref, out_ref, near, chip_sum, far, sends, recvs):
@@ -1144,7 +1211,7 @@
     )
     gain = gains[::8].reshape(1, -1)
     x_all = xs.reshape(tokens, model)
-    cot_pair = cots.reshape(2 * tokens, -1)
+    cot = cots.reshape(tokens, -1)
     if model // count % LANES == 0:
         normed_pair = normed_pair.reshape(2 * tokens, -1)
     else:
@@ -1180,17 +1247,20 @@
 
     gated_keep, gated_give = halves(gated.reshape(tokens, width), height // 4)
     cols = model // 4
-    gated_both, grad_z_got, block_output = middle(gated_keep, gated_give, grad_z, x_all, out_proj, seqs)
-    out_blocks = inner_dot(gated_both.reshape(2 * tokens, -1), cot_pair).astype(bf16).reshape(height, -1, cols)
-    z_blocks = inner_dot(normed_pair, both(grad_z, grad_z_got)).astype(bf16).reshape(height, -1, width)
-    out_own, out_sent = far_send(out_blocks)
+    keeps, gives, grad_z_both = collect(gated_keep, gated_give, grad_z)
+    z_blocks = inner_dot(normed_pair, grad_z_both.reshape(2 * tokens, -1)).astype(bf16).reshape(height, -1, width)
     z_own, z_sent = far_send(z_blocks)
-    rate, out_own, z_own = lax.optimization_barrier((rate, out_own, z_own))
+    keeps, z_own = lax.optimization_barrier((keeps, z_own))
+    gated_both, cot_both, block_output = middle(keeps, gives, gated_give, cot, x_all, out_proj, seqs)
+    out_blocks = inner_dot(gated_both.reshape(2 * tokens, -1), cot_both.reshape(2 * tokens, -1))
+    out_own, out_sent = far_send(out_blocks.astype(bf16).reshape(height, -1, cols))
+    rate, out_own = lax.optimization_barrier((rate, out_own))
 
     grad_conv_rec, grad_dt_low, grad_proj, grad_dt_proj, grad_dt_bias, grad_d_skip = recurrence_backward(
         rate, beta, conv_out, dy, proj, keep_lanes, dt_proj, states
     )
-    grad_proj, out_sent = lax.optimization_barrier((grad_proj, out_sent))
+    grad_proj, z_sent = lax.optimization_barrier((grad_proj, z_sent))
+    grad_w_z = far_total(z_own.astype(f32), z_sent).astype(bf16)
     grad_proj = group_total(grad_proj, 4).astype(bf16)
     grad_x_proj = rows_dot(grad_proj, conv_flat)
     grad_conv = dy * skip + grad_conv_rec + split(inner_dot(grad_proj, x_proj))
@@ -1216,15 +1286,11 @@
     padded = -(-small.shape[0] // unit) * unit
     small = jnp.pad(small, ((0, padded - small.shape[0]), (0, 0))).reshape(height, 2, -1, width)
     small_keep = jnp.where(side == 0, small[:, 0], small[:, 1])
-    small_give = jnp.where(side == 0, small[:, 1], small[:, 0]).astype(bf16).reshape(-1, width)
-    grad_x_got, grad_cols, small_got = to_home(grad_x, grad_z, small_give)
-    small_blocks = (small_keep + small_got.reshape(small_keep.shape).astype(f32)).astype(bf16)
-    x_blocks = inner_dot(normed_pair, both(grad_x, grad_x_got)).astype(bf16).reshape(height, -1, width)
-    x_blocks, z_sent = lax.optimization_barrier((x_blocks, z_sent))
-    grad_w_z = far_total(z_own.astype(f32), z_sent).astype(bf16)
+    small_give = jnp.where(side == 0, small[:, 1], small[:, 0]).astype(bf16)
+    grad_x, out_sent = lax.optimization_barrier((grad_x, out_sent))
     grad_out_proj = far_total(out_own.astype(f32), out_sent)
     grad_w_in, small, input_grad, grad_gain = finish(
-        x_blocks, small_blocks, grad_w_z, grad_cols, w_in, block_input, out_grad, gain
+        grad_x, grad_z, small_keep, small_give, grad_w_z, normed_pair, w_in, block_input, out_grad, gain
     )
     small = small.transpose(1, 0, 2, 3).reshape(padded, width).astype(f32)
 

time: 373 us -> 353 us (0.946); the launches traced: 368 us -> 352 us
  Pallas kernels: 299 us -> 262 us
  waiting for transfers between devices: 0.02 us -> 24 us
  matrix products: 10.8 us -> 6.12 us
  other arithmetic: 18.7 us -> 23.1 us
    pallas_call x3, Pallas kernels: 167 us -> 140 us  [the longest x1 83.3 us: finish(): pl.pallas_call(finish_kernel, in_specs=[VMEM_SPEC] * 6 + [ANY_SPEC] + [VM...]
    ppermute x6, waiting for transfers between devices: 0.02 us -> 24 us  [far_send(): lax.ppermute(out, 'replica', [(i, (i + 2 * step) % count) for i in range(...]
    pallas_call x1, Pallas kernels: 45.7 us -> 36.2 us  [recurrence_backward(): pl.pallas_call(backward_kernel, grid=(seqs, blocks), in_specs=[wide, wide...]
    pallas_call x1, Pallas kernels: 49.7 us -> 43.4 us  [front(): pl.pallas_call(front_kernel, in_specs=[VMEM_SPEC] * 3 + [ANY_SPEC] * 2, o...]
    pallas_call x2, Pallas kernels: 17.9 us -> 22.9 us  [group_total(): pl.pallas_call(total_kernel, in_specs=[VMEM_SPEC], out_specs=VMEM_SPEC, o...]
    dot_general x4 -> x3, matrix products: 9.1 us -> 5.28 us  [inner_dot(): lax.dot_general(a, b, (((0,), (0,)), ((), ())), preferred_element_type=f32)]
    unnamed x74 -> x64, local copies, waits for them, and re-layouts: 15.2 us -> 16.9 us
  transfers between devices with their start and end apart: 7 -> 7, of which waited for: 0 -> 2; matrix products, arithmetic and copies ran while one was open for 5% -> 4% of each run, Pallas kernels for 29% -> 18%
where the time goes in v4:
time: 353 us; the launch traced here: 352 us
  Pallas kernels  262 us (74%)
  local copies, waits for them, and re-layouts  25.9 us (7%)
  waiting for transfers between devices  24 us (7%)
  other arithmetic  23.1 us (7%)
  starting transfers between devices  9.85 us (3%)
  matrix products  6.12 us (2%)
    pallas_call x1, Pallas kernels, finish(): pl.pallas_call(finish_kernel, in_specs=[VMEM_SPEC] * 6 + [ANY_SPEC] + [VM...  83.3 us
    pallas_call x1, Pallas kernels, front(): pl.pallas_call(front_kernel, in_specs=[VMEM_SPEC] * 3 + [ANY_SPEC] * 2, o...  43.4 us
    pallas_call x1, Pallas kernels, recurrence_backward(): pl.pallas_call(backward_kernel, grid=(seqs, blocks), in_specs=[wide, wide...  36.2 us
    pallas_call x1, Pallas kernels, middle(): pl.pallas_call(middle_kernel, in_specs=[VMEM_SPEC] * 4 + [ANY_SPEC] * 2,...  29.7 us
    pallas_call x1, Pallas kernels, collect(): pl.pallas_call(collect_kernel, in_specs=[VMEM_SPEC] * 3, out_specs=[VMEM_...  27.2 us
    ppermute x6, waiting for transfers between devices, far_send(): lax.ppermute(out, 'replica', [(i, (i + 2 * step) % count) for i in range(...  24 us
    pallas_call x2, Pallas kernels, group_total(): pl.pallas_call(total_kernel, in_specs=[VMEM_SPEC], out_specs=VMEM_SPEC, o...  22.9 us
    pallas_call x1, Pallas kernels, recurrence_forward(): pl.pallas_call(forward_kernel, grid=(seqs, blocks), in_specs=[wide, wide,...  19.3 us
  transfers between devices with their start and end apart: 7, of which 2 were waited for; matrix products, arithmetic and copies ran while one was open for 4% of the time, Pallas kernels for 18%

profile of v4, /device:TPU:0, one launch (start us, length us, event | category | flops | bytes accessed | tf_op | source)
XLA Modules:
  0.0 352.1 jit_solution(9090862291355446254)
XLA Ops:
  0.7 0.7 convert_element_type.106
  1.4 0.9 compare_convert_fusion.2
  2.3 0.9 fusion.20
  3.2 0.7 broadcast_in_dim.12.gain_ref
  3.8 1.0 copy-done.4
  4.9 1.0 copy-done.5
  5.9 43.4 %front.1 = (bf16[2,256,2048]{2,1,0:T(8,128)(2,1)S(1)}, bf16[2,256,512]{2,1,0:T(8,128)(2,1)S(1)}, f32[32,512]{1,0:T(8,128)S(1)}, bf16[2,256,2048]{2,1,0:T(8,128)(...) custom-call(bf16[2,64,2048]{2,1,0:T(8,128)(2,1)S(1)} %copy-done.4, ...), custom_call_target="tpu_custom_call" | custom-call | tf_op jit(solution)/shard_map/front/pallas_call | solution.py:568
  49.3 2.6 slice_bitcast_fusion
  52.0 2.7 fusion.12
  54.6 0.5 convolution_bitcast_fusion.part_ref
  55.1 14.0 %group_total.2.proj_ref = f32[160,512]{1,0:T(8,128)S(1)} custom-call(f32[160,512]{1,0:T(8,128)S(1)} %convolution_bitcast_fusion.part_ref), custom_call_target="tpu_custom_call" | custom-call | tf_op jit(solution)/shard_map/group_total/pallas_call | solution.py:1136
  69.2 1.2 collective-permute-start
  70.4 0.6 copy.31
  71.0 0.1 broadcast_in_dim.13.keep_ref
  71.1 0.9 copy-done.8
  72.1 19.3 %recurrence_forward.1 = (f32[2,256,1024]{2,1,0:T(8,128)S(1)}, bf16[2,256,1024]{2,1,0:T(8,128)(2,1)S(1)}, f32[2,256,1024]{2,1,0:T(8,128)S(1)}, f32[2,256,1024]{2,1,0:T(8,128)S(1)}, bf16[2,4096,1024]{2,1,0:T(8,128)(2,1)S(1)}) custom-call(bf16[2,256,1024]{2,1,0:T(8,128)(2,1)S(1)} %get-tuple-element.106.conv_ref, ...), custom_call_target="tpu_custom_call" | custom-call | flops 16000000000 | bytes 25165824 | tf_op jit(solution)/shard_map/recurrence_forward/pallas_call | solution.py:270
  91.4 5.7 %copy-done.10 = bf16[2,4096,1024]{2,1,0:T(8,128)(2,1)} copy-done((bf16[2,4096,1024]{2,1,0:T(8,128)(2,1)}, bf16[2,4096,1024]{2,1,0:T(8,128)(2,1)S(1)}, u32[]{:S(2)}) %copy-start.10) | copy-done | bytes 16777240
  97.1 1.8 convert_add_fusion
  99.0 0.1 copy-done.14
  99.1 1.1 fusion.11
  100.2 0.1 broadcast_select_fusion
  100.3 27.2 %collect.1 = (bf16[512,2048]{1,0:T(8,128)(2,1)S(1)}, bf16[512,2048]{1,0:T(8,128)(2,1)S(1)}, bf16[2,512,1024]{2,1,0:T(8,128)(2,1)S(1)}) custom-call(bf16[512,512]{1,0:T(8,128)(2,1)S(1)} %get-tuple-element.127.keep_ref, bf16[512,512]{1,0:T(8,128)(2,1)S(1)} %get-tuple-element.126.give_ref, bf16[512,1024]{1,0:T(8,128)(2,1)S(1)} %bitcast.97), custom_call_target="tpu_custom_call" | custom-call | flops 24999999488 | bytes 1048576 | tf_op jit(solution)/shard_map/collect/pallas_call | solution.py:661
  127.6 2.4 convolution_convert_fusion
  130.0 1.0 dynamic-slice_bitcast_fusion.3
  131.0 1.4 copy-done.2
  132.4 29.7 %middle.1 = (bf16[2,512,2048]{2,1,0:T(8,128)(2,1)S(1)}, bf16[2,512,512]{2,1,0:T(8,128)(2,1)S(1)}, bf16[2,64,2048]{2,1,0:T(8,128)(2,1)S(1)}) custom-call(bf16[512,2048]{1,0:T(8,128)(2,1)S(1)} %get-tuple-element.66.keeps_ref, bf16[512,2048]{1,0:T(8,128)(2,1)S(1)} %get-tuple-element.67.gives_ref, bf16[512,512]{1,0:T(8,128)(2,1)S(1)} %get-tuple-element.126.give_ref, ...), custom_call_target="tpu_custom_call" | custom-call | flops 24999999488 | bytes 1048576 | tf_op jit(solution)/shard_map/middle/pallas_call | solution.py:772
  162.1 3.7 %collective-permute-start.3 = (bf16[256,1024]{1,0:T(8,128)(2,1)S(1)}, bf16[256,1024]{1,0:T(8,128)(2,1)S(1)}, u32[]{:S(2)}, u32[]{:S(2)}) collective-permute-start(bf16[256,1024]{1,0:T(8,128)(2,1)S(1)} %get-tuple-element.117), channel_id=1, source_target_pairs={{0,24},{4,28},{8,0},{12,4},{16,8},{20,12},{24,16},{28,20},{1,25},{... | collective-permute-start | bytes 1572872 | tf_op jit(solution)/shard_map/ppermute | solution.py:1166
  165.8 1.0 collective-permute-start.1
  166.8 2.4 bitcast_convert_fusion
  169.2 1.4 dynamic-slice_bitcast_fusion
  170.6 2.8 collective-permute-start.6
  173.4 1.1 collective-permute-start.5
  174.6 36.2 %recurrence_backward.1 = (f32[2,256,1024]{2,1,0:T(8,128)S(1)}, bf16[2,256,1024]{2,1,0:T(8,128)(2,1)}, f32[160,512]{1,0:T(8,128)S(1)}, f32[128,1024]{1,0:T(8,128)...) custom-call(f32[2,256,1024]{2,1,0:T(8,128)S(1)} %get-tuple-element.74.rate_ref, ...), custom_call_target="tpu_custom_call" | custom-call | flops 30000001024 | bytes 29360128 | tf_op jit(solution)/shard_map/recurrence_backward/pallas_call | solution.py:303
  210.8 0.1 collective-permute-start.4
  210.9 0.8 collective-permute-done.2
  211.7 0.8 copy-done.22
  212.5 0.2 copy-done.24
  212.7 8.9 %group_total.3 = f32[160,512]{1,0:T(8,128)S(1)} custom-call(f32[160,512]{1,0:T(8,128)S(1)} %get-tuple-element.79.part_ref), custom_call_target="tpu_custom_call" | custom-call | tf_op jit(solution)/shard_map/group_total/pallas_call | solution.py:1136
  221.6 0.3 fusion.14
  222.0 0.5 fusion.16
  222.4 0.7 copy-done.12
  223.2 0.6 copy-done.15
  223.8 3.5 fusion.18
  227.3 0.4 concatenate.3
  227.7 0.2 pad.29
  227.9 1.0 select_bitcast_fusion.small_keep_ref
  228.9 0.7 copy-done.13
  229.6 0.5 broadcast_multiply_fusion
  230.1 0.8 fusion.13.small_give_ref
  230.9 2.1 fusion.4
  233.0 23.1 %collective-permute-done.5 = bf16[512,512]{1,0:T(8,128)(2,1)} collective-permute-done((bf16[512,512]{1,0:T(8,128)(2,1)}, bf16[512,512]{1,0:T(8,128)(2,1)}, u32[]{:S(2)}, u32[]{:S(2)}) %collective-permute-start.5) | collective-permute-done | bytes 524320 | tf_op jit(solution)/shard_map/ppermute | solution.py:1166
  256.2 1.2 add_convert_fusion.wz_ref
  257.3 83.3 %finish.1 = (f32[256,2048]{1,0:T(8,128)}, bf16[2,4,48,1024]{3,2,1,0:T(8,128)(2,1)}, bf16[2,64,2048]{2,1,0:T(8,128)(2,1)}, f32[8,512]{1,0:T(8,128)}) custom-call(bf16[512,1024]{1,0:T(8,128)(2,1)} %bitcast.113, bf16[512,1024]{1,0:T(8,128)(2,1)} %bitcast.98, f32[4,48,1024]{2,1,0:T(8,128)} %select_bitcast_fusion.small_keep_ref, ...), custom_call_target="tpu_custom_call" | custom-call | flops 80000000000 | bytes 1048576 | tf_op jit(solution)/shard_map/finish/pallas_call | solution.py:1070
  340.7 1.3 convert_bitcast_fusion
  342.0 0.2 copy.27
  342.2 0.6 fusion.19
  342.8 0.6 slice.127
  343.4 0.8 slice.130
  344.2 0.9 slice.129
  345.1 1.3 slice.112
  346.4 2.7 convert_add_fusion.1
  349.1 0.8 copy.35
  349.9 0.8 copy.36
  350.7 1.3 copy.37
  (58 shorter events, 0.2 us)
Async XLA Ops:
  0.6 54.0 %copy-start = (bf16[160,1024]{1,0:T(8,128)(2,1)S(1)}, bf16[160,1024]{1,0:T(8,128)(2,1)}, u32[]{:S(2)}) copy-start(bf16[160,1024]{1,0:T(8,128)(2,1)} %param.18) | copy-start | bytes 983044
  3.8 1.0 copy-start.4
  4.9 1.0 copy-start.5
  49.3 2.6 copy-start.6
  52.0 2.7 copy-start.11
  54.6 15.7 %copy-start.27 = (bf16[1024]{0:T(1024)(128)(2,1)S(1)}, bf16[1024]{0:T(1024)(128)(2,1)}, u32[]{:S(2)}) copy-start(bf16[1024]{0:T(1024)(128)(2,1)} %param.21) | copy-start | bytes 6148
  54.6 15.7 %copy-start.28 = (bf16[1024]{0:T(1024)(128)(2,1)S(1)}, bf16[1024]{0:T(1024)(128)(2,1)}, u32[]{:S(2)}) copy-start(bf16[1024]{0:T(1024)(128)(2,1)} %param.20) | copy-start | bytes 6148
  69.2 28.0 %collective-permute-start = (bf16[512,1024]{1,0:T(8,128)(2,1)}, bf16[512,1024]{1,0:T(8,128)(2,1)}, u32[]{:S(2)}, u32[]{:S(2)}) collective-permute-start(bf16[512,1024]{1,0:T(8,128)(2,1)} %get-tuple-element.58), channel_id=1, source_target_pairs={{0,2},{1,3},{2,0},{3,1},{4,6},{5,7},{6,4},{7,5},{8,10},{9,11},{10,... | collective-permute-start | bytes 3145736 | tf_op jit(solution)/shard_map/ppermute | solution.py:1148
  71.1 1.0 copy-start.8
  72.1 25.1 %copy-start.16 = (f32[512,1024]{1,0:T(8,128)S(1)}, f32[512,1024]{1,0:T(8,128)}, u32[]{:S(2)}) copy-start(f32[512,1024]{1,0:T(8,128)} %get-tuple-element.60) | copy-start | bytes 6291460
  91.4 5.7 %copy-start.10 = (bf16[2,4096,1024]{2,1,0:T(8,128)(2,1)}, bf16[2,4096,1024]{2,1,0:T(8,128)(2,1)S(1)}, u32[]{:S(2)}) copy-start(bf16[2,4096,1024]{2,1,0:T(8,128)(2,1)S(1)} %get-tuple-element.76.state_ref.last_ref) | copy-start | bytes 50331652
  97.1 1.9 copy-start.14
  100.2 27.3 %copy-start.3 = (bf16[2,256,1024]{2,1,0:T(8,128)(2,1)}, bf16[2,256,1024]{2,1,0:T(8,128)(2,1)S(1)}, u32[]{:S(2)}) copy-start(bf16[2,256,1024]{2,1,0:T(8,128)(2,1)S(1)} %get-tuple-element.109) | copy-start | bytes 3145732
  100.3 27.2 %copy-start.29 = (bf16[2,2,256,1024]{3,2,1,0:T(8,128)(2,1)S(1)}, bf16[2,2,256,1024]{3,2,1,0:T(8,128)(2,1)}, u32[]{:S(2)}) copy-start(bf16[2,2,256,1024]{3,2,1,0:T(8,128)(2,1)} %get-tuple-element.64) | copy-start | bytes 6291460
  127.6 3.4 copy-start.7
  130.0 2.4 copy-start.2
  162.1 48.7 %collective-permute-start.3 = (bf16[256,1024]{1,0:T(8,128)(2,1)S(1)}, bf16[256,1024]{1,0:T(8,128)(2,1)S(1)}, u32[]{:S(2)}, u32[]{:S(2)}) collective-permute-start(bf16[256,1024]{1,0:T(8,128)(2,1)S(1)} %get-tuple-element.117), channel_id=1, source_target_pairs={{0,24},{4,28},{8,0},{12,4},{16,8},{20,12},{24,16},{28,20},{1,25},{... | collective-permute-start | bytes 1572872 | tf_op jit(solution)/shard_map/ppermute | solution.py:1166
  165.8 45.9 %collective-permute-start.2 = (bf16[256,1024]{1,0:T(8,128)(2,1)S(1)}, bf16[256,1024]{1,0:T(8,128)(2,1)S(1)}, u32[]{:S(2)}, u32[]{:S(2)}) collective-permute-start(bf16[256,1024]{1,0:T(8,128)(2,1)S(1)} %get-tuple-element.118), channel_id=1, source_target_pairs={{0,16},{4,20},{8,24},{12,28},{16,0},{20,4},{24,8},{28,12},{1,17},{... | collective-permute-start | bytes 1572872 | tf_op jit(solution)/shard_map/ppermute | solution.py:1166
  165.8 45.9 %collective-permute-start.1 = (bf16[256,1024]{1,0:T(8,128)(2,1)S(1)}, bf16[256,1024]{1,0:T(8,128)(2,1)S(1)}, u32[]{:S(2)}, u32[]{:S(2)}) collective-permute-start(bf16[256,1024]{1,0:T(8,128)(2,1)S(1)} %get-tuple-element.119), channel_id=1, source_target_pairs={{0,8},{4,12},{8,16},{12,20},{16,24},{20,28},{24,0},{28,4},{1,9},{5... | collective-permute-start | bytes 1572872 | tf_op jit(solution)/shard_map/ppermute | solution.py:1166
  169.2 5.4 %copy-start.9 = (bf16[128,1024]{1,0:T(8,128)(2,1)S(1)}, bf16[128,1024]{1,0:T(8,128)(2,1)}, u32[]{:S(2)}) copy-start(bf16[128,1024]{1,0:T(8,128)(2,1)} %dt_proj_ref.3) | copy-start | bytes 786436
  170.6 62.4 %collective-permute-start.6 = (bf16[512,512]{1,0:T(8,128)(2,1)}, bf16[512,512]{1,0:T(8,128)(2,1)}, u32[]{:S(2)}, u32[]{:S(2)}) collective-permute-start(bf16[512,512]{1,0:T(8,128)(2,1)} %get-tuple-element.110), channel_id=1, source_target_pairs={{0,24},{4,28},{8,0},{12,4},{16,8},{20,12},{24,16},{28,20},{1,25},{... | collective-permute-start | bytes 1572872 | tf_op jit(solution)/shard_map/ppermute | solution.py:1166
  173.4 82.7 %collective-permute-start.5 = (bf16[512,512]{1,0:T(8,128)(2,1)}, bf16[512,512]{1,0:T(8,128)(2,1)}, u32[]{:S(2)}, u32[]{:S(2)}) collective-permute-start(bf16[512,512]{1,0:T(8,128)(2,1)} %get-tuple-element.111), channel_id=1, source_target_pairs={{0,16},{4,20},{8,24},{12,28},{16,0},{20,4},{24,8},{28,12},{1,17},{... | collective-permute-start | bytes 1572872 | tf_op jit(solution)/shard_map/ppermute | solution.py:1166
  210.8 0.9 copy-start.20
  210.8 45.3 %collective-permute-start.4 = (bf16[512,512]{1,0:T(8,128)(2,1)}, bf16[512,512]{1,0:T(8,128)(2,1)}, u32[]{:S(2)}, u32[]{:S(2)}) collective-permute-start(bf16[512,512]{1,0:T(8,128)(2,1)} %get-tuple-element.112), channel_id=1, source_target_pairs={{0,8},{4,12},{8,16},{12,20},{16,24},{20,28},{24,0},{28,4},{1,9},{5... | collective-permute-start | bytes 1572872 | tf_op jit(solution)/shard_map/ppermute | solution.py:1166
  211.7 0.8 copy-start.22
  211.7 1.0 copy-start.24
  221.6 1.6 copy-start.12
  221.6 2.2 copy-start.15
  227.7 1.9 copy-start.13
  230.9 25.3 %copy-start.18 = (bf16[256,1024]{1,0:T(8,128)(2,1)S(1)}, bf16[256,1024]{1,0:T(8,128)(2,1)}, u32[]{:S(2)}) copy-start(bf16[256,1024]{1,0:T(8,128)(2,1)} %get-tuple-element.84) | copy-start | bytes 1572868
  230.9 25.3 %copy-start.21 = (bf16[256,1024]{1,0:T(8,128)(2,1)S(1)}, bf16[256,1024]{1,0:T(8,128)(2,1)}, u32[]{:S(2)}) copy-start(bf16[256,1024]{1,0:T(8,128)(2,1)} %copy-done.20) | copy-start | bytes 1572868
  230.9 25.3 %copy-start.23 = (bf16[256,1024]{1,0:T(8,128)(2,1)S(1)}, bf16[256,1024]{1,0:T(8,128)(2,1)}, u32[]{:S(2)}) copy-start(bf16[256,1024]{1,0:T(8,128)(2,1)} %copy-done.22) | copy-start | bytes 1572868
  230.9 25.3 %copy-start.25 = (bf16[256,1024]{1,0:T(8,128)(2,1)S(1)}, bf16[256,1024]{1,0:T(8,128)(2,1)}, u32[]{:S(2)}) copy-start(bf16[256,1024]{1,0:T(8,128)(2,1)} %copy-done.24) | copy-start | bytes 1572868
  342.0 4.4 %copy-start.19 = (bf16[512,512]{1,0:T(8,128)(2,1)S(1)}, bf16[512,512]{1,0:T(8,128)(2,1)}, u32[]{:S(2)}) copy-start(bf16[512,512]{1,0:T(8,128)(2,1)} %get-tuple-element.93) | copy-start | bytes 1572868
  346.4 3.5 %copy-start.26 = (bf16[2,64,2048]{2,1,0:T(8,128)(2,1)S(1)}, bf16[2,64,2048]{2,1,0:T(8,128)(2,1)}, u32[]{:S(2)}) copy-start(bf16[2,64,2048]{2,1,0:T(8,128)(2,1)} %get-tuple-element.147) | copy-start | bytes 1572868
  346.4 4.3 %copy-start.17 = (f32[256,2048]{1,0:T(8,128)S(1)}, f32[256,2048]{1,0:T(8,128)}, u32[]{:S(2)}) copy-start(f32[256,2048]{1,0:T(8,128)} %get-tuple-element.149) | copy-start | bytes 6291460
  349.9 2.1 copy-start.1

commit v5 on v4

--- a/solution.py
+++ b/solution.py
@@ -277,7 +277,7 @@
         out_specs=[wide, wide, wide, wide, spec(BLOCK * n, width)],
         out_shape=[
             full, jax.ShapeDtypeStruct((seqs, length, width), bf16), full, full,
-            jax.ShapeDtypeStruct((seqs, length * n, width), bf16),
+            pltpu.HBM((seqs, length * n, width), bf16),
         ],
         scratch_shapes=[
             pltpu.VMEM((n, width), f32),
@@ -377,8 +377,8 @@
 
 def front_kernel(
     x_ref, cot_ref, gain_ref, w_hbm, o_hbm,
-    xs_ref, cots_ref, gains_ref, normed_ref, pair_ref, parts_ref, own_ref, send_ref,
-    w_ref, o_ref, lhs, mixed, pairs, near, sends, recvs, local, part_sends, part_recvs, part_local,
+    xs_ref, cots_ref, gains_ref, half_ref, parts_ref, own_ref, send_ref,
+    w_ref, o_ref, normed_ref, lhs, mixed, pairs, near, sends, recvs, local, part_sends, part_recvs, part_local,
     pair_sends, pair_recvs, pair_local,
 ):
     me = lax.axis_index("shard")
@@ -386,10 +386,7 @@
     slot = me // 2
     seqs, rows, model = x_ref.shape
     cols = cots_ref.shape[2]
-    side = lax.rem(lax.axis_index("replica"), 2)
-    height = lax.axis_size("replica") // 2
-    block = model // 2 // height
-    aligned = block % LANES == 0
+    core = lax.rem(me, 2)
     width = parts_ref.shape[3]
     lift = gain_ref.shape[0]
     span = 2 * rows
@@ -400,7 +397,7 @@
     ]
     for copy in loads:
         copy.start()
-    other = meet_group_and_pair()
+    meet([quad(1), quad(2)])
 
     def mine(ref, owner):
         return ref.at[:, pl.ds(pl.multiple_of(owner * rows, 16), rows), :]
@@ -484,15 +481,11 @@
 
     def normed_copies(half):
         where = pl.ds(pl.multiple_of(jnp.bitwise_xor(chip, half) * span, 16), span)
-        copies = []
-        for b in range(height if aligned else 0):
-            def cut(which, b=b):
-                return normed_ref.at[:, where, pl.ds(pl.multiple_of((2 * b + which) * block, LANES), block)]
-
-            goal = (slice(None), where, slice(b * block, (b + 1) * block))
-            at = half * height + b
-            copies.append(pltpu.make_async_copy(cut(side), pair_ref.at[(0,) + goal], pair_local.at[at]))
-            copies.append(across(cut(1 - side), pair_ref.at[(1,) + goal], pair_sends, pair_recvs, at, other))
+        src = normed_ref.at[:, where, pl.ds(pl.multiple_of(core * (model // 2), LANES), model // 2)]
+        copies = [pltpu.make_async_copy(src, half_ref.at[0, :, where, :], pair_local.at[half])]
+        for hop in (1, 2):
+            at = 2 * half + hop - 1
+            copies.append(across(src, half_ref.at[hop, :, where, :], pair_sends, pair_recvs, at, quad(hop)))
         return copies
 
     run_half(0)
@@ -564,17 +557,16 @@
     width = w_in.shape[1] // 2
     tokens = seqs * length
     lifted = jnp.broadcast_to(gain.astype(f32)[None], (8, gain.shape[0]))
-    far_sems = pltpu.SemaphoreType.DMA((lax.axis_size("replica"),))
+    far_sems = pltpu.SemaphoreType.DMA((4,))
     return pl.pallas_call(
         front_kernel,
         in_specs=[VMEM_SPEC] * 3 + [ANY_SPEC] * 2,
-        out_specs=[VMEM_SPEC] * 8,
+        out_specs=[VMEM_SPEC] * 7,
         out_shape=[
             jax.ShapeDtypeStruct((seqs, length, model), bf16),
             jax.ShapeDtypeStruct((seqs, length, cols), bf16),
             jax.ShapeDtypeStruct((8 * group, gain.shape[0]), f32),
-            jax.ShapeDtypeStruct((seqs, length, model), bf16),
-            jax.ShapeDtypeStruct((2, seqs, length, model // 2), bf16),
+            jax.ShapeDtypeStruct((3, seqs, length, model // 2), bf16),
             jax.ShapeDtypeStruct((2, seqs, length, width), bf16),
             jax.ShapeDtypeStruct((tokens, width), f32),
             jax.ShapeDtypeStruct((tokens, width), bf16),
@@ -582,6 +574,7 @@
         scratch_shapes=[
             pltpu.VMEM(w_in.shape, bf16),
             pltpu.VMEM(out_proj.shape, bf16),
+            pltpu.VMEM((seqs, length, model), bf16),
             pltpu.VMEM((tokens // 2, model), bf16),
             pltpu.VMEM((2, 2, seqs, 2 * rows, width), bf16),
             pltpu.VMEM((2, tokens, width), bf16),
@@ -595,11 +588,13 @@
     )(x, cot, lifted, w_in, out_proj)
 
 
-def pair_signal(barrier):
+def quad(hop):
     home = lax.axis_index("replica")
-    other = home + 1 - 2 * lax.rem(home, 2)
-    pl.semaphore_signal(barrier, inc=1, device_id={"replica": other}, device_id_type=MESH)
-    return other
+    if hop & 1:
+        home = home + 1 - 2 * lax.rem(home, 2)
+    if hop & 2:
+        home = home + 2 - 4 * lax.rem(home // 2, 2)
+    return home
 
 
 def across(src, dst, sends, recvs, at, other):
@@ -609,19 +604,34 @@
     )
 
 
-def meet_group_and_pair():
+def meet(replicas):
     barrier = pltpu.get_barrier_semaphore()
     for hop in (1, 2, 3):
         pl.semaphore_signal(barrier, inc=1, device_id={"shard": peer(hop)}, device_id_type=MESH)
-    other = pair_signal(barrier)
-    pl.semaphore_wait(barrier, 4)
-    return other
-
-
-def collect_kernel(keep_ref, give_ref, gz_ref, keeps_ref, gives_ref, gz_both_ref, sends, recvs, local):
+    for other in replicas:
+        pl.semaphore_signal(barrier, inc=1, device_id={"replica": other}, device_id_type=MESH)
+    pl.semaphore_wait(barrier, 3 + len(replicas))
+
+
+def ahead(step):
+    count = lax.axis_size("replica")
+    return lax.rem(lax.axis_index("replica") + step, count)
+
+
+def collect_kernel(
+    keep_ref, give_ref, gz_ref, half_ref, last_ref, cot_ref,
+    keeps_ref, gives_ref, gz_ref4, norm_ref, cots_ref,
+    sends, recvs, local,
+):
     me = lax.axis_index("shard")
     half = keep_ref.shape[1]
-    other = meet_group_and_pair()
+    core = lax.rem(me, 2)
+    member = lax.rem(lax.axis_index("replica"), 4)
+    part = gz_ref4.shape[2]
+    meet([quad(hop) for hop in (1, 2, 3)])
+
+    def quarter(which):
+        return gz_ref.at[:, pl.ds(pl.multiple_of(which * part, LANES), part)]
 
     def spot(ref, owner):
         return ref.at[:, pl.ds(pl.multiple_of(owner * half, 128), half)]
@@ -630,13 +640,23 @@
     v_chip = remote(give_ref, spot(gives_ref, me), sends, recvs, 1, 2)
     k_core = remote(keep_ref, spot(keeps_ref, me), sends, recvs, 2, 1)
     v_core = remote(give_ref, spot(gives_ref, me), sends, recvs, 3, 1)
-    gz_pair = across(gz_ref, gz_both_ref.at[1], sends, recvs, 4, other)
+    quads = [
+        across(quarter(lax.rem(quad(hop), 4)), gz_ref4.at[hop], sends, recvs, 6 + hop, quad(hop)) for hop in (3, 1, 2)
+    ]
+    cot_pair = across(cot_ref, cots_ref.at[1], sends, recvs, 11, quad(1))
+    norms = [
+        remote(half_ref, norm_ref.at[core, 0:3], sends, recvs, 10, 1),
+        remote(last_ref, norm_ref.at[core, 3], sends, recvs, 4, 1),
+    ]
     own = [
         pltpu.make_async_copy(keep_ref, spot(keeps_ref, me), local.at[0]),
         pltpu.make_async_copy(give_ref, spot(gives_ref, me), local.at[1]),
-        pltpu.make_async_copy(gz_ref, gz_both_ref.at[0], local.at[2]),
+        pltpu.make_async_copy(quarter(member), gz_ref4.at[0], local.at[2]),
+        pltpu.make_async_copy(half_ref, norm_ref.at[core, 0:3], local.at[3]),
+        pltpu.make_async_copy(last_ref, norm_ref.at[core, 3], local.at[4]),
+        pltpu.make_async_copy(cot_ref, cots_ref.at[0], local.at[5]),
     ]
-    for copy in [k_chip, v_chip, gz_pair, k_core, v_core] + own:
+    for copy in [k_chip, v_chip] + quads + [cot_pair, k_core, v_core] + norms + own:
         copy.start()
     k_chip.wait_recv()
     k_on = remote(spot(keeps_ref, peer(2)), spot(keeps_ref, peer(2)), sends, recvs, 5, 1)
@@ -644,7 +664,7 @@
     v_chip.wait_recv()
     v_on = remote(spot(gives_ref, peer(2)), spot(gives_ref, peer(2)), sends, recvs, 6, 1)
     v_on.start()
-    for copy in own + [k_core, v_core, gz_pair, k_on, v_on]:
+    for copy in own + quads + norms + [cot_pair, k_core, v_core, k_on, v_on]:
         copy.wait()
     k_chip.wait_send()
     v_chip.wait_send()
@@ -654,28 +674,32 @@
     return pl.CostEstimate(flops=int(microseconds * 1e9), bytes_accessed=1 << 20, transcendentals=0)
 
 
-def collect(keep, give, grad_z):
+def collect(keep, give, grad_z, half_norm, last_norm, cot):
     tokens, half = keep.shape
     group = lax.axis_size("shard")
     wide = jax.ShapeDtypeStruct((tokens, half * group), bf16)
     return pl.pallas_call(
         collect_kernel,
-        in_specs=[VMEM_SPEC] * 3,
-        out_specs=[VMEM_SPEC] * 3,
-        out_shape=[wide, wide, jax.ShapeDtypeStruct((2,) + grad_z.shape, bf16)],
+        in_specs=[VMEM_SPEC] * 6,
+        out_specs=[VMEM_SPEC] * 5,
+        out_shape=[
+            wide, wide, jax.ShapeDtypeStruct((4, tokens, grad_z.shape[1] // 4), bf16),
+            jax.ShapeDtypeStruct((2, 4) + last_norm.shape, bf16),
+            jax.ShapeDtypeStruct((2,) + cot.shape, bf16),
+        ],
         scratch_shapes=[
-            pltpu.SemaphoreType.DMA((7,)), pltpu.SemaphoreType.DMA((7,)), pltpu.SemaphoreType.DMA((3,)),
+            pltpu.SemaphoreType.DMA((12,)), pltpu.SemaphoreType.DMA((12,)), pltpu.SemaphoreType.DMA((6,)),
         ],
-        compiler_params=group_params(6, 16 << 20),
+        compiler_params=group_params(6, 28 << 20),
         cost_estimate=cost(25),
         name="collect",
-    )(keep, give, grad_z)
+    )(keep, give, grad_z, half_norm, last_norm, cot)
 
 
 def middle_kernel(
-    keeps_ref, gives_ref, give_ref, cot_ref, x_hbm, o_hbm,
-    both_ref, cots_ref, out_ref,
-    o_ref, xcol, outs, sends, recvs, local, o_local,
+    keeps_ref, gives_ref, give_ref, z_ref, x_hbm, o_hbm,
+    both_ref, out_ref, z_got_ref,
+    o_ref, xcol, outs, sends, recvs, far_sends, far_recvs, local, o_local,
 ):
     me = lax.axis_index("shard")
     side = lax.rem(lax.axis_index("replica"), 2)
@@ -703,18 +727,24 @@
         x_hbm.at[:, pl.ds(pl.multiple_of(me * cols, 128), cols)], xcol, local.at[0]
     )
     fetch.start()
-    other = meet_group_and_pair()
+    home = lax.axis_index("replica")
+    count = lax.axis_size("replica")
+    other = quad(1)
+    meet([ahead(step) for step in range(1, count)])
 
     def spot(owner):
         return gots_ref.at[:, pl.ds(pl.multiple_of(owner * half, 128), half)]
 
     give_pair = across(give_ref, spot(me), sends, recvs, 0, other)
-    cot_pair = across(cot_ref, cots_ref.at[1], sends, recvs, 1, other)
     own = [
         pltpu.make_async_copy(keeps_ref, both_ref.at[0], local.at[1]),
-        pltpu.make_async_copy(cot_ref, cots_ref.at[0], local.at[2]),
     ]
-    for copy in [give_pair, cot_pair] + own:
+    own.append(pltpu.make_async_copy(z_ref.at[home], z_got_ref.at[home], local.at[3 + seqs]))
+    z_sends = [
+        across(z_ref.at[ahead(step)], z_got_ref.at[home], far_sends, far_recvs, step, ahead(step))
+        for step in range(1, count)
+    ]
+    for copy in [give_pair] + z_sends + own:
         copy.start()
     for copy in loads + [fetch]:
         copy.wait()
@@ -757,17 +787,18 @@
     g_chip.wait_recv()
     g_on = remote(spot(peer(2)), spot(peer(2)), sends, recvs, base + 2, 1)
     g_on.start()
-    for copy in out_sends + [g_on, g_core, cot_pair] + own:
+    for copy in out_sends + [g_on, g_core] + own + z_sends:
         copy.wait()
     g_chip.wait_send()
     give_pair.wait_send()
 
 
-def middle(keeps, gives, give, cot, x_all, out_proj, seqs):
+def middle(keeps, gives, give, z_blocks, x_all, out_proj, seqs):
     tokens, half = give.shape
     group = lax.axis_size("shard")
     model = x_all.shape[1]
     cols = model // group
+    far_sems = pltpu.SemaphoreType.DMA((lax.axis_size("replica"),))
     pieces = 8 * max(1, half * lax.axis_size("replica") // out_proj.shape[0])
     return pl.pallas_call(
         middle_kernel,
@@ -775,30 +806,30 @@
         out_specs=[VMEM_SPEC] * 3,
         out_shape=[
             jax.ShapeDtypeStruct((2, tokens, half * group), bf16),
-            jax.ShapeDtypeStruct((2, tokens, cols), bf16),
             jax.ShapeDtypeStruct((seqs, tokens // seqs // group, model), bf16),
+            jax.ShapeDtypeStruct(z_blocks.shape, bf16),
         ],
         scratch_shapes=[
             pltpu.VMEM((2, half * group, cols), bf16),
             pltpu.VMEM((tokens, cols), bf16),
             pltpu.VMEM((tokens, cols), bf16),
             pltpu.SemaphoreType.DMA((5 + 3 * seqs,)), pltpu.SemaphoreType.DMA((5 + 3 * seqs,)),
-            pltpu.SemaphoreType.DMA((3 + seqs,)), pltpu.SemaphoreType.DMA((pieces,)),
+            far_sems, far_sems, pltpu.SemaphoreType.DMA((4 + seqs,)), pltpu.SemaphoreType.DMA((pieces,)),
         ],
-        compiler_params=group_params(7, 20 << 20),
+        compiler_params=group_params(7, 22 << 20),
         cost_estimate=cost(25),
         name="middle",
-    )(keeps, gives, give, cot, x_all, out_proj)
-
-
-PARTS = 4
+    )(keeps, gives, give, z_blocks, x_all, out_proj)
+
+
+PARTS = 2
 
 
 def finish_kernel(
     gx_ref, gz_ref, small_keep_ref, small_give_ref, wz_ref, norm_ref, w_hbm, x_ref, cot_ref, gain_ref,
     gw_ref, small_ref, dx_ref, ggain_ref,
-    w_ref, got, cols_ref, turned, xb_ref, sb_ref, small_got, x_in, s_in, lhs, pairs, near, g_own, g_send, g_far,
-    h_send, h_cols, s_own, gains, gain_near, gain_sum, gain_pair, gain_two, gain_in,
+    w_ref, gx4, cols_ref, turned, xb_ref, sb_ref, small_got, x_in, s_in, lhs, pairs, near, g_hold, g_own, g_send, g_far,
+    h_send, h_cols, z_cols, s_own, gains, gain_near, gain_sum, gain_pair, gain_two, gain_in,
     sends, recvs, far_sends, far_recvs, home_sends, home_recvs, local,
 ):
     me = lax.axis_index("shard")
@@ -811,31 +842,38 @@
     tokens, width = gx_ref.shape
     length = tokens // seqs
     deep = wz_ref.shape[0]
-    part = width // PARTS
+    member = lax.rem(home, 4)
+    quarter = width // 4
+    part = quarter // PARTS
     tile = 256
-    span = seqs * rows
+    other = quad(1)
     load = pltpu.make_async_copy(w_hbm, w_ref, local.at[0])
     load.start()
-    barrier = pltpu.get_barrier_semaphore()
-    for hop in (1, 2, 3):
-        pl.semaphore_signal(barrier, inc=1, device_id={"shard": peer(hop)}, device_id_type=MESH)
-    other = pair_signal(barrier)
+    meet([ahead(step) for step in range(1, count)])
 
     def far(step):
-        return lax.rem(home + 2 * step, count)
-
-    for step in range(1, height):
-        pl.semaphore_signal(barrier, inc=1, device_id={"replica": far(step)}, device_id_type=MESH)
-    pl.semaphore_wait(barrier, 3 + height)
+        return ahead(2 * step)
 
     def cut(p):
         return slice(p * part, (p + 1) * part)
 
-    y_sends = [across(gx_ref.at[:, cut(p)], got.at[:, cut(p)], sends, recvs, p, other) for p in range(PARTS)]
-    small_send = across(small_give_ref, small_got, sends, recvs, PARTS, other)
-    y_sends[0].start()
-    small_send.start()
-    for copy in y_sends[1:]:
+    def piece_of(which, p):
+        return gx_ref.at[:, pl.ds(pl.multiple_of(which * quarter + p * part, LANES), part)]
+
+    def spot_of(hop, p):
+        return gx4.at[hop * tokens : (hop + 1) * tokens, cut(p)]
+
+    def quad_sends(p):
+        return [
+            across(piece_of(lax.rem(quad(hop), 4), p), spot_of(hop, p), sends, recvs, 3 * p + hop - 1, quad(hop))
+            for hop in (3, 1, 2)
+        ]
+
+    small_send = across(small_give_ref, small_got, sends, recvs, 3 * PARTS, other)
+    quad_own = [
+        pltpu.make_async_copy(piece_of(member, p), spot_of(0, p), local.at[PARTS + 2 + 2 * seqs + p]) for p in range(PARTS)
+    ]
+    for copy in quad_sends(0) + [small_send] + quad_sends(1) + quad_own:
         copy.start()
 
     def goal(slot):
@@ -845,13 +883,13 @@
 
     def home_pieces(at):
         if at == PARTS:
-            return 1, wz_ref, h_cols.at[:, spot]
-        if at == PARTS + 1:
-            return 0, gx_ref, cols_ref.at[:, spot]
-        if at == PARTS + 2:
-            return 1, gz_ref, cols_ref.at[:, spot]
-        place = pl.ds(pl.multiple_of(lax.rem(me, 2) * width + at * part, LANES), part)
-        return 0, h_send.at[:, cut(at)], h_cols.at[:, place]
+            return 1, wz_ref, z_cols.at[:, spot]
+        if at > PARTS:
+            slot, seq = (at - PARTS - 1) % 2, (at - PARTS - 1) // 2
+            some = slice(seq * length, (seq + 1) * length)
+            return slot, (gx_ref, gz_ref)[slot].at[some], cols_ref.at[some, spot]
+        some = 4 * part
+        return 0, h_send.at[at], h_cols.at[at, :, pl.ds(pl.multiple_of(lax.rem(me, 2) * some, LANES), some)]
 
     def home_send(at):
         slot, src, dst = home_pieces(at)
@@ -878,17 +916,23 @@
                 src = home_pieces(at)[1]
                 part_copy(src, src, home_sends.at[at], home_recvs.at[at * 2 + place], peer(1)).wait_recv()
 
-    for at in (PARTS + 1, PARTS + 2, PARTS):
+    for at in (*range(PARTS + 1, PARTS + 1 + 2 * seqs), PARTS):
         home_start(at)
 
-    for i in range(2 * tokens // tile):
-        for j in range(norm_ref.shape[1] // tile):
-            turned[j * tile : (j + 1) * tile, i * tile : (i + 1) * tile] = norm_ref[
-                i * tile : (i + 1) * tile, j * tile : (j + 1) * tile
-            ].T
+    features = norm_ref.shape[2]
+
+    def turn(i, carry):
+        at = pl.ds(pl.multiple_of(i * tile, tile), tile)
+        for side_half in range(2):
+            for j in range(features // tile):
+                low = side_half * features + j * tile
+                turned[low : low + tile, at] = norm_ref[side_half, at, j * tile : (j + 1) * tile].T
+        return carry
+
+    lax.fori_loop(0, 4 * tokens // tile, turn, 0)
 
     def far_copy(src, dst, kind, step):
-        return across(src, dst, far_sends, far_recvs, kind * height + step, far(step))
+        return across(src, dst, far_sends, far_recvs, kind * count + step, far(step))
 
     def block(step):
         return lax.rem(mine + step, height)
@@ -900,58 +944,86 @@
 
     def x_sends(p):
         return [
-            far_copy(xb_ref.at[lines(block(step)), cut(p)], x_in.at[step - 1, :, cut(p)], p, step) for step in order
+            across(
+                xb_ref.at[lines(ahead(step)), cut(p)], x_in.at[home, :, cut(p)], far_sends, far_recvs,
+                p * count + step, ahead(step),
+            )
+            for step in range(1, count)
         ]
 
     def x_part(p):
-        y_sends[p].wait_recv()
+        for copy in quad_sends(p):
+            copy.wait_recv()
+        quad_own[p].wait()
 
         def rows_of(t, carry):
             at = pl.ds(pl.multiple_of(t * tile, tile), tile)
-            value = rows_dot(turned[at, :tokens], gx_ref[:, cut(p)]) + rows_dot(turned[at, tokens:], got[:, cut(p)])
-            xb_ref[at, cut(p)] = value.astype(bf16)
+            xb_ref[at, cut(p)] = rows_dot(turned[at, :], gx4[:, cut(p)]).astype(bf16)
             return carry
 
         lax.fori_loop(0, xb_ref.shape[0] // tile, rows_of, 0)
+        x_in[home, :, cut(p)] = xb_ref[lines(home), cut(p)]
         for copy in x_sends(p):
             copy.start()
 
+    def lanes(t):
+        return pl.ds(pl.multiple_of(t * tile, tile), tile)
+
+    def near_send(seq):
+        return remote(pairs.at[seq], near.at[seq], sends, recvs, 3 * PARTS + 8 + 2 * seq, 1)
+
+    def chip_send(seq):
+        return remote(g_send.at[seq], g_far.at[seq], sends, recvs, 3 * PARTS + 9 + 2 * seq, 2)
+
+    def grads_of(seq):
+        home_wait(PARTS + 1 + 2 * seq)
+        home_wait(PARTS + 2 + 2 * seq)
+        for i, owner in enumerate((peer(3), peer(1), peer(2), me)):
+            at = pl.ds(pl.multiple_of(seq * length + owner * rows, 16), rows)
+            lhs[i * rows : (i + 1) * rows, :] = cols_ref[at, :]
+
+        def product(t, carry):
+            value = outer_dot(lhs[...], w_ref[lanes(t), :])
+            pairs[seq, :, lanes(t)] = value[: 2 * rows].astype(bf16)
+            g_hold[:, lanes(t)] = value[2 * rows : 3 * rows]
+            g_own[seq, :, lanes(t)] = value[3 * rows :]
+            return carry
+
+        lax.fori_loop(0, model // tile, product, 0)
+        near_send(seq).start()
+
+    def grads_on(seq):
+        near_send(seq).wait()
+        for low in range(0, model, tile):
+            at = slice(low, low + tile)
+            g_send[seq, :, at] = (g_hold[:, at] + near[seq, :rows, at].astype(f32)).astype(bf16)
+            g_own[seq, :, at] += near[seq, rows:, at].astype(f32)
+        chip_send(seq).start()
+
+    def home_sum(p):
+        for copy in x_sends(p):
+            copy.wait_recv()
+        for q in range(4):
+            total = x_in[q, :, cut(p)].astype(f32)
+            for group in range(1, count // 4):
+                total = total + x_in[4 * group + q, :, cut(p)].astype(f32)
+            h_send[p, :, q * part : (q + 1) * part] = total.astype(bf16)
+        home_start(p)
+
     x_part(0)
+    load.wait()
+    grads_of(0)
     small_send.wait_recv()
     for at in range(height):
         sb_ref[at] = (small_keep_ref[at] + small_got[at].astype(f32)).astype(bf16)
     s_sends = [far_copy(sb_ref.at[block(step)], s_in.at[step - 1], PARTS, step) for step in order]
     for copy in s_sends:
         copy.start()
+    grads_on(0)
     x_part(1)
-
-    def stage(owners):
-        for i, owner in enumerate(owners):
-            for seq in range(seqs):
-                at = pl.ds(pl.multiple_of(seq * length + owner * rows, 16), rows)
-                lhs[i * span + seq * rows : i * span + (seq + 1) * rows, :] = cols_ref[at, :]
-
-    def lanes(t):
-        return pl.ds(pl.multiple_of(t * tile, tile), tile)
-
-    def product(t):
-        return outer_dot(lhs[...], w_ref[lanes(t), :])
-
-    home_wait(PARTS + 1)
-    home_wait(PARTS + 2)
-    stage((peer(3), peer(1)))
-    load.wait()
-
-    def first(t, carry):
-        value = product(t)
-        pairs[0, :, lanes(t)] = value[:span].astype(bf16)
-        pairs[1, :, lanes(t)] = value[span:].astype(bf16)
-        return carry
-
-    lax.fori_loop(0, model // tile, first, 0)
-    near_send = remote(pairs, near, sends, recvs, PARTS + 1, 1)
-    near_send.start()
-    x_part(2)
+    grads_of(1)
+    home_sum(0)
+    grads_on(1)
 
     for copy in s_sends:
         copy.wait_recv()
@@ -963,40 +1035,15 @@
     spread = [far_copy(s_own, small_ref.at[side, mine], PARTS + 1, step) for step in order]
     for copy in spread:
         copy.start()
-    x_part(3)
-
-    stage((peer(2), me))
-    near_send.wait()
-
-    def second(t, carry):
-        value = product(t)
-        g_send[:, lanes(t)] = (value[:span] + near[0, :, lanes(t)].astype(f32)).astype(bf16)
-        g_own[:, lanes(t)] = value[span:] + near[1, :, lanes(t)].astype(f32)
-        return carry
-
-    lax.fori_loop(0, model // tile, second, 0)
-    chip_send = remote(g_send, g_far, sends, recvs, PARTS + 2, 2)
-    chip_send.start()
-
-    def home_sum(p):
-        for copy in x_sends(p):
-            copy.wait_recv()
-        total = xb_ref[lines(mine), cut(p)].astype(f32)
-        for step in order:
-            total = total + x_in[step - 1, :, cut(p)].astype(f32)
-        h_send[:, cut(p)] = total.astype(bf16)
-        home_start(p)
-
-    home_sum(0)
-    chip_send.wait()
 
     gains[...] = jnp.zeros_like(gains)
-    for seq in range(seqs):
-
-        def last(r, carry, seq=seq):
+
+    def finish_rows(seq):
+        chip_send(seq).wait()
+
+        def last(r, carry):
             at = pl.ds(pl.multiple_of(r * 16, 16), 16)
-            flat = pl.ds(pl.multiple_of(seq * rows + r * 16, 16), 16)
-            grad = g_own[flat, :] + g_far[flat, :].astype(f32)
+            grad = g_own[seq, at, :] + g_far[seq, at, :].astype(f32)
             vals = x_ref[seq, at, :].astype(f32)
             inv = lax.rsqrt(jnp.mean(vals * vals, axis=1, keepdims=True) + EPS)
             scaled = grad * gain_ref[...]
@@ -1008,6 +1055,10 @@
             return carry
 
         lax.fori_loop(0, rows // 16, last, 0)
+
+    finish_rows(0)
+    home_sum(1)
+    finish_rows(1)
     gains[...] = jnp.broadcast_to(jnp.sum(gains[...], axis=0, keepdims=True), gains.shape)
     wide = model // 4
 
@@ -1015,27 +1066,24 @@
         return gains.at[:, pl.ds(pl.multiple_of(owner * wide, LANES), wide)]
 
     gain_sends = [
-        remote(gain_part(peer(hop)), gain_near.at[hop - 1], sends, recvs, PARTS + 2 + hop, hop) for hop in (1, 2, 3)
+        remote(gain_part(peer(hop)), gain_near.at[hop - 1], sends, recvs, 3 * PARTS + 2 + hop, hop) for hop in (1, 2, 3)
     ]
     for copy in gain_sends:
         copy.start()
     for copy in gain_sends:
         copy.wait()
     gain_sum[...] = gains[:, pl.ds(pl.multiple_of(me * wide, LANES), wide)] + gain_near[0] + gain_near[1] + gain_near[2]
-    gain_copy = across(gain_sum, gain_pair, sends, recvs, PARTS + 6, other)
+    gain_copy = across(gain_sum, gain_pair, sends, recvs, 3 * PARTS + 6, other)
     gain_copy.start()
-    home_sum(1)
+    for copy in spread:
+        copy.wait_recv()
+    small_pair = across(small_ref.at[side], small_ref.at[side], sends, recvs, 3 * PARTS + 7, other)
+    small_pair.start()
     gain_copy.wait()
     gain_two[...] = gain_sum[...] + gain_pair[...]
     gain_far = [far_copy(gain_two, gain_in.at[step - 1], PARTS + 2, step) for step in order]
     for copy in gain_far:
         copy.start()
-    home_sum(2)
-    for copy in spread:
-        copy.wait_recv()
-    small_pair = across(small_ref.at[side], small_ref.at[side], sends, recvs, PARTS + 7, other)
-    small_pair.start()
-    home_sum(3)
     for copy in gain_far:
         copy.wait()
     total = gain_two[...]
@@ -1043,15 +1091,27 @@
         total = total + gain_in[step - 1]
     ggain_ref[...] = total
 
-    for at in (PARTS, 0, 1, 2, 3):
+    for at in range(PARTS + 1):
         home_wait(at)
-    for r in range(0, deep, 32):
-        gw_ref[r : r + 32, :] = h_cols[r : r + 32, :].astype(f32)
+
+    @pl.when(me // 2 == 0)
+    def _():
+        for place in range(2):
+            for q in range(4):
+                for p in range(PARTS):
+                    to = place * width + q * quarter + p * part
+                    low = (place * 4 + q) * part
+                    gw_ref[:, to : to + part] = h_cols[p, :, low : low + part].astype(f32)
+
+    @pl.when(me // 2 == 1)
+    def _():
+        for low in range(0, 2 * width, quarter):
+            gw_ref[:, low : low + quarter] = z_cols[:, low : low + quarter].astype(f32)
+
     small_pair.wait()
     small_send.wait_send()
     for p in range(PARTS):
-        y_sends[p].wait_send()
-        for copy in x_sends(p):
+        for copy in quad_sends(p) + x_sends(p):
             copy.wait_send()
     for copy in s_sends + spread:
         copy.wait_send()
@@ -1062,11 +1122,13 @@
     height, lines, _ = small_keep.shape
     deep = wz.shape[0]
     seqs, rows, model = x.shape
-    span = seqs * rows
     wide = model // 4
     gain_tile = pltpu.VMEM((8, wide), f32)
     other = max(height - 1, 1)
-    kinds = (PARTS + 3) * height
+    count = 2 * height
+    quarter = width // 4
+    kinds = (PARTS + 3) * count
+    homes = PARTS + 1 + 2 * seqs
     return pl.pallas_call(
         finish_kernel,
         in_specs=[VMEM_SPEC] * 6 + [ANY_SPEC] + [VMEM_SPEC] * 3,
@@ -1079,33 +1141,35 @@
         ],
         scratch_shapes=[
             pltpu.VMEM(w_in.shape, bf16),
-            pltpu.VMEM((tokens, width), bf16),
+            pltpu.VMEM((4 * tokens, quarter), bf16),
             pltpu.VMEM((tokens, 2 * width), bf16),
-            pltpu.VMEM((height * deep, 2 * tokens), bf16),
-            pltpu.VMEM((height * deep, width), bf16),
+            pltpu.VMEM((count * deep, 4 * tokens), bf16),
+            pltpu.VMEM((count * deep, quarter), bf16),
             pltpu.VMEM((height, lines, width), bf16),
             pltpu.VMEM((height, lines, width), bf16),
-            pltpu.VMEM((other, deep, width), bf16),
+            pltpu.VMEM((count, deep, quarter), bf16),
             pltpu.VMEM((other, lines, width), bf16),
-            pltpu.VMEM((2 * span, 2 * width), bf16),
-            pltpu.VMEM((2, span, model), bf16),
-            pltpu.VMEM((2, span, model), bf16),
-            pltpu.VMEM((span, model), f32),
-            pltpu.VMEM((span, model), bf16),
-            pltpu.VMEM((span, model), bf16),
-            pltpu.VMEM((deep, width), bf16),
+            pltpu.VMEM((4 * rows, 2 * width), bf16),
+            pltpu.VMEM((seqs, 2 * rows, model), bf16),
+            pltpu.VMEM((seqs, 2 * rows, model), bf16),
+            pltpu.VMEM((rows, model), f32),
+            pltpu.VMEM((seqs, rows, model), f32),
+            pltpu.VMEM((seqs, rows, model), bf16),
+            pltpu.VMEM((seqs, rows, model), bf16),
+            pltpu.VMEM((PARTS, deep, width // PARTS), bf16),
+            pltpu.VMEM((PARTS, deep, 2 * width // PARTS), bf16),
             pltpu.VMEM((deep, 2 * width), bf16),
             pltpu.VMEM((lines, width), bf16),
             pltpu.VMEM((8, model), f32),
             pltpu.VMEM((3, 8, wide), f32),
             gain_tile, gain_tile, gain_tile,
             pltpu.VMEM((other, 8, wide), f32),
-            pltpu.SemaphoreType.DMA((PARTS + 8,)), pltpu.SemaphoreType.DMA((PARTS + 8,)),
+            pltpu.SemaphoreType.DMA((3 * PARTS + 8 + 2 * seqs,)), pltpu.SemaphoreType.DMA((3 * PARTS + 8 + 2 * seqs,)),
             pltpu.SemaphoreType.DMA((kinds,)), pltpu.SemaphoreType.DMA((kinds,)),
-            pltpu.SemaphoreType.DMA((PARTS + 3,)), pltpu.SemaphoreType.DMA((2 * PARTS + 6,)),
-            pltpu.SemaphoreType.DMA((PARTS + 4,)),
+            pltpu.SemaphoreType.DMA((homes,)), pltpu.SemaphoreType.DMA((2 * homes,)),
+            pltpu.SemaphoreType.DMA((homes + 1 + PARTS,)),
         ],
-        compiler_params=group_params(8, 56 << 20),
+        compiler_params=group_params(8, 58 << 20),
         cost_estimate=cost(80),
         name="finish",
     )(gx, gz, small_keep, small_give, wz, norm, w_in, x, cot, gain)
@@ -1148,10 +1212,6 @@
     return lax.ppermute(value, "shard", [(i, i ^ hop) for i in range(4)])
 
 
-def pair(value):
-    return lax.ppermute(value, "replica", [(i, i ^ 1) for i in range(lax.axis_size("replica"))])
-
-
 def far_send(blocks):
     count = lax.axis_size("replica")
     height = count // 2
@@ -1203,20 +1263,12 @@
         odd = jnp.concatenate(cuts[1::2], axis=1)
         return jnp.where(side == 0, even, odd), jnp.where(side == 0, odd, even)
 
-    def both(keep, got):
-        return jnp.concatenate([keep, got], axis=0)
-
-    xs, cots, gains, normed, normed_pair, parts, gated_own, gated_send = front(
+    xs, cots, gains, half_norm, parts, gated_own, gated_send = front(
         block_input, out_grad, norm_gain, w_in, out_proj
     )
     gain = gains[::8].reshape(1, -1)
     x_all = xs.reshape(tokens, model)
     cot = cots.reshape(tokens, -1)
-    if model // count % LANES == 0:
-        normed_pair = normed_pair.reshape(2 * tokens, -1)
-    else:
-        normed_keep, normed_give = halves(normed.reshape(tokens, model), height)
-        normed_pair = jnp.concatenate([normed_keep, pair(normed_give)], axis=0)
     x_part, z_part = parts[0], parts[1]
 
     seg_padded = jnp.pad(segment_ids, ((0, 0), (KW - 1, 0)), constant_values=-1)
@@ -1232,6 +1284,8 @@
         conv_pre = conv_pre + conv_w[j] * x_padded[:, j : j + length] * taps[d][:, :, None]
     conv_out = jax.nn.silu(conv_pre).astype(bf16)
     conv_flat = conv_out.reshape(tokens, width)
+    half_norm = half_norm.reshape(3, tokens, -1)
+    last_norm = lax.ppermute(half_norm[0], "replica", [(i, i ^ 3) for i in range(count)])
     proj = group_total(outer_dot(x_proj, conv_flat), 3)
     gated_far = by_hop(after(gated_send, proj), 2)
     keep_lanes = jnp.broadcast_to(taps[1][:, :, None], (seqs, length, LANES))
@@ -1239,7 +1293,7 @@
     y_total, gated, rate, beta, states = recurrence_forward(
         conv_out, z_part, proj, keep_lanes, dt_proj, dt_bias.astype(f32)[None], skip[None]
     )
-    y_total, gated, gated_far = lax.optimization_barrier((y_total, gated, gated_far))
+    y_total, gated, gated_far, last_norm = lax.optimization_barrier((y_total, gated, gated_far, last_norm))
     grad_gated = split(gated_own + gated_far.astype(f32))
     z_vals = z_part.astype(f32)
     dy = grad_gated * jax.nn.silu(z_vals)
@@ -1247,11 +1301,17 @@
 
     gated_keep, gated_give = halves(gated.reshape(tokens, width), height // 4)
     cols = model // 4
-    keeps, gives, grad_z_both = collect(gated_keep, gated_give, grad_z)
-    z_blocks = inner_dot(normed_pair, grad_z_both.reshape(2 * tokens, -1)).astype(bf16).reshape(height, -1, width)
-    z_own, z_sent = far_send(z_blocks)
-    keeps, z_own = lax.optimization_barrier((keeps, z_own))
-    gated_both, cot_both, block_output = middle(keeps, gives, gated_give, cot, x_all, out_proj, seqs)
+    keeps, gives, grad_z_quad, norms, cot_both = collect(
+        gated_keep, gated_give, grad_z, half_norm, last_norm, cot
+    )
+    norms = norms.reshape(2, 4 * tokens, -1)
+    z_blocks = lax.dot_general(
+        norms, grad_z_quad.reshape(4 * tokens, -1), (((1,), (0,)), ((), ())), preferred_element_type=f32
+    )
+    z_blocks = z_blocks.astype(bf16).reshape(count, -1, width // 4)
+    gated_both, block_output, z_got = middle(keeps, gives, gated_give, z_blocks, x_all, out_proj, seqs)
+    z_sum = jnp.sum(z_got.reshape((-1, 4) + z_got.shape[1:]).astype(f32), axis=0)
+    grad_w_z = z_sum.transpose(1, 0, 2).reshape(-1, width).astype(bf16)
     out_blocks = inner_dot(gated_both.reshape(2 * tokens, -1), cot_both.reshape(2 * tokens, -1))
     out_own, out_sent = far_send(out_blocks.astype(bf16).reshape(height, -1, cols))
     rate, out_own = lax.optimization_barrier((rate, out_own))
@@ -1259,9 +1319,9 @@
     grad_conv_rec, grad_dt_low, grad_proj, grad_dt_proj, grad_dt_bias, grad_d_skip = recurrence_backward(
         rate, beta, conv_out, dy, proj, keep_lanes, dt_proj, states
     )
-    grad_proj, z_sent = lax.optimization_barrier((grad_proj, z_sent))
-    grad_w_z = far_total(z_own.astype(f32), z_sent).astype(bf16)
-    grad_proj = group_total(grad_proj, 4).astype(bf16)
+    grad_proj, out_sent = lax.optimization_barrier((group_total(grad_proj, 4), out_sent))
+    grad_proj = grad_proj.astype(bf16)
+    grad_out_proj = far_total(out_own.astype(f32), out_sent)
     grad_x_proj = rows_dot(grad_proj, conv_flat)
     grad_conv = dy * skip + grad_conv_rec + split(inner_dot(grad_proj, x_proj))
     grad_pre = grad_conv * silu_slope(conv_pre)
@@ -1287,10 +1347,8 @@
     small = jnp.pad(small, ((0, padded - small.shape[0]), (0, 0))).reshape(height, 2, -1, width)
     small_keep = jnp.where(side == 0, small[:, 0], small[:, 1])
     small_give = jnp.where(side == 0, small[:, 1], small[:, 0]).astype(bf16)
-    grad_x, out_sent = lax.optimization_barrier((grad_x, out_sent))
-    grad_out_proj = far_total(out_own.astype(f32), out_sent)
     grad_w_in, small, input_grad, grad_gain = finish(
-        grad_x, grad_z, small_keep, small_give, grad_w_z, normed_pair, w_in, block_input, out_grad, gain
+        grad_x, grad_z, small_keep, small_give, grad_w_z, norms, w_in, block_input, out_grad, gain
     )
     small = small.transpose(1, 0, 2, 3).reshape(padded, width).astype(f32)
 

time: 353 us -> 336 us (0.952)
  waiting for transfers between devices: 24 us -> 2.05 us
  Pallas kernels: 262 us -> 268 us
  starting transfers between devices: 9.85 us -> 5.75 us
    ppermute x6 -> x3, waiting for transfers between devices: 24 us -> 0.01 us  [far_send(): lax.ppermute(out, 'replica', [(i, (i + 2 * step) % count) for i in range(...]
    pallas_call x1, Pallas kernels: 29.7 us -> 40.7 us  [middle(): pl.pallas_call(middle_kernel, in_specs=[VMEM_SPEC] * 4 + [ANY_SPEC] * 2,...]
    pallas_call x1, Pallas kernels: 83.3 us -> 75.4 us  [finish(): pl.pallas_call(finish_kernel, in_specs=[VMEM_SPEC] * 6 + [ANY_SPEC] + [VM...]
    ppermute x6 -> x3, starting transfers between devices: 8.67 us -> 2.1 us  [far_send(): lax.ppermute(out, 'replica', [(i, (i + 2 * step) % count) for i in range(...]
    unnamed x64 -> x86, local copies, waits for them, and re-layouts: 16.9 us -> 15.2 us
  transfers between devices with their start and end apart: 7 -> 5, of which waited for: 2 -> 1; matrix products, arithmetic and copies ran while one was open for 4% -> 3% of each run, Pallas kernels for 18% -> 24%
where the time goes in v5:
time: 336 us; the launch traced here: 335 us
  Pallas kernels  268 us (80%)
  local copies, waits for them, and re-layouts  29.3 us (9%)
  other arithmetic  21.5 us (6%)
  matrix products  7.19 us (2%)
  starting transfers between devices  5.75 us (2%)
    pallas_call x1, Pallas kernels, finish(): pl.pallas_call(finish_kernel, in_specs=[VMEM_SPEC] * 6 + [ANY_SPEC] + [VM...  75.4 us
    pallas_call x1, Pallas kernels, front(): pl.pallas_call(front_kernel, in_specs=[VMEM_SPEC] * 3 + [ANY_SPEC] * 2, o...  43.1 us
    pallas_call x1, Pallas kernels, middle(): pl.pallas_call(middle_kernel, in_specs=[VMEM_SPEC] * 4 + [ANY_SPEC] * 2,...  40.7 us
    pallas_call x1, Pallas kernels, recurrence_backward(): pl.pallas_call(backward_kernel, grid=(seqs, blocks), in_specs=[wide, wide...  36.1 us
    pallas_call x1, Pallas kernels, collect(): pl.pallas_call(collect_kernel, in_specs=[VMEM_SPEC] * 6, out_specs=[VMEM_...  28.5 us
    pallas_call x2, Pallas kernels, group_total(): pl.pallas_call(total_kernel, in_specs=[VMEM_SPEC], out_specs=VMEM_SPEC, o...  22.6 us
    pallas_call x1, Pallas kernels, recurrence_forward(): pl.pallas_call(forward_kernel, grid=(seqs, blocks), in_specs=[wide, wide,...  21.4 us
    unnamed x86, local copies, waits for them, and re-layouts  15.2 us
  transfers between devices with their start and end apart: 5, of which 1 were waited for; matrix products, arithmetic and copies ran while one was open for 3% of the time, Pallas kernels for 24%

profile of v5, /device:TPU:0, one launch (start us, length us, event | category | flops | bytes accessed | tf_op | source)
XLA Modules:
  0.0 334.7 jit_solution(5452889213212005046)
XLA Ops:
  0.6 0.0 copy-start
  0.7 0.7 broadcast_in_dim.12.gain_ref
  1.4 1.0 copy-done.11
  2.4 1.0 copy-done.12
  3.5 43.1 %front.1 = (bf16[2,256,2048]{2,1,0:T(8,128)(2,1)S(1)}, bf16[2,256,512]{2,1,0:T(8,128)(2,1)S(1)}, f32[32,512]{1,0:T(8,128)S(1)}, bf16[3,2,256,1024]{3,2,1,0:T(8,1...) custom-call(bf16[2,64,2048]{2,1,0:T(8,128)(2,1)S(1)} %copy-done.11, ...), custom_call_target="tpu_custom_call" | custom-call | tf_op jit(solution)/shard_map/front/pallas_call | solution.py:561
  46.6 3.2 slice.108
  49.8 2.1 collective-permute-start.1
  51.9 0.1 compare_convert_fusion.2
  52.0 0.3 slice_bitcast_fusion
  52.4 2.7 fusion.12
  55.0 0.5 convolution_bitcast_fusion.part_ref
  55.5 13.7 %group_total.2.proj_ref = f32[160,512]{1,0:T(8,128)S(1)} custom-call(f32[160,512]{1,0:T(8,128)S(1)} %convolution_bitcast_fusion.part_ref), custom_call_target="tpu_custom_call" | custom-call | tf_op jit(solution)/shard_map/group_total/pallas_call | solution.py:1200
  69.3 1.6 collective-permute-start
  70.9 0.6 copy.42
  71.5 0.1 broadcast_in_dim.13.keep_ref
  71.7 21.4 %recurrence_forward.1 = (f32[2,256,1024]{2,1,0:T(8,128)S(1)}, bf16[2,256,1024]{2,1,0:T(8,128)(2,1)S(1)}, f32[2,256,1024]{2,1,0:T(8,128)S(1)}, f32[2,256,1024]{2,1,0:T(8,128)S(1)}, bf16[2,4096,1024]{2,1,0:T(8,128)(2,1)}) custom-call(bf16[2,256,1024]{2,1,0:T(8,128)(2,1)S(1)} %get-tuple-element.100.conv_ref, ...), custom_call_target="tpu_custom_call" | custom-call | flops 16000000000 | bytes 25165824 | tf_op jit(solution)/shard_map/recurrence_forward/pallas_call | solution.py:270
  93.1 2.0 collective-permute-done
  95.1 1.8 convert_add_fusion
  96.9 0.1 copy-done.31
  97.0 1.1 fusion.11
  98.1 0.1 broadcast_select_fusion
  98.2 0.7 copy-done.13
  98.9 0.8 copy-done.21
  99.7 28.5 %collect.1 = (bf16[512,2048]{1,0:T(8,128)(2,1)S(1)}, bf16[512,2048]{1,0:T(8,128)(2,1)S(1)}, bf16[4,512,256]{2,1,0:T(8,128)(2,1)S(1)}, bf16[2,4,512,1024]{3,2,1,0:T(8,128)(2,1)S(1)}, bf16[2,512,512]{2,1,0:T(8,128)(2,1)S(1)}) custom-call(bf16[512,512]{1,0:T(8,128)(2,1)S(1)} %get-tuple-element.117.keep_ref, bf16[512,512]{1,0:T(8,128)(2,1)S(1)} %get-tuple-element.116.give_ref, ...), custom_call_target="tpu_custom_call" | custom-call | flops 24999999488 | bytes 1048576 | tf_op jit(solution)/shard_map/collect/pallas_call | solution.py:681
  128.3 2.6 bitcast_convert_fusion.1
  130.9 1.6 copy-done.24
  132.5 1.0 copy-done.2
  133.5 0.7 copy-done.19
  134.1 40.7 %middle.1 = (bf16[2,512,2048]{2,1,0:T(8,128)(2,1)S(1)}, bf16[2,64,2048]{2,1,0:T(8,128)(2,1)S(1)}, bf16[8,256,256]{2,1,0:T(8,128)(2,1)S(1)}) custom-call(bf16[512,2048]{1,0:T(8,128)(2,1)S(1)} %get-tuple-element.63.keeps_ref, bf16[512,2048]{1,0:T(8,128)(2,1)S(1)} %get-tuple-element.64.gives_ref, bf16[512,512]{1,0:T(8,128)(2,1)S(1)} %get-tuple-element.116.give_ref, ...), custom_call_target="tpu_custom_call" | custom-call | flops 24999999488 | bytes 1048576 | tf_op jit(solution)/shard_map/middle/pallas_call | solution.py:803
  174.9 2.5 bitcast_convert_fusion
  177.4 1.4 dynamic-slice_bitcast_fusion
  178.8 0.1 collective-permute-start.3
  178.9 2.0 collective-permute-start.2
  180.9 36.1 %recurrence_backward.1 = (f32[2,256,1024]{2,1,0:T(8,128)S(1)}, bf16[2,256,1024]{2,1,0:T(8,128)(2,1)}, f32[160,512]{1,0:T(8,128)S(1)}, f32[128,1024]{1,0:T(8,128)...) custom-call(f32[2,256,1024]{2,1,0:T(8,128)S(1)} %get-tuple-element.72.rate_ref, f32[2,256,1024]{2,1,0:T(8,128)S(1)} %copy-done.26, ...), custom_call_target="tpu_custom_call" | custom-call | flops 30000001024 | bytes 29360128 | tf_op jit(solution)/shard_map/recurrence_backward/pallas_call | solution.py:303
  217.0 1.4 copy-done.3
  218.4 0.8 copy-done.7
  219.1 0.7 copy-done.16
  219.9 2.3 reduce
  222.2 1.9 copy.41
  224.1 1.0 copy-done.17
  225.1 8.9 %group_total.3 = f32[160,512]{1,0:T(8,128)S(1)} custom-call(f32[160,512]{1,0:T(8,128)S(1)} %copy-done.17), custom_call_target="tpu_custom_call" | custom-call | tf_op jit(solution)/shard_map/group_total/pallas_call | solution.py:1200
  234.1 1.2 fusion.15
  235.3 0.5 fusion.17
  235.7 0.1 copy-done.4
  235.9 0.6 copy-done.28
  236.5 4.7 %fusion.19 = (f32[1024]{0:T(1024)S(1)}, f32[1024]{0:T(1024)S(1)}, f32[1024]{0:T(1024)S(1)}, f32[1024]{0:T(1024)S(1)}, f32[1024]{0:T(1024)S(1)}, /*index=5*/f32[2,256,1024]{2,1,0:T(8,128)}) fusion(bf16[2,2,256,1024]{3,2,1,0:T(8,128)(2,1)} %get-tuple-element.51, f32[2,256]{1,0:T(2,128)S(1)} %get-tuple-element.122, f32[2,256,1024]{2,1,0:T(8,128)S(1)} %copy-done.28, ...), kind=kLoop, calls=%fused_computation.61 | loop fusion | flops 12577792 | bytes 13662208 | tf_op jit(solution)/shard_map/reduce_sum | solution.py:1328
  241.2 2.1 concatenate.3
  243.3 0.2 pad.29
  243.5 0.8 fusion.14.small_give_ref
  244.3 1.0 select_bitcast_fusion.small_keep_ref
  245.3 0.5 broadcast_multiply_fusion
  245.8 2.1 fusion.4
  247.9 75.4 %finish.1 = (f32[256,2048]{1,0:T(8,128)}, bf16[2,4,48,1024]{3,2,1,0:T(8,128)(2,1)}, bf16[2,64,2048]{2,1,0:T(8,128)(2,1)}, f32[8,512]{1,0:T(8,128)}) custom-call(bf16[512,1024]{1,0:T(8,128)(2,1)} %bitcast.118, bf16[512,1024]{1,0:T(8,128)(2,1)} %bitcast.101, f32[4,48,1024]{2,1,0:T(8,128)} %select_bitcast_fusion.small_keep_ref, ...), custom_call_target="tpu_custom_call" | custom-call | flops 80000000000 | bytes 1048576 | tf_op jit(solution)/shard_map/finish/pallas_call | solution.py:1132
  323.3 1.3 convert_bitcast_fusion
  324.6 0.2 copy.35
  324.8 0.6 fusion.20
  325.4 0.6 slice.132
  326.0 0.8 slice.135
  326.8 0.9 slice.134
  327.7 1.3 slice.117
  329.0 2.7 convert_add_fusion.1
  331.8 0.8 copy.46
  332.5 0.8 copy.47
  333.3 1.3 copy.48
  (77 shorter events, 0.2 us)
Async XLA Ops:
  0.6 54.4 %copy-start = (bf16[160,1024]{1,0:T(8,128)(2,1)S(1)}, bf16[160,1024]{1,0:T(8,128)(2,1)}, u32[]{:S(2)}) copy-start(bf16[160,1024]{1,0:T(8,128)(2,1)} %param.18) | copy-start | bytes 983044
  1.4 1.0 copy-start.11
  2.4 1.0 copy-start.12
  3.5 48.4 %copy-start.37 = (bf16[1024]{0:T(1024)(128)(2,1)S(1)}, bf16[1024]{0:T(1024)(128)(2,1)}, u32[]{:S(2)}) copy-start(bf16[1024]{0:T(1024)(128)(2,1)} %param.17) | copy-start | bytes 6148
  3.5 48.4 %copy-start.40 = (s32[2,256]{1,0:T(2,128)S(1)}, s32[2,256]{1,0:T(2,128)}, u32[]{:S(2)}) copy-start(s32[2,256]{1,0:T(2,128)} %param.13) | copy-start | bytes 6148
  46.6 5.8 %copy-start.18 = (bf16[2,256,2048]{2,1,0:T(8,128)(2,1)}, bf16[2,256,2048]{2,1,0:T(8,128)(2,1)S(1)}, u32[]{:S(2)}) copy-start(bf16[2,256,2048]{2,1,0:T(8,128)(2,1)S(1)} %get-tuple-element.67) | copy-start | bytes 6291460
  46.6 5.8 %copy-start.20 = (bf16[2,256,512]{2,1,0:T(8,128)(2,1)}, bf16[2,256,512]{2,1,0:T(8,128)(2,1)S(1)}, u32[]{:S(2)}) copy-start(bf16[2,256,512]{2,1,0:T(8,128)(2,1)S(1)} %get-tuple-element.62) | copy-start | bytes 1572868
  46.6 5.4 %copy-start.36 = (bf16[4,1024]{1,0:T(4,128)(2,1)S(1)}, bf16[4,1024]{1,0:T(4,128)(2,1)}, u32[]{:S(2)}) copy-start(bf16[4,1024]{1,0:T(4,128)(2,1)} %param.16) | copy-start | bytes 24580
  46.6 5.4 %copy-start.30 = (bf16[2,2,256,1024]{3,2,1,0:T(8,128)(2,1)S(1)}, bf16[2,2,256,1024]{3,2,1,0:T(8,128)(2,1)}, u32[]{:S(2)}) copy-start(bf16[2,2,256,1024]{3,2,1,0:T(8,128)(2,1)} %get-tuple-element.51) | copy-start | bytes 6291460
  49.8 43.2 %collective-permute-start.1 = (bf16[512,1024]{1,0:T(8,128)(2,1)}, bf16[512,1024]{1,0:T(8,128)(2,1)}, u32[]{:S(2)}, u32[]{:S(2)}) collective-permute-start(bf16[512,1024]{1,0:T(8,128)(2,1)} %bitcast.11), channel_id=1, source_target_pairs={{0,12},{4,8},{8,4},{12,0},{16,28},{20,24},{24,20},{28,16},{1,13},{... | collective-permute-start | bytes 3145736 | tf_op jit(solution)/shard_map/ppermute | solution.py:1288
  52.3 2.7 copy-start.27
  55.0 15.8 %copy-start.38 = (bf16[1024]{0:T(1024)(128)(2,1)S(1)}, bf16[1024]{0:T(1024)(128)(2,1)}, u32[]{:S(2)}) copy-start(bf16[1024]{0:T(1024)(128)(2,1)} %param.21) | copy-start | bytes 6148
  55.0 15.8 %copy-start.39 = (bf16[1024]{0:T(1024)(128)(2,1)S(1)}, bf16[1024]{0:T(1024)(128)(2,1)}, u32[]{:S(2)}) copy-start(bf16[1024]{0:T(1024)(128)(2,1)} %param.20) | copy-start | bytes 6148
  55.0 16.6 %copy-start.22 = (bf16[128,1024]{1,0:T(8,128)(2,1)S(1)}, bf16[128,1024]{1,0:T(8,128)(2,1)}, u32[]{:S(2)}) copy-start(bf16[128,1024]{1,0:T(8,128)(2,1)} %dt_proj_ref.3) | copy-start | bytes 786436
  69.3 23.8 %copy-start.14 = (f32[160,512]{1,0:T(8,128)}, f32[160,512]{1,0:T(8,128)S(1)}, u32[]{:S(2)}) copy-start(f32[160,512]{1,0:T(8,128)S(1)} %group_total.2.proj_ref) | copy-start | bytes 983044
  69.3 25.8 %collective-permute-start = (bf16[512,1024]{1,0:T(8,128)(2,1)}, bf16[512,1024]{1,0:T(8,128)(2,1)}, u32[]{:S(2)}, u32[]{:S(2)}) collective-permute-start(bf16[512,1024]{1,0:T(8,128)(2,1)} %get-tuple-element.55), channel_id=1, source_target_pairs={{0,2},{1,3},{2,0},{3,1},{4,6},{5,7},{6,4},{7,5},{8,10},{9,11},{10,... | collective-permute-start | bytes 3145736 | tf_op jit(solution)/shard_map/ppermute | solution.py:1212
  71.6 23.5 %copy-start.32 = (f32[512,1024]{1,0:T(8,128)S(1)}, f32[512,1024]{1,0:T(8,128)}, u32[]{:S(2)}) copy-start(f32[512,1024]{1,0:T(8,128)} %get-tuple-element.58) | copy-start | bytes 6291460
  93.1 3.9 %copy-start.25 = (f32[2,256,1024]{2,1,0:T(8,128)}, f32[2,256,1024]{2,1,0:T(8,128)S(1)}, u32[]{:S(2)}) copy-start(f32[2,256,1024]{2,1,0:T(8,128)S(1)} %get-tuple-element.73.beta_ref) | copy-start | bytes 6291460
  95.1 1.9 copy-start.31
  97.0 1.9 copy-start.13
  98.1 30.2 %copy-start.6 = (bf16[2,256,1024]{2,1,0:T(8,128)(2,1)}, bf16[2,256,1024]{2,1,0:T(8,128)(2,1)S(1)}, u32[]{:S(2)}) copy-start(bf16[2,256,1024]{2,1,0:T(8,128)(2,1)S(1)} %get-tuple-element.103) | copy-start | bytes 3145732
  98.1 1.6 copy-start.21
  128.3 4.3 %copy-start.24 = (bf16[2,4,512,1024]{3,2,1,0:T(8,128)(2,1)}, bf16[2,4,512,1024]{3,2,1,0:T(8,128)(2,1)S(1)}, u32[]{:S(2)}) copy-start(bf16[2,4,512,1024]{3,2,1,0:T(8,128)(2,1)S(1)} %get-tuple-element.65) | copy-start | bytes 25165828
  128.3 5.2 %copy-start.2 = (bf16[4096,512]{1,0:T(8,128)(2,1)S(1)}, bf16[4096,512]{1,0:T(8,128)(2,1)}, u32[]{:S(2)}) copy-start(bf16[4096,512]{1,0:T(8,128)(2,1)} %o_hbm.3) | copy-start | bytes 12582916
  128.3 5.9 %copy-start.19 = (bf16[2,256,2048]{2,1,0:T(8,128)(2,1)S(1)}, bf16[2,256,2048]{2,1,0:T(8,128)(2,1)}, u32[]{:S(2)}) copy-start(bf16[2,256,2048]{2,1,0:T(8,128)(2,1)} %copy-done.18) | copy-start | bytes 6291460
  174.9 2.5 copy-start.5
  174.9 2.5 copy-start.9
  177.4 3.5 %copy-start.15 = (f32[160,512]{1,0:T(8,128)S(1)}, f32[160,512]{1,0:T(8,128)}, u32[]{:S(2)}) copy-start(f32[160,512]{1,0:T(8,128)} %copy-done.14) | copy-start | bytes 983044
  177.4 3.5 %copy-start.23 = (bf16[128,1024]{1,0:T(8,128)(2,1)S(1)}, bf16[128,1024]{1,0:T(8,128)(2,1)}, u32[]{:S(2)}) copy-start(bf16[128,1024]{1,0:T(8,128)(2,1)} %dt_proj_ref.3) | copy-start | bytes 786436
  177.4 3.5 %copy-start.26 = (f32[2,256,1024]{2,1,0:T(8,128)S(1)}, f32[2,256,1024]{2,1,0:T(8,128)}, u32[]{:S(2)}) copy-start(f32[2,256,1024]{2,1,0:T(8,128)} %copy-done.25) | copy-start | bytes 6291460
  178.8 55.3 %collective-permute-start.4 = (bf16[512,512]{1,0:T(8,128)(2,1)}, bf16[512,512]{1,0:T(8,128)(2,1)}, u32[]{:S(2)}, u32[]{:S(2)}) collective-permute-start(bf16[512,512]{1,0:T(8,128)(2,1)} %get-tuple-element.107), channel_id=1, source_target_pairs={{0,24},{4,28},{8,0},{12,4},{16,8},{20,12},{24,16},{28,20},{1,25},{... | collective-permute-start | bytes 1572872 | tf_op jit(solution)/shard_map/ppermute | solution.py:1226
  178.8 55.3 %collective-permute-start.3 = (bf16[512,512]{1,0:T(8,128)(2,1)}, bf16[512,512]{1,0:T(8,128)(2,1)}, u32[]{:S(2)}, u32[]{:S(2)}) collective-permute-start(bf16[512,512]{1,0:T(8,128)(2,1)} %get-tuple-element.108), channel_id=1, source_target_pairs={{0,16},{4,20},{8,24},{12,28},{16,0},{20,4},{24,8},{28,12},{1,17},{... | collective-permute-start | bytes 1572872 | tf_op jit(solution)/shard_map/ppermute | solution.py:1226
  178.9 55.2 %collective-permute-start.2 = (bf16[512,512]{1,0:T(8,128)(2,1)}, bf16[512,512]{1,0:T(8,128)(2,1)}, u32[]{:S(2)}, u32[]{:S(2)}) collective-permute-start(bf16[512,512]{1,0:T(8,128)(2,1)} %get-tuple-element.109), channel_id=1, source_target_pairs={{0,8},{4,12},{8,16},{12,20},{16,24},{20,28},{24,0},{28,4},{1,9},{5... | collective-permute-start | bytes 1572872 | tf_op jit(solution)/shard_map/ppermute | solution.py:1226
  217.0 1.4 copy-start.3
  218.4 0.8 copy-start.7
  219.1 0.7 copy-start.16
  224.1 1.0 copy-start.17
  234.0 1.8 copy-start.4
  234.0 2.5 copy-start.28
  236.5 4.7 %copy-start.8 = (f32[128,1024]{1,0:T(8,128)S(1)}, f32[128,1024]{1,0:T(8,128)}, u32[]{:S(2)}) copy-start(f32[128,1024]{1,0:T(8,128)} %copy-done.7) | copy-start | bytes 1572868
  243.5 1.8 copy-start.29
  324.6 4.4 %copy-start.34 = (bf16[512,512]{1,0:T(8,128)(2,1)S(1)}, bf16[512,512]{1,0:T(8,128)(2,1)}, u32[]{:S(2)}) copy-start(bf16[512,512]{1,0:T(8,128)(2,1)} %get-tuple-element.87) | copy-start | bytes 1572868
  326.8 4.9 %copy-start.10 = (bf16[2,64,2048]{2,1,0:T(8,128)(2,1)S(1)}, bf16[2,64,2048]{2,1,0:T(8,128)(2,1)}, u32[]{:S(2)}) copy-start(bf16[2,64,2048]{2,1,0:T(8,128)(2,1)} %copy-done.9) | copy-start | bytes 1572868
  329.0 3.5 %copy-start.35 = (bf16[2,64,2048]{2,1,0:T(8,128)(2,1)S(1)}, bf16[2,64,2048]{2,1,0:T(8,128)(2,1)}, u32[]{:S(2)}) copy-start(bf16[2,64,2048]{2,1,0:T(8,128)(2,1)} %get-tuple-element.137) | copy-start | bytes 1572868
  329.0 4.3 %copy-start.33 = (f32[256,2048]{1,0:T(8,128)S(1)}, f32[256,2048]{1,0:T(8,128)}, u32[]{:S(2)}) copy-start(f32[256,2048]{1,0:T(8,128)} %get-tuple-element.139) | copy-start | bytes 6291460
  332.5 2.1 copy-start.1

commit v6 on v5

--- a/solution.py
+++ b/solution.py
@@ -377,7 +377,7 @@
 
 def front_kernel(
     x_ref, cot_ref, gain_ref, w_hbm, o_hbm,
-    xs_ref, cots_ref, gains_ref, half_ref, parts_ref, own_ref, send_ref,
+    xs_ref, cots_ref, gains_ref, own_half_ref, half_ref, parts_ref, own_ref, send_ref,
     w_ref, o_ref, normed_ref, lhs, mixed, pairs, near, sends, recvs, local, part_sends, part_recvs, part_local,
     pair_sends, pair_recvs, pair_local,
 ):
@@ -482,10 +482,10 @@
     def normed_copies(half):
         where = pl.ds(pl.multiple_of(jnp.bitwise_xor(chip, half) * span, 16), span)
         src = normed_ref.at[:, where, pl.ds(pl.multiple_of(core * (model // 2), LANES), model // 2)]
-        copies = [pltpu.make_async_copy(src, half_ref.at[0, :, where, :], pair_local.at[half])]
+        copies = [pltpu.make_async_copy(src, own_half_ref.at[:, where, :], pair_local.at[half])]
         for hop in (1, 2):
             at = 2 * half + hop - 1
-            copies.append(across(src, half_ref.at[hop, :, where, :], pair_sends, pair_recvs, at, quad(hop)))
+            copies.append(across(src, half_ref.at[hop - 1, :, where, :], pair_sends, pair_recvs, at, quad(hop)))
         return copies
 
     run_half(0)
@@ -561,12 +561,13 @@
     return pl.pallas_call(
         front_kernel,
         in_specs=[VMEM_SPEC] * 3 + [ANY_SPEC] * 2,
-        out_specs=[VMEM_SPEC] * 7,
+        out_specs=[VMEM_SPEC] * 8,
         out_shape=[
             jax.ShapeDtypeStruct((seqs, length, model), bf16),
             jax.ShapeDtypeStruct((seqs, length, cols), bf16),
             jax.ShapeDtypeStruct((8 * group, gain.shape[0]), f32),
-            jax.ShapeDtypeStruct((3, seqs, length, model // 2), bf16),
+            jax.ShapeDtypeStruct((seqs, length, model // 2), bf16),
+            jax.ShapeDtypeStruct((2, seqs, length, model // 2), bf16),
             jax.ShapeDtypeStruct((2, seqs, length, width), bf16),
             jax.ShapeDtypeStruct((tokens, width), f32),
             jax.ShapeDtypeStruct((tokens, width), bf16),
@@ -619,8 +620,8 @@
 
 
 def collect_kernel(
-    keep_ref, give_ref, gz_ref, half_ref, last_ref, cot_ref,
-    keeps_ref, gives_ref, gz_ref4, norm_ref, cots_ref,
+    keep_ref, give_ref, gz_ref, own_half_ref, half_ref, last_ref,
+    keeps_ref, gives_ref, gz_ref4, norm_ref, got_ref,
     sends, recvs, local,
 ):
     me = lax.axis_index("shard")
@@ -643,20 +644,21 @@
     quads = [
         across(quarter(lax.rem(quad(hop), 4)), gz_ref4.at[hop], sends, recvs, 6 + hop, quad(hop)) for hop in (3, 1, 2)
     ]
-    cot_pair = across(cot_ref, cots_ref.at[1], sends, recvs, 11, quad(1))
+    give_pair = across(give_ref, got_ref, sends, recvs, 11, quad(1))
     norms = [
-        remote(half_ref, norm_ref.at[core, 0:3], sends, recvs, 10, 1),
+        remote(own_half_ref, norm_ref.at[core, 0], sends, recvs, 12, 1),
+        remote(half_ref, norm_ref.at[core, 1:3], sends, recvs, 10, 1),
         remote(last_ref, norm_ref.at[core, 3], sends, recvs, 4, 1),
     ]
     own = [
         pltpu.make_async_copy(keep_ref, spot(keeps_ref, me), local.at[0]),
         pltpu.make_async_copy(give_ref, spot(gives_ref, me), local.at[1]),
         pltpu.make_async_copy(quarter(member), gz_ref4.at[0], local.at[2]),
-        pltpu.make_async_copy(half_ref, norm_ref.at[core, 0:3], local.at[3]),
+        pltpu.make_async_copy(own_half_ref, norm_ref.at[core, 0], local.at[5]),
+        pltpu.make_async_copy(half_ref, norm_ref.at[core, 1:3], local.at[3]),
         pltpu.make_async_copy(last_ref, norm_ref.at[core, 3], local.at[4]),
-        pltpu.make_async_copy(cot_ref, cots_ref.at[0], local.at[5]),
     ]
-    for copy in [k_chip, v_chip] + quads + [cot_pair, k_core, v_core] + norms + own:
+    for copy in [k_chip, v_chip] + quads + [give_pair, k_core, v_core] + norms + own:
         copy.start()
     k_chip.wait_recv()
     k_on = remote(spot(keeps_ref, peer(2)), spot(keeps_ref, peer(2)), sends, recvs, 5, 1)
@@ -664,7 +666,7 @@
     v_chip.wait_recv()
     v_on = remote(spot(gives_ref, peer(2)), spot(gives_ref, peer(2)), sends, recvs, 6, 1)
     v_on.start()
-    for copy in own + quads + norms + [cot_pair, k_core, v_core, k_on, v_on]:
+    for copy in own + quads + norms + [give_pair, k_core, v_core, k_on, v_on]:
         copy.wait()
     k_chip.wait_send()
     v_chip.wait_send()
@@ -674,7 +676,7 @@
     return pl.CostEstimate(flops=int(microseconds * 1e9), bytes_accessed=1 << 20, transcendentals=0)
 
 
-def collect(keep, give, grad_z, half_norm, last_norm, cot):
+def collect(keep, give, grad_z, own_half, half_norm, last_norm):
     tokens, half = keep.shape
     group = lax.axis_size("shard")
     wide = jax.ShapeDtypeStruct((tokens, half * group), bf16)
@@ -685,25 +687,25 @@
         out_shape=[
             wide, wide, jax.ShapeDtypeStruct((4, tokens, grad_z.shape[1] // 4), bf16),
             jax.ShapeDtypeStruct((2, 4) + last_norm.shape, bf16),
-            jax.ShapeDtypeStruct((2,) + cot.shape, bf16),
+            jax.ShapeDtypeStruct(give.shape, bf16),
         ],
         scratch_shapes=[
-            pltpu.SemaphoreType.DMA((12,)), pltpu.SemaphoreType.DMA((12,)), pltpu.SemaphoreType.DMA((6,)),
+            pltpu.SemaphoreType.DMA((13,)), pltpu.SemaphoreType.DMA((13,)), pltpu.SemaphoreType.DMA((6,)),
         ],
         compiler_params=group_params(6, 28 << 20),
         cost_estimate=cost(25),
         name="collect",
-    )(keep, give, grad_z, half_norm, last_norm, cot)
+    )(keep, give, grad_z, own_half, half_norm, last_norm)
 
 
 def middle_kernel(
-    keeps_ref, gives_ref, give_ref, z_ref, x_hbm, o_hbm,
-    both_ref, out_ref, z_got_ref,
-    o_ref, xcol, outs, sends, recvs, far_sends, far_recvs, local, o_local,
+    keeps_ref, gives_ref, got_ref, z_ref, x_hbm, o_hbm,
+    both_ref, out_ref, wz_ref,
+    z_got_ref, o_ref, xcol, outs, sends, recvs, far_sends, far_recvs, local, o_local,
 ):
     me = lax.axis_index("shard")
     side = lax.rem(lax.axis_index("replica"), 2)
-    tokens, half = give_ref.shape
+    tokens, half = got_ref.shape
     gots_ref = both_ref.at[1]
     seqs, rows, _ = out_ref.shape
     cols = xcol.shape[1]
@@ -729,13 +731,14 @@
     fetch.start()
     home = lax.axis_index("replica")
     count = lax.axis_size("replica")
-    other = quad(1)
     meet([ahead(step) for step in range(1, count)])
 
     def spot(owner):
         return gots_ref.at[:, pl.ds(pl.multiple_of(owner * half, 128), half)]
 
-    give_pair = across(give_ref, spot(me), sends, recvs, 0, other)
+    g_own = pltpu.make_async_copy(got_ref, spot(me), local.at[2])
+    g_chip = remote(got_ref, spot(me), sends, recvs, 0, 2)
+    g_core = remote(got_ref, spot(me), sends, recvs, 1, 1)
     own = [
         pltpu.make_async_copy(keeps_ref, both_ref.at[0], local.at[1]),
     ]
@@ -744,7 +747,8 @@
         across(z_ref.at[ahead(step)], z_got_ref.at[home], far_sends, far_recvs, step, ahead(step))
         for step in range(1, count)
     ]
-    for copy in [give_pair] + z_sends + own:
+    own.append(g_own)
+    for copy in [g_chip] + z_sends + [g_core] + own:
         copy.start()
     for copy in loads + [fetch]:
         copy.wait()
@@ -779,22 +783,22 @@
     for copy in out_sends:
         copy.start()
     base = 2 + seqs * 3
-    give_pair.wait_recv()
-    g_chip = remote(spot(me), spot(me), sends, recvs, base, 2)
-    g_core = remote(spot(me), spot(me), sends, recvs, base + 1, 1)
-    g_chip.start()
-    g_core.start()
     g_chip.wait_recv()
     g_on = remote(spot(peer(2)), spot(peer(2)), sends, recvs, base + 2, 1)
     g_on.start()
     for copy in out_sends + [g_on, g_core] + own + z_sends:
         copy.wait()
     g_chip.wait_send()
-    give_pair.wait_send()
-
-
-def middle(keeps, gives, give, z_blocks, x_all, out_proj, seqs):
-    tokens, half = give.shape
+    quarter = z_got_ref.shape[2]
+    for q in range(4):
+        total = z_got_ref[q].astype(f32)
+        for group in range(1, count // 4):
+            total = total + z_got_ref[4 * group + q].astype(f32)
+        wz_ref[:, q * quarter : (q + 1) * quarter] = total.astype(bf16)
+
+
+def middle(keeps, gives, got, z_blocks, x_all, out_proj, seqs):
+    tokens, half = got.shape
     group = lax.axis_size("shard")
     model = x_all.shape[1]
     cols = model // group
@@ -807,9 +811,10 @@
         out_shape=[
             jax.ShapeDtypeStruct((2, tokens, half * group), bf16),
             jax.ShapeDtypeStruct((seqs, tokens // seqs // group, model), bf16),
-            jax.ShapeDtypeStruct(z_blocks.shape, bf16),
+            jax.ShapeDtypeStruct((z_blocks.shape[1], 4 * z_blocks.shape[2]), bf16),
         ],
         scratch_shapes=[
+            pltpu.VMEM(z_blocks.shape, bf16),
             pltpu.VMEM((2, half * group, cols), bf16),
             pltpu.VMEM((tokens, cols), bf16),
             pltpu.VMEM((tokens, cols), bf16),
@@ -819,16 +824,16 @@
         compiler_params=group_params(7, 22 << 20),
         cost_estimate=cost(25),
         name="middle",
-    )(keeps, gives, give, z_blocks, x_all, out_proj)
+    )(keeps, gives, got, z_blocks, x_all, out_proj)
 
 
 PARTS = 2
 
 
 def finish_kernel(
-    gx_ref, gz_ref, small_keep_ref, small_give_ref, wz_ref, norm_ref, w_hbm, x_ref, cot_ref, gain_ref,
-    gw_ref, small_ref, dx_ref, ggain_ref,
-    w_ref, gx4, cols_ref, turned, xb_ref, sb_ref, small_got, x_in, s_in, lhs, pairs, near, g_hold, g_own, g_send, g_far,
+    gx_ref, gz_ref, small_keep_ref, small_give_ref, wz_ref, norm_hbm, w_hbm, x_ref, cot_ref, gain_ref,
+    gw_ref, gxp_ref, gdp_ref, rest_ref, dx_ref, ggain_ref,
+    small_ref, norm_ref, w_ref, gx4, cols_ref, turned, xb_ref, sb_ref, small_got, x_in, s_in, lhs, pairs, near, g_hold, g_own, g_send, g_far,
     h_send, h_cols, z_cols, s_own, gains, gain_near, gain_sum, gain_pair, gain_two, gain_in,
     sends, recvs, far_sends, far_recvs, home_sends, home_recvs, local,
 ):
@@ -848,6 +853,8 @@
     tile = 256
     other = quad(1)
     load = pltpu.make_async_copy(w_hbm, w_ref, local.at[0])
+    load_norm = pltpu.make_async_copy(norm_hbm, norm_ref, local.at[1])
+    load_norm.start()
     load.start()
     meet([ahead(step) for step in range(1, count)])
 
@@ -871,7 +878,7 @@
 
     small_send = across(small_give_ref, small_got, sends, recvs, 3 * PARTS, other)
     quad_own = [
-        pltpu.make_async_copy(piece_of(member, p), spot_of(0, p), local.at[PARTS + 2 + 2 * seqs + p]) for p in range(PARTS)
+        pltpu.make_async_copy(piece_of(member, p), spot_of(0, p), local.at[PARTS + 3 + 2 * seqs + p]) for p in range(PARTS)
     ]
     for copy in quad_sends(0) + [small_send] + quad_sends(1) + quad_own:
         copy.start()
@@ -897,7 +904,7 @@
 
     def home_keep(at):
         _, src, dst = home_pieces(at)
-        return pltpu.make_async_copy(src, dst, local.at[1 + at])
+        return pltpu.make_async_copy(src, dst, local.at[2 + at])
 
     def home_start(at):
         slot = home_pieces(at)[0]
@@ -929,6 +936,7 @@
                 turned[low : low + tile, at] = norm_ref[side_half, at, j * tile : (j + 1) * tile].T
         return carry
 
+    load_norm.wait()
     lax.fori_loop(0, 4 * tokens // tile, turn, 0)
 
     def far_copy(src, dst, kind, step):
@@ -1022,9 +1030,6 @@
     grads_on(0)
     x_part(1)
     grads_of(1)
-    home_sum(0)
-    grads_on(1)
-
     for copy in s_sends:
         copy.wait_recv()
     total = sb_ref[mine].astype(f32)
@@ -1035,6 +1040,17 @@
     spread = [far_copy(s_own, small_ref.at[side, mine], PARTS + 1, step) for step in order]
     for copy in spread:
         copy.start()
+
+    def pass_on(step):
+        at = lax.rem(mine + height - step, height)
+        return across(
+            small_ref.at[side, at], small_ref.at[side, at], far_sends, far_recvs, (PARTS + 3) * count + step, other
+        )
+
+    pass_on(0).start()
+    home_sum(0)
+    grads_on(1)
+
 
     gains[...] = jnp.zeros_like(gains)
 
@@ -1058,6 +1074,9 @@
 
     finish_rows(0)
     home_sum(1)
+    for step in order:
+        spread[step - 1].wait_recv()
+        pass_on(step).start()
     finish_rows(1)
     gains[...] = jnp.broadcast_to(jnp.sum(gains[...], axis=0, keepdims=True), gains.shape)
     wide = model // 4
@@ -1075,10 +1094,6 @@
     gain_sum[...] = gains[:, pl.ds(pl.multiple_of(me * wide, LANES), wide)] + gain_near[0] + gain_near[1] + gain_near[2]
     gain_copy = across(gain_sum, gain_pair, sends, recvs, 3 * PARTS + 6, other)
     gain_copy.start()
-    for copy in spread:
-        copy.wait_recv()
-    small_pair = across(small_ref.at[side], small_ref.at[side], sends, recvs, 3 * PARTS + 7, other)
-    small_pair.start()
     gain_copy.wait()
     gain_two[...] = gain_sum[...] + gain_pair[...]
     gain_far = [far_copy(gain_two, gain_in.at[step - 1], PARTS + 2, step) for step in order]
@@ -1108,7 +1123,16 @@
         for low in range(0, 2 * width, quarter):
             gw_ref[:, low : low + quarter] = z_cols[:, low : low + quarter].astype(f32)
 
-    small_pair.wait()
+    for step in range(height):
+        pass_on(step).wait()
+    lined = small_keep_ref.shape[1]
+    first, second = gxp_ref.shape[0], gxp_ref.shape[0] + gdp_ref.shape[0]
+    for at in range(count):
+        low, high = at * lined, (at + 1) * lined
+        for ref, start, stop in ((gxp_ref, 0, first), (gdp_ref, first, second), (rest_ref, second, second + 8)):
+            a, b = max(low, start), min(high, stop)
+            if a < b:
+                ref[a - start : b - start, :] = small_ref[at % 2, at // 2, a - low : b - low, :].astype(f32)
     small_send.wait_send()
     for p in range(PARTS):
         for copy in quad_sends(p) + x_sends(p):
@@ -1117,7 +1141,7 @@
         copy.wait_send()
 
 
-def finish(gx, gz, small_keep, small_give, wz, norm, w_in, x, cot, gain):
+def finish(gx, gz, small_keep, small_give, wz, norm, w_in, x, cot, gain, tops):
     tokens, width = gx.shape
     height, lines, _ = small_keep.shape
     deep = wz.shape[0]
@@ -1127,19 +1151,23 @@
     other = max(height - 1, 1)
     count = 2 * height
     quarter = width // 4
-    kinds = (PARTS + 3) * count
+    kinds = (PARTS + 4) * count
     homes = PARTS + 1 + 2 * seqs
     return pl.pallas_call(
         finish_kernel,
-        in_specs=[VMEM_SPEC] * 6 + [ANY_SPEC] + [VMEM_SPEC] * 3,
-        out_specs=[VMEM_SPEC] * 4,
+        in_specs=[VMEM_SPEC] * 5 + [ANY_SPEC] * 2 + [VMEM_SPEC] * 3,
+        out_specs=[VMEM_SPEC] * 6,
         out_shape=[
             jax.ShapeDtypeStruct((deep, 2 * width), f32),
-            jax.ShapeDtypeStruct((2, height, lines, width), bf16),
+            jax.ShapeDtypeStruct((tops[0], width), f32),
+            jax.ShapeDtypeStruct((tops[1], width), f32),
+            jax.ShapeDtypeStruct((8, width), f32),
             jax.ShapeDtypeStruct(x.shape, bf16),
             jax.ShapeDtypeStruct((8, wide), f32),
         ],
         scratch_shapes=[
+            pltpu.VMEM((2, height, lines, width), bf16),
+            pltpu.VMEM(norm.shape, bf16),
             pltpu.VMEM(w_in.shape, bf16),
             pltpu.VMEM((4 * tokens, quarter), bf16),
             pltpu.VMEM((tokens, 2 * width), bf16),
@@ -1167,7 +1195,7 @@
             pltpu.SemaphoreType.DMA((3 * PARTS + 8 + 2 * seqs,)), pltpu.SemaphoreType.DMA((3 * PARTS + 8 + 2 * seqs,)),
             pltpu.SemaphoreType.DMA((kinds,)), pltpu.SemaphoreType.DMA((kinds,)),
             pltpu.SemaphoreType.DMA((homes,)), pltpu.SemaphoreType.DMA((2 * homes,)),
-            pltpu.SemaphoreType.DMA((homes + 1 + PARTS,)),
+            pltpu.SemaphoreType.DMA((homes + 2 + PARTS,)),
         ],
         compiler_params=group_params(8, 58 << 20),
         cost_estimate=cost(80),
@@ -1263,7 +1291,7 @@
         odd = jnp.concatenate(cuts[1::2], axis=1)
         return jnp.where(side == 0, even, odd), jnp.where(side == 0, odd, even)
 
-    xs, cots, gains, half_norm, parts, gated_own, gated_send = front(
+    xs, cots, gains, own_half, half_norm, parts, gated_own, gated_send = front(
         block_input, out_grad, norm_gain, w_in, out_proj
     )
     gain = gains[::8].reshape(1, -1)
@@ -1284,8 +1312,10 @@
         conv_pre = conv_pre + conv_w[j] * x_padded[:, j : j + length] * taps[d][:, :, None]
     conv_out = jax.nn.silu(conv_pre).astype(bf16)
     conv_flat = conv_out.reshape(tokens, width)
-    half_norm = half_norm.reshape(3, tokens, -1)
-    last_norm = lax.ppermute(half_norm[0], "replica", [(i, i ^ 3) for i in range(count)])
+    half_norm = half_norm.reshape(2, tokens, -1)
+    own_half = own_half.reshape(tokens, -1)
+    last_norm = lax.ppermute(own_half, "replica", [(i, i ^ 3) for i in range(count)])
+    cot_got = lax.ppermute(cot, "replica", [(i, i ^ 1) for i in range(count)])
     proj = group_total(outer_dot(x_proj, conv_flat), 3)
     gated_far = by_hop(after(gated_send, proj), 2)
     keep_lanes = jnp.broadcast_to(taps[1][:, :, None], (seqs, length, LANES))
@@ -1293,7 +1323,10 @@
     y_total, gated, rate, beta, states = recurrence_forward(
         conv_out, z_part, proj, keep_lanes, dt_proj, dt_bias.astype(f32)[None], skip[None]
     )
-    y_total, gated, gated_far, last_norm = lax.optimization_barrier((y_total, gated, gated_far, last_norm))
+    y_total, gated, gated_far, last_norm, cot_got = lax.optimization_barrier(
+        (y_total, gated, gated_far, last_norm, cot_got)
+    )
+    cot_both = jnp.concatenate([cot, cot_got], axis=0)
     grad_gated = split(gated_own + gated_far.astype(f32))
     z_vals = z_part.astype(f32)
     dy = grad_gated * jax.nn.silu(z_vals)
@@ -1301,18 +1334,16 @@
 
     gated_keep, gated_give = halves(gated.reshape(tokens, width), height // 4)
     cols = model // 4
-    keeps, gives, grad_z_quad, norms, cot_both = collect(
-        gated_keep, gated_give, grad_z, half_norm, last_norm, cot
+    keeps, gives, grad_z_quad, norms, gated_got = collect(
+        gated_keep, gated_give, grad_z, own_half, half_norm, last_norm
     )
     norms = norms.reshape(2, 4 * tokens, -1)
     z_blocks = lax.dot_general(
         norms, grad_z_quad.reshape(4 * tokens, -1), (((1,), (0,)), ((), ())), preferred_element_type=f32
     )
     z_blocks = z_blocks.astype(bf16).reshape(count, -1, width // 4)
-    gated_both, block_output, z_got = middle(keeps, gives, gated_give, z_blocks, x_all, out_proj, seqs)
-    z_sum = jnp.sum(z_got.reshape((-1, 4) + z_got.shape[1:]).astype(f32), axis=0)
-    grad_w_z = z_sum.transpose(1, 0, 2).reshape(-1, width).astype(bf16)
-    out_blocks = inner_dot(gated_both.reshape(2 * tokens, -1), cot_both.reshape(2 * tokens, -1))
+    gated_both, block_output, grad_w_z = middle(keeps, gives, gated_got, z_blocks, x_all, out_proj, seqs)
+    out_blocks = inner_dot(gated_both.reshape(2 * tokens, -1), cot_both)
     out_own, out_sent = far_send(out_blocks.astype(bf16).reshape(height, -1, cols))
     rate, out_own = lax.optimization_barrier((rate, out_own))
 
@@ -1342,21 +1373,19 @@
     small = jnp.concatenate(
         [grad_x_proj, grad_dt_proj, grad_conv_weight, grad_conv_bias[None], grad_dt_bias, grad_d_skip]
     )
-    unit = 16 * count
+    unit = 8 * count
     padded = -(-small.shape[0] // unit) * unit
     small = jnp.pad(small, ((0, padded - small.shape[0]), (0, 0))).reshape(height, 2, -1, width)
     small_keep = jnp.where(side == 0, small[:, 0], small[:, 1])
     small_give = jnp.where(side == 0, small[:, 1], small[:, 0]).astype(bf16)
-    grad_w_in, small, input_grad, grad_gain = finish(
-        grad_x, grad_z, small_keep, small_give, grad_w_z, norms, w_in, block_input, out_grad, gain
+    top = x_proj.shape[0]
+    grad_w_in, grad_x_proj, grad_dt_proj, rest, input_grad, grad_gain = finish(
+        grad_x, grad_z, small_keep, small_give, grad_w_z, norms, w_in, block_input, out_grad, gain,
+        (top, rank),
     )
-    small = small.transpose(1, 0, 2, 3).reshape(padded, width).astype(f32)
-
-    top = x_proj.shape[0]
     return (
-        block_output, input_grad, grad_gain[0], grad_w_in,
-        small[top + rank : top + rank + KW], small[top + rank + KW], small[:top], small[top : top + rank],
-        small[top + rank + KW + 1], small[top + rank + KW + 2], grad_out_proj,
+        block_output, input_grad, grad_gain[0], grad_w_in, rest[:KW], rest[KW], grad_x_proj, grad_dt_proj,
+        rest[KW + 1], rest[KW + 2], grad_out_proj,
     )
 
 

time: 336 us -> 311 us (0.926)
  Pallas kernels: 268 us -> 247 us
  starting transfers between devices: 5.75 us -> 11.5 us
  other arithmetic: 21.5 us -> 16.9 us
    pallas_call x1, Pallas kernels: 40.7 us -> 22.9 us  [middle(): pl.pallas_call(middle_kernel, in_specs=[VMEM_SPEC] * 4 + [ANY_SPEC] * 2,...]
    ppermute x3, starting transfers between devices: 2.1 us -> 7.24 us  [far_send(): lax.ppermute(out, 'replica', [(i, (i + 2 * step) % count) for i in range(...]
    unnamed x86 -> x110, local copies, waits for them, and re-layouts: 15.2 us -> 19.4 us
    pallas_call x1, Pallas kernels: 75.4 us -> 71.9 us  [finish(): pl.pallas_call(finish_kernel, in_specs=[VMEM_SPEC] * 5 + [ANY_SPEC] * 2 +...]
  transfers between devices with their start and end apart: 5 -> 6, of which waited for: 1 -> 0; matrix products, arithmetic and copies ran while one was open for 3% -> 2% of each run, Pallas kernels for 24% -> 26%
where the time goes in v6:
time: 311 us
  Pallas kernels  247 us (79%)
  local copies, waits for them, and re-layouts  26.5 us (9%)
  other arithmetic  16.9 us (5%)
  starting transfers between devices  11.5 us (4%)
  matrix products  7.7 us (2%)
    pallas_call x1, Pallas kernels, finish(): pl.pallas_call(finish_kernel, in_specs=[VMEM_SPEC] * 5 + [ANY_SPEC] * 2 +...  71.9 us
    pallas_call x1, Pallas kernels, front(): pl.pallas_call(front_kernel, in_specs=[VMEM_SPEC] * 3 + [ANY_SPEC] * 2, o...  43.3 us
    pallas_call x1, Pallas kernels, recurrence_backward(): pl.pallas_call(backward_kernel, grid=(seqs, blocks), in_specs=[wide, wide...  36.1 us
    pallas_call x1, Pallas kernels, collect(): pl.pallas_call(collect_kernel, in_specs=[VMEM_SPEC] * 6, out_specs=[VMEM_...  28.9 us
    pallas_call x1, Pallas kernels, middle(): pl.pallas_call(middle_kernel, in_specs=[VMEM_SPEC] * 4 + [ANY_SPEC] * 2,...  22.9 us
    pallas_call x2, Pallas kernels, group_total(): pl.pallas_call(total_kernel, in_specs=[VMEM_SPEC], out_specs=VMEM_SPEC, o...  22.4 us
    pallas_call x1, Pallas kernels, recurrence_forward(): pl.pallas_call(forward_kernel, grid=(seqs, blocks), in_specs=[wide, wide,...  21.4 us
    unnamed x110, local copies, waits for them, and re-layouts  19.4 us
  transfers between devices with their start and end apart: 6, of which 0 were waited for; matrix products, arithmetic and copies ran while one was open for 2% of the time, Pallas kernels for 26%

profile of v6, /device:TPU:0, one launch (start us, length us, event | category | flops | bytes accessed | tf_op | source)
XLA Modules:
  0.0 310.5 jit_solution(5341596230047997846)
XLA Ops:
  0.6 0.0 copy-start
  0.7 0.7 broadcast_in_dim.12.gain_ref
  1.4 1.0 copy-done.6
  2.4 1.0 copy-done.7
  3.5 43.3 %front.1 = (bf16[2,256,2048]{2,1,0:T(8,128)(2,1)S(1)}, bf16[2,256,512]{2,1,0:T(8,128)(2,1)}, f32[32,512]{1,0:T(8,128)S(1)}, bf16[2,256,1024]{2,1,0:T(8,128)(2,1)...) custom-call(bf16[2,64,2048]{2,1,0:T(8,128)(2,1)S(1)} %copy-done.6, ...), custom_call_target="tpu_custom_call" | custom-call | tf_op jit(solution)/shard_map/front/pallas_call | solution.py:561
  46.8 1.6 collective-permute-start.2
  48.4 1.5 collective-permute-start.1
  49.9 0.1 compare_convert_fusion.2
  50.0 1.9 slice_bitcast_fusion
  51.9 2.7 fusion.12
  54.6 0.5 convolution_bitcast_fusion.part_ref
  55.1 13.4 %group_total.2.proj_ref = f32[160,512]{1,0:T(8,128)S(1)} custom-call(f32[160,512]{1,0:T(8,128)S(1)} %convolution_bitcast_fusion.part_ref), custom_call_target="tpu_custom_call" | custom-call | tf_op jit(solution)/shard_map/group_total/pallas_call | solution.py:1228
  68.6 1.2 collective-permute-start
  69.8 0.1 broadcast_in_dim.13.keep_ref
  69.9 21.4 %recurrence_forward.1 = (f32[2,256,1024]{2,1,0:T(8,128)S(1)}, bf16[2,256,1024]{2,1,0:T(8,128)(2,1)S(1)}, f32[2,256,1024]{2,1,0:T(8,128)S(1)}, f32[2,256,1024]{2,1,0:T(8,128)S(1)}, bf16[2,4096,1024]{2,1,0:T(8,128)(2,1)}) custom-call(bf16[2,256,1024]{2,1,0:T(8,128)(2,1)S(1)} %get-tuple-element.108.conv_ref, ...), custom_call_target="tpu_custom_call" | custom-call | flops 16000000000 | bytes 25165824 | tf_op jit(solution)/shard_map/recurrence_forward/pallas_call | solution.py:270
  91.3 1.0 copy-done.3
  92.3 1.3 copy-done.18
  93.6 1.3 copy-done.20
  94.9 0.6 slice.105
  95.5 1.3 copy.31
  96.8 2.3 convert_add_fusion
  99.1 0.2 copy-done.26
  99.3 1.1 fusion.11
  100.4 0.1 copy-done.4
  100.6 0.1 broadcast_select_fusion
  100.6 1.8 copy-done.14
  102.4 28.9 %collect.1 = (bf16[512,2048]{1,0:T(8,128)(2,1)S(1)}, bf16[512,2048]{1,0:T(8,128)(2,1)S(1)}, bf16[4,512,256]{2,1,0:T(8,128)(2,1)S(1)}, bf16[2,4,512,1024]{3,2,1,0:T(8,128)(2,1)S(1)}, bf16[512,512]{1,0:T(8,128)(2,1)S(1)}) custom-call(bf16[512,512]{1,0:T(8,128)(2,1)S(1)} %get-tuple-element.122.keep_ref, bf16[512,512]{1,0:T(8,128)(2,1)S(1)} %get-tuple-element.121.give_ref, ...), custom_call_target="tpu_custom_call" | custom-call | flops 24999999488 | bytes 1048576 | tf_op jit(solution)/shard_map/collect/pallas_call | solution.py:683
  131.4 2.6 bitcast_convert_fusion
  134.0 1.6 copy-done.17
  135.6 1.0 copy-done.2
  136.6 0.7 copy-done.13
  137.2 22.9 %middle.1 = (bf16[2,512,2048]{2,1,0:T(8,128)(2,1)S(1)}, bf16[2,64,2048]{2,1,0:T(8,128)(2,1)S(1)}, bf16[256,1024]{1,0:T(8,128)(2,1)S(1)}) custom-call(bf16[512,2048]{1,0:T(8,128)(2,1)S(1)} %get-tuple-element.68.keeps_ref, bf16[512,2048]{1,0:T(8,128)(2,1)S(1)} %get-tuple-element.69.gives_ref, bf16[512,512]{1,0:T(8,128)(2,1)S(1)} %get-tuple-element.70.got_ref, ...), custom_call_target="tpu_custom_call" | custom-call | flops 24999999488 | bytes 1048576 | tf_op jit(solution)/shard_map/middle/pallas_call | solution.py:807
  160.2 3.8 %convolution_convert_fusion = bf16[2048,512]{1,0:T(8,128)(2,1)S(1)} fusion(bf16[1024,2048]{1,0:T(8,128)(2,1)S(1)} %bitcast.97, bf16[512,512]{1,0:T(8,128)(2,1)} %collective-permute-done.2, bf16[512,512]{1,0:T(8,128)(2,1)} %bitcast.12), kind=kOutput, calls=%fused_computation | convolution fusion | flops 2150629376 | bytes 7340032 | tf_op jit(solution)/shard_map/dot_general | solution.py:23
  164.0 0.9 dynamic-slice_bitcast_fusion
  165.0 6.3 %collective-permute-start.5 = (bf16[512,512]{1,0:T(8,128)(2,1)S(1)}, bf16[512,512]{1,0:T(8,128)(2,1)S(1)}, u32[]{:S(2)}, u32[]{:S(2)}) collective-permute-start(bf16[512,512]{1,0:T(8,128)(2,1)S(1)} %get-tuple-element.115), channel_id=1, source_target_pairs={{0,24},{4,28},{8,0},{12,4},{16,8},{20,12},{24,16},{28,20},{1,25},{... | collective-permute-start | bytes 1572872 | tf_op jit(solution)/shard_map/ppermute | solution.py:1254
  171.3 0.3 collective-permute-start.4
  171.6 0.6 collective-permute-start.3
  172.2 36.1 %recurrence_backward.1 = (f32[2,256,1024]{2,1,0:T(8,128)S(1)}, bf16[2,256,1024]{2,1,0:T(8,128)(2,1)}, f32[160,512]{1,0:T(8,128)S(1)}, f32[128,1024]{1,0:T(8,128)...) custom-call(f32[2,256,1024]{2,1,0:T(8,128)S(1)} %copy-done.19, f32[2,256,1024]{2,1,0:T(8,128)S(1)} %copy-done.21, ...), custom_call_target="tpu_custom_call" | custom-call | flops 30000001024 | bytes 29360128 | tf_op jit(solution)/shard_map/recurrence_backward/pallas_call | solution.py:303
  208.4 8.9 %group_total.3 = f32[160,512]{1,0:T(8,128)S(1)} custom-call(f32[160,512]{1,0:T(8,128)S(1)} %get-tuple-element.82.part_ref), custom_call_target="tpu_custom_call" | custom-call | tf_op jit(solution)/shard_map/group_total/pallas_call | solution.py:1228
  217.4 0.8 copy-done.33
  218.1 0.3 fusion.18
  218.5 0.5 fusion.20
  219.0 0.1 copy-done.37
  219.1 1.0 copy-done.27
  220.1 3.3 %fusion.23 = (f32[1024]{0:T(1024)S(1)}, f32[1024]{0:T(1024)S(1)}, f32[1024]{0:T(1024)S(1)}, f32[1024]{0:T(1024)S(1)}, f32[1024]{0:T(1024)S(1)}, /*index=5*/f32[2,256,1024]{2,1,0:T(8,128)}) fusion(bf16[2,2,256,1024]{3,2,1,0:T(8,128)(2,1)S(1)} %copy-done.26, f32[2,256]{1,0:T(2,128)S(1)} %copy-done.44, f32[2,256,1024]{2,1,0:T(8,128)S(1)} %copy-done.24, ...), kind=kLoop, calls=%fused_computation.64 | loop fusion | flops 12577792 | bytes 13662208 | tf_op jit(solution)/shard_map/reduce_sum | solution.py:1359
  223.4 0.4 concatenate.7
  223.8 0.2 pad.29
  224.0 0.8 fusion.17.small_give_ref
  224.8 0.9 select_bitcast_fusion.small_keep_ref
  225.7 0.5 broadcast_multiply_fusion
  226.2 0.2 copy-done.40
  226.4 0.0 copy-done.42
  226.4 2.1 fusion.4
  228.5 71.9 %finish.1 = (f32[256,2048]{1,0:T(8,128)}, f32[160,1024]{1,0:T(8,128)}, f32[128,1024]{1,0:T(8,128)}, f32[8,1024]{1,0:T(8,128)}, bf16[2,64,2048]{2,1,0:T(8,128)(2,1)}, /*index=5*/f32[8,512]{1,0:T(8,128)}) custom-call(bf16[512,1024]{1,0:T(8,128)(2,1)} %bitcast.103, bf16[512,1024]{1,0:T(8,128)(2,1)} %bitcast.91, ...), custom_call_target="tpu_custom_call" | custom-call | flops 80000000000 | bytes 1048576 | tf_op jit(solution)/shard_map/finish/pallas_call | solution.py:1156
  300.4 1.5 fusion.24
  301.8 1.4 slice.107
  303.2 1.3 slice.106
  304.5 1.2 convert_add_fusion.1
  305.8 0.8 copy.37
  306.6 0.8 copy.38
  307.4 1.3 copy.39
  308.7 0.2 copy-done.30
  308.9 0.8 copy.40
  309.7 0.8 copy.41
  (96 shorter events, 0.2 us)
Async XLA Ops:
  0.6 54.0 %copy-start = (bf16[160,1024]{1,0:T(8,128)(2,1)S(1)}, bf16[160,1024]{1,0:T(8,128)(2,1)}, u32[]{:S(2)}) copy-start(bf16[160,1024]{1,0:T(8,128)(2,1)} %param.18) | copy-start | bytes 983044
  1.4 1.0 copy-start.6
  2.4 1.0 copy-start.7
  3.5 46.4 %copy-start.48 = (bf16[1024]{0:T(1024)(128)(2,1)S(1)}, bf16[1024]{0:T(1024)(128)(2,1)}, u32[]{:S(2)}) copy-start(bf16[1024]{0:T(1024)(128)(2,1)} %param.17) | copy-start | bytes 6148
  3.5 46.4 %copy-start.51 = (s32[2,256]{1,0:T(2,128)S(1)}, s32[2,256]{1,0:T(2,128)}, u32[]{:S(2)}) copy-start(s32[2,256]{1,0:T(2,128)} %param.13) | copy-start | bytes 6148
  3.5 46.5 %copy-start.47 = (bf16[4,1024]{1,0:T(4,128)(2,1)S(1)}, bf16[4,1024]{1,0:T(4,128)(2,1)}, u32[]{:S(2)}) copy-start(bf16[4,1024]{1,0:T(4,128)(2,1)} %param.16) | copy-start | bytes 24580
  46.8 5.1 %copy-start.12 = (bf16[2,256,2048]{2,1,0:T(8,128)(2,1)}, bf16[2,256,2048]{2,1,0:T(8,128)(2,1)S(1)}, u32[]{:S(2)}) copy-start(bf16[2,256,2048]{2,1,0:T(8,128)(2,1)S(1)} %get-tuple-element.73) | copy-start | bytes 6291460
  46.8 50.0 %collective-permute-start.2 = (bf16[512,512]{1,0:T(8,128)(2,1)}, bf16[512,512]{1,0:T(8,128)(2,1)}, u32[]{:S(2)}, u32[]{:S(2)}) collective-permute-start(bf16[512,512]{1,0:T(8,128)(2,1)} %bitcast.12), channel_id=1, source_target_pairs={{0,4},{4,0},{8,12},{12,8},{16,20},{20,16},{24,28},{28,24},{1,5},{5... | collective-permute-start | bytes 1572872 | tf_op jit(solution)/shard_map/ppermute | solution.py:1318
  48.4 48.4 %collective-permute-start.1 = (bf16[512,1024]{1,0:T(8,128)(2,1)}, bf16[512,1024]{1,0:T(8,128)(2,1)}, u32[]{:S(2)}, u32[]{:S(2)}) collective-permute-start(bf16[512,1024]{1,0:T(8,128)(2,1)} %bitcast.11.own_half_ref), channel_id=1, source_target_pairs={{0,12},{4,8},{8,4},{12,0},{16,28},{20,24},{24,20},{28,16},{1,13},{... | collective-permute-start | bytes 3145736 | tf_op jit(solution)/shard_map/ppermute | solution.py:1317
  49.9 2.0 copy-start.43
  49.9 2.0 copy-start.45
  50.0 1.9 copy-start.39
  50.0 1.9 copy-start.41
  51.9 2.7 copy-start.23
  54.6 15.2 %copy-start.49 = (bf16[1024]{0:T(1024)(128)(2,1)S(1)}, bf16[1024]{0:T(1024)(128)(2,1)}, u32[]{:S(2)}) copy-start(bf16[1024]{0:T(1024)(128)(2,1)} %param.21) | copy-start | bytes 6148
  54.6 15.2 %copy-start.50 = (bf16[1024]{0:T(1024)(128)(2,1)S(1)}, bf16[1024]{0:T(1024)(128)(2,1)}, u32[]{:S(2)}) copy-start(bf16[1024]{0:T(1024)(128)(2,1)} %param.20) | copy-start | bytes 6148
  54.6 15.3 %copy-start.15 = (bf16[128,1024]{1,0:T(8,128)(2,1)S(1)}, bf16[128,1024]{1,0:T(8,128)(2,1)}, u32[]{:S(2)}) copy-start(bf16[128,1024]{1,0:T(8,128)(2,1)} %dt_proj_ref.3) | copy-start | bytes 786436
  68.6 22.7 %copy-start.8 = (f32[160,512]{1,0:T(8,128)}, f32[160,512]{1,0:T(8,128)S(1)}, u32[]{:S(2)}) copy-start(f32[160,512]{1,0:T(8,128)S(1)} %group_total.2.proj_ref) | copy-start | bytes 983044
  68.6 28.2 %collective-permute-start = (bf16[512,1024]{1,0:T(8,128)(2,1)}, bf16[512,1024]{1,0:T(8,128)(2,1)}, u32[]{:S(2)}, u32[]{:S(2)}) collective-permute-start(bf16[512,1024]{1,0:T(8,128)(2,1)} %get-tuple-element.59), channel_id=1, source_target_pairs={{0,2},{1,3},{2,0},{3,1},{4,6},{5,7},{6,4},{7,5},{8,10},{9,11},{10,... | collective-permute-start | bytes 3145736 | tf_op jit(solution)/shard_map/ppermute | solution.py:1240
  69.9 21.4 %copy-start.10 = (f32[2,256,128]{2,1,0:T(8,128)}, f32[2,256,128]{2,1,0:T(8,128)S(1)}, u32[]{:S(2)}) copy-start(f32[2,256,128]{2,1,0:T(8,128)S(1)} %broadcast_in_dim.13.keep_ref) | copy-start | bytes 786436
  91.3 1.0 copy-start.3
  92.3 1.3 copy-start.18
  93.6 1.3 copy-start.20
  96.8 2.5 copy-start.26
  99.3 1.2 copy-start.4
  100.4 30.9 %copy-start.5 = (bf16[2,256,1024]{2,1,0:T(8,128)(2,1)}, bf16[2,256,1024]{2,1,0:T(8,128)(2,1)S(1)}, u32[]{:S(2)}) copy-start(bf16[2,256,1024]{2,1,0:T(8,128)(2,1)S(1)} %get-tuple-element.111) | copy-start | bytes 3145732
  100.4 2.0 copy-start.14
  131.3 4.3 %copy-start.17 = (bf16[2,4,512,1024]{3,2,1,0:T(8,128)(2,1)}, bf16[2,4,512,1024]{3,2,1,0:T(8,128)(2,1)S(1)}, u32[]{:S(2)}) copy-start(bf16[2,4,512,1024]{3,2,1,0:T(8,128)(2,1)S(1)} %get-tuple-element.71) | copy-start | bytes 25165828
  131.3 5.2 %copy-start.2 = (bf16[4096,512]{1,0:T(8,128)(2,1)S(1)}, bf16[4096,512]{1,0:T(8,128)(2,1)}, u32[]{:S(2)}) copy-start(bf16[4096,512]{1,0:T(8,128)(2,1)} %o_hbm.3) | copy-start | bytes 12582916
  131.4 5.9 %copy-start.13 = (bf16[2,256,2048]{2,1,0:T(8,128)(2,1)S(1)}, bf16[2,256,2048]{2,1,0:T(8,128)(2,1)}, u32[]{:S(2)}) copy-start(bf16[2,256,2048]{2,1,0:T(8,128)(2,1)} %copy-done.12) | copy-start | bytes 6291460
  160.1 3.8 %copy-start.22 = (bf16[256,1024]{1,0:T(8,128)(2,1)}, bf16[256,1024]{1,0:T(8,128)(2,1)S(1)}, u32[]{:S(2)}) copy-start(bf16[256,1024]{1,0:T(8,128)(2,1)S(1)} %get-tuple-element.87.wz_ref) | copy-start | bytes 1572868
  160.1 12.1 %copy-start.21 = (f32[2,256,1024]{2,1,0:T(8,128)S(1)}, f32[2,256,1024]{2,1,0:T(8,128)}, u32[]{:S(2)}) copy-start(f32[2,256,1024]{2,1,0:T(8,128)} %copy-done.20) | copy-start | bytes 6291460
  164.0 8.2 %copy-start.9 = (f32[160,512]{1,0:T(8,128)S(1)}, f32[160,512]{1,0:T(8,128)}, u32[]{:S(2)}) copy-start(f32[160,512]{1,0:T(8,128)} %copy-done.8) | copy-start | bytes 983044
  164.0 8.2 %copy-start.11 = (f32[2,256,128]{2,1,0:T(8,128)S(1)}, f32[2,256,128]{2,1,0:T(8,128)}, u32[]{:S(2)}) copy-start(f32[2,256,128]{2,1,0:T(8,128)} %copy-done.10) | copy-start | bytes 786436
  164.0 8.2 %copy-start.16 = (bf16[128,1024]{1,0:T(8,128)(2,1)S(1)}, bf16[128,1024]{1,0:T(8,128)(2,1)}, u32[]{:S(2)}) copy-start(bf16[128,1024]{1,0:T(8,128)(2,1)} %dt_proj_ref.3) | copy-start | bytes 786436
  164.0 8.2 %copy-start.19 = (f32[2,256,1024]{2,1,0:T(8,128)S(1)}, f32[2,256,1024]{2,1,0:T(8,128)}, u32[]{:S(2)}) copy-start(f32[2,256,1024]{2,1,0:T(8,128)} %copy-done.18) | copy-start | bytes 6291460
  165.0 52.4 %collective-permute-start.5 = (bf16[512,512]{1,0:T(8,128)(2,1)S(1)}, bf16[512,512]{1,0:T(8,128)(2,1)S(1)}, u32[]{:S(2)}, u32[]{:S(2)}) collective-permute-start(bf16[512,512]{1,0:T(8,128)(2,1)S(1)} %get-tuple-element.115), channel_id=1, source_target_pairs={{0,24},{4,28},{8,0},{12,4},{16,8},{20,12},{24,16},{28,20},{1,25},{... | collective-permute-start | bytes 1572872 | tf_op jit(solution)/shard_map/ppermute | solution.py:1254
  171.3 46.1 %collective-permute-start.4 = (bf16[512,512]{1,0:T(8,128)(2,1)S(1)}, bf16[512,512]{1,0:T(8,128)(2,1)S(1)}, u32[]{:S(2)}, u32[]{:S(2)}) collective-permute-start(bf16[512,512]{1,0:T(8,128)(2,1)S(1)} %get-tuple-element.116), channel_id=1, source_target_pairs={{0,16},{4,20},{8,24},{12,28},{16,0},{20,4},{24,8},{28,12},{1,17},{... | collective-permute-start | bytes 1572872 | tf_op jit(solution)/shard_map/ppermute | solution.py:1254
  171.6 46.5 %collective-permute-start.3 = (bf16[512,512]{1,0:T(8,128)(2,1)S(1)}, bf16[512,512]{1,0:T(8,128)(2,1)S(1)}, u32[]{:S(2)}, u32[]{:S(2)}) collective-permute-start(bf16[512,512]{1,0:T(8,128)(2,1)S(1)} %get-tuple-element.117), channel_id=1, source_target_pairs={{0,8},{4,12},{8,16},{12,20},{16,24},{20,28},{24,0},{28,4},{1,9},{5... | collective-permute-start | bytes 1572872 | tf_op jit(solution)/shard_map/ppermute | solution.py:1254
  217.3 1.8 copy-start.24
  217.3 2.8 copy-start.27
  217.3 2.8 copy-start.44
  217.3 2.8 copy-start.46
  217.3 0.8 copy-start.33
  218.1 0.8 copy-start.35
  218.1 1.0 copy-start.37
  224.0 1.7 copy-start.25
  225.7 0.7 copy-start.40
  225.7 0.7 copy-start.42
  228.5 76.0 %copy-start.29 = (bf16[512,512]{1,0:T(8,128)(2,1)S(1)}, bf16[512,512]{1,0:T(8,128)(2,1)}, u32[]{:S(2)}) copy-start(bf16[512,512]{1,0:T(8,128)(2,1)} %get-tuple-element.95) | copy-start | bytes 1572868
  228.5 76.0 %copy-start.34 = (bf16[512,512]{1,0:T(8,128)(2,1)S(1)}, bf16[512,512]{1,0:T(8,128)(2,1)}, u32[]{:S(2)}) copy-start(bf16[512,512]{1,0:T(8,128)(2,1)} %copy-done.33) | copy-start | bytes 1572868
  228.5 76.0 %copy-start.36 = (bf16[512,512]{1,0:T(8,128)(2,1)S(1)}, bf16[512,512]{1,0:T(8,128)(2,1)}, u32[]{:S(2)}) copy-start(bf16[512,512]{1,0:T(8,128)(2,1)} %copy-done.35) | copy-start | bytes 1572868
  228.5 76.0 %copy-start.38 = (bf16[512,512]{1,0:T(8,128)(2,1)S(1)}, bf16[512,512]{1,0:T(8,128)(2,1)}, u32[]{:S(2)}) copy-start(bf16[512,512]{1,0:T(8,128)(2,1)} %copy-done.37) | copy-start | bytes 1572868
  304.5 2.1 copy-start.32
  304.5 2.8 copy-start.28
  307.4 1.5 copy-start.30
  307.4 2.4 copy-start.31
  307.4 3.1 %copy-start.1 = (bf16[160,1024]{1,0:T(8,128)(2,1)S(1)}, bf16[160,1024]{1,0:T(8,128)(2,1)}, u32[]{:S(2)}) copy-start(bf16[160,1024]{1,0:T(8,128)(2,1)} %param.18) | copy-start | bytes 983044

commit v7 on v6

--- a/solution.py
+++ b/solution.py
@@ -33,6 +33,7 @@
 
 MESH = pl.DeviceIdType.MESH
 BLOCK = 128
+UNROLL = 4
 PIECES = 1
 
 
@@ -82,7 +83,7 @@
 def forward_kernel(
     conv_ref, z_ref, proj_ref, keep_ref, dt_proj_ref, dt_bias_ref, skip_ref,
     y_ref, gated_ref, rate_ref, beta_ref, state_ref,
-    held_ref, rk, u, kept, query_rows,
+    held_ref, rk, u, kept, query_rows, fresh,
 ):
     width = conv_ref.shape[2]
     rank = dt_proj_ref.shape[0]
@@ -103,30 +104,42 @@
     rate_ref[0] = beta / (1.0 + beta * key_square)
     mask, pick = spread_mask(n), picker(n)
 
-    def chunk(j, held):
+    def states_of(j, held, rk, u, kept, fresh):
         base = pl.multiple_of(j * CHUNK, CHUNK)
-        rows = pl.ds(base, CHUNK)
-        _, conv, _ = prepare(base, rate_ref, conv_ref, keep_ref, rk, u, kept)
+        prepare(base, rate_ref, conv_ref, keep_ref, rk, u, kept)
         near_keys = shifted(keys, j)
-        held = list(held)
         for t in range(CHUNK):
             key = column(near_keys, t)
             key2 = key * key
             keep = jnp.broadcast_to(kept[t : t + 1, :], (n, LANES))
-            at = pl.ds(pl.multiple_of((base + t) * n, n), n)
+            at = slice(t * n, (t + 1) * n)
             for g in range(groups):
                 decay = keep - row(rk, t, g, n) * key2
                 held[g] = decay * held[g] + row(u, t, g, n) * key
-                state_ref[0, at, lane(g)] = held[g].astype(bf16)
-        block = state_ref[0, pl.ds(pl.multiple_of(base * n, span), span), :]
+                fresh[at, lane(g)] = held[g].astype(fresh.dtype)
+
+    def outputs_of(j, fresh):
+        base = pl.multiple_of(j * CHUNK, CHUNK)
+        rows = pl.ds(base, CHUNK)
+        block = fresh[...].astype(bf16)
+        state_ref[0, pl.ds(pl.multiple_of(base * n, span), span), :] = block
+        conv = conv_ref[0, rows, :].astype(f32)
         total = rows_dot(diagonal(query_rows[rows, :], mask, pick), block) + skip_ref[...] * conv
         y_ref[0, rows, :] = total
         z = z_ref[0, rows, :].astype(f32)
         gated_ref[0, rows, :] = (total * (z * jax.nn.sigmoid(z))).astype(bf16)
+
+    def step(i, held):
+        held = list(held)
+        for k in range(UNROLL):
+            states_of(i * UNROLL + k, held, rk[k], u[k], kept[k], fresh[k])
+            if k > 0:
+                outputs_of(i * UNROLL + k - 1, fresh[k - 1])
+        outputs_of(i * UNROLL + UNROLL - 1, fresh[UNROLL - 1])
         return tuple(held)
 
     start = tuple(held_ref[:, lane(g)] for g in range(groups))
-    end = lax.fori_loop(0, conv_ref.shape[1] // CHUNK, chunk, start)
+    end = lax.fori_loop(0, conv_ref.shape[1] // CHUNK // UNROLL, step, start)
     for g in range(groups):
         held_ref[:, lane(g)] = end[g]
 
@@ -265,6 +278,7 @@
     rank = dt_proj.shape[0]
     n = (proj.shape[0] - rank) // 2
     blocks, spec, across_spec, whole = specs_for(length, False)
+    span = CHUNK * n
     wide = spec(BLOCK, width)
     full = jax.ShapeDtypeStruct((seqs, length, width), f32)
     return pl.pallas_call(
@@ -276,15 +290,17 @@
         ],
         out_specs=[wide, wide, wide, wide, spec(BLOCK * n, width)],
         out_shape=[
-            full, jax.ShapeDtypeStruct((seqs, length, width), bf16), full, full,
+            full, jax.ShapeDtypeStruct((seqs, length, width), bf16),
+            pltpu.HBM((seqs, length, width), f32), pltpu.HBM((seqs, length, width), f32),
             pltpu.HBM((seqs, length * n, width), bf16),
         ],
         scratch_shapes=[
             pltpu.VMEM((n, width), f32),
-            pltpu.VMEM((CHUNK, width), f32),
-            pltpu.VMEM((CHUNK, width), f32),
-            pltpu.VMEM((CHUNK, LANES), f32),
+            [pltpu.VMEM((CHUNK, width), f32)] * UNROLL,
+            [pltpu.VMEM((CHUNK, width), f32)] * UNROLL,
+            [pltpu.VMEM((CHUNK, LANES), f32)] * UNROLL,
             pltpu.VMEM((BLOCK, n), f32),
+            [pltpu.VMEM((span, width), f32)] * UNROLL,
         ],
         compiler_params=pltpu.CompilerParams(vmem_limit_bytes=24 << 20),
         cost_estimate=pl.CostEstimate(flops=16_000_000_000, bytes_accessed=24 << 20, transcendentals=0),
@@ -377,8 +393,8 @@
 
 def front_kernel(
     x_ref, cot_ref, gain_ref, w_hbm, o_hbm,
-    xs_ref, cots_ref, gains_ref, own_half_ref, half_ref, parts_ref, own_ref, send_ref,
-    w_ref, o_ref, normed_ref, lhs, mixed, pairs, near, sends, recvs, local, part_sends, part_recvs, part_local,
+    xs_ref, inv_ref, cots_ref, gain_row_ref, own_half_ref, half_ref, parts_ref, own_ref, send_ref, send_more_ref,
+    gains_ref, w_ref, o_ref, normed_ref, lhs, mixed, pairs, near, sends, recvs, local, part_sends, part_recvs, part_local,
     pair_sends, pair_recvs, pair_local,
 ):
     me = lax.axis_index("shard")
@@ -427,6 +443,7 @@
         copy.wait()
     x_core.wait()
     gain = jnp.concatenate([gains_ref[lift * d : lift * d + 1, :] for d in range(4)], axis=1)
+    gain_row_ref[...] = jnp.broadcast_to(gain, gain_row_ref.shape)
     loads[0].wait()
 
     def piece(half, i):
@@ -458,6 +475,7 @@
                 at = pl.ds(pl.multiple_of(where + r * 16, 16), 16)
                 vals = xs_ref[seq, at, :].astype(f32)
                 inv = lax.rsqrt(jnp.mean(vals * vals, axis=1, keepdims=True) + EPS)
+                inv_ref[seq, at, :] = jnp.broadcast_to(inv, (16, LANES))
                 out = (vals * inv * gain).astype(bf16)
                 normed_ref[seq, at, :] = out
                 lhs[pl.ds(pl.multiple_of(seq * span + r * 16, 16), 16), :] = out
@@ -521,11 +539,16 @@
         near_sends.append(copy)
     near_sends[0].wait()
 
-    def to_send(t, carry):
-        send_ref[:, lanes(t)] = (partial(peer(2), t) + near[0, :, lanes(t)].astype(f32)).astype(bf16)
-        return carry
-
-    lax.fori_loop(0, width // tile, to_send, 0)
+    pieces = width // tile // 2
+    for first, ref in ((0, send_ref), (pieces, send_more_ref)):
+
+        def to_send(t, carry, first=first, ref=ref):
+            ref[:, lanes(t)] = (
+                partial(peer(2), first + t) + near[0, :, lanes(first + t)].astype(f32)
+            ).astype(bf16)
+            return carry
+
+        lax.fori_loop(0, pieces, to_send, 0)
     near_sends[1].wait()
 
     def to_own(t, carry):
@@ -561,18 +584,21 @@
     return pl.pallas_call(
         front_kernel,
         in_specs=[VMEM_SPEC] * 3 + [ANY_SPEC] * 2,
-        out_specs=[VMEM_SPEC] * 8,
+        out_specs=[VMEM_SPEC] * 10,
         out_shape=[
             jax.ShapeDtypeStruct((seqs, length, model), bf16),
+            jax.ShapeDtypeStruct((seqs, length, LANES), f32),
             jax.ShapeDtypeStruct((seqs, length, cols), bf16),
-            jax.ShapeDtypeStruct((8 * group, gain.shape[0]), f32),
+            jax.ShapeDtypeStruct((8, model), f32),
             jax.ShapeDtypeStruct((seqs, length, model // 2), bf16),
             jax.ShapeDtypeStruct((2, seqs, length, model // 2), bf16),
             jax.ShapeDtypeStruct((2, seqs, length, width), bf16),
             jax.ShapeDtypeStruct((tokens, width), f32),
-            jax.ShapeDtypeStruct((tokens, width), bf16),
+            jax.ShapeDtypeStruct((tokens, width // 2), bf16),
+            jax.ShapeDtypeStruct((tokens, width // 2), bf16),
         ],
         scratch_shapes=[
+            pltpu.VMEM((8 * group, gain.shape[0]), f32),
             pltpu.VMEM(w_in.shape, bf16),
             pltpu.VMEM(out_proj.shape, bf16),
             pltpu.VMEM((seqs, length, model), bf16),
@@ -683,10 +709,10 @@
     return pl.pallas_call(
         collect_kernel,
         in_specs=[VMEM_SPEC] * 6,
-        out_specs=[VMEM_SPEC] * 5,
+        out_specs=[VMEM_SPEC] * 3 + [ANY_SPEC, VMEM_SPEC],
         out_shape=[
             wide, wide, jax.ShapeDtypeStruct((4, tokens, grad_z.shape[1] // 4), bf16),
-            jax.ShapeDtypeStruct((2, 4) + last_norm.shape, bf16),
+            pltpu.HBM((2, 4) + last_norm.shape, bf16),
             jax.ShapeDtypeStruct(give.shape, bf16),
         ],
         scratch_shapes=[
@@ -831,10 +857,10 @@
 
 
 def finish_kernel(
-    gx_ref, gz_ref, small_keep_ref, small_give_ref, wz_ref, norm_hbm, w_hbm, x_ref, cot_ref, gain_ref,
-    gw_ref, gxp_ref, gdp_ref, rest_ref, dx_ref, ggain_ref,
+    gx_ref, gz_ref, small_keep_ref, small_give_ref, wz_ref, norm_hbm, w_hbm, x_ref, cot_ref, gain_ref, xs_ref, inv_ref,
+    gw_ref, gxp_ref, gdp_ref, gcw_ref, gcb_ref, gdb_ref, gsk_ref, dx_ref, ggain_ref,
     small_ref, norm_ref, w_ref, gx4, cols_ref, turned, xb_ref, sb_ref, small_got, x_in, s_in, lhs, pairs, near, g_hold, g_own, g_send, g_far,
-    h_send, h_cols, z_cols, s_own, gains, gain_near, gain_sum, gain_pair, gain_two, gain_in,
+    h_send, h_cols, z_cols, s_own, gains, gain_near, gain_sum, gain_in, unit_x,
     sends, recvs, far_sends, far_recvs, home_sends, home_recvs, local,
 ):
     me = lax.axis_index("shard")
@@ -926,19 +952,6 @@
     for at in (*range(PARTS + 1, PARTS + 1 + 2 * seqs), PARTS):
         home_start(at)
 
-    features = norm_ref.shape[2]
-
-    def turn(i, carry):
-        at = pl.ds(pl.multiple_of(i * tile, tile), tile)
-        for side_half in range(2):
-            for j in range(features // tile):
-                low = side_half * features + j * tile
-                turned[low : low + tile, at] = norm_ref[side_half, at, j * tile : (j + 1) * tile].T
-        return carry
-
-    load_norm.wait()
-    lax.fori_loop(0, 4 * tokens // tile, turn, 0)
-
     def far_copy(src, dst, kind, step):
         return across(src, dst, far_sends, far_recvs, kind * count + step, far(step))
 
@@ -964,9 +977,14 @@
             copy.wait_recv()
         quad_own[p].wait()
 
+        for at in range(0, 4 * tokens, tile):
+            turned[:, at : at + tile] = gx4[at : at + tile, cut(p)].T
+        wide = norm_ref.shape[2] // tile
+
         def rows_of(t, carry):
-            at = pl.ds(pl.multiple_of(t * tile, tile), tile)
-            xb_ref[at, cut(p)] = rows_dot(turned[at, :], gx4[:, cut(p)]).astype(bf16)
+            feature = pl.ds(pl.multiple_of(lax.rem(t, wide) * tile, tile), tile)
+            value = rows_dot(turned[...], norm_ref[t // wide, :, feature])
+            xb_ref[pl.ds(pl.multiple_of(t * tile, tile), tile), cut(p)] = value.astype(bf16).T
             return carry
 
         lax.fori_loop(0, xb_ref.shape[0] // tile, rows_of, 0)
@@ -989,12 +1007,18 @@
         for i, owner in enumerate((peer(3), peer(1), peer(2), me)):
             at = pl.ds(pl.multiple_of(seq * length + owner * rows, 16), rows)
             lhs[i * rows : (i + 1) * rows, :] = cols_ref[at, :]
+            here = pl.ds(pl.multiple_of(owner * rows, 16), rows)
+            inv = inv_ref[seq, here, :]
+            for low in range(0, model, LANES):
+                unit_x[i * rows : (i + 1) * rows, low : low + LANES] = xs_ref[seq, here, low : low + LANES].astype(f32) * inv
 
         def product(t, carry):
             value = outer_dot(lhs[...], w_ref[lanes(t), :])
             pairs[seq, :, lanes(t)] = value[: 2 * rows].astype(bf16)
             g_hold[:, lanes(t)] = value[2 * rows : 3 * rows]
             g_own[seq, :, lanes(t)] = value[3 * rows :]
+            terms = value * unit_x[:, lanes(t)]
+            gains[:, lanes(t)] += jnp.sum(terms.reshape(rows // 2, 8, tile), axis=0)
             return carry
 
         lax.fori_loop(0, model // tile, product, 0)
@@ -1018,6 +1042,8 @@
             h_send[p, :, q * part : (q + 1) * part] = total.astype(bf16)
         home_start(p)
 
+    gains[...] = jnp.zeros_like(gains)
+    load_norm.wait()
     x_part(0)
     load.wait()
     grads_of(0)
@@ -1030,6 +1056,16 @@
     grads_on(0)
     x_part(1)
     grads_of(1)
+    wide = model // 4
+
+    def gain_part(owner):
+        return gains.at[:, pl.ds(pl.multiple_of(owner * wide, LANES), wide)]
+
+    gain_sends = [
+        remote(gain_part(peer(hop)), gain_near.at[hop - 1], sends, recvs, 3 * PARTS + 2 + hop, hop) for hop in (1, 2, 3)
+    ]
+    for copy in gain_sends:
+        copy.start()
     for copy in s_sends:
         copy.wait_recv()
     total = sb_ref[mine].astype(f32)
@@ -1050,9 +1086,16 @@
     pass_on(0).start()
     home_sum(0)
     grads_on(1)
-
-
-    gains[...] = jnp.zeros_like(gains)
+    for copy in gain_sends:
+        copy.wait()
+    gain_sum[...] = gains[:, pl.ds(pl.multiple_of(me * wide, LANES), wide)] + gain_near[0] + gain_near[1] + gain_near[2]
+    gain_far = [
+        across(gain_sum, gain_in.at[step - 1], far_sends, far_recvs, (PARTS + 2) * count + step, ahead(step))
+        for step in range(1, count)
+    ]
+    for copy in gain_far:
+        copy.start()
+
 
     def finish_rows(seq):
         chip_send(seq).wait()
@@ -1062,12 +1105,10 @@
             grad = g_own[seq, at, :] + g_far[seq, at, :].astype(f32)
             vals = x_ref[seq, at, :].astype(f32)
             inv = lax.rsqrt(jnp.mean(vals * vals, axis=1, keepdims=True) + EPS)
-            scaled = grad * gain_ref[...]
+            scaled = grad * gain_ref[0:1, :]
             mean = jnp.mean(scaled * vals, axis=1, keepdims=True)
             out = inv * (scaled - vals * (inv * inv * mean))
             dx_ref[seq, at, :] = (cot_ref[seq, at, :].astype(f32) + out).astype(bf16)
-            terms = grad * (vals * inv)
-            gains[...] += terms[:8] + terms[8:]
             return carry
 
         lax.fori_loop(0, rows // 16, last, 0)
@@ -1078,34 +1119,6 @@
         spread[step - 1].wait_recv()
         pass_on(step).start()
     finish_rows(1)
-    gains[...] = jnp.broadcast_to(jnp.sum(gains[...], axis=0, keepdims=True), gains.shape)
-    wide = model // 4
-
-    def gain_part(owner):
-        return gains.at[:, pl.ds(pl.multiple_of(owner * wide, LANES), wide)]
-
-    gain_sends = [
-        remote(gain_part(peer(hop)), gain_near.at[hop - 1], sends, recvs, 3 * PARTS + 2 + hop, hop) for hop in (1, 2, 3)
-    ]
-    for copy in gain_sends:
-        copy.start()
-    for copy in gain_sends:
-        copy.wait()
-    gain_sum[...] = gains[:, pl.ds(pl.multiple_of(me * wide, LANES), wide)] + gain_near[0] + gain_near[1] + gain_near[2]
-    gain_copy = across(gain_sum, gain_pair, sends, recvs, 3 * PARTS + 6, other)
-    gain_copy.start()
-    gain_copy.wait()
-    gain_two[...] = gain_sum[...] + gain_pair[...]
-    gain_far = [far_copy(gain_two, gain_in.at[step - 1], PARTS + 2, step) for step in order]
-    for copy in gain_far:
-        copy.start()
-    for copy in gain_far:
-        copy.wait()
-    total = gain_two[...]
-    for step in order:
-        total = total + gain_in[step - 1]
-    ggain_ref[...] = total
-
     for at in range(PARTS + 1):
         home_wait(at)
 
@@ -1123,16 +1136,27 @@
         for low in range(0, 2 * width, quarter):
             gw_ref[:, low : low + quarter] = z_cols[:, low : low + quarter].astype(f32)
 
+    for copy in gain_far:
+        copy.wait()
+    total = gain_sum[...]
+    for step in range(1, count):
+        total = total + gain_in[step - 1]
+    ggain_ref[...] = jnp.broadcast_to(jnp.sum(total, axis=0, keepdims=True), total.shape)
     for step in range(height):
         pass_on(step).wait()
     lined = small_keep_ref.shape[1]
-    first, second = gxp_ref.shape[0], gxp_ref.shape[0] + gdp_ref.shape[0]
+    goals, start = [], 0
+    for ref in (gxp_ref, gdp_ref, gcw_ref, gcb_ref, gdb_ref, gsk_ref):
+        goals.append((ref, start, start + ref.shape[0]))
+        start += ref.shape[0]
     for at in range(count):
         low, high = at * lined, (at + 1) * lined
-        for ref, start, stop in ((gxp_ref, 0, first), (gdp_ref, first, second), (rest_ref, second, second + 8)):
-            a, b = max(low, start), min(high, stop)
+        if low < start:
+            value = small_ref[at % 2, at // 2].astype(f32)
+        for ref, begin, stop in goals:
+            a, b = max(low, begin), min(high, stop)
             if a < b:
-                ref[a - start : b - start, :] = small_ref[at % 2, at // 2, a - low : b - low, :].astype(f32)
+                ref[a - begin : b - begin, :] = value[a - low : b - low]
     small_send.wait_send()
     for p in range(PARTS):
         for copy in quad_sends(p) + x_sends(p):
@@ -1141,7 +1165,7 @@
         copy.wait_send()
 
 
-def finish(gx, gz, small_keep, small_give, wz, norm, w_in, x, cot, gain, tops):
+def finish(gx, gz, small_keep, small_give, wz, norm, w_in, x, cot, gain, xs, inv, tops):
     tokens, width = gx.shape
     height, lines, _ = small_keep.shape
     deep = wz.shape[0]
@@ -1153,15 +1177,17 @@
     quarter = width // 4
     kinds = (PARTS + 4) * count
     homes = PARTS + 1 + 2 * seqs
+    line = jax.ShapeDtypeStruct((1, width), f32)
     return pl.pallas_call(
         finish_kernel,
-        in_specs=[VMEM_SPEC] * 5 + [ANY_SPEC] * 2 + [VMEM_SPEC] * 3,
-        out_specs=[VMEM_SPEC] * 6,
+        in_specs=[VMEM_SPEC] * 5 + [ANY_SPEC] * 2 + [VMEM_SPEC] * 5,
+        out_specs=[VMEM_SPEC] * 9,
         out_shape=[
             jax.ShapeDtypeStruct((deep, 2 * width), f32),
             jax.ShapeDtypeStruct((tops[0], width), f32),
             jax.ShapeDtypeStruct((tops[1], width), f32),
-            jax.ShapeDtypeStruct((8, width), f32),
+            jax.ShapeDtypeStruct((KW, width), f32),
+            line, line, line,
             jax.ShapeDtypeStruct(x.shape, bf16),
             jax.ShapeDtypeStruct((8, wide), f32),
         ],
@@ -1171,7 +1197,7 @@
             pltpu.VMEM(w_in.shape, bf16),
             pltpu.VMEM((4 * tokens, quarter), bf16),
             pltpu.VMEM((tokens, 2 * width), bf16),
-            pltpu.VMEM((count * deep, 4 * tokens), bf16),
+            pltpu.VMEM((quarter // PARTS, 4 * tokens), bf16),
             pltpu.VMEM((count * deep, quarter), bf16),
             pltpu.VMEM((height, lines, width), bf16),
             pltpu.VMEM((height, lines, width), bf16),
@@ -1190,8 +1216,9 @@
             pltpu.VMEM((lines, width), bf16),
             pltpu.VMEM((8, model), f32),
             pltpu.VMEM((3, 8, wide), f32),
-            gain_tile, gain_tile, gain_tile,
-            pltpu.VMEM((other, 8, wide), f32),
+            gain_tile,
+            pltpu.VMEM((count - 1, 8, wide), f32),
+            pltpu.VMEM((4 * rows, model), f32),
             pltpu.SemaphoreType.DMA((3 * PARTS + 8 + 2 * seqs,)), pltpu.SemaphoreType.DMA((3 * PARTS + 8 + 2 * seqs,)),
             pltpu.SemaphoreType.DMA((kinds,)), pltpu.SemaphoreType.DMA((kinds,)),
             pltpu.SemaphoreType.DMA((homes,)), pltpu.SemaphoreType.DMA((2 * homes,)),
@@ -1200,7 +1227,7 @@
         compiler_params=group_params(8, 58 << 20),
         cost_estimate=cost(80),
         name="finish",
-    )(gx, gz, small_keep, small_give, wz, norm, w_in, x, cot, gain)
+    )(gx, gz, small_keep, small_give, wz, norm, w_in, x, cot, gain, xs, inv)
 
 
 def total_kernel(part_ref, out_ref, near, chip_sum, far, sends, recvs):
@@ -1291,10 +1318,9 @@
         odd = jnp.concatenate(cuts[1::2], axis=1)
         return jnp.where(side == 0, even, odd), jnp.where(side == 0, odd, even)
 
-    xs, cots, gains, own_half, half_norm, parts, gated_own, gated_send = front(
+    xs, inv, cots, gain, own_half, half_norm, parts, gated_own, gated_send, gated_more = front(
         block_input, out_grad, norm_gain, w_in, out_proj
     )
-    gain = gains[::8].reshape(1, -1)
     x_all = xs.reshape(tokens, model)
     cot = cots.reshape(tokens, -1)
     x_part, z_part = parts[0], parts[1]
@@ -1317,17 +1343,19 @@
     last_norm = lax.ppermute(own_half, "replica", [(i, i ^ 3) for i in range(count)])
     cot_got = lax.ppermute(cot, "replica", [(i, i ^ 1) for i in range(count)])
     proj = group_total(outer_dot(x_proj, conv_flat), 3)
-    gated_far = by_hop(after(gated_send, proj), 2)
+    gated_far = by_hop(gated_send, 2)
+    proj, gated_far = lax.optimization_barrier((proj, gated_far))
+    gated_rest = by_hop(after(gated_more, proj), 2)
     keep_lanes = jnp.broadcast_to(taps[1][:, :, None], (seqs, length, LANES))
     skip = d_skip.astype(f32)
     y_total, gated, rate, beta, states = recurrence_forward(
         conv_out, z_part, proj, keep_lanes, dt_proj, dt_bias.astype(f32)[None], skip[None]
     )
-    y_total, gated, gated_far, last_norm, cot_got = lax.optimization_barrier(
-        (y_total, gated, gated_far, last_norm, cot_got)
+    y_total, gated, gated_rest, last_norm, cot_got = lax.optimization_barrier(
+        (y_total, gated, gated_rest, last_norm, cot_got)
     )
     cot_both = jnp.concatenate([cot, cot_got], axis=0)
-    grad_gated = split(gated_own + gated_far.astype(f32))
+    grad_gated = split(gated_own + jnp.concatenate([gated_far, gated_rest], axis=1).astype(f32))
     z_vals = z_part.astype(f32)
     dy = grad_gated * jax.nn.silu(z_vals)
     grad_z = (grad_gated * y_total * silu_slope(z_vals)).astype(bf16).reshape(tokens, width)
@@ -1379,13 +1407,13 @@
     small_keep = jnp.where(side == 0, small[:, 0], small[:, 1])
     small_give = jnp.where(side == 0, small[:, 1], small[:, 0]).astype(bf16)
     top = x_proj.shape[0]
-    grad_w_in, grad_x_proj, grad_dt_proj, rest, input_grad, grad_gain = finish(
-        grad_x, grad_z, small_keep, small_give, grad_w_z, norms, w_in, block_input, out_grad, gain,
+    grad_w_in, grad_x_proj, grad_dt_proj, grad_conv_weight, conv_line, bias_line, skip_line, input_grad, grad_gain = finish(
+        grad_x, grad_z, small_keep, small_give, grad_w_z, norms, w_in, block_input, out_grad, gain, xs, inv,
         (top, rank),
     )
     return (
-        block_output, input_grad, grad_gain[0], grad_w_in, rest[:KW], rest[KW], grad_x_proj, grad_dt_proj,
-        rest[KW + 1], rest[KW + 2], grad_out_proj,
+        block_output, input_grad, grad_gain[0], grad_w_in, grad_conv_weight, conv_line[0], grad_x_proj, grad_dt_proj,
+        bias_line[0], skip_line[0], grad_out_proj,
     )
 
 

time: 311 us -> 301 us (0.968)
  Pallas kernels: 247 us -> 230 us
  local copies, waits for them, and re-layouts: 26.5 us -> 20.2 us
  starting transfers between devices: 11.5 us -> 17.7 us
  matrix products: 7.7 us -> 11.8 us
    pallas_call x1, Pallas kernels: 21.4 us -> 14.3 us  [recurrence_forward(): pl.pallas_call(forward_kernel, grid=(seqs, blocks), in_specs=[wide, wide,...]
    unnamed x110 -> x115, local copies, waits for them, and re-layouts: 19.4 us -> 12.7 us
    ppermute x1 -> x2, starting transfers between devices: 1.17 us -> 7.39 us  [by_hop(): return lax.ppermute(value, 'shard', [(i, i ^ hop) for i in range(4)])]
    pallas_call x1, Pallas kernels: 71.9 us -> 66.7 us  [finish(): pl.pallas_call(finish_kernel, in_specs=[VMEM_SPEC] * 5 + [ANY_SPEC] * 2 +...]
    pallas_call x2, Pallas kernels: 22.4 us -> 18.1 us  [group_total(): pl.pallas_call(total_kernel, in_specs=[VMEM_SPEC], out_specs=VMEM_SPEC, o...]
    dot_general x1, matrix products: 2.58 us -> 6.06 us  [body(): lax.dot_general(norms, grad_z_quad.reshape(4 * tokens, -1), (((1,), (0,))...]
    slice x3 -> x0, local copies, waits for them, and re-layouts: 3.46 us -> none  [the longest x1 1.48 us: body(): rest[KW + 2]]
  transfers between devices with their start and end apart: 6 -> 7, of which waited for: 0 -> 1; matrix products, arithmetic and copies ran while one was open for 2% -> 2% of each run, Pallas kernels for 26% -> 23%
where the time goes in v7:
time: 301 us; the launch traced here: 300 us
  Pallas kernels  230 us (76%)
  local copies, waits for them, and re-layouts  20.2 us (7%)
  starting transfers between devices  17.7 us (6%)
  other arithmetic  16.3 us (5%)
  matrix products  11.8 us (4%)
  waiting for transfers between devices  3.12 us (1%)
    pallas_call x1, Pallas kernels, finish(): pl.pallas_call(finish_kernel, in_specs=[VMEM_SPEC] * 5 + [ANY_SPEC] * 2 +...  66.7 us
    pallas_call x1, Pallas kernels, front(): pl.pallas_call(front_kernel, in_specs=[VMEM_SPEC] * 3 + [ANY_SPEC] * 2, o...  42.9 us
    pallas_call x1, Pallas kernels, recurrence_backward(): pl.pallas_call(backward_kernel, grid=(seqs, blocks), in_specs=[wide, wide...  36.1 us
    pallas_call x1, Pallas kernels, collect(): pl.pallas_call(collect_kernel, in_specs=[VMEM_SPEC] * 6, out_specs=[VMEM_...  28.9 us
    pallas_call x1, Pallas kernels, middle(): pl.pallas_call(middle_kernel, in_specs=[VMEM_SPEC] * 4 + [ANY_SPEC] * 2,...  23 us
    pallas_call x2, Pallas kernels, group_total(): pl.pallas_call(total_kernel, in_specs=[VMEM_SPEC], out_specs=VMEM_SPEC, o...  18.1 us
    pallas_call x1, Pallas kernels, recurrence_forward(): pl.pallas_call(forward_kernel, grid=(seqs, blocks), in_specs=[wide, wide,...  14.3 us
    unnamed x115, local copies, waits for them, and re-layouts  12.7 us
  transfers between devices with their start and end apart: 7, of which 1 were waited for; matrix products, arithmetic and copies ran while one was open for 2% of the time, Pallas kernels for 23%

profile of v7, /device:TPU:0, one launch (start us, length us, event | category | flops | bytes accessed | tf_op | source)
XLA Modules:
  0.0 300.4 jit_solution(3465735968858274075)
XLA Ops:
  0.6 0.0 copy-start
  0.7 0.7 broadcast_in_dim.12.gain_ref
  1.4 1.0 copy-done.4
  2.4 1.0 copy-done.5
  3.5 42.9 %front.1 = (bf16[2,256,2048]{2,1,0:T(8,128)(2,1)S(1)}, f32[2,256,128]{2,1,0:T(8,128)S(1)}, bf16[2,256,512]{2,1,0:T(8,128)(2,1)S(1)}, f32[8,2048]{1,0:T(8,128)S(1...) custom-call(bf16[2,64,2048]{2,1,0:T(8,128)(2,1)S(1)} %copy-done.4, ...), custom_call_target="tpu_custom_call" | custom-call | tf_op jit(solution)/shard_map/front/pallas_call | solution.py:584
  46.5 5.2 %collective-permute-start = (bf16[512,512]{1,0:T(8,128)(2,1)}, bf16[512,512]{1,0:T(8,128)(2,1)}, u32[]{:S(2)}, u32[]{:S(2)}) collective-permute-start(bf16[512,512]{1,0:T(8,128)(2,1)} %get-tuple-element.63), channel_id=1, source_target_pairs={{0,2},{1,3},{2,0},{3,1},{4,6},{5,7},{6,4},{7,5},{8,10},{9,11},{10,... | collective-permute-start | bytes 1572872 | tf_op jit(solution)/shard_map/ppermute | solution.py:1267
  51.7 1.5 collective-permute-start.3
  53.2 1.5 collective-permute-start.2
  54.7 0.1 compare_convert_fusion.2
  54.8 0.0 copy-start.34
  54.8 0.0 copy-start.36
  54.8 1.9 slice_bitcast_fusion
  56.8 0.0 copy-start.50
  56.8 2.7 fusion.12
  59.5 0.5 convolution_bitcast_fusion.part_ref
  60.0 9.2 %group_total.2.proj_ref = f32[160,512]{1,0:T(8,128)S(1)} custom-call(f32[160,512]{1,0:T(8,128)S(1)} %convolution_bitcast_fusion.part_ref), custom_call_target="tpu_custom_call" | custom-call | tf_op jit(solution)/shard_map/group_total/pallas_call | solution.py:1255
  69.3 2.2 collective-permute-start.1
  71.5 0.1 broadcast_in_dim.13.keep_ref
  71.6 14.3 %recurrence_forward.1 = (f32[2,256,1024]{2,1,0:T(8,128)S(1)}, bf16[2,256,1024]{2,1,0:T(8,128)(2,1)S(1)}, f32[2,256,1024]{2,1,0:T(8,128)}, f32[2,256,1024]{2,1,0:T(8,128)}, bf16[2,4096,1024]{2,1,0:T(8,128)(2,1)}) custom-call(bf16[2,256,1024]{2,1,0:T(8,128)(2,1)S(1)} %get-tuple-element.122.conv_ref, bf16[2,256,1024]{2,1,0:T(8,128)(2,1)S(1)} %get-tuple-element.133.z_ref, ...), custom_call_target="tpu_custom_call" | custom-call | flops 16000000000 | bytes 25165824 | tf_op jit(solution)/shard_map/recurrence_forward/pallas_call | solution.py:284
  85.9 3.1 %collective-permute-done.3 = bf16[512,512]{1,0:T(8,128)(2,1)} collective-permute-done((bf16[512,512]{1,0:T(8,128)(2,1)S(1)}, bf16[512,512]{1,0:T(8,128)(2,1)}, u32[]{:S(2)}, u32[]{:S(2)}) %collective-permute-start.3) | collective-permute-done | bytes 524320 | tf_op jit(solution)/shard_map/ppermute | solution.py:1344
  89.0 1.6 convert_add_fusion
  90.7 0.1 copy-done.19
  90.8 1.1 fusion.11
  91.9 0.1 broadcast_select_fusion
  92.0 1.9 copy-done.8
  93.9 28.9 %collect.1 = (bf16[512,2048]{1,0:T(8,128)(2,1)S(1)}, bf16[512,2048]{1,0:T(8,128)(2,1)S(1)}, bf16[4,512,256]{2,1,0:T(8,128)(2,1)S(1)}, bf16[2,4,512,1024]{3,2,1,0:T(8,128)(2,1)}, bf16[512,512]{1,0:T(8,128)(2,1)S(1)}) custom-call(bf16[512,512]{1,0:T(8,128)(2,1)S(1)} %get-tuple-element.136.keep_ref, bf16[512,512]{1,0:T(8,128)(2,1)S(1)} %get-tuple-element.135.give_ref, ...), custom_call_target="tpu_custom_call" | custom-call | flops 24999999488 | bytes 1048576 | tf_op jit(solution)/shard_map/collect/pallas_call | solution.py:709
  122.8 0.0 copy-start.2
  122.8 6.1 %bitcast_convert_fusion = bf16[2,1024,256]{2,1,0:T(8,128)(2,1)S(1)} fusion(bf16[2,4,512,1024]{3,2,1,0:T(8,128)(2,1)} %get-tuple-element.81, bf16[4,512,256]{2,1,0:T(8,128)(2,1)S(1)} %get-tuple-element.82), kind=kOutput, calls=%fused_computation.16 | convolution fusion | flops 2148007936 | bytes 10485760 | tf_op jit(solution)/shard_map/dot_general | solution.py:1369
  128.9 23.0 %middle.1 = (bf16[2,512,2048]{2,1,0:T(8,128)(2,1)S(1)}, bf16[2,64,2048]{2,1,0:T(8,128)(2,1)S(1)}, bf16[256,1024]{1,0:T(8,128)(2,1)S(1)}) custom-call(bf16[512,2048]{1,0:T(8,128)(2,1)S(1)} %get-tuple-element.78.keeps_ref, bf16[512,2048]{1,0:T(8,128)(2,1)S(1)} %get-tuple-element.79.gives_ref, bf16[512,512]{1,0:T(8,128)(2,1)S(1)} %get-tuple-element.80.got_ref, ...), custom_call_target="tpu_custom_call" | custom-call | flops 24999999488 | bytes 1048576 | tf_op jit(solution)/shard_map/middle/pallas_call | solution.py:833
  151.9 0.0 copy-start.15
  151.9 3.6 %convolution_convert_fusion = bf16[2048,512]{1,0:T(8,128)(2,1)S(1)} fusion(bf16[1024,2048]{1,0:T(8,128)(2,1)S(1)} %bitcast.95, bf16[512,512]{1,0:T(8,128)(2,1)} %collective-permute-done.3, bf16[512,512]{1,0:T(8,128)(2,1)S(1)} %bitcast.94), kind=kOutput, calls=%fused_computation | convolution fusion | flops 2150629376 | bytes 7340032 | tf_op jit(solution)/shard_map/dot_general | solution.py:23
  155.5 0.9 dynamic-slice_bitcast_fusion
  156.5 6.6 %collective-permute-start.6 = (bf16[512,512]{1,0:T(8,128)(2,1)S(1)}, bf16[512,512]{1,0:T(8,128)(2,1)S(1)}, u32[]{:S(2)}, u32[]{:S(2)}) collective-permute-start(bf16[512,512]{1,0:T(8,128)(2,1)S(1)} %get-tuple-element.129), channel_id=1, source_target_pairs={{0,24},{4,28},{8,0},{12,4},{16,8},{20,12},{24,16},{28,20},{1,25},{... | collective-permute-start | bytes 1572872 | tf_op jit(solution)/shard_map/ppermute | solution.py:1281
  163.0 0.2 collective-permute-start.5
  163.2 0.6 collective-permute-start.4
  163.8 36.1 %recurrence_backward.1 = (f32[2,256,1024]{2,1,0:T(8,128)S(1)}, bf16[2,256,1024]{2,1,0:T(8,128)(2,1)}, f32[160,512]{1,0:T(8,128)S(1)}, f32[128,1024]{1,0:T(8,128)...) custom-call(f32[2,256,1024]{2,1,0:T(8,128)S(1)} %copy-done.13, f32[2,256,1024]{2,1,0:T(8,128)S(1)} %copy-done.14, ...), custom_call_target="tpu_custom_call" | custom-call | flops 30000001024 | bytes 29360128 | tf_op jit(solution)/shard_map/recurrence_backward/pallas_call | solution.py:319
  199.9 8.9 %group_total.3 = f32[160,512]{1,0:T(8,128)S(1)} custom-call(f32[160,512]{1,0:T(8,128)S(1)} %get-tuple-element.92.part_ref), custom_call_target="tpu_custom_call" | custom-call | tf_op jit(solution)/shard_map/group_total/pallas_call | solution.py:1255
  208.9 0.8 copy-done.28
  209.7 0.2 copy-done.30
  209.8 1.2 fusion.18
  211.0 0.5 fusion.20
  211.5 0.3 copy-done.20
  211.9 3.3 %fusion.23 = (f32[1024]{0:T(1024)S(1)}, f32[1024]{0:T(1024)S(1)}, f32[1024]{0:T(1024)S(1)}, f32[1024]{0:T(1024)S(1)}, f32[1024]{0:T(1024)S(1)}, /*index=5*/f32[2,256,1024]{2,1,0:T(8,128)}) fusion(bf16[2,2,256,1024]{3,2,1,0:T(8,128)(2,1)S(1)} %copy-done.19, f32[2,256]{1,0:T(2,128)S(1)} %copy-done.41, f32[2,256,1024]{2,1,0:T(8,128)S(1)} %copy-done.17, ...), kind=kLoop, calls=%fused_computation.64 | loop fusion | flops 12577792 | bytes 13662208 | tf_op jit(solution)/shard_map/reduce_sum | solution.py:1387
  215.2 3.0 concatenate.11
  218.2 1.4 pad.29
  219.6 0.8 fusion.17.small_give_ref
  220.4 0.9 select_bitcast_fusion.small_keep_ref
  221.4 0.5 broadcast_multiply_fusion
  221.8 0.2 copy-done.35
  222.0 0.0 copy-done.37
  222.1 0.0 copy-done.39
  222.1 2.1 fusion.4
  224.2 66.7 %finish.1 = (f32[256,2048]{1,0:T(8,128)}, f32[160,1024]{1,0:T(8,128)}, f32[128,1024]{1,0:T(8,128)}, f32[4,1024]{1,0:T(4,128)}, f32[1,1024]{1,0:T(1,128)}, /*inde...) custom-call(bf16[512,1024]{1,0:T(8,128)(2,1)} %bitcast.101, ...), custom_call_target="tpu_custom_call" | custom-call | flops 80000000000 | bytes 1048576 | tf_op jit(solution)/shard_map/finish/pallas_call | solution.py:1181
  290.8 1.3 slice.90
  292.2 1.2 convert_add_fusion.1
  293.4 0.8 copy.40
  294.2 0.8 copy.41
  295.0 1.3 copy.42
  296.4 0.6 copy.43
  297.0 0.6 copy.44
  297.6 0.8 copy.45
  298.4 0.8 copy.46
  299.2 0.6 copy.47
  299.8 0.6 copy.48
  (100 shorter events, 0.2 us)
Async XLA Ops:
  0.6 58.9 %copy-start = (bf16[160,1024]{1,0:T(8,128)(2,1)S(1)}, bf16[160,1024]{1,0:T(8,128)(2,1)}, u32[]{:S(2)}) copy-start(bf16[160,1024]{1,0:T(8,128)(2,1)} %param.18) | copy-start | bytes 983044
  1.4 1.0 copy-start.4
  2.4 1.0 copy-start.5
  3.5 51.2 %copy-start.49 = (bf16[1024]{0:T(1024)(128)(2,1)S(1)}, bf16[1024]{0:T(1024)(128)(2,1)}, u32[]{:S(2)}) copy-start(bf16[1024]{0:T(1024)(128)(2,1)} %param.17) | copy-start | bytes 6148
  3.5 51.2 %copy-start.52 = (s32[2,256]{1,0:T(2,128)S(1)}, s32[2,256]{1,0:T(2,128)}, u32[]{:S(2)}) copy-start(s32[2,256]{1,0:T(2,128)} %param.13) | copy-start | bytes 6148
  3.5 51.3 %copy-start.44 = (bf16[4,1024]{1,0:T(4,128)(2,1)S(1)}, bf16[4,1024]{1,0:T(4,128)(2,1)}, u32[]{:S(2)}) copy-start(bf16[4,1024]{1,0:T(4,128)(2,1)} %param.16) | copy-start | bytes 24580
  46.4 10.3 %copy-start.6 = (bf16[2,256,2048]{2,1,0:T(8,128)(2,1)}, bf16[2,256,2048]{2,1,0:T(8,128)(2,1)S(1)}, u32[]{:S(2)}) copy-start(bf16[2,256,2048]{2,1,0:T(8,128)(2,1)S(1)} %get-tuple-element.83.xs_ref) | copy-start | bytes 6291460
  46.4 10.3 %copy-start.9 = (bf16[512,512]{1,0:T(8,128)(2,1)}, bf16[512,512]{1,0:T(8,128)(2,1)S(1)}, u32[]{:S(2)}) copy-start(bf16[512,512]{1,0:T(8,128)(2,1)S(1)} %get-tuple-element.68) | copy-start | bytes 1572868
  46.4 10.3 %copy-start.11 = (f32[2,256,128]{2,1,0:T(8,128)}, f32[2,256,128]{2,1,0:T(8,128)S(1)}, u32[]{:S(2)}) copy-start(f32[2,256,128]{2,1,0:T(8,128)S(1)} %get-tuple-element.99.inv_ref) | copy-start | bytes 786436
  46.4 10.3 %copy-start.12 = (f32[8,2048]{1,0:T(8,128)}, f32[8,2048]{1,0:T(8,128)S(1)}, u32[]{:S(2)}) copy-start(f32[8,2048]{1,0:T(8,128)S(1)} %get-tuple-element.98.gain_ref) | copy-start | bytes 196612
  46.5 22.9 %collective-permute-start = (bf16[512,512]{1,0:T(8,128)(2,1)}, bf16[512,512]{1,0:T(8,128)(2,1)}, u32[]{:S(2)}, u32[]{:S(2)}) collective-permute-start(bf16[512,512]{1,0:T(8,128)(2,1)} %get-tuple-element.63), channel_id=1, source_target_pairs={{0,2},{1,3},{2,0},{3,1},{4,6},{5,7},{6,4},{7,5},{8,10},{9,11},{10,... | collective-permute-start | bytes 1572872 | tf_op jit(solution)/shard_map/ppermute | solution.py:1267
  51.7 37.3 %collective-permute-start.3 = (bf16[512,512]{1,0:T(8,128)(2,1)S(1)}, bf16[512,512]{1,0:T(8,128)(2,1)}, u32[]{:S(2)}, u32[]{:S(2)}) collective-permute-start(bf16[512,512]{1,0:T(8,128)(2,1)S(1)} %bitcast.93), channel_id=1, source_target_pairs={{0,4},{4,0},{8,12},{12,8},{16,20},{20,16},{24,28},{28,24},{1,5},{5... | collective-permute-start | bytes 1572872 | tf_op jit(solution)/shard_map/ppermute | solution.py:1344
  53.2 35.8 %collective-permute-start.2 = (bf16[512,1024]{1,0:T(8,128)(2,1)}, bf16[512,1024]{1,0:T(8,128)(2,1)}, u32[]{:S(2)}, u32[]{:S(2)}) collective-permute-start(bf16[512,1024]{1,0:T(8,128)(2,1)} %bitcast.11.own_half_ref), channel_id=1, source_target_pairs={{0,12},{4,8},{8,4},{12,0},{16,28},{20,24},{24,20},{28,16},{1,13},{... | collective-permute-start | bytes 3145736 | tf_op jit(solution)/shard_map/ppermute | solution.py:1343
  54.8 2.0 copy-start.40
  54.8 2.0 copy-start.42
  54.8 2.0 copy-start.34
  54.8 2.0 copy-start.36
  54.8 2.0 copy-start.38
  56.7 2.8 copy-start.16
  56.8 2.7 copy-start.50
  56.8 2.7 copy-start.51
  59.5 12.1 %copy-start.10 = (bf16[128,1024]{1,0:T(8,128)(2,1)S(1)}, bf16[128,1024]{1,0:T(8,128)(2,1)}, u32[]{:S(2)}) copy-start(bf16[128,1024]{1,0:T(8,128)(2,1)} %dt_proj_ref.3) | copy-start | bytes 786436
  69.3 19.7 %collective-permute-start.1 = (bf16[512,512]{1,0:T(8,128)(2,1)}, bf16[512,512]{1,0:T(8,128)(2,1)S(1)}, u32[]{:S(2)}, u32[]{:S(2)}) collective-permute-start(bf16[512,512]{1,0:T(8,128)(2,1)} %copy-done.9), channel_id=1, source_target_pairs={{0,2},{1,3},{2,0},{3,1},{4,6},{5,7},{6,4},{7,5},{8,10},{9,11},{10,... | collective-permute-start | bytes 1572872 | tf_op jit(solution)/shard_map/ppermute | solution.py:1267
  71.6 17.4 %copy-start.22 = (f32[512,1024]{1,0:T(8,128)S(1)}, f32[512,1024]{1,0:T(8,128)}, u32[]{:S(2)}) copy-start(f32[512,1024]{1,0:T(8,128)} %get-tuple-element.72) | copy-start | bytes 6291460
  89.0 1.7 copy-start.19
  91.9 30.9 %copy-start.3 = (bf16[2,256,1024]{2,1,0:T(8,128)(2,1)}, bf16[2,256,1024]{2,1,0:T(8,128)(2,1)S(1)}, u32[]{:S(2)}) copy-start(bf16[2,256,1024]{2,1,0:T(8,128)(2,1)S(1)} %get-tuple-element.125) | copy-start | bytes 3145732
  91.9 2.0 copy-start.8
  122.8 6.1 %copy-start.2 = (bf16[4096,512]{1,0:T(8,128)(2,1)S(1)}, bf16[4096,512]{1,0:T(8,128)(2,1)}, u32[]{:S(2)}) copy-start(bf16[4096,512]{1,0:T(8,128)(2,1)} %o_hbm.3) | copy-start | bytes 12582916
  122.8 6.1 %copy-start.7 = (bf16[2,256,2048]{2,1,0:T(8,128)(2,1)S(1)}, bf16[2,256,2048]{2,1,0:T(8,128)(2,1)}, u32[]{:S(2)}) copy-start(bf16[2,256,2048]{2,1,0:T(8,128)(2,1)} %copy-done.6) | copy-start | bytes 6291460
  151.9 3.6 %copy-start.15 = (bf16[256,1024]{1,0:T(8,128)(2,1)}, bf16[256,1024]{1,0:T(8,128)(2,1)S(1)}, u32[]{:S(2)}) copy-start(bf16[256,1024]{1,0:T(8,128)(2,1)S(1)} %get-tuple-element.97.wz_ref) | copy-start | bytes 1572868
  155.5 8.3 %copy-start.13 = (f32[2,256,1024]{2,1,0:T(8,128)S(1)}, f32[2,256,1024]{2,1,0:T(8,128)}, u32[]{:S(2)}) copy-start(f32[2,256,1024]{2,1,0:T(8,128)} %get-tuple-element.88.rate_ref) | copy-start | bytes 6291460
  155.5 8.3 %copy-start.14 = (f32[2,256,1024]{2,1,0:T(8,128)S(1)}, f32[2,256,1024]{2,1,0:T(8,128)}, u32[]{:S(2)}) copy-start(f32[2,256,1024]{2,1,0:T(8,128)} %get-tuple-element.89.beta_ref) | copy-start | bytes 6291460
  156.5 52.4 %collective-permute-start.6 = (bf16[512,512]{1,0:T(8,128)(2,1)S(1)}, bf16[512,512]{1,0:T(8,128)(2,1)S(1)}, u32[]{:S(2)}, u32[]{:S(2)}) collective-permute-start(bf16[512,512]{1,0:T(8,128)(2,1)S(1)} %get-tuple-element.129), channel_id=1, source_target_pairs={{0,24},{4,28},{8,0},{12,4},{16,8},{20,12},{24,16},{28,20},{1,25},{... | collective-permute-start | bytes 1572872 | tf_op jit(solution)/shard_map/ppermute | solution.py:1281
  163.0 45.9 %collective-permute-start.5 = (bf16[512,512]{1,0:T(8,128)(2,1)S(1)}, bf16[512,512]{1,0:T(8,128)(2,1)S(1)}, u32[]{:S(2)}, u32[]{:S(2)}) collective-permute-start(bf16[512,512]{1,0:T(8,128)(2,1)S(1)} %get-tuple-element.130), channel_id=1, source_target_pairs={{0,16},{4,20},{8,24},{12,28},{16,0},{20,4},{24,8},{28,12},{1,17},{... | collective-permute-start | bytes 1572872 | tf_op jit(solution)/shard_map/ppermute | solution.py:1281
  163.2 45.7 %collective-permute-start.4 = (bf16[512,512]{1,0:T(8,128)(2,1)S(1)}, bf16[512,512]{1,0:T(8,128)(2,1)S(1)}, u32[]{:S(2)}, u32[]{:S(2)}) collective-permute-start(bf16[512,512]{1,0:T(8,128)(2,1)S(1)} %get-tuple-element.131), channel_id=1, source_target_pairs={{0,8},{4,12},{8,16},{12,20},{16,24},{20,28},{24,0},{28,4},{1,9},{5... | collective-permute-start | bytes 1572872 | tf_op jit(solution)/shard_map/ppermute | solution.py:1281
  208.8 2.7 copy-start.17
  208.8 3.0 %copy-start.20 = (f32[2,256,1024]{2,1,0:T(8,128)S(1)}, f32[2,256,1024]{2,1,0:T(8,128)}, u32[]{:S(2)}) copy-start(f32[2,256,1024]{2,1,0:T(8,128)} %get-tuple-element.123) | copy-start | bytes 6291460
  208.8 3.0 %copy-start.41 = (f32[2,256]{1,0:T(2,128)S(1)}, f32[2,256]{1,0:T(2,128)}, u32[]{:S(2)}) copy-start(f32[2,256]{1,0:T(2,128)} %copy-done.40) | copy-start | bytes 6148
  208.8 3.0 copy-start.43
  208.9 0.8 copy-start.28
  208.9 0.9 copy-start.30
  209.8 1.7 copy-start.32
  211.8 3.3 %copy-start.21 = (f32[160,1024]{1,0:T(8,128)S(1)}, f32[160,1024]{1,0:T(8,128)}, u32[]{:S(2)}) copy-start(f32[160,1024]{1,0:T(8,128)} %fusion.18) | copy-start | bytes 1966084
  219.6 1.8 copy-start.18
  221.4 0.7 copy-start.35
  221.4 0.7 copy-start.37
  221.4 0.7 copy-start.39
  224.2 68.0 %copy-start.24 = (bf16[512,512]{1,0:T(8,128)(2,1)S(1)}, bf16[512,512]{1,0:T(8,128)(2,1)}, u32[]{:S(2)}) copy-start(bf16[512,512]{1,0:T(8,128)(2,1)} %get-tuple-element.109) | copy-start | bytes 1572868
  224.2 68.0 %copy-start.29 = (bf16[512,512]{1,0:T(8,128)(2,1)S(1)}, bf16[512,512]{1,0:T(8,128)(2,1)}, u32[]{:S(2)}) copy-start(bf16[512,512]{1,0:T(8,128)(2,1)} %copy-done.28) | copy-start | bytes 1572868
  224.2 68.0 %copy-start.31 = (bf16[512,512]{1,0:T(8,128)(2,1)S(1)}, bf16[512,512]{1,0:T(8,128)(2,1)}, u32[]{:S(2)}) copy-start(bf16[512,512]{1,0:T(8,128)(2,1)} %copy-done.30) | copy-start | bytes 1572868
  224.2 68.0 %copy-start.33 = (bf16[512,512]{1,0:T(8,128)(2,1)S(1)}, bf16[512,512]{1,0:T(8,128)(2,1)}, u32[]{:S(2)}) copy-start(bf16[512,512]{1,0:T(8,128)(2,1)} %copy-done.32) | copy-start | bytes 1572868
  292.2 2.1 copy-start.27
  292.2 2.8 copy-start.23
  295.0 1.4 copy-start.45
  295.0 2.0 copy-start.48
  295.0 2.6 copy-start.25
  295.0 3.4 %copy-start.26 = (f32[128,1024]{1,0:T(8,128)S(1)}, f32[128,1024]{1,0:T(8,128)}, u32[]{:S(2)}) copy-start(f32[128,1024]{1,0:T(8,128)} %get-tuple-element.162) | copy-start | bytes 1572868
  295.0 5.4 %copy-start.1 = (bf16[160,1024]{1,0:T(8,128)(2,1)S(1)}, bf16[160,1024]{1,0:T(8,128)(2,1)}, u32[]{:S(2)}) copy-start(bf16[160,1024]{1,0:T(8,128)(2,1)} %param.18) | copy-start | bytes 983044
  296.4 2.8 copy-start.47
  296.4 3.4 %copy-start.46 = (f32[1,1024]{1,0:T(1,128)S(1)}, f32[1,1024]{1,0:T(1,128)}, u32[]{:S(2)}) copy-start(f32[1,1024]{1,0:T(1,128)} %get-tuple-element.108) | copy-start | bytes 12292

commit v8 on v7

--- a/solution.py
+++ b/solution.py
@@ -34,7 +34,7 @@
 MESH = pl.DeviceIdType.MESH
 BLOCK = 128
 UNROLL = 4
-PIECES = 1
+BACK_UNROLL = 4
 
 
 def lane(g):
@@ -147,7 +147,7 @@
 def backward_kernel(
     rate_ref, beta_ref, conv_ref, dy_ref, proj_ref, keep_ref, dt_proj_ref, state_ref, last_ref,
     gconv_ref, gdt_ref, gproj_ref, gdt_proj_ref, gdt_bias_ref, gskip_ref,
-    held_ref, grate, rk, u, dys, kept, key_rows, adj, adj_state, sums,
+    held_ref, grate, rk, u, dys, kept, key_rows, adj, adj_state, totals, lined,
 ):
     block_rows, width = rate_ref.shape[1:]
     rank = dt_proj_ref.shape[0]
@@ -168,36 +168,21 @@
     keys = proj_ref[rank : rank + n, :]
     queries = proj_ref[rank + n :, :]
     key_rows[...] = keys.T
-    mask, pick = spread_mask(n, CHUNK // PIECES), picker(n, CHUNK // PIECES)
-
-    spot = lax.broadcasted_iota(jnp.int32, (n, LANES), 1)
-    sums[...] = jnp.zeros_like(sums)
-
-    def chunk(step, held):
-        j = chunks - 1 - step
+    mask, pick = spread_mask(n), picker(n)
+
+    ones = jnp.ones((CHUNK, LANES), bf16)
+
+    def walk(j, held, rk, u, dys, kept, adj, adj_state, totals):
         base = pl.multiple_of(j * CHUNK, CHUNK)
         rows = pl.ds(base, CHUNK)
-        rate, conv, keeps = prepare(base, rate_ref, conv_ref, keep_ref, rk, u, kept)
+        prepare(base, rate_ref, conv_ref, keep_ref, rk, u, kept)
         dys[...] = dy_ref[0, rows, :]
         near_keys = shifted(keys, j)
         near_queries = shifted(queries, j)
-        held = list(held)
-        after = [state_ref[0, pl.ds(pl.multiple_of((base + CHUNK - 1) * n, n), n), lane(g)] for g in range(groups)]
-        found = [jnp.zeros((n, LANES), f32) for _ in range(3)]
-        def settle(p):
-            size = CHUNK // PIECES
-            part = slice(p * size, (p + 1) * size)
-            some = pl.ds(base + p * size, size)
-            key_block = key_rows[some, :]
-            w1 = rows_dot(diagonal(key_block, mask, pick), adj[p][...].astype(bf16))
-            w2 = rows_dot(diagonal(key_block * key_block, mask, pick), adj_state[p][...].astype(bf16))
-            for g in range(groups):
-                grate[some, lane(g)] = conv[part, lane(g)] * w1[:, lane(g)] - keeps[part] * w2[:, lane(g)]
-            gconv_ref[0, some, :] = rate[part] * w1
-
+        late = pl.ds(pl.multiple_of((base + CHUNK - 1) * n, n), n)
+        after = [state_ref[0, late, lane(g)] for g in range(groups)]
         for t in reversed(range(CHUNK)):
-            piece, place = t // (CHUNK // PIECES), t % (CHUNK // PIECES)
-            own = slice(place * n, (place + 1) * n)
+            own = slice(t * n, (t + 1) * n)
             key = column(near_keys, t)
             key2 = key * key
             query = column(near_queries, t)
@@ -215,21 +200,41 @@
                 if t == 0:
                     before = jnp.where(j == 0, last_ref[0, :, lane(g)], before)
                 cross = grad * before.astype(f32)
-                adj[piece][own, lane(g)] = grad
-                adj_state[piece][own, lane(g)] = cross
+                adj[own, lane(g)] = grad
+                adj_state[own, lane(g)] = cross
                 terms = (grad * row(u, t, g, n), cross * pace, after[g].astype(f32) * slope)
                 parts = [v if p is None else p + v for p, v in zip(parts, terms)]
                 after[g] = before
-            if place == 0:
-                settle(piece)
-            here = spot == base + t
-            found = [jnp.where(here, jnp.sum(p, axis=1, keepdims=True), f) for p, f in zip(parts, found)]
+            for i in range(3):
+                totals[i, own, :] = parts[i]
+
+    def settle(j, adj, adj_state, totals):
+        base = pl.multiple_of(j * CHUNK, CHUNK)
+        rows = pl.ds(base, CHUNK)
+        key_block = key_rows[rows, :]
+        w1 = rows_dot(diagonal(key_block, mask, pick), adj[...].astype(bf16))
+        w2 = rows_dot(diagonal(key_block * key_block, mask, pick), adj_state[...].astype(bf16))
         for i in range(3):
-            sums[i] += found[i]
+            lined[i, rows, :] = jnp.where(mask, outer_dot(ones, totals[i].astype(bf16)), 0.0)
+        keeps = keep_ref[0, rows, :]
+        for g in range(groups):
+            conv = conv_ref[0, rows, lane(g)].astype(f32)
+            grate[rows, lane(g)] = conv * w1[:, lane(g)] - keeps * w2[:, lane(g)]
+        gconv_ref[0, rows, :] = rate_ref[0, rows, :] * w1
+
+    def step(i, held):
+        held = list(held)
+        first = chunks - 1 - i * BACK_UNROLL
+        for k in range(BACK_UNROLL):
+            walk(first - k, held, rk[k], u[k], dys[k], kept[k], adj[k], adj_state[k], totals[k])
+            if k > 0:
+                settle(first - k + 1, adj[k - 1], adj_state[k - 1], totals[k - 1])
+        last = BACK_UNROLL - 1
+        settle(first - last, adj[last], adj_state[last], totals[last])
         return tuple(held)
 
     start = tuple(held_ref[:, lane(g)] for g in range(groups))
-    end = lax.fori_loop(0, chunks, chunk, start)
+    end = lax.fori_loop(0, chunks // BACK_UNROLL, step, start)
     for g in range(groups):
         held_ref[:, lane(g)] = end[g]
 
@@ -251,8 +256,8 @@
     gskip_ref[...] += jnp.sum(dy_ref[0] * conv_ref[0].astype(f32), axis=0, keepdims=True)
     gdt_proj_ref[...] += rows_dot(proj_ref[0:rank, :].astype(bf16), low)
     gproj_ref[0:rank, :] = outer_dot(dt_proj_ref[...], low)
-    gproj_ref[rank : rank + n, :] = sums[0] - 2.0 * keys * (sums[1] + self_term)
-    gproj_ref[rank + n :, :] = sums[2]
+    gproj_ref[rank : rank + n, :] = picked(pick, lined[0]) - 2.0 * keys * (picked(pick, lined[1]) + self_term)
+    gproj_ref[rank + n :, :] = picked(pick, lined[2])
 
 
 def specs_for(length, reverse):
@@ -335,16 +340,17 @@
         scratch_shapes=[
             pltpu.VMEM((n, width), f32),
             pltpu.VMEM((BLOCK, width), f32),
-            pltpu.VMEM((CHUNK, width), f32),
-            pltpu.VMEM((CHUNK, width), f32),
-            pltpu.VMEM((CHUNK, width), f32),
-            pltpu.VMEM((CHUNK, LANES), f32),
+            [pltpu.VMEM((CHUNK, width), f32)] * BACK_UNROLL,
+            [pltpu.VMEM((CHUNK, width), f32)] * BACK_UNROLL,
+            [pltpu.VMEM((CHUNK, width), f32)] * BACK_UNROLL,
+            [pltpu.VMEM((CHUNK, LANES), f32)] * BACK_UNROLL,
             pltpu.VMEM((BLOCK, n), f32),
-            [pltpu.VMEM((span // PIECES, width), f32)] * PIECES,
-            [pltpu.VMEM((span // PIECES, width), f32)] * PIECES,
-            pltpu.VMEM((3, n, BLOCK), f32),
+            [pltpu.VMEM((span, width), f32)] * BACK_UNROLL,
+            [pltpu.VMEM((span, width), f32)] * BACK_UNROLL,
+            [pltpu.VMEM((3, span, LANES), f32)] * BACK_UNROLL,
+            pltpu.VMEM((3, BLOCK, span), f32),
         ],
-        compiler_params=pltpu.CompilerParams(vmem_limit_bytes=28 << 20),
+        compiler_params=pltpu.CompilerParams(vmem_limit_bytes=36 << 20),
         cost_estimate=pl.CostEstimate(flops=30_000_000_000, bytes_accessed=28 << 20, transcendentals=0),
         name="recurrence_backward",
     )(rate, beta, conv, dy, proj, keep_lanes, dt_proj, states, states)
@@ -857,9 +863,9 @@
 
 
 def finish_kernel(
-    gx_ref, gz_ref, small_keep_ref, small_give_ref, wz_ref, norm_hbm, w_hbm, x_ref, cot_ref, gain_ref, xs_ref, inv_ref,
+    gx_ref, gz_ref, xp_ref, dp_ref, cw_ref, cb_ref, db_ref, sk_ref, wz_ref, norm_hbm, w_hbm, x_ref, cot_ref, gain_ref, xs_ref, inv_ref,
     gw_ref, gxp_ref, gdp_ref, gcw_ref, gcb_ref, gdb_ref, gsk_ref, dx_ref, ggain_ref,
-    small_ref, norm_ref, w_ref, gx4, cols_ref, turned, xb_ref, sb_ref, small_got, x_in, s_in, lhs, pairs, near, g_hold, g_own, g_send, g_far,
+    small_keep_ref, small_give_ref, small_ref, norm_ref, w_ref, gx4, cols_ref, turned, xb_ref, sb_ref, small_got, x_in, s_in, lhs, pairs, near, g_hold, g_own, g_send, g_far,
     h_send, h_cols, z_cols, s_own, gains, gain_near, gain_sum, gain_in, unit_x,
     sends, recvs, far_sends, far_recvs, home_sends, home_recvs, local,
 ):
@@ -906,7 +912,35 @@
     quad_own = [
         pltpu.make_async_copy(piece_of(member, p), spot_of(0, p), local.at[PARTS + 3 + 2 * seqs + p]) for p in range(PARTS)
     ]
-    for copy in quad_sends(0) + [small_send] + quad_sends(1) + quad_own:
+    for copy in quad_sends(0):
+        copy.start()
+    lined = small_keep_ref.shape[1]
+
+    def fill(at, put):
+        low, high, begin = at * lined, (at + 1) * lined, 0
+        for ref in (xp_ref, dp_ref, cw_ref, cb_ref, db_ref, sk_ref):
+            stop = begin + ref.shape[0]
+            a, b = max(low, begin), min(high, stop)
+            if a < b:
+                put(at // 2, slice(a - low, b - low), ref[a - begin : b - begin, :])
+            begin = stop
+        if high > begin:
+            a = max(low, begin)
+            put(at // 2, slice(a - low, lined), jnp.zeros((high - a, width), f32))
+
+    def keep_rows(at, rows_at, value):
+        small_keep_ref[at, rows_at, :] = value
+
+    for at in range(count):
+        pl.when(side == at % 2)(lambda at=at: fill(at, keep_rows))
+
+        @pl.when(side != at % 2)
+        def _(at=at):
+            values = []
+            fill(at, lambda where, rows_at, value: values.append(value))
+            small_give_ref[at // 2] = jnp.concatenate(values, axis=0).astype(bf16)
+
+    for copy in [small_send] + quad_sends(1) + quad_own:
         copy.start()
 
     def goal(slot):
@@ -1045,16 +1079,16 @@
     gains[...] = jnp.zeros_like(gains)
     load_norm.wait()
     x_part(0)
-    load.wait()
-    grads_of(0)
     small_send.wait_recv()
     for at in range(height):
         sb_ref[at] = (small_keep_ref[at] + small_got[at].astype(f32)).astype(bf16)
     s_sends = [far_copy(sb_ref.at[block(step)], s_in.at[step - 1], PARTS, step) for step in order]
     for copy in s_sends:
         copy.start()
+    load.wait()
+    grads_of(0)
+    x_part(1)
     grads_on(0)
-    x_part(1)
     grads_of(1)
     wide = model // 4
 
@@ -1144,7 +1178,6 @@
     ggain_ref[...] = jnp.broadcast_to(jnp.sum(total, axis=0, keepdims=True), total.shape)
     for step in range(height):
         pass_on(step).wait()
-    lined = small_keep_ref.shape[1]
     goals, start = [], 0
     for ref in (gxp_ref, gdp_ref, gcw_ref, gcb_ref, gdb_ref, gsk_ref):
         goals.append((ref, start, start + ref.shape[0]))
@@ -1165,9 +1198,10 @@
         copy.wait_send()
 
 
-def finish(gx, gz, small_keep, small_give, wz, norm, w_in, x, cot, gain, xs, inv, tops):
+def finish(gx, gz, smalls, wz, norm, w_in, x, cot, gain, xs, inv):
     tokens, width = gx.shape
-    height, lines, _ = small_keep.shape
+    height = lax.axis_size("replica") // 2
+    lines = -(-sum(value.shape[0] for value in smalls) // (16 * height)) * 8
     deep = wz.shape[0]
     seqs, rows, model = x.shape
     wide = model // 4
@@ -1180,18 +1214,20 @@
     line = jax.ShapeDtypeStruct((1, width), f32)
     return pl.pallas_call(
         finish_kernel,
-        in_specs=[VMEM_SPEC] * 5 + [ANY_SPEC] * 2 + [VMEM_SPEC] * 5,
+        in_specs=[VMEM_SPEC] * 9 + [ANY_SPEC] * 2 + [VMEM_SPEC] * 5,
         out_specs=[VMEM_SPEC] * 9,
         out_shape=[
             jax.ShapeDtypeStruct((deep, 2 * width), f32),
-            jax.ShapeDtypeStruct((tops[0], width), f32),
-            jax.ShapeDtypeStruct((tops[1], width), f32),
+            jax.ShapeDtypeStruct(smalls[0].shape, f32),
+            jax.ShapeDtypeStruct(smalls[1].shape, f32),
             jax.ShapeDtypeStruct((KW, width), f32),
             line, line, line,
             jax.ShapeDtypeStruct(x.shape, bf16),
             jax.ShapeDtypeStruct((8, wide), f32),
         ],
         scratch_shapes=[
+            pltpu.VMEM((height, lines, width), f32),
+            pltpu.VMEM((height, lines, width), bf16),
             pltpu.VMEM((2, height, lines, width), bf16),
             pltpu.VMEM(norm.shape, bf16),
             pltpu.VMEM(w_in.shape, bf16),
@@ -1227,7 +1263,7 @@
         compiler_params=group_params(8, 58 << 20),
         cost_estimate=cost(80),
         name="finish",
-    )(gx, gz, small_keep, small_give, wz, norm, w_in, x, cot, gain, xs, inv)
+    )(gx, gz, *smalls, wz, norm, w_in, x, cot, gain, xs, inv)
 
 
 def total_kernel(part_ref, out_ref, near, chip_sum, far, sends, recvs):
@@ -1398,18 +1434,9 @@
         grad_x = grad_x + conv_w[j] * ahead
     grad_x = grad_x.astype(bf16).reshape(tokens, width)
 
-    small = jnp.concatenate(
-        [grad_x_proj, grad_dt_proj, grad_conv_weight, grad_conv_bias[None], grad_dt_bias, grad_d_skip]
-    )
-    unit = 8 * count
-    padded = -(-small.shape[0] // unit) * unit
-    small = jnp.pad(small, ((0, padded - small.shape[0]), (0, 0))).reshape(height, 2, -1, width)
-    small_keep = jnp.where(side == 0, small[:, 0], small[:, 1])
-    small_give = jnp.where(side == 0, small[:, 1], small[:, 0]).astype(bf16)
-    top = x_proj.shape[0]
+    smalls = (grad_x_proj, grad_dt_proj, grad_conv_weight, grad_conv_bias[None], grad_dt_bias, grad_d_skip)
     grad_w_in, grad_x_proj, grad_dt_proj, grad_conv_weight, conv_line, bias_line, skip_line, input_grad, grad_gain = finish(
-        grad_x, grad_z, small_keep, small_give, grad_w_z, norms, w_in, block_input, out_grad, gain, xs, inv,
-        (top, rank),
+        grad_x, grad_z, smalls, grad_w_z, norms, w_in, block_input, out_grad, gain, xs, inv
     )
     return (
         block_output, input_grad, grad_gain[0], grad_w_in, grad_conv_weight, conv_line[0], grad_x_proj, grad_dt_proj,

time: 301 us -> 289 us (0.960)
  Pallas kernels: 230 us -> 219 us
  local copies, waits for them, and re-layouts: 20.2 us -> 13.3 us
  waiting for transfers between devices: 3.12 us -> 9.46 us
    pallas_call x1, Pallas kernels: 36.1 us -> 28.3 us  [recurrence_backward(): pl.pallas_call(backward_kernel, grid=(seqs, blocks), in_specs=[wide, wide...]
    ppermute x3, waiting for transfers between devices: 0.01 us -> 6.36 us  [far_send(): lax.ppermute(out, 'replica', [(i, (i + 2 * step) % count) for i in range(...]
    pallas_call x1, Pallas kernels: 66.7 us -> 63.4 us  [finish(): pl.pallas_call(finish_kernel, in_specs=[VMEM_SPEC] * 9 + [ANY_SPEC] * 2 +...]
    unnamed x115 -> x103, local copies, waits for them, and re-layouts: 12.7 us -> 11 us
  transfers between devices with their start and end apart: 7 -> 7, of which waited for: 1 -> 2; matrix products, arithmetic and copies ran while one was open for 2% -> 2% of each run, Pallas kernels for 23% -> 21%
where the time goes in v8:
time: 289 us; the launch traced here: 287 us
  Pallas kernels  219 us (76%)
  starting transfers between devices  17.8 us (6%)
  other arithmetic  14.7 us (5%)
  local copies, waits for them, and re-layouts  13.3 us (5%)
  matrix products  11.9 us (4%)
  waiting for transfers between devices  9.46 us (3%)
    pallas_call x1, Pallas kernels, finish(): pl.pallas_call(finish_kernel, in_specs=[VMEM_SPEC] * 9 + [ANY_SPEC] * 2 +...  63.4 us
    pallas_call x1, Pallas kernels, front(): pl.pallas_call(front_kernel, in_specs=[VMEM_SPEC] * 3 + [ANY_SPEC] * 2, o...  42.9 us
    pallas_call x1, Pallas kernels, collect(): pl.pallas_call(collect_kernel, in_specs=[VMEM_SPEC] * 6, out_specs=[VMEM_...  28.9 us
    pallas_call x1, Pallas kernels, recurrence_backward(): pl.pallas_call(backward_kernel, grid=(seqs, blocks), in_specs=[wide, wide...  28.3 us
    pallas_call x1, Pallas kernels, middle(): pl.pallas_call(middle_kernel, in_specs=[VMEM_SPEC] * 4 + [ANY_SPEC] * 2,...  23 us
    pallas_call x2, Pallas kernels, group_total(): pl.pallas_call(total_kernel, in_specs=[VMEM_SPEC], out_specs=VMEM_SPEC, o...  18.1 us
    pallas_call x1, Pallas kernels, recurrence_forward(): pl.pallas_call(forward_kernel, grid=(seqs, blocks), in_specs=[wide, wide,...  14.3 us
    unnamed x103, local copies, waits for them, and re-layouts  11 us
  transfers between devices with their start and end apart: 7, of which 2 were waited for; matrix products, arithmetic and copies ran while one was open for 2% of the time, Pallas kernels for 21%

profile of v8, /device:TPU:0, one launch (start us, length us, event | category | flops | bytes accessed | tf_op | source)
XLA Modules:
  0.0 287.2 jit_solution(5890365472905025526)
XLA Ops:
  0.6 0.0 copy-start
  0.7 0.7 broadcast_in_dim.12.gain_ref
  1.4 1.0 copy-done.4
  2.4 1.0 copy-done.5
  3.5 42.9 %front.1 = (bf16[2,256,2048]{2,1,0:T(8,128)(2,1)S(1)}, f32[2,256,128]{2,1,0:T(8,128)S(1)}, bf16[2,256,512]{2,1,0:T(8,128)(2,1)S(1)}, f32[8,2048]{1,0:T(8,128)S(1...) custom-call(bf16[2,64,2048]{2,1,0:T(8,128)(2,1)S(1)} %copy-done.4, ...), custom_call_target="tpu_custom_call" | custom-call | tf_op jit(solution)/shard_map/front/pallas_call | solution.py:590
  46.4 0.0 copy-start.9
  46.4 0.0 copy-start.11
  46.4 5.2 %collective-permute-start = (bf16[512,512]{1,0:T(8,128)(2,1)}, bf16[512,512]{1,0:T(8,128)(2,1)}, u32[]{:S(2)}, u32[]{:S(2)}) collective-permute-start(bf16[512,512]{1,0:T(8,128)(2,1)} %get-tuple-element.63), channel_id=1, source_target_pairs={{0,2},{1,3},{2,0},{3,1},{4,6},{5,7},{6,4},{7,5},{8,10},{9,11},{10,... | collective-permute-start | bytes 1572872 | tf_op jit(solution)/shard_map/ppermute | solution.py:1303
  51.7 1.5 collective-permute-start.3
  53.2 1.5 collective-permute-start.2
  54.7 0.1 compare_convert_fusion.2
  54.7 0.0 copy-start.36
  54.8 0.0 copy-start.30
  54.8 0.0 copy-start.32
  54.8 1.9 slice_bitcast_fusion
  56.8 0.0 copy-start.44
  56.8 0.0 copy-start.45
  56.8 2.7 fusion.12
  59.5 0.5 convolution_bitcast_fusion.part_ref
  60.0 9.2 %group_total.2.proj_ref = f32[160,512]{1,0:T(8,128)S(1)} custom-call(f32[160,512]{1,0:T(8,128)S(1)} %convolution_bitcast_fusion.part_ref), custom_call_target="tpu_custom_call" | custom-call | tf_op jit(solution)/shard_map/group_total/pallas_call | solution.py:1291
  69.3 2.2 collective-permute-start.1
  71.5 0.1 broadcast_in_dim.13.keep_ref
  71.6 14.3 %recurrence_forward.1 = (f32[2,256,1024]{2,1,0:T(8,128)S(1)}, bf16[2,256,1024]{2,1,0:T(8,128)(2,1)S(1)}, f32[2,256,1024]{2,1,0:T(8,128)}, f32[2,256,1024]{2,1,0:T(8,128)}, bf16[2,4096,1024]{2,1,0:T(8,128)(2,1)}) custom-call(bf16[2,256,1024]{2,1,0:T(8,128)(2,1)S(1)} %get-tuple-element.122.conv_ref, bf16[2,256,1024]{2,1,0:T(8,128)(2,1)S(1)} %get-tuple-element.133.z_ref, ...), custom_call_target="tpu_custom_call" | custom-call | flops 16000000000 | bytes 25165824 | tf_op jit(solution)/shard_map/recurrence_forward/pallas_call | solution.py:289
  85.9 3.1 %collective-permute-done.3 = bf16[512,512]{1,0:T(8,128)(2,1)} collective-permute-done((bf16[512,512]{1,0:T(8,128)(2,1)S(1)}, bf16[512,512]{1,0:T(8,128)(2,1)}, u32[]{:S(2)}, u32[]{:S(2)}) %collective-permute-start.3) | collective-permute-done | bytes 524320 | tf_op jit(solution)/shard_map/ppermute | solution.py:1380
  89.0 0.1 broadcast_select_fusion
  89.1 1.5 convert_add_fusion
  90.6 0.3 copy-done.21
  90.8 1.1 fusion.11
  92.0 0.5 copy-done.8
  92.4 28.9 %collect.1 = (bf16[512,2048]{1,0:T(8,128)(2,1)S(1)}, bf16[512,2048]{1,0:T(8,128)(2,1)S(1)}, bf16[4,512,256]{2,1,0:T(8,128)(2,1)S(1)}, bf16[2,4,512,1024]{3,2,1,0:T(8,128)(2,1)}, bf16[512,512]{1,0:T(8,128)(2,1)S(1)}) custom-call(bf16[512,512]{1,0:T(8,128)(2,1)S(1)} %get-tuple-element.136.keep_ref, bf16[512,512]{1,0:T(8,128)(2,1)S(1)} %get-tuple-element.135.give_ref, ...), custom_call_target="tpu_custom_call" | custom-call | flops 24999999488 | bytes 1048576 | tf_op jit(solution)/shard_map/collect/pallas_call | solution.py:715
  121.3 6.1 %bitcast_convert_fusion = bf16[2,1024,256]{2,1,0:T(8,128)(2,1)S(1)} fusion(bf16[2,4,512,1024]{3,2,1,0:T(8,128)(2,1)} %get-tuple-element.81, bf16[4,512,256]{2,1,0:T(8,128)(2,1)S(1)} %get-tuple-element.82), kind=kOutput, calls=%fused_computation.16 | convolution fusion | flops 2148007936 | bytes 10485760 | tf_op jit(solution)/shard_map/dot_general | solution.py:1405
  127.4 23.0 %middle.1 = (bf16[2,512,2048]{2,1,0:T(8,128)(2,1)S(1)}, bf16[2,64,2048]{2,1,0:T(8,128)(2,1)S(1)}, bf16[256,1024]{1,0:T(8,128)(2,1)S(1)}) custom-call(bf16[512,2048]{1,0:T(8,128)(2,1)S(1)} %get-tuple-element.78.keeps_ref, bf16[512,2048]{1,0:T(8,128)(2,1)S(1)} %get-tuple-element.79.gives_ref, bf16[512,512]{1,0:T(8,128)(2,1)S(1)} %get-tuple-element.80.got_ref, ...), custom_call_target="tpu_custom_call" | custom-call | flops 24999999488 | bytes 1048576 | tf_op jit(solution)/shard_map/middle/pallas_call | solution.py:839
  150.4 3.7 %convolution_convert_fusion = bf16[2048,512]{1,0:T(8,128)(2,1)S(1)} fusion(bf16[1024,2048]{1,0:T(8,128)(2,1)S(1)} %bitcast.74, bf16[512,512]{1,0:T(8,128)(2,1)} %collective-permute-done.3, bf16[512,512]{1,0:T(8,128)(2,1)S(1)} %bitcast.73), kind=kOutput, calls=%fused_computation | convolution fusion | flops 2150629376 | bytes 7340032 | tf_op jit(solution)/shard_map/dot_general | solution.py:23
  154.1 0.2 dynamic-slice_bitcast_fusion
  154.3 6.6 %collective-permute-start.6 = (bf16[512,512]{1,0:T(8,128)(2,1)S(1)}, bf16[512,512]{1,0:T(8,128)(2,1)S(1)}, u32[]{:S(2)}, u32[]{:S(2)}) collective-permute-start(bf16[512,512]{1,0:T(8,128)(2,1)S(1)} %get-tuple-element.129), channel_id=1, source_target_pairs={{0,24},{4,28},{8,0},{12,4},{16,8},{20,12},{24,16},{28,20},{1,25},{... | collective-permute-start | bytes 1572872 | tf_op jit(solution)/shard_map/ppermute | solution.py:1317
  160.9 0.2 collective-permute-start.5
  161.1 0.6 collective-permute-start.4
  161.7 28.3 %recurrence_backward.1 = (f32[2,256,1024]{2,1,0:T(8,128)S(1)}, bf16[2,256,1024]{2,1,0:T(8,128)(2,1)}, f32[160,512]{1,0:T(8,128)S(1)}, f32[128,1024]{1,0:T(8,128)...) custom-call(f32[2,256,1024]{2,1,0:T(8,128)S(1)} %copy-done.13, f32[2,256,1024]{2,1,0:T(8,128)S(1)} %copy-done.14, ...), custom_call_target="tpu_custom_call" | custom-call | flops 30000001024 | bytes 29360128 | tf_op jit(solution)/shard_map/recurrence_backward/pallas_call | solution.py:324
  190.1 0.8 copy-done.15
  190.9 8.9 %group_total.3 = f32[160,512]{1,0:T(8,128)S(1)} custom-call(f32[160,512]{1,0:T(8,128)S(1)} %get-tuple-element.92.part_ref), custom_call_target="tpu_custom_call" | custom-call | tf_op jit(solution)/shard_map/group_total/pallas_call | solution.py:1291
  199.8 0.0 copy-start.35
  199.8 0.0 copy-start.37
  199.8 6.3 %collective-permute-done.5 = bf16[512,512]{1,0:T(8,128)(2,1)S(1)} collective-permute-done((bf16[512,512]{1,0:T(8,128)(2,1)S(1)}, bf16[512,512]{1,0:T(8,128)(2,1)S(1)}, u32[]{:S(2)}, u32[]{:S(2)}) %collective-permute-start.5) | collective-permute-done | bytes 524320 | tf_op jit(solution)/shard_map/ppermute | solution.py:1317
  206.2 1.2 fusion.17.xp_ref
  207.4 0.5 fusion.19
  207.9 3.0 %fusion.22 = (f32[1024]{0:T(1024)}, f32[1024]{0:T(1024)S(1)}, f32[1024]{0:T(1024)S(1)}, f32[1024]{0:T(1024)S(1)}, f32[1024]{0:T(1024)S(1)}, /*index=5*/f32[2,256,1024]{2,1,0:T(8,128)S(1)}) fusion(bf16[2,2,256,1024]{3,2,1,0:T(8,128)(2,1)S(1)} %copy-done.21, f32[2,256]{1,0:T(2,128)S(1)} %copy-done.37, f32[2,256,1024]{2,1,0:T(8,128)S(1)} %copy-done.20, ...), kind=kLoop, calls=%fused_computation.60 | loop fusion | flops 12577792 | bytes 13662208 | tf_op jit(solution)/shard_map/reduce_sum | solution.py:1423
  210.9 0.5 broadcast_multiply_fusion
  211.4 0.2 copy-done.29
  211.6 0.0 copy-done.31
  211.6 0.0 copy-done.33
  211.6 2.1 fusion.4
  213.7 0.6 pad_maximum_fusion.cw_ref
  214.4 63.4 %finish.1 = (f32[256,2048]{1,0:T(8,128)}, f32[160,1024]{1,0:T(8,128)}, f32[128,1024]{1,0:T(8,128)}, f32[4,1024]{1,0:T(4,128)}, f32[1,1024]{1,0:T(1,128)}, /*inde...) custom-call(bf16[512,1024]{1,0:T(8,128)(2,1)} %bitcast.78, ...), custom_call_target="tpu_custom_call" | custom-call | flops 80000000000 | bytes 1048576 | tf_op jit(solution)/shard_map/finish/pallas_call | solution.py:1215
  277.7 1.3 slice.80
  279.0 1.2 convert_add_fusion.1
  280.2 0.8 copy.35
  281.0 0.8 copy.36
  281.9 1.3 copy.37
  283.2 0.6 copy.38
  283.8 0.6 copy.39
  284.4 0.8 copy.40
  285.2 0.8 copy.41
  286.0 0.6 copy.42
  286.6 0.6 copy.43
  (85 shorter events, 0.2 us)
Async XLA Ops:
  0.6 58.9 %copy-start = (bf16[160,1024]{1,0:T(8,128)(2,1)S(1)}, bf16[160,1024]{1,0:T(8,128)(2,1)}, u32[]{:S(2)}) copy-start(bf16[160,1024]{1,0:T(8,128)(2,1)} %param.18) | copy-start | bytes 983044
  1.4 1.0 copy-start.4
  2.4 1.0 copy-start.5
  3.5 51.2 %copy-start.43 = (bf16[1024]{0:T(1024)(128)(2,1)S(1)}, bf16[1024]{0:T(1024)(128)(2,1)}, u32[]{:S(2)}) copy-start(bf16[1024]{0:T(1024)(128)(2,1)} %param.17) | copy-start | bytes 6148
  3.5 51.2 %copy-start.46 = (s32[2,256]{1,0:T(2,128)S(1)}, s32[2,256]{1,0:T(2,128)}, u32[]{:S(2)}) copy-start(s32[2,256]{1,0:T(2,128)} %param.13) | copy-start | bytes 6148
  3.5 51.3 %copy-start.38 = (bf16[4,1024]{1,0:T(4,128)(2,1)S(1)}, bf16[4,1024]{1,0:T(4,128)(2,1)}, u32[]{:S(2)}) copy-start(bf16[4,1024]{1,0:T(4,128)(2,1)} %param.16) | copy-start | bytes 24580
  46.4 10.3 %copy-start.6 = (bf16[2,256,2048]{2,1,0:T(8,128)(2,1)}, bf16[2,256,2048]{2,1,0:T(8,128)(2,1)S(1)}, u32[]{:S(2)}) copy-start(bf16[2,256,2048]{2,1,0:T(8,128)(2,1)S(1)} %get-tuple-element.83.xs_ref) | copy-start | bytes 6291460
  46.4 10.3 %copy-start.9 = (bf16[512,512]{1,0:T(8,128)(2,1)}, bf16[512,512]{1,0:T(8,128)(2,1)S(1)}, u32[]{:S(2)}) copy-start(bf16[512,512]{1,0:T(8,128)(2,1)S(1)} %get-tuple-element.68) | copy-start | bytes 1572868
  46.4 10.3 %copy-start.11 = (f32[2,256,128]{2,1,0:T(8,128)}, f32[2,256,128]{2,1,0:T(8,128)S(1)}, u32[]{:S(2)}) copy-start(f32[2,256,128]{2,1,0:T(8,128)S(1)} %get-tuple-element.99.inv_ref) | copy-start | bytes 786436
  46.4 10.3 %copy-start.12 = (f32[8,2048]{1,0:T(8,128)}, f32[8,2048]{1,0:T(8,128)S(1)}, u32[]{:S(2)}) copy-start(f32[8,2048]{1,0:T(8,128)S(1)} %get-tuple-element.98.gain_ref) | copy-start | bytes 196612
  46.4 22.9 %collective-permute-start = (bf16[512,512]{1,0:T(8,128)(2,1)}, bf16[512,512]{1,0:T(8,128)(2,1)}, u32[]{:S(2)}, u32[]{:S(2)}) collective-permute-start(bf16[512,512]{1,0:T(8,128)(2,1)} %get-tuple-element.63), channel_id=1, source_target_pairs={{0,2},{1,3},{2,0},{3,1},{4,6},{5,7},{6,4},{7,5},{8,10},{9,11},{10,... | collective-permute-start | bytes 1572872 | tf_op jit(solution)/shard_map/ppermute | solution.py:1303
  51.7 37.3 %collective-permute-start.3 = (bf16[512,512]{1,0:T(8,128)(2,1)S(1)}, bf16[512,512]{1,0:T(8,128)(2,1)}, u32[]{:S(2)}, u32[]{:S(2)}) collective-permute-start(bf16[512,512]{1,0:T(8,128)(2,1)S(1)} %bitcast.72), channel_id=1, source_target_pairs={{0,4},{4,0},{8,12},{12,8},{16,20},{20,16},{24,28},{28,24},{1,5},{5... | collective-permute-start | bytes 1572872 | tf_op jit(solution)/shard_map/ppermute | solution.py:1380
  53.2 35.8 %collective-permute-start.2 = (bf16[512,1024]{1,0:T(8,128)(2,1)}, bf16[512,1024]{1,0:T(8,128)(2,1)}, u32[]{:S(2)}, u32[]{:S(2)}) collective-permute-start(bf16[512,1024]{1,0:T(8,128)(2,1)} %bitcast.11.own_half_ref), channel_id=1, source_target_pairs={{0,12},{4,8},{8,4},{12,0},{16,28},{20,24},{24,20},{28,16},{1,13},{... | collective-permute-start | bytes 3145736 | tf_op jit(solution)/shard_map/ppermute | solution.py:1379
  54.7 2.0 copy-start.34
  54.7 2.0 copy-start.36
  54.8 2.0 copy-start.28
  54.8 2.0 copy-start.30
  54.8 2.0 copy-start.32
  56.7 2.8 copy-start.19
  56.8 2.7 copy-start.44
  56.8 2.7 copy-start.45
  59.5 12.1 %copy-start.10 = (bf16[128,1024]{1,0:T(8,128)(2,1)S(1)}, bf16[128,1024]{1,0:T(8,128)(2,1)}, u32[]{:S(2)}) copy-start(bf16[128,1024]{1,0:T(8,128)(2,1)} %dt_proj_ref.3) | copy-start | bytes 786436
  69.3 19.7 %collective-permute-start.1 = (bf16[512,512]{1,0:T(8,128)(2,1)}, bf16[512,512]{1,0:T(8,128)(2,1)S(1)}, u32[]{:S(2)}, u32[]{:S(2)}) collective-permute-start(bf16[512,512]{1,0:T(8,128)(2,1)} %copy-done.9), channel_id=1, source_target_pairs={{0,2},{1,3},{2,0},{3,1},{4,6},{5,7},{6,4},{7,5},{8,10},{9,11},{10,... | collective-permute-start | bytes 1572872 | tf_op jit(solution)/shard_map/ppermute | solution.py:1303
  85.9 3.2 %copy-start.23 = (f32[512,1024]{1,0:T(8,128)S(1)}, f32[512,1024]{1,0:T(8,128)}, u32[]{:S(2)}) copy-start(f32[512,1024]{1,0:T(8,128)} %get-tuple-element.72) | copy-start | bytes 6291460
  89.1 1.7 copy-start.21
  90.8 1.6 copy-start.8
  92.0 29.3 %copy-start.3 = (bf16[2,256,1024]{2,1,0:T(8,128)(2,1)}, bf16[2,256,1024]{2,1,0:T(8,128)(2,1)S(1)}, u32[]{:S(2)}) copy-start(bf16[2,256,1024]{2,1,0:T(8,128)(2,1)S(1)} %get-tuple-element.125) | copy-start | bytes 3145732
  121.3 6.1 %copy-start.2 = (bf16[4096,512]{1,0:T(8,128)(2,1)S(1)}, bf16[4096,512]{1,0:T(8,128)(2,1)}, u32[]{:S(2)}) copy-start(bf16[4096,512]{1,0:T(8,128)(2,1)} %o_hbm.3) | copy-start | bytes 12582916
  121.3 6.1 %copy-start.7 = (bf16[2,256,2048]{2,1,0:T(8,128)(2,1)S(1)}, bf16[2,256,2048]{2,1,0:T(8,128)(2,1)}, u32[]{:S(2)}) copy-start(bf16[2,256,2048]{2,1,0:T(8,128)(2,1)} %copy-done.6) | copy-start | bytes 6291460
  150.4 3.7 %copy-start.16 = (bf16[256,1024]{1,0:T(8,128)(2,1)}, bf16[256,1024]{1,0:T(8,128)(2,1)S(1)}, u32[]{:S(2)}) copy-start(bf16[256,1024]{1,0:T(8,128)(2,1)S(1)} %get-tuple-element.97.wz_ref) | copy-start | bytes 1572868
  154.1 7.6 %copy-start.13 = (f32[2,256,1024]{2,1,0:T(8,128)S(1)}, f32[2,256,1024]{2,1,0:T(8,128)}, u32[]{:S(2)}) copy-start(f32[2,256,1024]{2,1,0:T(8,128)} %get-tuple-element.88.rate_ref) | copy-start | bytes 6291460
  154.1 7.6 %copy-start.14 = (f32[2,256,1024]{2,1,0:T(8,128)S(1)}, f32[2,256,1024]{2,1,0:T(8,128)}, u32[]{:S(2)}) copy-start(f32[2,256,1024]{2,1,0:T(8,128)} %get-tuple-element.89.beta_ref) | copy-start | bytes 6291460
  154.3 45.5 %collective-permute-start.6 = (bf16[512,512]{1,0:T(8,128)(2,1)S(1)}, bf16[512,512]{1,0:T(8,128)(2,1)S(1)}, u32[]{:S(2)}, u32[]{:S(2)}) collective-permute-start(bf16[512,512]{1,0:T(8,128)(2,1)S(1)} %get-tuple-element.129), channel_id=1, source_target_pairs={{0,24},{4,28},{8,0},{12,4},{16,8},{20,12},{24,16},{28,20},{1,25},{... | collective-permute-start | bytes 1572872 | tf_op jit(solution)/shard_map/ppermute | solution.py:1317
  160.9 45.2 %collective-permute-start.5 = (bf16[512,512]{1,0:T(8,128)(2,1)S(1)}, bf16[512,512]{1,0:T(8,128)(2,1)S(1)}, u32[]{:S(2)}, u32[]{:S(2)}) collective-permute-start(bf16[512,512]{1,0:T(8,128)(2,1)S(1)} %get-tuple-element.130), channel_id=1, source_target_pairs={{0,16},{4,20},{8,24},{12,28},{16,0},{20,4},{24,8},{28,12},{1,17},{... | collective-permute-start | bytes 1572872 | tf_op jit(solution)/shard_map/ppermute | solution.py:1317
  161.1 45.1 %collective-permute-start.4 = (bf16[512,512]{1,0:T(8,128)(2,1)S(1)}, bf16[512,512]{1,0:T(8,128)(2,1)S(1)}, u32[]{:S(2)}, u32[]{:S(2)}) collective-permute-start(bf16[512,512]{1,0:T(8,128)(2,1)S(1)} %get-tuple-element.131), channel_id=1, source_target_pairs={{0,8},{4,12},{8,16},{12,20},{16,24},{20,28},{24,0},{28,4},{1,9},{5... | collective-permute-start | bytes 1572872 | tf_op jit(solution)/shard_map/ppermute | solution.py:1317
  190.1 0.8 copy-start.15
  190.8 17.0 %copy-start.17 = (f32[1,1024]{1,0:T(1,128)}, f32[1,1024]{1,0:T(1,128)S(1)}, u32[]{:S(2)}) copy-start(f32[1,1024]{1,0:T(1,128)S(1)} %get-tuple-element.95.db_ref) | copy-start | bytes 12292
  190.9 17.0 %copy-start.18 = (f32[1,1024]{1,0:T(1,128)}, f32[1,1024]{1,0:T(1,128)S(1)}, u32[]{:S(2)}) copy-start(f32[1,1024]{1,0:T(1,128)S(1)} %get-tuple-element.96.sk_ref) | copy-start | bytes 12292
  199.8 8.1 %copy-start.20 = (f32[2,256,1024]{2,1,0:T(8,128)S(1)}, f32[2,256,1024]{2,1,0:T(8,128)}, u32[]{:S(2)}) copy-start(f32[2,256,1024]{2,1,0:T(8,128)} %copy-done.19) | copy-start | bytes 6291460
  199.8 8.1 %copy-start.22 = (f32[2,256,1024]{2,1,0:T(8,128)S(1)}, f32[2,256,1024]{2,1,0:T(8,128)}, u32[]{:S(2)}) copy-start(f32[2,256,1024]{2,1,0:T(8,128)} %get-tuple-element.123) | copy-start | bytes 6291460
  199.8 8.1 %copy-start.35 = (f32[2,256]{1,0:T(2,128)S(1)}, f32[2,256]{1,0:T(2,128)}, u32[]{:S(2)}) copy-start(f32[2,256]{1,0:T(2,128)} %copy-done.34) | copy-start | bytes 6148
  199.8 8.1 %copy-start.37 = (f32[2,256]{1,0:T(2,128)S(1)}, f32[2,256]{1,0:T(2,128)}, u32[]{:S(2)}) copy-start(f32[2,256]{1,0:T(2,128)} %copy-done.36) | copy-start | bytes 6148
  210.9 0.7 copy-start.29
  210.9 0.7 copy-start.31
  210.9 0.7 copy-start.33
  279.0 2.0 copy-start.27
  279.0 2.8 copy-start.24
  281.8 1.4 copy-start.39
  281.8 2.0 copy-start.42
  281.8 2.6 copy-start.25
  281.8 3.4 %copy-start.26 = (f32[128,1024]{1,0:T(8,128)S(1)}, f32[128,1024]{1,0:T(8,128)}, u32[]{:S(2)}) copy-start(f32[128,1024]{1,0:T(8,128)} %get-tuple-element.162) | copy-start | bytes 1572868
  281.9 5.4 %copy-start.1 = (bf16[160,1024]{1,0:T(8,128)(2,1)S(1)}, bf16[160,1024]{1,0:T(8,128)(2,1)}, u32[]{:S(2)}) copy-start(bf16[160,1024]{1,0:T(8,128)(2,1)} %param.18) | copy-start | bytes 983044
  283.2 2.8 copy-start.41
  283.2 3.4 %copy-start.40 = (f32[1,1024]{1,0:T(1,128)S(1)}, f32[1,1024]{1,0:T(1,128)}, u32[]{:S(2)}) copy-start(f32[1,1024]{1,0:T(1,128)} %get-tuple-element.108) | copy-start | bytes 12292

commit v9 on v8

--- a/solution.py
+++ b/solution.py
@@ -399,7 +399,7 @@
 
 def front_kernel(
     x_ref, cot_ref, gain_ref, w_hbm, o_hbm,
-    xs_ref, inv_ref, cots_ref, gain_row_ref, own_half_ref, half_ref, parts_ref, own_ref, send_ref, send_more_ref,
+    xs_ref, inv_ref, cots_ref, gain_row_ref, own_half_ref, y_half_ref, z_half_ref, x_part_ref, z_part_ref, own_ref, send_ref, send_more_ref,
     gains_ref, w_ref, o_ref, normed_ref, lhs, mixed, pairs, near, sends, recvs, local, part_sends, part_recvs, part_local,
     pair_sends, pair_recvs, pair_local,
 ):
@@ -409,7 +409,7 @@
     seqs, rows, model = x_ref.shape
     cols = cots_ref.shape[2]
     core = lax.rem(me, 2)
-    width = parts_ref.shape[3]
+    width = x_part_ref.shape[2]
     lift = gain_ref.shape[0]
     span = 2 * rows
     tile = 256
@@ -452,25 +452,26 @@
     gain_row_ref[...] = jnp.broadcast_to(gain, gain_row_ref.shape)
     loads[0].wait()
 
-    def piece(half, i):
+    def piece(half, kind):
         where = jnp.bitwise_xor(chip, half)
-        return parts_ref.at[slot, :, pl.ds(pl.multiple_of(where * span, 16), span), :]
+        return (x_part_ref, z_part_ref)[kind].at[:, pl.ds(pl.multiple_of(where * span, 16), span), :]
 
     def away(i):
         return lax.rem(2 * me + i, 4) != me
 
-    def send(half, i):
+    def send(half, i, kind):
         return part_copy(
-            mixed.at[half, i], piece(half, i), part_sends.at[2 * half + i], part_recvs.at[2 * slot + half],
+            mixed.at[half, i], piece(half, kind), part_sends.at[2 * half + i], part_recvs.at[2 * kind + half],
             lax.rem(2 * me + i, 4),
         )
 
-    def keep(half, i):
-        return pltpu.make_async_copy(mixed.at[half, i], piece(half, i), part_local.at[half])
-
-    def either(i, yes, no):
-        pl.when(away(i))(yes)
-        pl.when(jnp.logical_not(away(i)))(no)
+    def keep(half, i, kind):
+        return pltpu.make_async_copy(mixed.at[half, i], piece(half, kind), part_local.at[half])
+
+    def either(half, i, send_does, keep_does):
+        for kind in range(2):
+            pl.when(away(i) & (slot == kind))(lambda kind=kind: send_does(send(half, i, kind)))
+            pl.when(jnp.logical_not(away(i)) & (slot == kind))(lambda kind=kind: keep_does(keep(half, i, kind)))
 
     def run_half(half):
         where = jnp.bitwise_xor(chip, half) * span
@@ -501,7 +502,7 @@
                 return carry
 
             lax.fori_loop(0, width // tile, product, 0)
-            either(i, lambda i=i: send(half, i).start(), lambda i=i: keep(half, i).start())
+            either(half, i, lambda copy: copy.start(), lambda copy: copy.start())
 
     def normed_copies(half):
         where = pl.ds(pl.multiple_of(jnp.bitwise_xor(chip, half) * span, 16), span)
@@ -509,7 +510,8 @@
         copies = [pltpu.make_async_copy(src, own_half_ref.at[:, where, :], pair_local.at[half])]
         for hop in (1, 2):
             at = 2 * half + hop - 1
-            copies.append(across(src, half_ref.at[hop - 1, :, where, :], pair_sends, pair_recvs, at, quad(hop)))
+            half_ref = (y_half_ref, z_half_ref)[hop - 1]
+            copies.append(across(src, half_ref.at[:, where, :], pair_sends, pair_recvs, at, quad(hop)))
         return copies
 
     run_half(0)
@@ -568,7 +570,7 @@
         copy.wait()
     for half in range(2):
         for i in range(2):
-            either(i, lambda half=half, i=i: send(half, i).wait_send(), lambda half=half, i=i: keep(half, i).wait())
+            either(half, i, lambda copy: copy.wait_send(), lambda copy: copy.wait())
         for at in range(2):
 
             @pl.when(2 * at + me // 2 != me)
@@ -590,15 +592,17 @@
     return pl.pallas_call(
         front_kernel,
         in_specs=[VMEM_SPEC] * 3 + [ANY_SPEC] * 2,
-        out_specs=[VMEM_SPEC] * 10,
+        out_specs=[VMEM_SPEC] * 12,
         out_shape=[
             jax.ShapeDtypeStruct((seqs, length, model), bf16),
             jax.ShapeDtypeStruct((seqs, length, LANES), f32),
             jax.ShapeDtypeStruct((seqs, length, cols), bf16),
             jax.ShapeDtypeStruct((8, model), f32),
             jax.ShapeDtypeStruct((seqs, length, model // 2), bf16),
-            jax.ShapeDtypeStruct((2, seqs, length, model // 2), bf16),
-            jax.ShapeDtypeStruct((2, seqs, length, width), bf16),
+            jax.ShapeDtypeStruct((seqs, length, model // 2), bf16),
+            jax.ShapeDtypeStruct((seqs, length, model // 2), bf16),
+            jax.ShapeDtypeStruct((seqs, length, width), bf16),
+            jax.ShapeDtypeStruct((seqs, length, width), bf16),
             jax.ShapeDtypeStruct((tokens, width), f32),
             jax.ShapeDtypeStruct((tokens, width // 2), bf16),
             jax.ShapeDtypeStruct((tokens, width // 2), bf16),
@@ -652,7 +656,7 @@
 
 
 def collect_kernel(
-    keep_ref, give_ref, gz_ref, own_half_ref, half_ref, last_ref,
+    keep_ref, give_ref, gz_ref, own_half_ref, y_half_ref, z_half_ref, last_ref,
     keeps_ref, gives_ref, gz_ref4, norm_ref, got_ref,
     sends, recvs, local,
 ):
@@ -679,7 +683,8 @@
     give_pair = across(give_ref, got_ref, sends, recvs, 11, quad(1))
     norms = [
         remote(own_half_ref, norm_ref.at[core, 0], sends, recvs, 12, 1),
-        remote(half_ref, norm_ref.at[core, 1:3], sends, recvs, 10, 1),
+        remote(y_half_ref, norm_ref.at[core, 1], sends, recvs, 10, 1),
+        remote(z_half_ref, norm_ref.at[core, 2], sends, recvs, 13, 1),
         remote(last_ref, norm_ref.at[core, 3], sends, recvs, 4, 1),
     ]
     own = [
@@ -687,7 +692,8 @@
         pltpu.make_async_copy(give_ref, spot(gives_ref, me), local.at[1]),
         pltpu.make_async_copy(quarter(member), gz_ref4.at[0], local.at[2]),
         pltpu.make_async_copy(own_half_ref, norm_ref.at[core, 0], local.at[5]),
-        pltpu.make_async_copy(half_ref, norm_ref.at[core, 1:3], local.at[3]),
+        pltpu.make_async_copy(y_half_ref, norm_ref.at[core, 1], local.at[3]),
+        pltpu.make_async_copy(z_half_ref, norm_ref.at[core, 2], local.at[6]),
         pltpu.make_async_copy(last_ref, norm_ref.at[core, 3], local.at[4]),
     ]
     for copy in [k_chip, v_chip] + quads + [give_pair, k_core, v_core] + norms + own:
@@ -708,13 +714,13 @@
     return pl.CostEstimate(flops=int(microseconds * 1e9), bytes_accessed=1 << 20, transcendentals=0)
 
 
-def collect(keep, give, grad_z, own_half, half_norm, last_norm):
+def collect(keep, give, grad_z, own_half, y_half, z_half, last_norm):
     tokens, half = keep.shape
     group = lax.axis_size("shard")
     wide = jax.ShapeDtypeStruct((tokens, half * group), bf16)
     return pl.pallas_call(
         collect_kernel,
-        in_specs=[VMEM_SPEC] * 6,
+        in_specs=[VMEM_SPEC] * 7,
         out_specs=[VMEM_SPEC] * 3 + [ANY_SPEC, VMEM_SPEC],
         out_shape=[
             wide, wide, jax.ShapeDtypeStruct((4, tokens, grad_z.shape[1] // 4), bf16),
@@ -722,12 +728,12 @@
             jax.ShapeDtypeStruct(give.shape, bf16),
         ],
         scratch_shapes=[
-            pltpu.SemaphoreType.DMA((13,)), pltpu.SemaphoreType.DMA((13,)), pltpu.SemaphoreType.DMA((6,)),
+            pltpu.SemaphoreType.DMA((14,)), pltpu.SemaphoreType.DMA((14,)), pltpu.SemaphoreType.DMA((7,)),
         ],
         compiler_params=group_params(6, 28 << 20),
         cost_estimate=cost(25),
         name="collect",
-    )(keep, give, grad_z, own_half, half_norm, last_norm)
+    )(keep, give, grad_z, own_half, y_half, z_half, last_norm)
 
 
 def middle_kernel(
@@ -1175,7 +1181,7 @@
     total = gain_sum[...]
     for step in range(1, count):
         total = total + gain_in[step - 1]
-    ggain_ref[...] = jnp.broadcast_to(jnp.sum(total, axis=0, keepdims=True), total.shape)
+    ggain_ref[...] = jnp.sum(total, axis=0, keepdims=True)
     for step in range(height):
         pass_on(step).wait()
     goals, start = [], 0
@@ -1223,7 +1229,7 @@
             jax.ShapeDtypeStruct((KW, width), f32),
             line, line, line,
             jax.ShapeDtypeStruct(x.shape, bf16),
-            jax.ShapeDtypeStruct((8, wide), f32),
+            jax.ShapeDtypeStruct((1, wide), f32),
         ],
         scratch_shapes=[
             pltpu.VMEM((height, lines, width), f32),
@@ -1354,12 +1360,11 @@
         odd = jnp.concatenate(cuts[1::2], axis=1)
         return jnp.where(side == 0, even, odd), jnp.where(side == 0, odd, even)
 
-    xs, inv, cots, gain, own_half, half_norm, parts, gated_own, gated_send, gated_more = front(
+    xs, inv, cots, gain, own_half, y_half, z_half, x_part, z_part, gated_own, gated_send, gated_more = front(
         block_input, out_grad, norm_gain, w_in, out_proj
     )
     x_all = xs.reshape(tokens, model)
     cot = cots.reshape(tokens, -1)
-    x_part, z_part = parts[0], parts[1]
 
     seg_padded = jnp.pad(segment_ids, ((0, 0), (KW - 1, 0)), constant_values=-1)
     taps = [
@@ -1374,9 +1379,8 @@
         conv_pre = conv_pre + conv_w[j] * x_padded[:, j : j + length] * taps[d][:, :, None]
     conv_out = jax.nn.silu(conv_pre).astype(bf16)
     conv_flat = conv_out.reshape(tokens, width)
-    half_norm = half_norm.reshape(2, tokens, -1)
-    own_half = own_half.reshape(tokens, -1)
-    last_norm = lax.ppermute(own_half, "replica", [(i, i ^ 3) for i in range(count)])
+    own_half, y_half, z_half = (value.reshape(tokens, -1) for value in (own_half, y_half, z_half))
+    last_norm = lax.ppermute(y_half, "replica", [(i, i ^ 2) for i in range(count)])
     cot_got = lax.ppermute(cot, "replica", [(i, i ^ 1) for i in range(count)])
     proj = group_total(outer_dot(x_proj, conv_flat), 3)
     gated_far = by_hop(gated_send, 2)
@@ -1399,7 +1403,7 @@
     gated_keep, gated_give = halves(gated.reshape(tokens, width), height // 4)
     cols = model // 4
     keeps, gives, grad_z_quad, norms, gated_got = collect(
-        gated_keep, gated_give, grad_z, own_half, half_norm, last_norm
+        gated_keep, gated_give, grad_z, own_half, y_half, z_half, last_norm
     )
     norms = norms.reshape(2, 4 * tokens, -1)
     z_blocks = lax.dot_general(

time: 289 us -> 287 us (level)
  waiting for transfers between devices: 9.46 us -> 6.35 us
    ppermute x1, waiting for transfers between devices: 3.1 us -> 0.01 us  [body(): cot_got = lax.ppermute(cot, 'replica', [(i, i ^ 1) for i in range(count)])]
    unnamed x103 -> x126, local copies, waits for them, and re-layouts: 11 us -> 12.8 us
  transfers between devices with their start and end apart: 7 -> 7, of which waited for: 2 -> 1; matrix products, arithmetic and copies ran while one was open for 2% -> 2% of each run, Pallas kernels for 21% -> 22%
where the time goes in v9:
time: 287 us; the launch traced here: 286 us
  Pallas kernels  219 us (76%)
  starting transfers between devices  17.9 us (6%)
  local copies, waits for them, and re-layouts  14.6 us (5%)
  other arithmetic  14.2 us (5%)
  matrix products  11.9 us (4%)
  waiting for transfers between devices  6.35 us (2%)
    pallas_call x1, Pallas kernels, finish(): pl.pallas_call(finish_kernel, in_specs=[VMEM_SPEC] * 9 + [ANY_SPEC] * 2 +...  63.3 us
    pallas_call x1, Pallas kernels, front(): pl.pallas_call(front_kernel, in_specs=[VMEM_SPEC] * 3 + [ANY_SPEC] * 2, o...  42.9 us
    pallas_call x1, Pallas kernels, collect(): pl.pallas_call(collect_kernel, in_specs=[VMEM_SPEC] * 7, out_specs=[VMEM_...  28.9 us
    pallas_call x1, Pallas kernels, recurrence_backward(): pl.pallas_call(backward_kernel, grid=(seqs, blocks), in_specs=[wide, wide...  28.3 us
    pallas_call x1, Pallas kernels, middle(): pl.pallas_call(middle_kernel, in_specs=[VMEM_SPEC] * 4 + [ANY_SPEC] * 2,...  22.7 us
    pallas_call x2, Pallas kernels, group_total(): pl.pallas_call(total_kernel, in_specs=[VMEM_SPEC], out_specs=VMEM_SPEC, o...  18.9 us
    pallas_call x1, Pallas kernels, recurrence_forward(): pl.pallas_call(forward_kernel, grid=(seqs, blocks), in_specs=[wide, wide,...  14.3 us
    unnamed x126, local copies, waits for them, and re-layouts  12.8 us
  transfers between devices with their start and end apart: 7, of which 1 were waited for; matrix products, arithmetic and copies ran while one was open for 2% of the time, Pallas kernels for 22%

profile of v9, /device:TPU:0, one launch (start us, length us, event | category | flops | bytes accessed | tf_op | source)
XLA Modules:
  0.0 285.8 jit_solution(10670837702911540582)
XLA Ops:
  0.6 0.0 copy-start
  0.7 0.7 broadcast_in_dim.12.gain_ref
  1.4 1.0 copy-done.5
  2.4 1.0 copy-done.6
  3.5 42.9 %front.1 = (bf16[2,256,2048]{2,1,0:T(8,128)(2,1)}, f32[2,256,128]{2,1,0:T(8,128)S(1)}, bf16[2,256,512]{2,1,0:T(8,128)(2,1)S(1)}, f32[8,2048]{1,0:T(8,128)S(1)}, ...) custom-call(bf16[2,64,2048]{2,1,0:T(8,128)(2,1)S(1)} %copy-done.5, ...), custom_call_target="tpu_custom_call" | custom-call | tf_op jit(solution)/shard_map/front/pallas_call | solution.py:592
  46.5 5.2 %collective-permute-start = (bf16[512,512]{1,0:T(8,128)(2,1)}, bf16[512,512]{1,0:T(8,128)(2,1)}, u32[]{:S(2)}, u32[]{:S(2)}) collective-permute-start(bf16[512,512]{1,0:T(8,128)(2,1)} %get-tuple-element.66), channel_id=1, source_target_pairs={{0,2},{1,3},{2,0},{3,1},{4,6},{5,7},{6,4},{7,5},{8,10},{9,11},{10,... | collective-permute-start | bytes 1572872 | tf_op jit(solution)/shard_map/ppermute | solution.py:1309
  51.7 1.5 collective-permute-start.3
  53.2 1.1 collective-permute-start.2
  54.3 0.1 compare_convert_fusion.2
  54.4 0.0 copy-start.46
  54.5 0.0 copy-start.40
  54.5 0.0 copy-start.42
  54.5 1.5 convert_element_type.75
  56.0 0.0 copy-start.54
  56.0 0.0 copy-start.55
  56.0 2.7 fusion.12
  58.9 0.5 convolution_bitcast_fusion.part_ref
  59.4 10.0 %group_total.2.proj_ref = f32[160,512]{1,0:T(8,128)S(1)} custom-call(f32[160,512]{1,0:T(8,128)S(1)} %convolution_bitcast_fusion.part_ref), custom_call_target="tpu_custom_call" | custom-call | tf_op jit(solution)/shard_map/group_total/pallas_call | solution.py:1297
  69.4 2.1 collective-permute-start.1
  71.5 0.1 broadcast_in_dim.13.keep_ref
  71.7 14.3 %recurrence_forward.1 = (f32[2,256,1024]{2,1,0:T(8,128)S(1)}, bf16[2,256,1024]{2,1,0:T(8,128)(2,1)S(1)}, f32[2,256,1024]{2,1,0:T(8,128)}, f32[2,256,1024]{2,1,0:T(8,128)}, bf16[2,4096,1024]{2,1,0:T(8,128)(2,1)}) custom-call(bf16[2,256,1024]{2,1,0:T(8,128)(2,1)S(1)} %get-tuple-element.126.conv_ref, bf16[2,256,1024]{2,1,0:T(8,128)(2,1)S(1)} %copy-done.3, ...), custom_call_target="tpu_custom_call" | custom-call | flops 16000000000 | bytes 25165824 | tf_op jit(solution)/shard_map/recurrence_forward/pallas_call | solution.py:289
  86.0 0.1 broadcast_select_fusion
  86.1 1.5 copy-done.26
  87.6 1.3 convert_add_fusion
  88.9 0.0 copy-start.9
  88.9 1.1 fusion.11
  90.0 0.1 copy-done.9
  90.1 0.3 copy-done.11
  90.4 28.9 %collect.1 = (bf16[512,2048]{1,0:T(8,128)(2,1)S(1)}, bf16[512,2048]{1,0:T(8,128)(2,1)S(1)}, bf16[4,512,256]{2,1,0:T(8,128)(2,1)S(1)}, bf16[2,4,512,1024]{3,2,1,0:T(8,128)(2,1)}, bf16[512,512]{1,0:T(8,128)(2,1)S(1)}) custom-call(bf16[512,512]{1,0:T(8,128)(2,1)S(1)} %get-tuple-element.138.keep_ref, bf16[512,512]{1,0:T(8,128)(2,1)S(1)} %get-tuple-element.137.give_ref, ...), custom_call_target="tpu_custom_call" | custom-call | flops 24999999488 | bytes 1048576 | tf_op jit(solution)/shard_map/collect/pallas_call | solution.py:721
  119.3 0.0 copy-start.2
  119.4 6.1 %bitcast_convert_fusion = bf16[2,1024,256]{2,1,0:T(8,128)(2,1)S(1)} fusion(bf16[2,4,512,1024]{3,2,1,0:T(8,128)(2,1)} %get-tuple-element.85, bf16[4,512,256]{2,1,0:T(8,128)(2,1)S(1)} %get-tuple-element.86), kind=kOutput, calls=%fused_computation.16 | convolution fusion | flops 2148007936 | bytes 10485760 | tf_op jit(solution)/shard_map/dot_general | solution.py:1409
  125.5 22.7 %middle.1 = (bf16[2,512,2048]{2,1,0:T(8,128)(2,1)S(1)}, bf16[2,64,2048]{2,1,0:T(8,128)(2,1)S(1)}, bf16[256,1024]{1,0:T(8,128)(2,1)S(1)}) custom-call(bf16[512,2048]{1,0:T(8,128)(2,1)S(1)} %get-tuple-element.82.keeps_ref, bf16[512,2048]{1,0:T(8,128)(2,1)S(1)} %get-tuple-element.83.gives_ref, bf16[512,512]{1,0:T(8,128)(2,1)S(1)} %get-tuple-element.84.got_ref, ...), custom_call_target="tpu_custom_call" | custom-call | flops 24999999488 | bytes 1048576 | tf_op jit(solution)/shard_map/middle/pallas_call | solution.py:845
  148.2 3.7 %convolution_convert_fusion = bf16[2048,512]{1,0:T(8,128)(2,1)S(1)} fusion(bf16[1024,2048]{1,0:T(8,128)(2,1)S(1)} %bitcast.65, bf16[512,512]{1,0:T(8,128)(2,1)} %collective-permute-done.3, bf16[512,512]{1,0:T(8,128)(2,1)S(1)} %bitcast.64), kind=kOutput, calls=%fused_computation | convolution fusion | flops 2150629376 | bytes 7340032 | tf_op jit(solution)/shard_map/dot_general | solution.py:23
  151.9 0.9 dynamic-slice_bitcast_fusion
  152.9 6.9 %collective-permute-start.6 = (bf16[512,512]{1,0:T(8,128)(2,1)S(1)}, bf16[512,512]{1,0:T(8,128)(2,1)S(1)}, u32[]{:S(2)}, u32[]{:S(2)}) collective-permute-start(bf16[512,512]{1,0:T(8,128)(2,1)S(1)} %get-tuple-element.133), channel_id=1, source_target_pairs={{0,24},{4,28},{8,0},{12,4},{16,8},{20,12},{24,16},{28,20},{1,25},{... | collective-permute-start | bytes 1572872 | tf_op jit(solution)/shard_map/ppermute | solution.py:1323
  159.8 0.5 collective-permute-start.5
  160.3 0.6 collective-permute-start.4
  160.9 28.3 %recurrence_backward.1 = (f32[2,256,1024]{2,1,0:T(8,128)S(1)}, bf16[2,256,1024]{2,1,0:T(8,128)(2,1)}, f32[160,512]{1,0:T(8,128)S(1)}, f32[128,1024]{1,0:T(8,128)...) custom-call(f32[2,256,1024]{2,1,0:T(8,128)S(1)} %copy-done.16, f32[2,256,1024]{2,1,0:T(8,128)S(1)} %copy-done.17, ...), custom_call_target="tpu_custom_call" | custom-call | flops 30000001024 | bytes 29360128 | tf_op jit(solution)/shard_map/recurrence_backward/pallas_call | solution.py:324
  189.2 0.8 copy-done.18
  190.0 8.9 %group_total.3 = f32[160,512]{1,0:T(8,128)S(1)} custom-call(f32[160,512]{1,0:T(8,128)S(1)} %get-tuple-element.96.part_ref), custom_call_target="tpu_custom_call" | custom-call | tf_op jit(solution)/shard_map/group_total/pallas_call | solution.py:1297
  198.9 0.0 copy-start.24
  198.9 0.0 copy-start.45
  199.0 6.3 %collective-permute-done.5 = bf16[512,512]{1,0:T(8,128)(2,1)S(1)} collective-permute-done((bf16[512,512]{1,0:T(8,128)(2,1)S(1)}, bf16[512,512]{1,0:T(8,128)(2,1)S(1)}, u32[]{:S(2)}, u32[]{:S(2)}) %collective-permute-start.5) | collective-permute-done | bytes 524320 | tf_op jit(solution)/shard_map/ppermute | solution.py:1323
  205.3 1.2 fusion.17.xp_ref
  206.5 0.5 fusion.19
  207.1 3.1 %fusion.22 = (f32[1024]{0:T(1024)}, f32[1024]{0:T(1024)S(1)}, f32[1024]{0:T(1024)S(1)}, f32[1024]{0:T(1024)S(1)}, f32[1024]{0:T(1024)S(1)}, /*index=5*/f32[2,256,1024]{2,1,0:T(8,128)S(1)}) fusion(bf16[2,256,1024]{2,1,0:T(8,128)(2,1)S(1)} %copy-done.25, f32[2,256]{1,0:T(2,128)S(1)} %copy-done.47, f32[2,256,1024]{2,1,0:T(8,128)S(1)} %copy-done.23, ...), kind=kLoop, calls=%fused_computation.58 | loop fusion | flops 12577792 | bytes 13662208 | tf_op jit(solution)/shard_map/reduce_sum | solution.py:1427
  210.2 0.5 broadcast_multiply_fusion
  210.7 0.2 copy-done.39
  210.9 0.0 copy-done.41
  210.9 0.0 copy-done.43
  210.9 2.1 fusion.4
  213.0 0.6 pad_maximum_fusion.cw_ref
  213.7 63.3 %finish.1 = (f32[256,2048]{1,0:T(8,128)}, f32[160,1024]{1,0:T(8,128)}, f32[128,1024]{1,0:T(8,128)}, f32[4,1024]{1,0:T(4,128)}, f32[1,1024]{1,0:T(1,128)}, /*inde...) custom-call(bf16[512,1024]{1,0:T(8,128)(2,1)} %bitcast.69, ...), custom_call_target="tpu_custom_call" | custom-call | flops 80000000000 | bytes 1048576 | tf_op jit(solution)/shard_map/finish/pallas_call | solution.py:1221
  277.0 1.2 convert_add_fusion.1
  278.2 0.8 copy.36
  279.0 0.8 copy.37
  279.8 0.6 copy.38
  280.4 1.3 copy.39
  281.8 0.6 copy.40
  282.4 0.6 copy.41
  283.0 0.8 copy.42
  283.8 0.8 copy.43
  284.6 0.6 copy.44
  285.2 0.6 copy.45
  (107 shorter events, 0.2 us)
Async XLA Ops:
  0.6 58.3 %copy-start = (bf16[160,1024]{1,0:T(8,128)(2,1)S(1)}, bf16[160,1024]{1,0:T(8,128)(2,1)}, u32[]{:S(2)}) copy-start(bf16[160,1024]{1,0:T(8,128)(2,1)} %param.18) | copy-start | bytes 983044
  1.4 1.0 copy-start.5
  2.4 1.0 copy-start.6
  3.5 50.9 %copy-start.53 = (bf16[1024]{0:T(1024)(128)(2,1)S(1)}, bf16[1024]{0:T(1024)(128)(2,1)}, u32[]{:S(2)}) copy-start(bf16[1024]{0:T(1024)(128)(2,1)} %param.17) | copy-start | bytes 6148
  3.5 50.9 %copy-start.57 = (s32[2,256]{1,0:T(2,128)S(1)}, s32[2,256]{1,0:T(2,128)}, u32[]{:S(2)}) copy-start(s32[2,256]{1,0:T(2,128)} %param.13) | copy-start | bytes 6148
  3.5 50.9 %copy-start.48 = (bf16[4,1024]{1,0:T(4,128)(2,1)S(1)}, bf16[4,1024]{1,0:T(4,128)(2,1)}, u32[]{:S(2)}) copy-start(bf16[4,1024]{1,0:T(4,128)(2,1)} %param.16) | copy-start | bytes 24580
  46.4 9.6 %copy-start.14 = (f32[2,256,128]{2,1,0:T(8,128)}, f32[2,256,128]{2,1,0:T(8,128)S(1)}, u32[]{:S(2)}) copy-start(f32[2,256,128]{2,1,0:T(8,128)S(1)} %get-tuple-element.103.inv_ref) | copy-start | bytes 786436
  46.4 9.6 %copy-start.15 = (f32[8,2048]{1,0:T(8,128)}, f32[8,2048]{1,0:T(8,128)S(1)}, u32[]{:S(2)}) copy-start(f32[8,2048]{1,0:T(8,128)S(1)} %get-tuple-element.102.gain_ref) | copy-start | bytes 196612
  46.4 12.3 %copy-start.8 = (bf16[2,256,1024]{2,1,0:T(8,128)(2,1)}, bf16[2,256,1024]{2,1,0:T(8,128)(2,1)S(1)}, u32[]{:S(2)}) copy-start(bf16[2,256,1024]{2,1,0:T(8,128)(2,1)S(1)} %get-tuple-element.79) | copy-start | bytes 3145732
  46.4 12.3 %copy-start.10 = (bf16[2,256,1024]{2,1,0:T(8,128)(2,1)}, bf16[2,256,1024]{2,1,0:T(8,128)(2,1)S(1)}, u32[]{:S(2)}) copy-start(bf16[2,256,1024]{2,1,0:T(8,128)(2,1)S(1)} %get-tuple-element.80) | copy-start | bytes 3145732
  46.5 12.3 %copy-start.12 = (bf16[512,512]{1,0:T(8,128)(2,1)}, bf16[512,512]{1,0:T(8,128)(2,1)S(1)}, u32[]{:S(2)}) copy-start(bf16[512,512]{1,0:T(8,128)(2,1)S(1)} %get-tuple-element.71) | copy-start | bytes 1572868
  46.5 22.9 %collective-permute-start = (bf16[512,512]{1,0:T(8,128)(2,1)}, bf16[512,512]{1,0:T(8,128)(2,1)}, u32[]{:S(2)}, u32[]{:S(2)}) collective-permute-start(bf16[512,512]{1,0:T(8,128)(2,1)} %get-tuple-element.66), channel_id=1, source_target_pairs={{0,2},{1,3},{2,0},{3,1},{4,6},{5,7},{6,4},{7,5},{8,10},{9,11},{10,... | collective-permute-start | bytes 1572872 | tf_op jit(solution)/shard_map/ppermute | solution.py:1309
  51.7 34.3 %collective-permute-start.3 = (bf16[512,512]{1,0:T(8,128)(2,1)S(1)}, bf16[512,512]{1,0:T(8,128)(2,1)}, u32[]{:S(2)}, u32[]{:S(2)}) collective-permute-start(bf16[512,512]{1,0:T(8,128)(2,1)S(1)} %bitcast.63), channel_id=1, source_target_pairs={{0,4},{4,0},{8,12},{12,8},{16,20},{20,16},{24,28},{28,24},{1,5},{5... | collective-permute-start | bytes 1572872 | tf_op jit(solution)/shard_map/ppermute | solution.py:1384
  53.2 32.8 %collective-permute-start.2 = (bf16[512,1024]{1,0:T(8,128)(2,1)}, bf16[512,1024]{1,0:T(8,128)(2,1)}, u32[]{:S(2)}, u32[]{:S(2)}) collective-permute-start(bf16[512,1024]{1,0:T(8,128)(2,1)} %bitcast.8.y_half_ref), channel_id=1, source_target_pairs={{0,8},{4,12},{8,0},{12,4},{16,24},{20,28},{24,16},{28,20},{1,9},{5... | collective-permute-start | bytes 3145736 | tf_op jit(solution)/shard_map/ppermute | solution.py:1383
  54.4 4.3 %copy-start.44 = (f32[2,256]{1,0:T(2,128)}, f32[2,256]{1,0:T(2,128)S(1)}, u32[]{:S(2)}) copy-start(f32[2,256]{1,0:T(2,128)S(1)} %get-tuple-element.143) | copy-start | bytes 6148
  54.4 4.3 %copy-start.46 = (f32[2,256]{1,0:T(2,128)}, f32[2,256]{1,0:T(2,128)S(1)}, u32[]{:S(2)}) copy-start(f32[2,256]{1,0:T(2,128)S(1)} %get-tuple-element.145) | copy-start | bytes 6148
  54.5 4.3 %copy-start.38 = (f32[1,1024]{1,0:T(1,128)}, f32[1,1024]{1,0:T(1,128)S(1)}, u32[]{:S(2)}) copy-start(f32[1,1024]{1,0:T(1,128)S(1)} %get-tuple-element.140) | copy-start | bytes 12292
  54.5 4.3 %copy-start.40 = (f32[1,1024]{1,0:T(1,128)}, f32[1,1024]{1,0:T(1,128)S(1)}, u32[]{:S(2)}) copy-start(f32[1,1024]{1,0:T(1,128)S(1)} %get-tuple-element.141) | copy-start | bytes 12292
  54.5 4.3 %copy-start.42 = (f32[1,1024]{1,0:T(1,128)}, f32[1,1024]{1,0:T(1,128)S(1)}, u32[]{:S(2)}) copy-start(f32[1,1024]{1,0:T(1,128)S(1)} %get-tuple-element.142) | copy-start | bytes 12292
  56.0 2.8 copy-start.22
  56.0 2.9 copy-start.54
  56.0 2.9 %copy-start.55 = (bf16[1024]{0:T(1024)(128)(2,1)S(1)}, bf16[1024]{0:T(1024)(128)(2,1)}, u32[]{:S(2)}) copy-start(bf16[1024]{0:T(1024)(128)(2,1)} %param.20) | copy-start | bytes 6148
  58.8 12.9 %copy-start.3 = (bf16[2,256,1024]{2,1,0:T(8,128)(2,1)S(1)}, bf16[2,256,1024]{2,1,0:T(8,128)(2,1)}, u32[]{:S(2)}) copy-start(bf16[2,256,1024]{2,1,0:T(8,128)(2,1)} %get-tuple-element.65.z_ref) | copy-start | bytes 3145732
  58.8 12.9 %copy-start.13 = (bf16[128,1024]{1,0:T(8,128)(2,1)S(1)}, bf16[128,1024]{1,0:T(8,128)(2,1)}, u32[]{:S(2)}) copy-start(bf16[128,1024]{1,0:T(8,128)(2,1)} %dt_proj_ref.3) | copy-start | bytes 786436
  69.4 16.6 %collective-permute-start.1 = (bf16[512,512]{1,0:T(8,128)(2,1)}, bf16[512,512]{1,0:T(8,128)(2,1)S(1)}, u32[]{:S(2)}, u32[]{:S(2)}) collective-permute-start(bf16[512,512]{1,0:T(8,128)(2,1)} %copy-done.12), channel_id=1, source_target_pairs={{0,2},{1,3},{2,0},{3,1},{4,6},{5,7},{6,4},{7,5},{8,10},{9,11},{10,... | collective-permute-start | bytes 1572872 | tf_op jit(solution)/shard_map/ppermute | solution.py:1309
  86.0 1.6 copy-start.26
  88.9 1.2 copy-start.9
  88.9 1.5 copy-start.11
  90.0 29.4 %copy-start.4 = (bf16[2,256,1024]{2,1,0:T(8,128)(2,1)}, bf16[2,256,1024]{2,1,0:T(8,128)(2,1)S(1)}, u32[]{:S(2)}) copy-start(bf16[2,256,1024]{2,1,0:T(8,128)(2,1)S(1)} %get-tuple-element.129) | copy-start | bytes 3145732
  119.3 6.1 %copy-start.2 = (bf16[4096,512]{1,0:T(8,128)(2,1)S(1)}, bf16[4096,512]{1,0:T(8,128)(2,1)}, u32[]{:S(2)}) copy-start(bf16[4096,512]{1,0:T(8,128)(2,1)} %o_hbm.3) | copy-start | bytes 12582916
  119.4 6.1 %copy-start.7 = (bf16[2,256,2048]{2,1,0:T(8,128)(2,1)S(1)}, bf16[2,256,2048]{2,1,0:T(8,128)(2,1)}, u32[]{:S(2)}) copy-start(bf16[2,256,2048]{2,1,0:T(8,128)(2,1)} %get-tuple-element.87.xs_ref) | copy-start | bytes 6291460
  148.2 3.7 %copy-start.19 = (bf16[256,1024]{1,0:T(8,128)(2,1)}, bf16[256,1024]{1,0:T(8,128)(2,1)S(1)}, u32[]{:S(2)}) copy-start(bf16[256,1024]{1,0:T(8,128)(2,1)S(1)} %get-tuple-element.101.wz_ref) | copy-start | bytes 1572868
  151.9 9.0 %copy-start.16 = (f32[2,256,1024]{2,1,0:T(8,128)S(1)}, f32[2,256,1024]{2,1,0:T(8,128)}, u32[]{:S(2)}) copy-start(f32[2,256,1024]{2,1,0:T(8,128)} %get-tuple-element.92.rate_ref) | copy-start | bytes 6291460
  151.9 8.9 %copy-start.17 = (f32[2,256,1024]{2,1,0:T(8,128)S(1)}, f32[2,256,1024]{2,1,0:T(8,128)}, u32[]{:S(2)}) copy-start(f32[2,256,1024]{2,1,0:T(8,128)} %get-tuple-element.93.beta_ref) | copy-start | bytes 6291460
  152.9 46.1 %collective-permute-start.6 = (bf16[512,512]{1,0:T(8,128)(2,1)S(1)}, bf16[512,512]{1,0:T(8,128)(2,1)S(1)}, u32[]{:S(2)}, u32[]{:S(2)}) collective-permute-start(bf16[512,512]{1,0:T(8,128)(2,1)S(1)} %get-tuple-element.133), channel_id=1, source_target_pairs={{0,24},{4,28},{8,0},{12,4},{16,8},{20,12},{24,16},{28,20},{1,25},{... | collective-permute-start | bytes 1572872 | tf_op jit(solution)/shard_map/ppermute | solution.py:1323
  159.8 45.6 %collective-permute-start.5 = (bf16[512,512]{1,0:T(8,128)(2,1)S(1)}, bf16[512,512]{1,0:T(8,128)(2,1)S(1)}, u32[]{:S(2)}, u32[]{:S(2)}) collective-permute-start(bf16[512,512]{1,0:T(8,128)(2,1)S(1)} %get-tuple-element.134), channel_id=1, source_target_pairs={{0,16},{4,20},{8,24},{12,28},{16,0},{20,4},{24,8},{28,12},{1,17},{... | collective-permute-start | bytes 1572872 | tf_op jit(solution)/shard_map/ppermute | solution.py:1323
  160.3 45.1 %collective-permute-start.4 = (bf16[512,512]{1,0:T(8,128)(2,1)S(1)}, bf16[512,512]{1,0:T(8,128)(2,1)S(1)}, u32[]{:S(2)}, u32[]{:S(2)}) collective-permute-start(bf16[512,512]{1,0:T(8,128)(2,1)S(1)} %get-tuple-element.135), channel_id=1, source_target_pairs={{0,8},{4,12},{8,16},{12,20},{16,24},{20,28},{24,0},{28,4},{1,9},{5... | collective-permute-start | bytes 1572872 | tf_op jit(solution)/shard_map/ppermute | solution.py:1323
  189.2 0.8 copy-start.18
  190.0 17.0 %copy-start.20 = (f32[1,1024]{1,0:T(1,128)}, f32[1,1024]{1,0:T(1,128)S(1)}, u32[]{:S(2)}) copy-start(f32[1,1024]{1,0:T(1,128)S(1)} %get-tuple-element.99.db_ref) | copy-start | bytes 12292
  190.0 17.0 %copy-start.21 = (f32[1,1024]{1,0:T(1,128)}, f32[1,1024]{1,0:T(1,128)S(1)}, u32[]{:S(2)}) copy-start(f32[1,1024]{1,0:T(1,128)S(1)} %get-tuple-element.100.sk_ref) | copy-start | bytes 12292
  190.0 17.1 %copy-start.25 = (bf16[2,256,1024]{2,1,0:T(8,128)(2,1)S(1)}, bf16[2,256,1024]{2,1,0:T(8,128)(2,1)}, u32[]{:S(2)}) copy-start(bf16[2,256,1024]{2,1,0:T(8,128)(2,1)} %get-tuple-element.64) | copy-start | bytes 3145732
  198.9 8.1 %copy-start.23 = (f32[2,256,1024]{2,1,0:T(8,128)S(1)}, f32[2,256,1024]{2,1,0:T(8,128)}, u32[]{:S(2)}) copy-start(f32[2,256,1024]{2,1,0:T(8,128)} %copy-done.22) | copy-start | bytes 6291460
  198.9 8.1 %copy-start.24 = (f32[2,256,1024]{2,1,0:T(8,128)S(1)}, f32[2,256,1024]{2,1,0:T(8,128)}, u32[]{:S(2)}) copy-start(f32[2,256,1024]{2,1,0:T(8,128)} %get-tuple-element.127) | copy-start | bytes 6291460
  198.9 8.1 %copy-start.45 = (f32[2,256]{1,0:T(2,128)S(1)}, f32[2,256]{1,0:T(2,128)}, u32[]{:S(2)}) copy-start(f32[2,256]{1,0:T(2,128)} %copy-done.44) | copy-start | bytes 6148
  199.0 8.1 %copy-start.47 = (f32[2,256]{1,0:T(2,128)S(1)}, f32[2,256]{1,0:T(2,128)}, u32[]{:S(2)}) copy-start(f32[2,256]{1,0:T(2,128)} %copy-done.46) | copy-start | bytes 6148
  199.0 8.1 %copy-start.32 = (bf16[512,512]{1,0:T(8,128)(2,1)}, bf16[512,512]{1,0:T(8,128)(2,1)S(1)}, u32[]{:S(2)}) copy-start(bf16[512,512]{1,0:T(8,128)(2,1)S(1)} %collective-permute-done.6) | copy-start | bytes 1572868
  205.3 1.7 copy-start.34
  205.3 1.7 copy-start.36
  210.2 0.7 copy-start.41
  210.2 0.7 copy-start.43
  213.6 63.3 %copy-start.28 = (bf16[512,512]{1,0:T(8,128)(2,1)S(1)}, bf16[512,512]{1,0:T(8,128)(2,1)}, u32[]{:S(2)}) copy-start(bf16[512,512]{1,0:T(8,128)(2,1)} %get-tuple-element.113) | copy-start | bytes 1572868
  213.6 63.3 %copy-start.33 = (bf16[512,512]{1,0:T(8,128)(2,1)S(1)}, bf16[512,512]{1,0:T(8,128)(2,1)}, u32[]{:S(2)}) copy-start(bf16[512,512]{1,0:T(8,128)(2,1)} %copy-done.32) | copy-start | bytes 1572868
  213.6 63.3 %copy-start.35 = (bf16[512,512]{1,0:T(8,128)(2,1)S(1)}, bf16[512,512]{1,0:T(8,128)(2,1)}, u32[]{:S(2)}) copy-start(bf16[512,512]{1,0:T(8,128)(2,1)} %copy-done.34) | copy-start | bytes 1572868
  213.6 63.3 %copy-start.37 = (bf16[512,512]{1,0:T(8,128)(2,1)S(1)}, bf16[512,512]{1,0:T(8,128)(2,1)}, u32[]{:S(2)}) copy-start(bf16[512,512]{1,0:T(8,128)(2,1)} %copy-done.36) | copy-start | bytes 1572868
  277.0 2.1 copy-start.31
  277.0 2.8 copy-start.56
  277.0 3.4 %copy-start.27 = (f32[256,2048]{1,0:T(8,128)S(1)}, f32[256,2048]{1,0:T(8,128)}, u32[]{:S(2)}) copy-start(f32[256,2048]{1,0:T(8,128)} %get-tuple-element.160) | copy-start | bytes 6291460
  280.4 1.4 copy-start.49
  280.4 2.0 copy-start.52
  280.4 2.6 copy-start.29
  280.4 3.4 %copy-start.30 = (f32[128,1024]{1,0:T(8,128)S(1)}, f32[128,1024]{1,0:T(8,128)}, u32[]{:S(2)}) copy-start(f32[128,1024]{1,0:T(8,128)} %get-tuple-element.164) | copy-start | bytes 1572868
  280.4 5.4 %copy-start.1 = (bf16[160,1024]{1,0:T(8,128)(2,1)S(1)}, bf16[160,1024]{1,0:T(8,128)(2,1)}, u32[]{:S(2)}) copy-start(bf16[160,1024]{1,0:T(8,128)(2,1)} %param.18) | copy-start | bytes 983044
  281.8 2.8 copy-start.51
  281.8 3.4 %copy-start.50 = (f32[1,1024]{1,0:T(1,128)S(1)}, f32[1,1024]{1,0:T(1,128)}, u32[]{:S(2)}) copy-start(f32[1,1024]{1,0:T(1,128)} %get-tuple-element.112) | copy-start | bytes 12292
  (1 other events, 0.7 us)

commit v10 on v9

--- a/solution.py
+++ b/solution.py
@@ -657,14 +657,19 @@
 
 def collect_kernel(
     keep_ref, give_ref, gz_ref, own_half_ref, y_half_ref, z_half_ref, last_ref,
-    keeps_ref, gives_ref, gz_ref4, norm_ref, got_ref,
-    sends, recvs, local,
+    keeps_ref, gives_ref, zb_ref, norm_out_ref, got_ref,
+    gz_ref4, norm_ref, turned, sends, recvs, local,
 ):
     me = lax.axis_index("shard")
     half = keep_ref.shape[1]
     core = lax.rem(me, 2)
     member = lax.rem(lax.axis_index("replica"), 4)
-    part = gz_ref4.shape[2]
+    tokens, part = gz_ref4.shape[1:]
+    tile = 256
+
+    def norm_rows(which):
+        return norm_ref.at[core, which * tokens : (which + 1) * tokens]
+
     meet([quad(hop) for hop in (1, 2, 3)])
 
     def quarter(which):
@@ -682,29 +687,45 @@
     ]
     give_pair = across(give_ref, got_ref, sends, recvs, 11, quad(1))
     norms = [
-        remote(own_half_ref, norm_ref.at[core, 0], sends, recvs, 12, 1),
-        remote(y_half_ref, norm_ref.at[core, 1], sends, recvs, 10, 1),
-        remote(z_half_ref, norm_ref.at[core, 2], sends, recvs, 13, 1),
-        remote(last_ref, norm_ref.at[core, 3], sends, recvs, 4, 1),
+        remote(own_half_ref, norm_rows(0), sends, recvs, 12, 1),
+        remote(y_half_ref, norm_rows(1), sends, recvs, 10, 1),
+        remote(z_half_ref, norm_rows(2), sends, recvs, 13, 1),
+        remote(last_ref, norm_rows(3), sends, recvs, 4, 1),
     ]
     own = [
         pltpu.make_async_copy(keep_ref, spot(keeps_ref, me), local.at[0]),
         pltpu.make_async_copy(give_ref, spot(gives_ref, me), local.at[1]),
         pltpu.make_async_copy(quarter(member), gz_ref4.at[0], local.at[2]),
-        pltpu.make_async_copy(own_half_ref, norm_ref.at[core, 0], local.at[5]),
-        pltpu.make_async_copy(y_half_ref, norm_ref.at[core, 1], local.at[3]),
-        pltpu.make_async_copy(z_half_ref, norm_ref.at[core, 2], local.at[6]),
-        pltpu.make_async_copy(last_ref, norm_ref.at[core, 3], local.at[4]),
+        pltpu.make_async_copy(own_half_ref, norm_rows(0), local.at[5]),
+        pltpu.make_async_copy(y_half_ref, norm_rows(1), local.at[3]),
+        pltpu.make_async_copy(z_half_ref, norm_rows(2), local.at[6]),
+        pltpu.make_async_copy(last_ref, norm_rows(3), local.at[4]),
     ]
     for copy in [k_chip, v_chip] + quads + [give_pair, k_core, v_core] + norms + own:
         copy.start()
+    for copy in own + quads + norms:
+        copy.wait()
+    out_copy = pltpu.make_async_copy(norm_ref, norm_out_ref, local.at[7])
+    out_copy.start()
+    for hop in range(4):
+        for at in range(0, tokens, tile):
+            turned[:, hop * tokens + at : hop * tokens + at + tile] = gz_ref4[hop, at : at + tile, :].T
+    wide = norm_ref.shape[2] // tile
+
+    def rows_of(t, carry):
+        feature = pl.ds(pl.multiple_of(lax.rem(t, wide) * tile, tile), tile)
+        value = rows_dot(turned[...], norm_ref[t // wide, :, feature])
+        zb_ref[pl.ds(pl.multiple_of(t * tile, tile), tile), :] = value.astype(bf16).T
+        return carry
+
+    lax.fori_loop(0, zb_ref.shape[0] // tile, rows_of, 0)
     k_chip.wait_recv()
     k_on = remote(spot(keeps_ref, peer(2)), spot(keeps_ref, peer(2)), sends, recvs, 5, 1)
     k_on.start()
     v_chip.wait_recv()
     v_on = remote(spot(gives_ref, peer(2)), spot(gives_ref, peer(2)), sends, recvs, 6, 1)
     v_on.start()
-    for copy in own + quads + norms + [give_pair, k_core, v_core, k_on, v_on]:
+    for copy in [give_pair, k_core, v_core, k_on, v_on, out_copy]:
         copy.wait()
     k_chip.wait_send()
     v_chip.wait_send()
@@ -718,19 +739,23 @@
     tokens, half = keep.shape
     group = lax.axis_size("shard")
     wide = jax.ShapeDtypeStruct((tokens, half * group), bf16)
+    features, quarter = last_norm.shape[1], grad_z.shape[1] // 4
     return pl.pallas_call(
         collect_kernel,
         in_specs=[VMEM_SPEC] * 7,
         out_specs=[VMEM_SPEC] * 3 + [ANY_SPEC, VMEM_SPEC],
         out_shape=[
-            wide, wide, jax.ShapeDtypeStruct((4, tokens, grad_z.shape[1] // 4), bf16),
-            pltpu.HBM((2, 4) + last_norm.shape, bf16),
+            wide, wide, jax.ShapeDtypeStruct((2 * features, quarter), bf16),
+            pltpu.HBM((2, 4 * tokens, features), bf16),
             jax.ShapeDtypeStruct(give.shape, bf16),
         ],
         scratch_shapes=[
-            pltpu.SemaphoreType.DMA((14,)), pltpu.SemaphoreType.DMA((14,)), pltpu.SemaphoreType.DMA((7,)),
+            pltpu.VMEM((4, tokens, quarter), bf16),
+            pltpu.VMEM((2, 4 * tokens, features), bf16),
+            pltpu.VMEM((quarter, 4 * tokens), bf16),
+            pltpu.SemaphoreType.DMA((14,)), pltpu.SemaphoreType.DMA((14,)), pltpu.SemaphoreType.DMA((8,)),
         ],
-        compiler_params=group_params(6, 28 << 20),
+        compiler_params=group_params(6, 34 << 20),
         cost_estimate=cost(25),
         name="collect",
     )(keep, give, grad_z, own_half, y_half, z_half, last_norm)
@@ -1402,14 +1427,10 @@
 
     gated_keep, gated_give = halves(gated.reshape(tokens, width), height // 4)
     cols = model // 4
-    keeps, gives, grad_z_quad, norms, gated_got = collect(
+    keeps, gives, z_blocks, norms, gated_got = collect(
         gated_keep, gated_give, grad_z, own_half, y_half, z_half, last_norm
     )
-    norms = norms.reshape(2, 4 * tokens, -1)
-    z_blocks = lax.dot_general(
-        norms, grad_z_quad.reshape(4 * tokens, -1), (((1,), (0,)), ((), ())), preferred_element_type=f32
-    )
-    z_blocks = z_blocks.astype(bf16).reshape(count, -1, width // 4)
+    z_blocks = z_blocks.reshape(count, -1, width // 4)
     gated_both, block_output, grad_w_z = middle(keeps, gives, gated_got, z_blocks, x_all, out_proj, seqs)
     out_blocks = inner_dot(gated_both.reshape(2 * tokens, -1), cot_both)
     out_own, out_sent = far_send(out_blocks.astype(bf16).reshape(height, -1, cols))

time: 287 us -> 280 us (0.976)
  matrix products: 11.9 us -> 5.76 us
    dot_general x1 -> x0, matrix products: 6.07 us -> none  [body(): lax.dot_general(norms, grad_z_quad.reshape(4 * tokens, -1), (((1,), (0,))...]
    unnamed x126 -> x112, local copies, waits for them, and re-layouts: 12.8 us -> 12.8 us
where the time goes in v10:
time: 280 us; the launch traced here: 279 us
  Pallas kernels  219 us (78%)
  starting transfers between devices  18 us (6%)
  other arithmetic  14.2 us (5%)
  local copies, waits for them, and re-layouts  13.8 us (5%)
  waiting for transfers between devices  6.36 us (2%)
  matrix products  5.76 us (2%)
    pallas_call x1, Pallas kernels, finish(): pl.pallas_call(finish_kernel, in_specs=[VMEM_SPEC] * 9 + [ANY_SPEC] * 2 +...  63.1 us
    pallas_call x1, Pallas kernels, front(): pl.pallas_call(front_kernel, in_specs=[VMEM_SPEC] * 3 + [ANY_SPEC] * 2, o...  42.9 us
    pallas_call x1, Pallas kernels, collect(): pl.pallas_call(collect_kernel, in_specs=[VMEM_SPEC] * 7, out_specs=[VMEM_...  29 us
    pallas_call x1, Pallas kernels, recurrence_backward(): pl.pallas_call(backward_kernel, grid=(seqs, blocks), in_specs=[wide, wide...  28.3 us
    pallas_call x1, Pallas kernels, middle(): pl.pallas_call(middle_kernel, in_specs=[VMEM_SPEC] * 4 + [ANY_SPEC] * 2,...  22.7 us
    pallas_call x2, Pallas kernels, group_total(): pl.pallas_call(total_kernel, in_specs=[VMEM_SPEC], out_specs=VMEM_SPEC, o...  18.9 us
    pallas_call x1, Pallas kernels, recurrence_forward(): pl.pallas_call(forward_kernel, grid=(seqs, blocks), in_specs=[wide, wide,...  14.3 us
    unnamed x112, local copies, waits for them, and re-layouts  12.8 us
  transfers between devices with their start and end apart: 7, of which 1 were waited for; matrix products, arithmetic and copies ran while one was open for 2% of the time, Pallas kernels for 22%

profile of v10, /device:TPU:0, one launch (start us, length us, event | category | flops | bytes accessed | tf_op | source)
XLA Modules:
  0.0 278.8 jit_solution(17976106246132558494)
XLA Ops:
  0.6 0.0 copy-start
  0.7 0.7 broadcast_in_dim.12.gain_ref
  1.4 1.0 copy-done.5
  2.4 1.0 copy-done.6
  3.5 42.9 %front.1 = (bf16[2,256,2048]{2,1,0:T(8,128)(2,1)}, f32[2,256,128]{2,1,0:T(8,128)S(1)}, bf16[2,256,512]{2,1,0:T(8,128)(2,1)S(1)}, f32[8,2048]{1,0:T(8,128)S(1)}, ...) custom-call(bf16[2,64,2048]{2,1,0:T(8,128)(2,1)S(1)} %copy-done.5, ...), custom_call_target="tpu_custom_call" | custom-call | tf_op jit(solution)/shard_map/front/pallas_call | solution.py:592
  46.4 0.0 copy-start.8
  46.4 0.0 copy-start.12
  46.5 5.2 %collective-permute-start = (bf16[512,512]{1,0:T(8,128)(2,1)}, bf16[512,512]{1,0:T(8,128)(2,1)}, u32[]{:S(2)}, u32[]{:S(2)}) collective-permute-start(bf16[512,512]{1,0:T(8,128)(2,1)} %get-tuple-element.66), channel_id=1, source_target_pairs={{0,2},{1,3},{2,0},{3,1},{4,6},{5,7},{6,4},{7,5},{8,10},{9,11},{10,... | collective-permute-start | bytes 1572872 | tf_op jit(solution)/shard_map/ppermute | solution.py:1334
  51.7 1.5 collective-permute-start.3
  53.2 1.1 collective-permute-start.2
  54.3 0.1 compare_convert_fusion.2
  54.4 0.0 copy-start.39
  54.5 0.0 copy-start.33
  54.5 0.0 copy-start.35
  54.5 1.5 convert_element_type.72
  56.0 0.0 copy-start.47
  56.0 0.0 copy-start.48
  56.0 2.7 fusion.12
  58.9 0.5 convolution_bitcast_fusion.part_ref
  59.4 10.0 %group_total.2.proj_ref = f32[160,512]{1,0:T(8,128)S(1)} custom-call(f32[160,512]{1,0:T(8,128)S(1)} %convolution_bitcast_fusion.part_ref), custom_call_target="tpu_custom_call" | custom-call | tf_op jit(solution)/shard_map/group_total/pallas_call | solution.py:1322
  69.4 2.1 collective-permute-start.1
  71.5 0.1 broadcast_in_dim.13.keep_ref
  71.6 14.3 %recurrence_forward.1 = (f32[2,256,1024]{2,1,0:T(8,128)S(1)}, bf16[2,256,1024]{2,1,0:T(8,128)(2,1)S(1)}, f32[2,256,1024]{2,1,0:T(8,128)}, f32[2,256,1024]{2,1,0:T(8,128)}, bf16[2,4096,1024]{2,1,0:T(8,128)(2,1)}) custom-call(bf16[2,256,1024]{2,1,0:T(8,128)(2,1)S(1)} %get-tuple-element.126.conv_ref, bf16[2,256,1024]{2,1,0:T(8,128)(2,1)S(1)} %copy-done.3, ...), custom_call_target="tpu_custom_call" | custom-call | flops 16000000000 | bytes 25165824 | tf_op jit(solution)/shard_map/recurrence_forward/pallas_call | solution.py:289
  85.9 0.1 broadcast_select_fusion
  86.0 1.5 copy-done.26
  87.5 1.5 convert_add_fusion
  89.0 0.0 copy-start.9
  89.0 1.1 fusion.11
  90.1 0.1 copy-done.9
  90.2 0.3 copy-done.11
  90.5 29.0 %collect.1 = (bf16[512,2048]{1,0:T(8,128)(2,1)S(1)}, bf16[512,2048]{1,0:T(8,128)(2,1)S(1)}, bf16[2048,256]{1,0:T(8,128)(2,1)S(1)}, bf16[2,2048,1024]{2,1,0:T(8,128)(2,1)}, bf16[512,512]{1,0:T(8,128)(2,1)S(1)}) custom-call(bf16[512,512]{1,0:T(8,128)(2,1)S(1)} %get-tuple-element.138.keep_ref, bf16[512,512]{1,0:T(8,128)(2,1)S(1)} %get-tuple-element.137.give_ref, ...), custom_call_target="tpu_custom_call" | custom-call | flops 24999999488 | bytes 1048576 | tf_op jit(solution)/shard_map/collect/pallas_call | solution.py:743
  119.6 22.7 %middle.1 = (bf16[2,512,2048]{2,1,0:T(8,128)(2,1)S(1)}, bf16[2,64,2048]{2,1,0:T(8,128)(2,1)S(1)}, bf16[256,1024]{1,0:T(8,128)(2,1)S(1)}) custom-call(bf16[512,2048]{1,0:T(8,128)(2,1)S(1)} %get-tuple-element.82.keeps_ref, bf16[512,2048]{1,0:T(8,128)(2,1)S(1)} %get-tuple-element.83.gives_ref, bf16[512,512]{1,0:T(8,128)(2,1)S(1)} %get-tuple-element.84.got_ref, ...), custom_call_target="tpu_custom_call" | custom-call | flops 24999999488 | bytes 1048576 | tf_op jit(solution)/shard_map/middle/pallas_call | solution.py:870
  142.4 3.6 %convolution_convert_fusion = bf16[2048,512]{1,0:T(8,128)(2,1)S(1)} fusion(bf16[1024,2048]{1,0:T(8,128)(2,1)S(1)} %bitcast.57, bf16[512,512]{1,0:T(8,128)(2,1)} %collective-permute-done.3, bf16[512,512]{1,0:T(8,128)(2,1)S(1)} %bitcast.56), kind=kOutput, calls=%fused_computation | convolution fusion | flops 2150629376 | bytes 7340032 | tf_op jit(solution)/shard_map/dot_general | solution.py:23
  146.0 0.2 dynamic-slice_bitcast_fusion
  146.2 6.9 %collective-permute-start.6 = (bf16[512,512]{1,0:T(8,128)(2,1)S(1)}, bf16[512,512]{1,0:T(8,128)(2,1)S(1)}, u32[]{:S(2)}, u32[]{:S(2)}) collective-permute-start(bf16[512,512]{1,0:T(8,128)(2,1)S(1)} %get-tuple-element.133), channel_id=1, source_target_pairs={{0,24},{4,28},{8,0},{12,4},{16,8},{20,12},{24,16},{28,20},{1,25},{... | collective-permute-start | bytes 1572872 | tf_op jit(solution)/shard_map/ppermute | solution.py:1348
  153.1 0.5 collective-permute-start.5
  153.6 0.6 collective-permute-start.4
  154.2 28.3 %recurrence_backward.1 = (f32[2,256,1024]{2,1,0:T(8,128)S(1)}, bf16[2,256,1024]{2,1,0:T(8,128)(2,1)}, f32[160,512]{1,0:T(8,128)S(1)}, f32[128,1024]{1,0:T(8,128)...) custom-call(f32[2,256,1024]{2,1,0:T(8,128)S(1)} %copy-done.16, f32[2,256,1024]{2,1,0:T(8,128)S(1)} %copy-done.17, ...), custom_call_target="tpu_custom_call" | custom-call | flops 30000001024 | bytes 29360128 | tf_op jit(solution)/shard_map/recurrence_backward/pallas_call | solution.py:324
  182.6 0.8 copy-done.18
  183.4 8.9 %group_total.3 = f32[160,512]{1,0:T(8,128)S(1)} custom-call(f32[160,512]{1,0:T(8,128)S(1)} %get-tuple-element.95.part_ref), custom_call_target="tpu_custom_call" | custom-call | tf_op jit(solution)/shard_map/group_total/pallas_call | solution.py:1322
  192.3 0.0 copy-start.38
  192.3 0.0 copy-start.40
  192.3 6.3 %collective-permute-done.5 = bf16[512,512]{1,0:T(8,128)(2,1)S(1)} collective-permute-done((bf16[512,512]{1,0:T(8,128)(2,1)S(1)}, bf16[512,512]{1,0:T(8,128)(2,1)S(1)}, u32[]{:S(2)}, u32[]{:S(2)}) %collective-permute-start.5) | collective-permute-done | bytes 524320 | tf_op jit(solution)/shard_map/ppermute | solution.py:1348
  198.7 1.2 fusion.16.xp_ref
  199.9 0.5 fusion.18
  200.4 3.0 %fusion.21 = (f32[1024]{0:T(1024)}, f32[1024]{0:T(1024)S(1)}, f32[1024]{0:T(1024)S(1)}, f32[1024]{0:T(1024)S(1)}, f32[1024]{0:T(1024)S(1)}, /*index=5*/f32[2,256,1024]{2,1,0:T(8,128)S(1)}) fusion(bf16[2,256,1024]{2,1,0:T(8,128)(2,1)S(1)} %copy-done.25, f32[2,256]{1,0:T(2,128)S(1)} %copy-done.40, f32[2,256,1024]{2,1,0:T(8,128)S(1)} %copy-done.23, ...), kind=kLoop, calls=%fused_computation.56 | loop fusion | flops 12577792 | bytes 13662208 | tf_op jit(solution)/shard_map/reduce_sum | solution.py:1448
  203.4 0.5 broadcast_multiply_fusion
  203.9 0.2 copy-done.32
  204.1 0.0 copy-done.34
  204.1 0.0 copy-done.36
  204.1 2.1 fusion.4
  206.2 0.6 pad_maximum_fusion.cw_ref
  206.8 63.1 %finish.1 = (f32[256,2048]{1,0:T(8,128)}, f32[160,1024]{1,0:T(8,128)}, f32[128,1024]{1,0:T(8,128)}, f32[4,1024]{1,0:T(4,128)}, f32[1,1024]{1,0:T(1,128)}, /*inde...) custom-call(bf16[512,1024]{1,0:T(8,128)(2,1)} %bitcast.61, ...), custom_call_target="tpu_custom_call" | custom-call | flops 80000000000 | bytes 1048576 | tf_op jit(solution)/shard_map/finish/pallas_call | solution.py:1246
  270.0 1.2 convert_add_fusion.1
  271.2 0.8 copy.33
  272.0 0.8 copy.34
  272.8 0.6 copy.35
  273.4 1.3 copy.36
  274.8 0.6 copy.37
  275.4 0.6 copy.38
  276.0 0.8 copy.39
  276.8 0.8 copy.40
  277.6 0.6 copy.41
  278.2 0.6 copy.42
  (92 shorter events, 0.2 us)
Async XLA Ops:
  0.6 58.2 %copy-start = (bf16[160,1024]{1,0:T(8,128)(2,1)S(1)}, bf16[160,1024]{1,0:T(8,128)(2,1)}, u32[]{:S(2)}) copy-start(bf16[160,1024]{1,0:T(8,128)(2,1)} %param.18) | copy-start | bytes 983044
  1.4 1.0 copy-start.5
  2.4 1.0 copy-start.6
  3.5 50.9 %copy-start.46 = (bf16[1024]{0:T(1024)(128)(2,1)S(1)}, bf16[1024]{0:T(1024)(128)(2,1)}, u32[]{:S(2)}) copy-start(bf16[1024]{0:T(1024)(128)(2,1)} %param.17) | copy-start | bytes 6148
  3.5 50.9 %copy-start.50 = (s32[2,256]{1,0:T(2,128)S(1)}, s32[2,256]{1,0:T(2,128)}, u32[]{:S(2)}) copy-start(s32[2,256]{1,0:T(2,128)} %param.13) | copy-start | bytes 6148
  3.5 50.9 %copy-start.41 = (bf16[4,1024]{1,0:T(4,128)(2,1)S(1)}, bf16[4,1024]{1,0:T(4,128)(2,1)}, u32[]{:S(2)}) copy-start(bf16[4,1024]{1,0:T(4,128)(2,1)} %param.16) | copy-start | bytes 24580
  46.4 12.3 %copy-start.8 = (bf16[2,256,1024]{2,1,0:T(8,128)(2,1)}, bf16[2,256,1024]{2,1,0:T(8,128)(2,1)S(1)}, u32[]{:S(2)}) copy-start(bf16[2,256,1024]{2,1,0:T(8,128)(2,1)S(1)} %get-tuple-element.79) | copy-start | bytes 3145732
  46.4 12.3 %copy-start.10 = (bf16[2,256,1024]{2,1,0:T(8,128)(2,1)}, bf16[2,256,1024]{2,1,0:T(8,128)(2,1)S(1)}, u32[]{:S(2)}) copy-start(bf16[2,256,1024]{2,1,0:T(8,128)(2,1)S(1)} %get-tuple-element.80) | copy-start | bytes 3145732
  46.4 12.3 %copy-start.12 = (bf16[512,512]{1,0:T(8,128)(2,1)}, bf16[512,512]{1,0:T(8,128)(2,1)S(1)}, u32[]{:S(2)}) copy-start(bf16[512,512]{1,0:T(8,128)(2,1)S(1)} %get-tuple-element.71) | copy-start | bytes 1572868
  46.4 12.3 %copy-start.14 = (f32[2,256,128]{2,1,0:T(8,128)}, f32[2,256,128]{2,1,0:T(8,128)S(1)}, u32[]{:S(2)}) copy-start(f32[2,256,128]{2,1,0:T(8,128)S(1)} %get-tuple-element.103.inv_ref) | copy-start | bytes 786436
  46.4 12.2 %copy-start.15 = (f32[8,2048]{1,0:T(8,128)}, f32[8,2048]{1,0:T(8,128)S(1)}, u32[]{:S(2)}) copy-start(f32[8,2048]{1,0:T(8,128)S(1)} %get-tuple-element.102.gain_ref) | copy-start | bytes 196612
  46.5 22.9 %collective-permute-start = (bf16[512,512]{1,0:T(8,128)(2,1)}, bf16[512,512]{1,0:T(8,128)(2,1)}, u32[]{:S(2)}, u32[]{:S(2)}) collective-permute-start(bf16[512,512]{1,0:T(8,128)(2,1)} %get-tuple-element.66), channel_id=1, source_target_pairs={{0,2},{1,3},{2,0},{3,1},{4,6},{5,7},{6,4},{7,5},{8,10},{9,11},{10,... | collective-permute-start | bytes 1572872 | tf_op jit(solution)/shard_map/ppermute | solution.py:1334
  51.7 34.2 %collective-permute-start.3 = (bf16[512,512]{1,0:T(8,128)(2,1)S(1)}, bf16[512,512]{1,0:T(8,128)(2,1)}, u32[]{:S(2)}, u32[]{:S(2)}) collective-permute-start(bf16[512,512]{1,0:T(8,128)(2,1)S(1)} %bitcast.55), channel_id=1, source_target_pairs={{0,4},{4,0},{8,12},{12,8},{16,20},{20,16},{24,28},{28,24},{1,5},{5... | collective-permute-start | bytes 1572872 | tf_op jit(solution)/shard_map/ppermute | solution.py:1409
  53.2 32.7 %collective-permute-start.2 = (bf16[512,1024]{1,0:T(8,128)(2,1)}, bf16[512,1024]{1,0:T(8,128)(2,1)}, u32[]{:S(2)}, u32[]{:S(2)}) collective-permute-start(bf16[512,1024]{1,0:T(8,128)(2,1)} %bitcast.8.y_half_ref), channel_id=1, source_target_pairs={{0,8},{4,12},{8,0},{12,4},{16,24},{20,28},{24,16},{28,20},{1,9},{5... | collective-permute-start | bytes 3145736 | tf_op jit(solution)/shard_map/ppermute | solution.py:1408
  54.4 4.3 %copy-start.37 = (f32[2,256]{1,0:T(2,128)}, f32[2,256]{1,0:T(2,128)S(1)}, u32[]{:S(2)}) copy-start(f32[2,256]{1,0:T(2,128)S(1)} %get-tuple-element.143) | copy-start | bytes 6148
  54.4 4.3 %copy-start.39 = (f32[2,256]{1,0:T(2,128)}, f32[2,256]{1,0:T(2,128)S(1)}, u32[]{:S(2)}) copy-start(f32[2,256]{1,0:T(2,128)S(1)} %get-tuple-element.145) | copy-start | bytes 6148
  54.5 4.3 %copy-start.31 = (f32[1,1024]{1,0:T(1,128)}, f32[1,1024]{1,0:T(1,128)S(1)}, u32[]{:S(2)}) copy-start(f32[1,1024]{1,0:T(1,128)S(1)} %get-tuple-element.140) | copy-start | bytes 12292
  54.5 4.3 %copy-start.33 = (f32[1,1024]{1,0:T(1,128)}, f32[1,1024]{1,0:T(1,128)S(1)}, u32[]{:S(2)}) copy-start(f32[1,1024]{1,0:T(1,128)S(1)} %get-tuple-element.141) | copy-start | bytes 12292
  54.5 4.3 %copy-start.35 = (f32[1,1024]{1,0:T(1,128)}, f32[1,1024]{1,0:T(1,128)S(1)}, u32[]{:S(2)}) copy-start(f32[1,1024]{1,0:T(1,128)S(1)} %get-tuple-element.142) | copy-start | bytes 12292
  56.0 2.8 %copy-start.22 = (f32[2,256,1024]{2,1,0:T(8,128)}, f32[2,256,1024]{2,1,0:T(8,128)S(1)}, u32[]{:S(2)}) copy-start(f32[2,256,1024]{2,1,0:T(8,128)S(1)} %convert_element_type.72) | copy-start | bytes 6291460
  56.0 2.9 %copy-start.47 = (bf16[1024]{0:T(1024)(128)(2,1)S(1)}, bf16[1024]{0:T(1024)(128)(2,1)}, u32[]{:S(2)}) copy-start(bf16[1024]{0:T(1024)(128)(2,1)} %param.21) | copy-start | bytes 6148
  56.0 2.9 %copy-start.48 = (bf16[1024]{0:T(1024)(128)(2,1)S(1)}, bf16[1024]{0:T(1024)(128)(2,1)}, u32[]{:S(2)}) copy-start(bf16[1024]{0:T(1024)(128)(2,1)} %param.20) | copy-start | bytes 6148
  58.8 12.9 %copy-start.3 = (bf16[2,256,1024]{2,1,0:T(8,128)(2,1)S(1)}, bf16[2,256,1024]{2,1,0:T(8,128)(2,1)}, u32[]{:S(2)}) copy-start(bf16[2,256,1024]{2,1,0:T(8,128)(2,1)} %get-tuple-element.65.z_ref) | copy-start | bytes 3145732
  58.8 12.9 %copy-start.13 = (bf16[128,1024]{1,0:T(8,128)(2,1)S(1)}, bf16[128,1024]{1,0:T(8,128)(2,1)}, u32[]{:S(2)}) copy-start(bf16[128,1024]{1,0:T(8,128)(2,1)} %dt_proj_ref.3) | copy-start | bytes 786436
  69.4 16.5 %collective-permute-start.1 = (bf16[512,512]{1,0:T(8,128)(2,1)}, bf16[512,512]{1,0:T(8,128)(2,1)S(1)}, u32[]{:S(2)}, u32[]{:S(2)}) collective-permute-start(bf16[512,512]{1,0:T(8,128)(2,1)} %copy-done.12), channel_id=1, source_target_pairs={{0,2},{1,3},{2,0},{3,1},{4,6},{5,7},{6,4},{7,5},{8,10},{9,11},{10,... | collective-permute-start | bytes 1572872 | tf_op jit(solution)/shard_map/ppermute | solution.py:1334
  85.9 1.6 copy-start.26
  89.0 1.2 copy-start.9
  89.0 1.5 copy-start.11
  90.1 29.5 %copy-start.4 = (bf16[2,256,1024]{2,1,0:T(8,128)(2,1)}, bf16[2,256,1024]{2,1,0:T(8,128)(2,1)S(1)}, u32[]{:S(2)}) copy-start(bf16[2,256,1024]{2,1,0:T(8,128)(2,1)S(1)} %get-tuple-element.129) | copy-start | bytes 3145732
  90.5 29.1 %copy-start.2 = (bf16[4096,512]{1,0:T(8,128)(2,1)S(1)}, bf16[4096,512]{1,0:T(8,128)(2,1)}, u32[]{:S(2)}) copy-start(bf16[4096,512]{1,0:T(8,128)(2,1)} %o_hbm.3) | copy-start | bytes 12582916
  90.5 29.1 %copy-start.7 = (bf16[2,256,2048]{2,1,0:T(8,128)(2,1)S(1)}, bf16[2,256,2048]{2,1,0:T(8,128)(2,1)}, u32[]{:S(2)}) copy-start(bf16[2,256,2048]{2,1,0:T(8,128)(2,1)} %get-tuple-element.86.xs_ref) | copy-start | bytes 6291460
  142.4 3.6 %copy-start.19 = (bf16[256,1024]{1,0:T(8,128)(2,1)}, bf16[256,1024]{1,0:T(8,128)(2,1)S(1)}, u32[]{:S(2)}) copy-start(bf16[256,1024]{1,0:T(8,128)(2,1)S(1)} %get-tuple-element.100.wz_ref) | copy-start | bytes 1572868
  146.0 8.2 %copy-start.16 = (f32[2,256,1024]{2,1,0:T(8,128)S(1)}, f32[2,256,1024]{2,1,0:T(8,128)}, u32[]{:S(2)}) copy-start(f32[2,256,1024]{2,1,0:T(8,128)} %get-tuple-element.91.rate_ref) | copy-start | bytes 6291460
  146.0 8.2 %copy-start.17 = (f32[2,256,1024]{2,1,0:T(8,128)S(1)}, f32[2,256,1024]{2,1,0:T(8,128)}, u32[]{:S(2)}) copy-start(f32[2,256,1024]{2,1,0:T(8,128)} %get-tuple-element.92.beta_ref) | copy-start | bytes 6291460
  146.2 46.1 %collective-permute-start.6 = (bf16[512,512]{1,0:T(8,128)(2,1)S(1)}, bf16[512,512]{1,0:T(8,128)(2,1)S(1)}, u32[]{:S(2)}, u32[]{:S(2)}) collective-permute-start(bf16[512,512]{1,0:T(8,128)(2,1)S(1)} %get-tuple-element.133), channel_id=1, source_target_pairs={{0,24},{4,28},{8,0},{12,4},{16,8},{20,12},{24,16},{28,20},{1,25},{... | collective-permute-start | bytes 1572872 | tf_op jit(solution)/shard_map/ppermute | solution.py:1348
  153.1 45.6 %collective-permute-start.5 = (bf16[512,512]{1,0:T(8,128)(2,1)S(1)}, bf16[512,512]{1,0:T(8,128)(2,1)S(1)}, u32[]{:S(2)}, u32[]{:S(2)}) collective-permute-start(bf16[512,512]{1,0:T(8,128)(2,1)S(1)} %get-tuple-element.134), channel_id=1, source_target_pairs={{0,16},{4,20},{8,24},{12,28},{16,0},{20,4},{24,8},{28,12},{1,17},{... | collective-permute-start | bytes 1572872 | tf_op jit(solution)/shard_map/ppermute | solution.py:1348
  153.6 45.1 %collective-permute-start.4 = (bf16[512,512]{1,0:T(8,128)(2,1)S(1)}, bf16[512,512]{1,0:T(8,128)(2,1)S(1)}, u32[]{:S(2)}, u32[]{:S(2)}) collective-permute-start(bf16[512,512]{1,0:T(8,128)(2,1)S(1)} %get-tuple-element.135), channel_id=1, source_target_pairs={{0,8},{4,12},{8,16},{12,20},{16,24},{20,28},{24,0},{28,4},{1,9},{5... | collective-permute-start | bytes 1572872 | tf_op jit(solution)/shard_map/ppermute | solution.py:1348
  182.6 0.8 copy-start.18
  183.4 17.0 %copy-start.20 = (f32[1,1024]{1,0:T(1,128)}, f32[1,1024]{1,0:T(1,128)S(1)}, u32[]{:S(2)}) copy-start(f32[1,1024]{1,0:T(1,128)S(1)} %get-tuple-element.98.db_ref) | copy-start | bytes 12292
  183.4 17.0 %copy-start.21 = (f32[1,1024]{1,0:T(1,128)}, f32[1,1024]{1,0:T(1,128)S(1)}, u32[]{:S(2)}) copy-start(f32[1,1024]{1,0:T(1,128)S(1)} %get-tuple-element.99.sk_ref) | copy-start | bytes 12292
  183.4 17.0 %copy-start.25 = (bf16[2,256,1024]{2,1,0:T(8,128)(2,1)S(1)}, bf16[2,256,1024]{2,1,0:T(8,128)(2,1)}, u32[]{:S(2)}) copy-start(bf16[2,256,1024]{2,1,0:T(8,128)(2,1)} %get-tuple-element.64) | copy-start | bytes 3145732
  192.3 8.1 %copy-start.23 = (f32[2,256,1024]{2,1,0:T(8,128)S(1)}, f32[2,256,1024]{2,1,0:T(8,128)}, u32[]{:S(2)}) copy-start(f32[2,256,1024]{2,1,0:T(8,128)} %copy-done.22) | copy-start | bytes 6291460
  192.3 8.1 %copy-start.24 = (f32[2,256,1024]{2,1,0:T(8,128)S(1)}, f32[2,256,1024]{2,1,0:T(8,128)}, u32[]{:S(2)}) copy-start(f32[2,256,1024]{2,1,0:T(8,128)} %get-tuple-element.127) | copy-start | bytes 6291460
  192.3 8.1 %copy-start.38 = (f32[2,256]{1,0:T(2,128)S(1)}, f32[2,256]{1,0:T(2,128)}, u32[]{:S(2)}) copy-start(f32[2,256]{1,0:T(2,128)} %copy-done.37) | copy-start | bytes 6148
  192.3 8.1 %copy-start.40 = (f32[2,256]{1,0:T(2,128)S(1)}, f32[2,256]{1,0:T(2,128)}, u32[]{:S(2)}) copy-start(f32[2,256]{1,0:T(2,128)} %copy-done.39) | copy-start | bytes 6148
  203.4 0.7 copy-start.32
  203.4 0.7 copy-start.34
  203.4 0.7 copy-start.36
  270.0 2.1 copy-start.30
  270.0 2.8 %copy-start.49 = (f32[1,512]{1,0:T(1,128)S(1)}, f32[1,512]{1,0:T(1,128)}, u32[]{:S(2)}) copy-start(f32[1,512]{1,0:T(1,128)} %get-tuple-element.105) | copy-start | bytes 6148
  270.0 3.4 %copy-start.27 = (f32[256,2048]{1,0:T(8,128)S(1)}, f32[256,2048]{1,0:T(8,128)}, u32[]{:S(2)}) copy-start(f32[256,2048]{1,0:T(8,128)} %get-tuple-element.160) | copy-start | bytes 6291460
  273.4 1.4 copy-start.42
  273.4 2.0 copy-start.45
  273.4 2.6 copy-start.28
  273.4 3.4 %copy-start.29 = (f32[128,1024]{1,0:T(8,128)S(1)}, f32[128,1024]{1,0:T(8,128)}, u32[]{:S(2)}) copy-start(f32[128,1024]{1,0:T(8,128)} %get-tuple-element.164) | copy-start | bytes 1572868
  273.4 5.4 %copy-start.1 = (bf16[160,1024]{1,0:T(8,128)(2,1)S(1)}, bf16[160,1024]{1,0:T(8,128)(2,1)}, u32[]{:S(2)}) copy-start(bf16[160,1024]{1,0:T(8,128)(2,1)} %param.18) | copy-start | bytes 983044
  274.8 2.8 %copy-start.44 = (f32[1,1024]{1,0:T(1,128)S(1)}, f32[1,1024]{1,0:T(1,128)}, u32[]{:S(2)}) copy-start(f32[1,1024]{1,0:T(1,128)} %get-tuple-element.111) | copy-start | bytes 12292
  274.8 3.4 %copy-start.43 = (f32[1,1024]{1,0:T(1,128)S(1)}, f32[1,1024]{1,0:T(1,128)}, u32[]{:S(2)}) copy-start(f32[1,1024]{1,0:T(1,128)} %get-tuple-element.112) | copy-start | bytes 12292

commit v11 on v10

--- a/solution.py
+++ b/solution.py
@@ -1397,11 +1397,11 @@
     ]
     conv_w = conv_weight.astype(f32)
     xv = x_part.astype(f32)
-    x_padded = jnp.pad(xv, ((0, 0), (KW - 1, 0), (0, 0)))
+    x_padded = jnp.pad(x_part, ((0, 0), (KW - 1, 0), (0, 0)))
     conv_pre = conv_bias.astype(f32) + conv_w[KW - 1] * xv
     for j in range(KW - 1):
         d = KW - 1 - j
-        conv_pre = conv_pre + conv_w[j] * x_padded[:, j : j + length] * taps[d][:, :, None]
+        conv_pre = conv_pre + conv_w[j] * x_padded[:, j : j + length].astype(f32) * taps[d][:, :, None]
     conv_out = jax.nn.silu(conv_pre).astype(bf16)
     conv_flat = conv_out.reshape(tokens, width)
     own_half, y_half, z_half = (value.reshape(tokens, -1) for value in (own_half, y_half, z_half))
@@ -1448,7 +1448,7 @@
     grad_conv_bias = jnp.sum(grad_pre, axis=(0, 1))
     grad_conv_weight = jnp.stack(
         [
-            jnp.sum(grad_pre * x_padded[:, j : j + length] * taps[KW - 1 - j][:, :, None], axis=(0, 1))
+            jnp.sum(grad_pre * x_padded[:, j : j + length].astype(f32) * taps[KW - 1 - j][:, :, None], axis=(0, 1))
             for j in range(KW)
         ]
     )

time: 280 us -> 286 us (1.021)
  local copies, waits for them, and re-layouts: 13.8 us -> 18.9 us
    unnamed x112 -> x124, local copies, waits for them, and re-layouts: 12.8 us -> 16.4 us
where the time goes in v11:
time: 286 us; the launch traced here: 285 us
  Pallas kernels  220 us (77%)
  local copies, waits for them, and re-layouts  18.9 us (7%)
  starting transfers between devices  17.5 us (6%)
  other arithmetic  16 us (6%)
  matrix products  5.83 us (2%)
  waiting for transfers between devices  4.77 us (2%)
    pallas_call x1, Pallas kernels, finish(): pl.pallas_call(finish_kernel, in_specs=[VMEM_SPEC] * 9 + [ANY_SPEC] * 2 +...  63 us
    pallas_call x1, Pallas kernels, front(): pl.pallas_call(front_kernel, in_specs=[VMEM_SPEC] * 3 + [ANY_SPEC] * 2, o...  42.9 us
    pallas_call x1, Pallas kernels, recurrence_backward(): pl.pallas_call(backward_kernel, grid=(seqs, blocks), in_specs=[wide, wide...  29.9 us
    pallas_call x1, Pallas kernels, collect(): pl.pallas_call(collect_kernel, in_specs=[VMEM_SPEC] * 7, out_specs=[VMEM_...  29 us
    pallas_call x1, Pallas kernels, middle(): pl.pallas_call(middle_kernel, in_specs=[VMEM_SPEC] * 4 + [ANY_SPEC] * 2,...  22.7 us
    pallas_call x2, Pallas kernels, group_total(): pl.pallas_call(total_kernel, in_specs=[VMEM_SPEC], out_specs=VMEM_SPEC, o...  18.4 us
    unnamed x124, local copies, waits for them, and re-layouts  16.4 us
    pallas_call x1, Pallas kernels, recurrence_forward(): pl.pallas_call(forward_kernel, grid=(seqs, blocks), in_specs=[wide, wide,...  14.3 us
  transfers between devices with their start and end apart: 7, of which 1 were waited for; matrix products, arithmetic and copies ran while one was open for 2% of the time, Pallas kernels for 22%

profile of v11, /device:TPU:0, one launch (start us, length us, event | category | flops | bytes accessed | tf_op | source)
XLA Modules:
  0.0 284.8 jit_solution(17716044837820059472)
XLA Ops:
  0.6 0.0 copy-start
  0.7 0.7 broadcast_in_dim.12.gain_ref
  1.4 1.0 copy-done.5
  2.4 1.0 copy-done.6
  3.5 42.9 %front.1 = (bf16[2,256,2048]{2,1,0:T(8,128)(2,1)}, f32[2,256,128]{2,1,0:T(8,128)S(1)}, bf16[2,256,512]{2,1,0:T(8,128)(2,1)S(1)}, f32[8,2048]{1,0:T(8,128)S(1)}, ...) custom-call(bf16[2,64,2048]{2,1,0:T(8,128)(2,1)S(1)} %copy-done.5, ...), custom_call_target="tpu_custom_call" | custom-call | tf_op jit(solution)/shard_map/front/pallas_call | solution.py:592
  46.4 1.0 copy-done.8
  47.4 1.0 copy-done.10
  48.4 0.8 copy-done.12
  49.1 0.7 copy-done.14
  49.9 5.2 %collective-permute-start = (bf16[512,512]{1,0:T(8,128)(2,1)}, bf16[512,512]{1,0:T(8,128)(2,1)}, u32[]{:S(2)}, u32[]{:S(2)}) collective-permute-start(bf16[512,512]{1,0:T(8,128)(2,1)} %get-tuple-element.66), channel_id=1, source_target_pairs={{0,2},{1,3},{2,0},{3,1},{4,6},{5,7},{6,4},{7,5},{8,10},{9,11},{10,... | collective-permute-start | bytes 1572872 | tf_op jit(solution)/shard_map/ppermute | solution.py:1334
  55.0 1.5 collective-permute-start.3
  56.5 1.1 collective-permute-start.2
  57.7 0.1 compare_convert_fusion.2
  57.8 0.0 copy-start.44
  57.8 0.0 copy-start.37
  57.8 0.5 copy-done.39
  58.3 4.5 %fusion.26.conv_ref = bf16[2,256,1024]{2,1,0:T(8,128)(2,1)S(1)} fusion(f32[2,256]{1,0:T(2,128)S(1)} %get-tuple-element.139, bf16[2,256,1024]{2,1,0:T(8,128)(2,1)} %get-tuple-element.64, f32[1024]{0:T(1024)S(1)} %bitcast.71, f32[2,256]{1,0:T(2,128)S(1)} %get-tuple-element.140, f32[1024]{0:T(1024)S(1)} %bitcast.68, f32[2,256]{1,0:T(2,128)S(1)} %get-tuple-element.138, ...), kind=kLoop, calls=%fused_computation.44 | loop fusion | flops 10485760 | bytes 2123776 | tf_op jit(solution)/shard_map/convert_element_type | solution.py:1405
  63.0 0.5 convolution_bitcast_fusion.part_ref
  63.5 9.5 %group_total.2.proj_ref = f32[160,512]{1,0:T(8,128)S(1)} custom-call(f32[160,512]{1,0:T(8,128)S(1)} %convolution_bitcast_fusion.part_ref), custom_call_target="tpu_custom_call" | custom-call | tf_op jit(solution)/shard_map/group_total/pallas_call | solution.py:1322
  73.1 1.8 collective-permute-start.1
  74.8 0.8 broadcast_in_dim.13.keep_ref
  75.7 14.3 %recurrence_forward.1 = (f32[2,256,1024]{2,1,0:T(8,128)S(1)}, bf16[2,256,1024]{2,1,0:T(8,128)(2,1)S(1)}, f32[2,256,1024]{2,1,0:T(8,128)}, f32[2,256,1024]{2,1,0:T(8,128)}, bf16[2,4096,1024]{2,1,0:T(8,128)(2,1)}) custom-call(bf16[2,256,1024]{2,1,0:T(8,128)(2,1)S(1)} %fusion.26.conv_ref, bf16[2,256,1024]{2,1,0:T(8,128)(2,1)S(1)} %copy-done.3, ...), custom_call_target="tpu_custom_call" | custom-call | flops 16000000000 | bytes 25165824 | tf_op jit(solution)/shard_map/recurrence_forward/pallas_call | solution.py:289
  90.0 0.1 broadcast_select_fusion
  90.1 1.5 copy-done.23
  91.6 1.3 convert_add_fusion
  92.9 0.0 copy-start.9
  93.0 1.1 fusion.25
  94.1 0.1 copy-done.9
  94.2 0.3 copy-done.11
  94.5 29.0 %collect.1 = (bf16[512,2048]{1,0:T(8,128)(2,1)S(1)}, bf16[512,2048]{1,0:T(8,128)(2,1)S(1)}, bf16[2048,256]{1,0:T(8,128)(2,1)S(1)}, bf16[2,2048,1024]{2,1,0:T(8,128)(2,1)}, bf16[512,512]{1,0:T(8,128)(2,1)S(1)}) custom-call(bf16[512,512]{1,0:T(8,128)(2,1)S(1)} %get-tuple-element.133.keep_ref, bf16[512,512]{1,0:T(8,128)(2,1)S(1)} %get-tuple-element.132.give_ref, ...), custom_call_target="tpu_custom_call" | custom-call | flops 24999999488 | bytes 1048576 | tf_op jit(solution)/shard_map/collect/pallas_call | solution.py:743
  123.6 22.7 %middle.1 = (bf16[2,512,2048]{2,1,0:T(8,128)(2,1)S(1)}, bf16[2,64,2048]{2,1,0:T(8,128)(2,1)S(1)}, bf16[256,1024]{1,0:T(8,128)(2,1)S(1)}) custom-call(bf16[512,2048]{1,0:T(8,128)(2,1)S(1)} %get-tuple-element.82.keeps_ref, bf16[512,2048]{1,0:T(8,128)(2,1)S(1)} %get-tuple-element.83.gives_ref, bf16[512,512]{1,0:T(8,128)(2,1)S(1)} %get-tuple-element.84.got_ref, ...), custom_call_target="tpu_custom_call" | custom-call | flops 24999999488 | bytes 1048576 | tf_op jit(solution)/shard_map/middle/pallas_call | solution.py:870
  146.3 0.0 copy-start.19
  146.3 3.7 %convolution_convert_fusion = bf16[2048,512]{1,0:T(8,128)(2,1)S(1)} fusion(bf16[1024,2048]{1,0:T(8,128)(2,1)S(1)} %bitcast.57, bf16[512,512]{1,0:T(8,128)(2,1)} %collective-permute-done.3, bf16[512,512]{1,0:T(8,128)(2,1)S(1)} %bitcast.56), kind=kOutput, calls=%fused_computation | convolution fusion | flops 2150629376 | bytes 7340032 | tf_op jit(solution)/shard_map/dot_general | solution.py:23
  150.0 0.0 copy-start.16
  150.0 0.9 dynamic-slice_bitcast_fusion
  151.0 6.9 %collective-permute-start.6 = (bf16[512,512]{1,0:T(8,128)(2,1)S(1)}, bf16[512,512]{1,0:T(8,128)(2,1)S(1)}, u32[]{:S(2)}, u32[]{:S(2)}) collective-permute-start(bf16[512,512]{1,0:T(8,128)(2,1)S(1)} %get-tuple-element.128), channel_id=1, source_target_pairs={{0,24},{4,28},{8,0},{12,4},{16,8},{20,12},{24,16},{28,20},{1,25},{... | collective-permute-start | bytes 1572872 | tf_op jit(solution)/shard_map/ppermute | solution.py:1348
  157.9 0.5 collective-permute-start.5
  158.4 0.6 collective-permute-start.4
  159.0 29.9 %recurrence_backward.1 = (f32[2,256,1024]{2,1,0:T(8,128)S(1)}, bf16[2,256,1024]{2,1,0:T(8,128)(2,1)}, f32[160,512]{1,0:T(8,128)S(1)}, f32[128,1024]{1,0:T(8,128)...) custom-call(f32[2,256,1024]{2,1,0:T(8,128)S(1)} %copy-done.16, f32[2,256,1024]{2,1,0:T(8,128)S(1)} %copy-done.17, ...), custom_call_target="tpu_custom_call" | custom-call | flops 30000001024 | bytes 29360128 | tf_op jit(solution)/shard_map/recurrence_backward/pallas_call | solution.py:324
  188.9 0.8 copy-done.18
  189.7 8.9 %group_total.3 = f32[160,512]{1,0:T(8,128)S(1)} custom-call(f32[160,512]{1,0:T(8,128)S(1)} %get-tuple-element.95.part_ref), custom_call_target="tpu_custom_call" | custom-call | tf_op jit(solution)/shard_map/group_total/pallas_call | solution.py:1322
  198.6 0.0 copy-start.40
  198.6 0.0 copy-start.42
  198.7 0.0 copy-start.29
  198.7 4.8 %collective-permute-done.5 = bf16[512,512]{1,0:T(8,128)(2,1)S(1)} collective-permute-done((bf16[512,512]{1,0:T(8,128)(2,1)S(1)}, bf16[512,512]{1,0:T(8,128)(2,1)S(1)}, u32[]{:S(2)}, u32[]{:S(2)}) %collective-permute-start.5) | collective-permute-done | bytes 524320 | tf_op jit(solution)/shard_map/ppermute | solution.py:1348
  203.4 1.2 fusion.30.xp_ref
  204.6 0.5 fusion.32
  205.2 4.5 %fusion.14 = (f32[1024]{0:T(1024)S(1)}, f32[1024]{0:T(1024)S(1)}, f32[1024]{0:T(1024)S(1)}, f32[1024]{0:T(1024)S(1)}, f32[1024]{0:T(1024)}, /*index=5*/f32[2,256,1024]{2,1,0:T(8,128)S(1)}) fusion(f32[2,256]{1,0:T(2,128)S(1)} %copy-done.45, bf16[2,256,1024]{2,1,0:T(8,128)(2,1)S(1)} %copy-done.22, f32[2,256]{1,0:T(2,128)S(1)} %copy-done.40, ...), kind=kLoop, calls=%fused_computation.28 | loop fusion | flops 21490688 | bytes 9488384 | tf_op jit(solution)/shard_map/reduce_sum | solution.py:1451
  209.7 0.5 broadcast_multiply_fusion
  210.2 2.1 fusion.4
  212.3 0.6 pad_maximum_fusion.cw_ref
  212.9 63.0 %finish.1 = (f32[256,2048]{1,0:T(8,128)}, f32[160,1024]{1,0:T(8,128)}, f32[128,1024]{1,0:T(8,128)}, f32[4,1024]{1,0:T(4,128)}, f32[1,1024]{1,0:T(1,128)}, /*inde...) custom-call(bf16[512,1024]{1,0:T(8,128)(2,1)} %bitcast.61, ...), custom_call_target="tpu_custom_call" | custom-call | flops 80000000000 | bytes 1048576 | tf_op jit(solution)/shard_map/finish/pallas_call | solution.py:1246
  276.0 1.2 convert_add_fusion.1
  277.2 0.8 copy.33
  278.0 0.8 copy.34
  278.8 0.6 copy.35
  279.4 0.0 copy-start.1
  279.4 1.3 copy.36
  280.7 0.6 copy.37
  281.3 0.6 copy.38
  281.9 0.8 copy.39
  282.8 0.8 copy.40
  283.6 0.6 copy.41
  284.2 0.6 copy.42
  (103 shorter events, 0.2 us)
Async XLA Ops:
  0.6 62.4 %copy-start = (bf16[160,1024]{1,0:T(8,128)(2,1)S(1)}, bf16[160,1024]{1,0:T(8,128)(2,1)}, u32[]{:S(2)}) copy-start(bf16[160,1024]{1,0:T(8,128)(2,1)} %param.18) | copy-start | bytes 983044
  1.4 1.0 copy-start.5
  2.4 1.0 copy-start.6
  3.5 54.2 %copy-start.52 = (bf16[1024]{0:T(1024)(128)(2,1)S(1)}, bf16[1024]{0:T(1024)(128)(2,1)}, u32[]{:S(2)}) copy-start(bf16[1024]{0:T(1024)(128)(2,1)} %param.17) | copy-start | bytes 6148
  3.5 54.2 %copy-start.56 = (s32[2,256]{1,0:T(2,128)S(1)}, s32[2,256]{1,0:T(2,128)}, u32[]{:S(2)}) copy-start(s32[2,256]{1,0:T(2,128)} %param.13) | copy-start | bytes 6148
  3.5 54.3 %copy-start.43 = (bf16[4,1024]{1,0:T(4,128)(2,1)S(1)}, bf16[4,1024]{1,0:T(4,128)(2,1)}, u32[]{:S(2)}) copy-start(bf16[4,1024]{1,0:T(4,128)(2,1)} %param.16) | copy-start | bytes 24580
  46.4 1.0 copy-start.8
  47.4 1.0 copy-start.10
  48.4 0.8 copy-start.12
  49.1 0.7 copy-start.14
  49.9 8.0 %copy-start.15 = (f32[8,2048]{1,0:T(8,128)}, f32[8,2048]{1,0:T(8,128)S(1)}, u32[]{:S(2)}) copy-start(f32[8,2048]{1,0:T(8,128)S(1)} %get-tuple-element.102.gain_ref) | copy-start | bytes 196612
  49.9 13.1 %copy-start.53 = (bf16[1024]{0:T(1024)(128)(2,1)S(1)}, bf16[1024]{0:T(1024)(128)(2,1)}, u32[]{:S(2)}) copy-start(bf16[1024]{0:T(1024)(128)(2,1)} %param.21) | copy-start | bytes 6148
  49.9 13.2 %copy-start.54 = (bf16[1024]{0:T(1024)(128)(2,1)S(1)}, bf16[1024]{0:T(1024)(128)(2,1)}, u32[]{:S(2)}) copy-start(bf16[1024]{0:T(1024)(128)(2,1)} %param.20) | copy-start | bytes 6148
  49.9 23.2 %collective-permute-start = (bf16[512,512]{1,0:T(8,128)(2,1)}, bf16[512,512]{1,0:T(8,128)(2,1)}, u32[]{:S(2)}, u32[]{:S(2)}) collective-permute-start(bf16[512,512]{1,0:T(8,128)(2,1)} %get-tuple-element.66), channel_id=1, source_target_pairs={{0,2},{1,3},{2,0},{3,1},{4,6},{5,7},{6,4},{7,5},{8,10},{9,11},{10,... | collective-permute-start | bytes 1572872 | tf_op jit(solution)/shard_map/ppermute | solution.py:1334
  55.0 35.0 %collective-permute-start.3 = (bf16[512,512]{1,0:T(8,128)(2,1)S(1)}, bf16[512,512]{1,0:T(8,128)(2,1)}, u32[]{:S(2)}, u32[]{:S(2)}) collective-permute-start(bf16[512,512]{1,0:T(8,128)(2,1)S(1)} %bitcast.55), channel_id=1, source_target_pairs={{0,4},{4,0},{8,12},{12,8},{16,20},{20,16},{24,28},{28,24},{1,5},{5... | collective-permute-start | bytes 1572872 | tf_op jit(solution)/shard_map/ppermute | solution.py:1409
  56.5 33.5 %collective-permute-start.2 = (bf16[512,1024]{1,0:T(8,128)(2,1)}, bf16[512,1024]{1,0:T(8,128)(2,1)}, u32[]{:S(2)}, u32[]{:S(2)}) collective-permute-start(bf16[512,1024]{1,0:T(8,128)(2,1)} %bitcast.8.y_half_ref), channel_id=1, source_target_pairs={{0,8},{4,12},{8,0},{12,4},{16,24},{20,28},{24,16},{28,20},{1,9},{5... | collective-permute-start | bytes 3145736 | tf_op jit(solution)/shard_map/ppermute | solution.py:1408
  57.7 5.2 %copy-start.41 = (f32[1024]{0:T(1024)}, f32[1024]{0:T(1024)S(1)}, u32[]{:S(2)}) copy-start(f32[1024]{0:T(1024)S(1)} %convert_element_type.82) | copy-start | bytes 12292
  57.8 0.6 copy-start.39
  57.8 5.1 %copy-start.44 = (f32[2,256]{1,0:T(2,128)}, f32[2,256]{1,0:T(2,128)S(1)}, u32[]{:S(2)}) copy-start(f32[2,256]{1,0:T(2,128)S(1)} %get-tuple-element.138) | copy-start | bytes 6148
  57.8 5.1 %copy-start.46 = (f32[2,256]{1,0:T(2,128)}, f32[2,256]{1,0:T(2,128)S(1)}, u32[]{:S(2)}) copy-start(f32[2,256]{1,0:T(2,128)S(1)} %get-tuple-element.140) | copy-start | bytes 6148
  57.8 5.2 %copy-start.35 = (f32[1,1024]{1,0:T(1,128)}, f32[1,1024]{1,0:T(1,128)S(1)}, u32[]{:S(2)}) copy-start(f32[1,1024]{1,0:T(1,128)S(1)} %get-tuple-element.136) | copy-start | bytes 12292
  57.8 5.2 %copy-start.37 = (f32[1,1024]{1,0:T(1,128)}, f32[1,1024]{1,0:T(1,128)S(1)}, u32[]{:S(2)}) copy-start(f32[1,1024]{1,0:T(1,128)S(1)} %get-tuple-element.137) | copy-start | bytes 12292
  58.3 17.3 %copy-start.3 = (bf16[2,256,1024]{2,1,0:T(8,128)(2,1)S(1)}, bf16[2,256,1024]{2,1,0:T(8,128)(2,1)}, u32[]{:S(2)}) copy-start(bf16[2,256,1024]{2,1,0:T(8,128)(2,1)} %get-tuple-element.65.z_ref) | copy-start | bytes 3145732
  58.3 17.3 %copy-start.13 = (bf16[128,1024]{1,0:T(8,128)(2,1)S(1)}, bf16[128,1024]{1,0:T(8,128)(2,1)}, u32[]{:S(2)}) copy-start(bf16[128,1024]{1,0:T(8,128)(2,1)} %dt_proj_ref.3) | copy-start | bytes 786436
  73.1 16.9 %collective-permute-start.1 = (bf16[512,512]{1,0:T(8,128)(2,1)}, bf16[512,512]{1,0:T(8,128)(2,1)S(1)}, u32[]{:S(2)}, u32[]{:S(2)}) collective-permute-start(bf16[512,512]{1,0:T(8,128)(2,1)} %copy-done.12), channel_id=1, source_target_pairs={{0,2},{1,3},{2,0},{3,1},{4,6},{5,7},{6,4},{7,5},{8,10},{9,11},{10,... | collective-permute-start | bytes 1572872 | tf_op jit(solution)/shard_map/ppermute | solution.py:1334
  90.0 1.6 copy-start.23
  92.9 1.2 copy-start.9
  92.9 1.5 copy-start.11
  94.1 29.5 %copy-start.4 = (bf16[2,256,1024]{2,1,0:T(8,128)(2,1)}, bf16[2,256,1024]{2,1,0:T(8,128)(2,1)S(1)}, u32[]{:S(2)}) copy-start(bf16[2,256,1024]{2,1,0:T(8,128)(2,1)S(1)} %get-tuple-element.124) | copy-start | bytes 3145732
  94.5 29.1 %copy-start.2 = (bf16[4096,512]{1,0:T(8,128)(2,1)S(1)}, bf16[4096,512]{1,0:T(8,128)(2,1)}, u32[]{:S(2)}) copy-start(bf16[4096,512]{1,0:T(8,128)(2,1)} %o_hbm.3) | copy-start | bytes 12582916
  94.5 29.1 %copy-start.7 = (bf16[2,256,2048]{2,1,0:T(8,128)(2,1)S(1)}, bf16[2,256,2048]{2,1,0:T(8,128)(2,1)}, u32[]{:S(2)}) copy-start(bf16[2,256,2048]{2,1,0:T(8,128)(2,1)} %get-tuple-element.86.xs_ref) | copy-start | bytes 6291460
  146.3 3.7 %copy-start.19 = (bf16[256,1024]{1,0:T(8,128)(2,1)}, bf16[256,1024]{1,0:T(8,128)(2,1)S(1)}, u32[]{:S(2)}) copy-start(bf16[256,1024]{1,0:T(8,128)(2,1)S(1)} %get-tuple-element.100.wz_ref) | copy-start | bytes 1572868
  150.0 9.0 %copy-start.16 = (f32[2,256,1024]{2,1,0:T(8,128)S(1)}, f32[2,256,1024]{2,1,0:T(8,128)}, u32[]{:S(2)}) copy-start(f32[2,256,1024]{2,1,0:T(8,128)} %get-tuple-element.91.rate_ref) | copy-start | bytes 6291460
  150.0 8.9 %copy-start.17 = (f32[2,256,1024]{2,1,0:T(8,128)S(1)}, f32[2,256,1024]{2,1,0:T(8,128)}, u32[]{:S(2)}) copy-start(f32[2,256,1024]{2,1,0:T(8,128)} %get-tuple-element.92.beta_ref) | copy-start | bytes 6291460
  151.0 47.7 %collective-permute-start.6 = (bf16[512,512]{1,0:T(8,128)(2,1)S(1)}, bf16[512,512]{1,0:T(8,128)(2,1)S(1)}, u32[]{:S(2)}, u32[]{:S(2)}) collective-permute-start(bf16[512,512]{1,0:T(8,128)(2,1)S(1)} %get-tuple-element.128), channel_id=1, source_target_pairs={{0,24},{4,28},{8,0},{12,4},{16,8},{20,12},{24,16},{28,20},{1,25},{... | collective-permute-start | bytes 1572872 | tf_op jit(solution)/shard_map/ppermute | solution.py:1348
  157.9 45.6 %collective-permute-start.5 = (bf16[512,512]{1,0:T(8,128)(2,1)S(1)}, bf16[512,512]{1,0:T(8,128)(2,1)S(1)}, u32[]{:S(2)}, u32[]{:S(2)}) collective-permute-start(bf16[512,512]{1,0:T(8,128)(2,1)S(1)} %get-tuple-element.129), channel_id=1, source_target_pairs={{0,16},{4,20},{8,24},{12,28},{16,0},{20,4},{24,8},{28,12},{1,17},{... | collective-permute-start | bytes 1572872 | tf_op jit(solution)/shard_map/ppermute | solution.py:1348
  158.4 45.1 %collective-permute-start.4 = (bf16[512,512]{1,0:T(8,128)(2,1)S(1)}, bf16[512,512]{1,0:T(8,128)(2,1)S(1)}, u32[]{:S(2)}, u32[]{:S(2)}) collective-permute-start(bf16[512,512]{1,0:T(8,128)(2,1)S(1)} %get-tuple-element.130), channel_id=1, source_target_pairs={{0,8},{4,12},{8,16},{12,20},{16,24},{20,28},{24,0},{28,4},{1,9},{5... | collective-permute-start | bytes 1572872 | tf_op jit(solution)/shard_map/ppermute | solution.py:1348
  188.9 0.8 copy-start.18
  189.7 15.4 %copy-start.20 = (f32[1,1024]{1,0:T(1,128)}, f32[1,1024]{1,0:T(1,128)S(1)}, u32[]{:S(2)}) copy-start(f32[1,1024]{1,0:T(1,128)S(1)} %get-tuple-element.98.db_ref) | copy-start | bytes 12292
  189.7 15.4 %copy-start.21 = (f32[1,1024]{1,0:T(1,128)}, f32[1,1024]{1,0:T(1,128)S(1)}, u32[]{:S(2)}) copy-start(f32[1,1024]{1,0:T(1,128)S(1)} %get-tuple-element.99.sk_ref) | copy-start | bytes 12292
  198.6 6.6 %copy-start.22 = (bf16[2,256,1024]{2,1,0:T(8,128)(2,1)S(1)}, bf16[2,256,1024]{2,1,0:T(8,128)(2,1)}, u32[]{:S(2)}) copy-start(bf16[2,256,1024]{2,1,0:T(8,128)(2,1)} %get-tuple-element.64) | copy-start | bytes 3145732
  198.6 6.6 %copy-start.36 = (f32[1,1024]{1,0:T(1,128)S(1)}, f32[1,1024]{1,0:T(1,128)}, u32[]{:S(2)}) copy-start(f32[1,1024]{1,0:T(1,128)} %copy-done.35) | copy-start | bytes 12292
  198.6 6.6 %copy-start.38 = (f32[1,1024]{1,0:T(1,128)S(1)}, f32[1,1024]{1,0:T(1,128)}, u32[]{:S(2)}) copy-start(f32[1,1024]{1,0:T(1,128)} %copy-done.37) | copy-start | bytes 12292
  198.6 6.6 %copy-start.40 = (f32[2,256]{1,0:T(2,128)S(1)}, f32[2,256]{1,0:T(2,128)}, u32[]{:S(2)}) copy-start(f32[2,256]{1,0:T(2,128)} %copy-done.39) | copy-start | bytes 6148
  198.6 6.6 %copy-start.42 = (f32[1024]{0:T(1024)S(1)}, f32[1024]{0:T(1024)}, u32[]{:S(2)}) copy-start(f32[1024]{0:T(1024)} %copy-done.41) | copy-start | bytes 12292
  198.6 6.6 %copy-start.45 = (f32[2,256]{1,0:T(2,128)S(1)}, f32[2,256]{1,0:T(2,128)}, u32[]{:S(2)}) copy-start(f32[2,256]{1,0:T(2,128)} %copy-done.44) | copy-start | bytes 6148
  198.6 6.6 %copy-start.47 = (f32[2,256]{1,0:T(2,128)S(1)}, f32[2,256]{1,0:T(2,128)}, u32[]{:S(2)}) copy-start(f32[2,256]{1,0:T(2,128)} %copy-done.46) | copy-start | bytes 6148
  198.7 6.5 %copy-start.29 = (bf16[512,512]{1,0:T(8,128)(2,1)}, bf16[512,512]{1,0:T(8,128)(2,1)S(1)}, u32[]{:S(2)}) copy-start(bf16[512,512]{1,0:T(8,128)(2,1)S(1)} %collective-permute-done.6) | copy-start | bytes 1572868
  203.4 1.7 copy-start.31
  203.4 1.7 copy-start.33
  212.9 63.0 %copy-start.25 = (bf16[512,512]{1,0:T(8,128)(2,1)S(1)}, bf16[512,512]{1,0:T(8,128)(2,1)}, u32[]{:S(2)}) copy-start(bf16[512,512]{1,0:T(8,128)(2,1)} %get-tuple-element.113) | copy-start | bytes 1572868
  212.9 63.0 %copy-start.30 = (bf16[512,512]{1,0:T(8,128)(2,1)S(1)}, bf16[512,512]{1,0:T(8,128)(2,1)}, u32[]{:S(2)}) copy-start(bf16[512,512]{1,0:T(8,128)(2,1)} %copy-done.29) | copy-start | bytes 1572868
  212.9 63.0 %copy-start.32 = (bf16[512,512]{1,0:T(8,128)(2,1)S(1)}, bf16[512,512]{1,0:T(8,128)(2,1)}, u32[]{:S(2)}) copy-start(bf16[512,512]{1,0:T(8,128)(2,1)} %copy-done.31) | copy-start | bytes 1572868
  212.9 63.0 %copy-start.34 = (bf16[512,512]{1,0:T(8,128)(2,1)S(1)}, bf16[512,512]{1,0:T(8,128)(2,1)}, u32[]{:S(2)}) copy-start(bf16[512,512]{1,0:T(8,128)(2,1)} %copy-done.33) | copy-start | bytes 1572868
  275.9 2.1 copy-start.28
  275.9 2.8 copy-start.55
  276.0 3.4 %copy-start.24 = (f32[256,2048]{1,0:T(8,128)S(1)}, f32[256,2048]{1,0:T(8,128)}, u32[]{:S(2)}) copy-start(f32[256,2048]{1,0:T(8,128)} %get-tuple-element.155) | copy-start | bytes 6291460
  279.4 1.4 copy-start.48
  279.4 2.0 copy-start.51
  279.4 2.6 copy-start.26
  279.4 3.4 %copy-start.27 = (f32[128,1024]{1,0:T(8,128)S(1)}, f32[128,1024]{1,0:T(8,128)}, u32[]{:S(2)}) copy-start(f32[128,1024]{1,0:T(8,128)} %get-tuple-element.159) | copy-start | bytes 1572868
  279.4 5.4 %copy-start.1 = (bf16[160,1024]{1,0:T(8,128)(2,1)S(1)}, bf16[160,1024]{1,0:T(8,128)(2,1)}, u32[]{:S(2)}) copy-start(bf16[160,1024]{1,0:T(8,128)(2,1)} %param.18) | copy-start | bytes 983044
  280.7 2.8 copy-start.50
  280.7 3.4 %copy-start.49 = (f32[1,1024]{1,0:T(1,128)S(1)}, f32[1,1024]{1,0:T(1,128)}, u32[]{:S(2)}) copy-start(f32[1,1024]{1,0:T(1,128)} %get-tuple-element.112) | copy-start | bytes 12292

commit v12 on v10

--- a/solution.py
+++ b/solution.py
@@ -1149,8 +1149,8 @@
         )
 
     pass_on(0).start()
+    grads_on(1)
     home_sum(0)
-    grads_on(1)
     for copy in gain_sends:
         copy.wait()
     gain_sum[...] = gains[:, pl.ds(pl.multiple_of(me * wide, LANES), wide)] + gain_near[0] + gain_near[1] + gain_near[2]

time: 280 us -> 280 us (level)
  no operation moved by 1% of the time
where the time goes in v12:
time: 280 us; the launch traced here: 279 us
  Pallas kernels  219 us (78%)
  starting transfers between devices  18 us (6%)
  other arithmetic  14.2 us (5%)
  local copies, waits for them, and re-layouts  13.8 us (5%)
  waiting for transfers between devices  6.36 us (2%)
  matrix products  5.76 us (2%)
    pallas_call x1, Pallas kernels, finish(): pl.pallas_call(finish_kernel, in_specs=[VMEM_SPEC] * 9 + [ANY_SPEC] * 2 +...  63.1 us
    pallas_call x1, Pallas kernels, front(): pl.pallas_call(front_kernel, in_specs=[VMEM_SPEC] * 3 + [ANY_SPEC] * 2, o...  42.9 us
    pallas_call x1, Pallas kernels, collect(): pl.pallas_call(collect_kernel, in_specs=[VMEM_SPEC] * 7, out_specs=[VMEM_...  29 us
    pallas_call x1, Pallas kernels, recurrence_backward(): pl.pallas_call(backward_kernel, grid=(seqs, blocks), in_specs=[wide, wide...  28.3 us
    pallas_call x1, Pallas kernels, middle(): pl.pallas_call(middle_kernel, in_specs=[VMEM_SPEC] * 4 + [ANY_SPEC] * 2,...  22.7 us
    pallas_call x2, Pallas kernels, group_total(): pl.pallas_call(total_kernel, in_specs=[VMEM_SPEC], out_specs=VMEM_SPEC, o...  18.9 us
    pallas_call x1, Pallas kernels, recurrence_forward(): pl.pallas_call(forward_kernel, grid=(seqs, blocks), in_specs=[wide, wide,...  14.3 us
    unnamed x112, local copies, waits for them, and re-layouts  12.8 us
  transfers between devices with their start and end apart: 7, of which 1 were waited for; matrix products, arithmetic and copies ran while one was open for 2% of the time, Pallas kernels for 22%

profile of v12, /device:TPU:0, one launch (start us, length us, event | category | flops | bytes accessed | tf_op | source)
XLA Modules:
  0.0 278.8 jit_solution(9632509814558122606)
XLA Ops:
  0.6 0.0 copy-start
  0.7 0.7 broadcast_in_dim.12.gain_ref
  1.4 1.0 copy-done.5
  2.4 1.0 copy-done.6
  3.5 42.9 %front.1 = (bf16[2,256,2048]{2,1,0:T(8,128)(2,1)}, f32[2,256,128]{2,1,0:T(8,128)S(1)}, bf16[2,256,512]{2,1,0:T(8,128)(2,1)S(1)}, f32[8,2048]{1,0:T(8,128)S(1)}, ...) custom-call(bf16[2,64,2048]{2,1,0:T(8,128)(2,1)S(1)} %copy-done.5, ...), custom_call_target="tpu_custom_call" | custom-call | tf_op jit(solution)/shard_map/front/pallas_call | solution.py:592
  46.4 0.0 copy-start.8
  46.4 0.0 copy-start.12
  46.5 5.2 %collective-permute-start = (bf16[512,512]{1,0:T(8,128)(2,1)}, bf16[512,512]{1,0:T(8,128)(2,1)}, u32[]{:S(2)}, u32[]{:S(2)}) collective-permute-start(bf16[512,512]{1,0:T(8,128)(2,1)} %get-tuple-element.66), channel_id=1, source_target_pairs={{0,2},{1,3},{2,0},{3,1},{4,6},{5,7},{6,4},{7,5},{8,10},{9,11},{10,... | collective-permute-start | bytes 1572872 | tf_op jit(solution)/shard_map/ppermute | solution.py:1334
  51.7 1.5 collective-permute-start.3
  53.2 1.1 collective-permute-start.2
  54.3 0.1 compare_convert_fusion.2
  54.4 0.0 copy-start.39
  54.5 0.0 copy-start.33
  54.5 0.0 copy-start.35
  54.5 1.5 convert_element_type.72
  56.0 0.0 copy-start.47
  56.0 0.0 copy-start.48
  56.0 2.7 fusion.12
  58.9 0.5 convolution_bitcast_fusion.part_ref
  59.4 10.0 %group_total.2.proj_ref = f32[160,512]{1,0:T(8,128)S(1)} custom-call(f32[160,512]{1,0:T(8,128)S(1)} %convolution_bitcast_fusion.part_ref), custom_call_target="tpu_custom_call" | custom-call | tf_op jit(solution)/shard_map/group_total/pallas_call | solution.py:1322
  69.4 2.1 collective-permute-start.1
  71.5 0.1 broadcast_in_dim.13.keep_ref
  71.6 14.3 %recurrence_forward.1 = (f32[2,256,1024]{2,1,0:T(8,128)S(1)}, bf16[2,256,1024]{2,1,0:T(8,128)(2,1)S(1)}, f32[2,256,1024]{2,1,0:T(8,128)}, f32[2,256,1024]{2,1,0:T(8,128)}, bf16[2,4096,1024]{2,1,0:T(8,128)(2,1)}) custom-call(bf16[2,256,1024]{2,1,0:T(8,128)(2,1)S(1)} %get-tuple-element.126.conv_ref, bf16[2,256,1024]{2,1,0:T(8,128)(2,1)S(1)} %copy-done.3, ...), custom_call_target="tpu_custom_call" | custom-call | flops 16000000000 | bytes 25165824 | tf_op jit(solution)/shard_map/recurrence_forward/pallas_call | solution.py:289
  85.9 0.1 broadcast_select_fusion
  86.0 1.5 copy-done.26
  87.5 1.5 convert_add_fusion
  89.0 0.0 copy-start.9
  89.0 1.1 fusion.11
  90.1 0.1 copy-done.9
  90.2 0.3 copy-done.11
  90.5 29.0 %collect.1 = (bf16[512,2048]{1,0:T(8,128)(2,1)S(1)}, bf16[512,2048]{1,0:T(8,128)(2,1)S(1)}, bf16[2048,256]{1,0:T(8,128)(2,1)S(1)}, bf16[2,2048,1024]{2,1,0:T(8,128)(2,1)}, bf16[512,512]{1,0:T(8,128)(2,1)S(1)}) custom-call(bf16[512,512]{1,0:T(8,128)(2,1)S(1)} %get-tuple-element.138.keep_ref, bf16[512,512]{1,0:T(8,128)(2,1)S(1)} %get-tuple-element.137.give_ref, ...), custom_call_target="tpu_custom_call" | custom-call | flops 24999999488 | bytes 1048576 | tf_op jit(solution)/shard_map/collect/pallas_call | solution.py:743
  119.6 22.7 %middle.1 = (bf16[2,512,2048]{2,1,0:T(8,128)(2,1)S(1)}, bf16[2,64,2048]{2,1,0:T(8,128)(2,1)S(1)}, bf16[256,1024]{1,0:T(8,128)(2,1)S(1)}) custom-call(bf16[512,2048]{1,0:T(8,128)(2,1)S(1)} %get-tuple-element.82.keeps_ref, bf16[512,2048]{1,0:T(8,128)(2,1)S(1)} %get-tuple-element.83.gives_ref, bf16[512,512]{1,0:T(8,128)(2,1)S(1)} %get-tuple-element.84.got_ref, ...), custom_call_target="tpu_custom_call" | custom-call | flops 24999999488 | bytes 1048576 | tf_op jit(solution)/shard_map/middle/pallas_call | solution.py:870
  142.4 3.6 %convolution_convert_fusion = bf16[2048,512]{1,0:T(8,128)(2,1)S(1)} fusion(bf16[1024,2048]{1,0:T(8,128)(2,1)S(1)} %bitcast.57, bf16[512,512]{1,0:T(8,128)(2,1)} %collective-permute-done.3, bf16[512,512]{1,0:T(8,128)(2,1)S(1)} %bitcast.56), kind=kOutput, calls=%fused_computation | convolution fusion | flops 2150629376 | bytes 7340032 | tf_op jit(solution)/shard_map/dot_general | solution.py:23
  146.0 0.2 dynamic-slice_bitcast_fusion
  146.2 6.9 %collective-permute-start.6 = (bf16[512,512]{1,0:T(8,128)(2,1)S(1)}, bf16[512,512]{1,0:T(8,128)(2,1)S(1)}, u32[]{:S(2)}, u32[]{:S(2)}) collective-permute-start(bf16[512,512]{1,0:T(8,128)(2,1)S(1)} %get-tuple-element.133), channel_id=1, source_target_pairs={{0,24},{4,28},{8,0},{12,4},{16,8},{20,12},{24,16},{28,20},{1,25},{... | collective-permute-start | bytes 1572872 | tf_op jit(solution)/shard_map/ppermute | solution.py:1348
  153.1 0.5 collective-permute-start.5
  153.6 0.6 collective-permute-start.4
  154.2 28.3 %recurrence_backward.1 = (f32[2,256,1024]{2,1,0:T(8,128)S(1)}, bf16[2,256,1024]{2,1,0:T(8,128)(2,1)}, f32[160,512]{1,0:T(8,128)S(1)}, f32[128,1024]{1,0:T(8,128)...) custom-call(f32[2,256,1024]{2,1,0:T(8,128)S(1)} %copy-done.16, f32[2,256,1024]{2,1,0:T(8,128)S(1)} %copy-done.17, ...), custom_call_target="tpu_custom_call" | custom-call | flops 30000001024 | bytes 29360128 | tf_op jit(solution)/shard_map/recurrence_backward/pallas_call | solution.py:324
  182.6 0.8 copy-done.18
  183.4 8.9 %group_total.3 = f32[160,512]{1,0:T(8,128)S(1)} custom-call(f32[160,512]{1,0:T(8,128)S(1)} %get-tuple-element.95.part_ref), custom_call_target="tpu_custom_call" | custom-call | tf_op jit(solution)/shard_map/group_total/pallas_call | solution.py:1322
  192.3 0.0 copy-start.38
  192.3 0.0 copy-start.40
  192.3 6.3 %collective-permute-done.5 = bf16[512,512]{1,0:T(8,128)(2,1)S(1)} collective-permute-done((bf16[512,512]{1,0:T(8,128)(2,1)S(1)}, bf16[512,512]{1,0:T(8,128)(2,1)S(1)}, u32[]{:S(2)}, u32[]{:S(2)}) %collective-permute-start.5) | collective-permute-done | bytes 524320 | tf_op jit(solution)/shard_map/ppermute | solution.py:1348
  198.7 1.2 fusion.16.xp_ref
  199.9 0.5 fusion.18
  200.4 3.0 %fusion.21 = (f32[1024]{0:T(1024)}, f32[1024]{0:T(1024)S(1)}, f32[1024]{0:T(1024)S(1)}, f32[1024]{0:T(1024)S(1)}, f32[1024]{0:T(1024)S(1)}, /*index=5*/f32[2,256,1024]{2,1,0:T(8,128)S(1)}) fusion(bf16[2,256,1024]{2,1,0:T(8,128)(2,1)S(1)} %copy-done.25, f32[2,256]{1,0:T(2,128)S(1)} %copy-done.40, f32[2,256,1024]{2,1,0:T(8,128)S(1)} %copy-done.23, ...), kind=kLoop, calls=%fused_computation.56 | loop fusion | flops 12577792 | bytes 13662208 | tf_op jit(solution)/shard_map/reduce_sum | solution.py:1448
  203.4 0.5 broadcast_multiply_fusion
  203.9 0.2 copy-done.32
  204.1 0.0 copy-done.34
  204.1 0.0 copy-done.36
  204.1 2.1 fusion.4
  206.2 0.6 pad_maximum_fusion.cw_ref
  206.8 63.1 %finish.1 = (f32[256,2048]{1,0:T(8,128)}, f32[160,1024]{1,0:T(8,128)}, f32[128,1024]{1,0:T(8,128)}, f32[4,1024]{1,0:T(4,128)}, f32[1,1024]{1,0:T(1,128)}, /*inde...) custom-call(bf16[512,1024]{1,0:T(8,128)(2,1)} %bitcast.61, ...), custom_call_target="tpu_custom_call" | custom-call | flops 80000000000 | bytes 1048576 | tf_op jit(solution)/shard_map/finish/pallas_call | solution.py:1246
  270.0 1.2 convert_add_fusion.1
  271.2 0.8 copy.33
  272.0 0.8 copy.34
  272.8 0.6 copy.35
  273.4 1.3 copy.36
  274.8 0.6 copy.37
  275.4 0.6 copy.38
  276.0 0.8 copy.39
  276.8 0.8 copy.40
  277.6 0.6 copy.41
  278.2 0.6 copy.42
  (92 shorter events, 0.2 us)
Async XLA Ops:
  0.6 58.2 %copy-start = (bf16[160,1024]{1,0:T(8,128)(2,1)S(1)}, bf16[160,1024]{1,0:T(8,128)(2,1)}, u32[]{:S(2)}) copy-start(bf16[160,1024]{1,0:T(8,128)(2,1)} %param.18) | copy-start | bytes 983044
  1.4 1.0 copy-start.5
  2.4 1.0 copy-start.6
  3.5 50.9 %copy-start.46 = (bf16[1024]{0:T(1024)(128)(2,1)S(1)}, bf16[1024]{0:T(1024)(128)(2,1)}, u32[]{:S(2)}) copy-start(bf16[1024]{0:T(1024)(128)(2,1)} %param.17) | copy-start | bytes 6148
  3.5 50.9 %copy-start.50 = (s32[2,256]{1,0:T(2,128)S(1)}, s32[2,256]{1,0:T(2,128)}, u32[]{:S(2)}) copy-start(s32[2,256]{1,0:T(2,128)} %param.13) | copy-start | bytes 6148
  3.5 50.9 %copy-start.41 = (bf16[4,1024]{1,0:T(4,128)(2,1)S(1)}, bf16[4,1024]{1,0:T(4,128)(2,1)}, u32[]{:S(2)}) copy-start(bf16[4,1024]{1,0:T(4,128)(2,1)} %param.16) | copy-start | bytes 24580
  46.4 12.3 %copy-start.8 = (bf16[2,256,1024]{2,1,0:T(8,128)(2,1)}, bf16[2,256,1024]{2,1,0:T(8,128)(2,1)S(1)}, u32[]{:S(2)}) copy-start(bf16[2,256,1024]{2,1,0:T(8,128)(2,1)S(1)} %get-tuple-element.79) | copy-start | bytes 3145732
  46.4 12.3 %copy-start.10 = (bf16[2,256,1024]{2,1,0:T(8,128)(2,1)}, bf16[2,256,1024]{2,1,0:T(8,128)(2,1)S(1)}, u32[]{:S(2)}) copy-start(bf16[2,256,1024]{2,1,0:T(8,128)(2,1)S(1)} %get-tuple-element.80) | copy-start | bytes 3145732
  46.4 12.3 %copy-start.12 = (bf16[512,512]{1,0:T(8,128)(2,1)}, bf16[512,512]{1,0:T(8,128)(2,1)S(1)}, u32[]{:S(2)}) copy-start(bf16[512,512]{1,0:T(8,128)(2,1)S(1)} %get-tuple-element.71) | copy-start | bytes 1572868
  46.4 12.3 %copy-start.14 = (f32[2,256,128]{2,1,0:T(8,128)}, f32[2,256,128]{2,1,0:T(8,128)S(1)}, u32[]{:S(2)}) copy-start(f32[2,256,128]{2,1,0:T(8,128)S(1)} %get-tuple-element.103.inv_ref) | copy-start | bytes 786436
  46.4 12.2 %copy-start.15 = (f32[8,2048]{1,0:T(8,128)}, f32[8,2048]{1,0:T(8,128)S(1)}, u32[]{:S(2)}) copy-start(f32[8,2048]{1,0:T(8,128)S(1)} %get-tuple-element.102.gain_ref) | copy-start | bytes 196612
  46.5 22.9 %collective-permute-start = (bf16[512,512]{1,0:T(8,128)(2,1)}, bf16[512,512]{1,0:T(8,128)(2,1)}, u32[]{:S(2)}, u32[]{:S(2)}) collective-permute-start(bf16[512,512]{1,0:T(8,128)(2,1)} %get-tuple-element.66), channel_id=1, source_target_pairs={{0,2},{1,3},{2,0},{3,1},{4,6},{5,7},{6,4},{7,5},{8,10},{9,11},{10,... | collective-permute-start | bytes 1572872 | tf_op jit(solution)/shard_map/ppermute | solution.py:1334
  51.7 34.2 %collective-permute-start.3 = (bf16[512,512]{1,0:T(8,128)(2,1)S(1)}, bf16[512,512]{1,0:T(8,128)(2,1)}, u32[]{:S(2)}, u32[]{:S(2)}) collective-permute-start(bf16[512,512]{1,0:T(8,128)(2,1)S(1)} %bitcast.55), channel_id=1, source_target_pairs={{0,4},{4,0},{8,12},{12,8},{16,20},{20,16},{24,28},{28,24},{1,5},{5... | collective-permute-start | bytes 1572872 | tf_op jit(solution)/shard_map/ppermute | solution.py:1409
  53.2 32.7 %collective-permute-start.2 = (bf16[512,1024]{1,0:T(8,128)(2,1)}, bf16[512,1024]{1,0:T(8,128)(2,1)}, u32[]{:S(2)}, u32[]{:S(2)}) collective-permute-start(bf16[512,1024]{1,0:T(8,128)(2,1)} %bitcast.8.y_half_ref), channel_id=1, source_target_pairs={{0,8},{4,12},{8,0},{12,4},{16,24},{20,28},{24,16},{28,20},{1,9},{5... | collective-permute-start | bytes 3145736 | tf_op jit(solution)/shard_map/ppermute | solution.py:1408
  54.4 4.3 %copy-start.37 = (f32[2,256]{1,0:T(2,128)}, f32[2,256]{1,0:T(2,128)S(1)}, u32[]{:S(2)}) copy-start(f32[2,256]{1,0:T(2,128)S(1)} %get-tuple-element.143) | copy-start | bytes 6148
  54.4 4.3 %copy-start.39 = (f32[2,256]{1,0:T(2,128)}, f32[2,256]{1,0:T(2,128)S(1)}, u32[]{:S(2)}) copy-start(f32[2,256]{1,0:T(2,128)S(1)} %get-tuple-element.145) | copy-start | bytes 6148
  54.5 4.3 %copy-start.31 = (f32[1,1024]{1,0:T(1,128)}, f32[1,1024]{1,0:T(1,128)S(1)}, u32[]{:S(2)}) copy-start(f32[1,1024]{1,0:T(1,128)S(1)} %get-tuple-element.140) | copy-start | bytes 12292
  54.5 4.3 %copy-start.33 = (f32[1,1024]{1,0:T(1,128)}, f32[1,1024]{1,0:T(1,128)S(1)}, u32[]{:S(2)}) copy-start(f32[1,1024]{1,0:T(1,128)S(1)} %get-tuple-element.141) | copy-start | bytes 12292
  54.5 4.3 %copy-start.35 = (f32[1,1024]{1,0:T(1,128)}, f32[1,1024]{1,0:T(1,128)S(1)}, u32[]{:S(2)}) copy-start(f32[1,1024]{1,0:T(1,128)S(1)} %get-tuple-element.142) | copy-start | bytes 12292
  56.0 2.8 %copy-start.22 = (f32[2,256,1024]{2,1,0:T(8,128)}, f32[2,256,1024]{2,1,0:T(8,128)S(1)}, u32[]{:S(2)}) copy-start(f32[2,256,1024]{2,1,0:T(8,128)S(1)} %convert_element_type.72) | copy-start | bytes 6291460
  56.0 2.9 %copy-start.47 = (bf16[1024]{0:T(1024)(128)(2,1)S(1)}, bf16[1024]{0:T(1024)(128)(2,1)}, u32[]{:S(2)}) copy-start(bf16[1024]{0:T(1024)(128)(2,1)} %param.21) | copy-start | bytes 6148
  56.0 2.9 %copy-start.48 = (bf16[1024]{0:T(1024)(128)(2,1)S(1)}, bf16[1024]{0:T(1024)(128)(2,1)}, u32[]{:S(2)}) copy-start(bf16[1024]{0:T(1024)(128)(2,1)} %param.20) | copy-start | bytes 6148
  58.8 12.9 %copy-start.3 = (bf16[2,256,1024]{2,1,0:T(8,128)(2,1)S(1)}, bf16[2,256,1024]{2,1,0:T(8,128)(2,1)}, u32[]{:S(2)}) copy-start(bf16[2,256,1024]{2,1,0:T(8,128)(2,1)} %get-tuple-element.65.z_ref) | copy-start | bytes 3145732
  58.8 12.9 %copy-start.13 = (bf16[128,1024]{1,0:T(8,128)(2,1)S(1)}, bf16[128,1024]{1,0:T(8,128)(2,1)}, u32[]{:S(2)}) copy-start(bf16[128,1024]{1,0:T(8,128)(2,1)} %dt_proj_ref.3) | copy-start | bytes 786436
  69.4 16.5 %collective-permute-start.1 = (bf16[512,512]{1,0:T(8,128)(2,1)}, bf16[512,512]{1,0:T(8,128)(2,1)S(1)}, u32[]{:S(2)}, u32[]{:S(2)}) collective-permute-start(bf16[512,512]{1,0:T(8,128)(2,1)} %copy-done.12), channel_id=1, source_target_pairs={{0,2},{1,3},{2,0},{3,1},{4,6},{5,7},{6,4},{7,5},{8,10},{9,11},{10,... | collective-permute-start | bytes 1572872 | tf_op jit(solution)/shard_map/ppermute | solution.py:1334
  85.9 1.6 copy-start.26
  89.0 1.2 copy-start.9
  89.0 1.5 copy-start.11
  90.1 29.5 %copy-start.4 = (bf16[2,256,1024]{2,1,0:T(8,128)(2,1)}, bf16[2,256,1024]{2,1,0:T(8,128)(2,1)S(1)}, u32[]{:S(2)}) copy-start(bf16[2,256,1024]{2,1,0:T(8,128)(2,1)S(1)} %get-tuple-element.129) | copy-start | bytes 3145732
  90.5 29.1 %copy-start.2 = (bf16[4096,512]{1,0:T(8,128)(2,1)S(1)}, bf16[4096,512]{1,0:T(8,128)(2,1)}, u32[]{:S(2)}) copy-start(bf16[4096,512]{1,0:T(8,128)(2,1)} %o_hbm.3) | copy-start | bytes 12582916
  90.5 29.1 %copy-start.7 = (bf16[2,256,2048]{2,1,0:T(8,128)(2,1)S(1)}, bf16[2,256,2048]{2,1,0:T(8,128)(2,1)}, u32[]{:S(2)}) copy-start(bf16[2,256,2048]{2,1,0:T(8,128)(2,1)} %get-tuple-element.86.xs_ref) | copy-start | bytes 6291460
  142.4 3.6 %copy-start.19 = (bf16[256,1024]{1,0:T(8,128)(2,1)}, bf16[256,1024]{1,0:T(8,128)(2,1)S(1)}, u32[]{:S(2)}) copy-start(bf16[256,1024]{1,0:T(8,128)(2,1)S(1)} %get-tuple-element.100.wz_ref) | copy-start | bytes 1572868
  146.0 8.2 %copy-start.16 = (f32[2,256,1024]{2,1,0:T(8,128)S(1)}, f32[2,256,1024]{2,1,0:T(8,128)}, u32[]{:S(2)}) copy-start(f32[2,256,1024]{2,1,0:T(8,128)} %get-tuple-element.91.rate_ref) | copy-start | bytes 6291460
  146.0 8.2 %copy-start.17 = (f32[2,256,1024]{2,1,0:T(8,128)S(1)}, f32[2,256,1024]{2,1,0:T(8,128)}, u32[]{:S(2)}) copy-start(f32[2,256,1024]{2,1,0:T(8,128)} %get-tuple-element.92.beta_ref) | copy-start | bytes 6291460
  146.2 46.1 %collective-permute-start.6 = (bf16[512,512]{1,0:T(8,128)(2,1)S(1)}, bf16[512,512]{1,0:T(8,128)(2,1)S(1)}, u32[]{:S(2)}, u32[]{:S(2)}) collective-permute-start(bf16[512,512]{1,0:T(8,128)(2,1)S(1)} %get-tuple-element.133), channel_id=1, source_target_pairs={{0,24},{4,28},{8,0},{12,4},{16,8},{20,12},{24,16},{28,20},{1,25},{... | collective-permute-start | bytes 1572872 | tf_op jit(solution)/shard_map/ppermute | solution.py:1348
  153.1 45.6 %collective-permute-start.5 = (bf16[512,512]{1,0:T(8,128)(2,1)S(1)}, bf16[512,512]{1,0:T(8,128)(2,1)S(1)}, u32[]{:S(2)}, u32[]{:S(2)}) collective-permute-start(bf16[512,512]{1,0:T(8,128)(2,1)S(1)} %get-tuple-element.134), channel_id=1, source_target_pairs={{0,16},{4,20},{8,24},{12,28},{16,0},{20,4},{24,8},{28,12},{1,17},{... | collective-permute-start | bytes 1572872 | tf_op jit(solution)/shard_map/ppermute | solution.py:1348
  153.6 45.1 %collective-permute-start.4 = (bf16[512,512]{1,0:T(8,128)(2,1)S(1)}, bf16[512,512]{1,0:T(8,128)(2,1)S(1)}, u32[]{:S(2)}, u32[]{:S(2)}) collective-permute-start(bf16[512,512]{1,0:T(8,128)(2,1)S(1)} %get-tuple-element.135), channel_id=1, source_target_pairs={{0,8},{4,12},{8,16},{12,20},{16,24},{20,28},{24,0},{28,4},{1,9},{5... | collective-permute-start | bytes 1572872 | tf_op jit(solution)/shard_map/ppermute | solution.py:1348
  182.6 0.8 copy-start.18
  183.4 17.0 %copy-start.20 = (f32[1,1024]{1,0:T(1,128)}, f32[1,1024]{1,0:T(1,128)S(1)}, u32[]{:S(2)}) copy-start(f32[1,1024]{1,0:T(1,128)S(1)} %get-tuple-element.98.db_ref) | copy-start | bytes 12292
  183.4 17.0 %copy-start.21 = (f32[1,1024]{1,0:T(1,128)}, f32[1,1024]{1,0:T(1,128)S(1)}, u32[]{:S(2)}) copy-start(f32[1,1024]{1,0:T(1,128)S(1)} %get-tuple-element.99.sk_ref) | copy-start | bytes 12292
  183.4 17.0 %copy-start.25 = (bf16[2,256,1024]{2,1,0:T(8,128)(2,1)S(1)}, bf16[2,256,1024]{2,1,0:T(8,128)(2,1)}, u32[]{:S(2)}) copy-start(bf16[2,256,1024]{2,1,0:T(8,128)(2,1)} %get-tuple-element.64) | copy-start | bytes 3145732
  192.3 8.1 %copy-start.23 = (f32[2,256,1024]{2,1,0:T(8,128)S(1)}, f32[2,256,1024]{2,1,0:T(8,128)}, u32[]{:S(2)}) copy-start(f32[2,256,1024]{2,1,0:T(8,128)} %copy-done.22) | copy-start | bytes 6291460
  192.3 8.1 %copy-start.24 = (f32[2,256,1024]{2,1,0:T(8,128)S(1)}, f32[2,256,1024]{2,1,0:T(8,128)}, u32[]{:S(2)}) copy-start(f32[2,256,1024]{2,1,0:T(8,128)} %get-tuple-element.127) | copy-start | bytes 6291460
  192.3 8.1 %copy-start.38 = (f32[2,256]{1,0:T(2,128)S(1)}, f32[2,256]{1,0:T(2,128)}, u32[]{:S(2)}) copy-start(f32[2,256]{1,0:T(2,128)} %copy-done.37) | copy-start | bytes 6148
  192.3 8.1 %copy-start.40 = (f32[2,256]{1,0:T(2,128)S(1)}, f32[2,256]{1,0:T(2,128)}, u32[]{:S(2)}) copy-start(f32[2,256]{1,0:T(2,128)} %copy-done.39) | copy-start | bytes 6148
  203.4 0.7 copy-start.32
  203.4 0.7 copy-start.34
  203.4 0.7 copy-start.36
  270.0 2.1 copy-start.30
  270.0 2.8 %copy-start.49 = (f32[1,512]{1,0:T(1,128)S(1)}, f32[1,512]{1,0:T(1,128)}, u32[]{:S(2)}) copy-start(f32[1,512]{1,0:T(1,128)} %get-tuple-element.105) | copy-start | bytes 6148
  270.0 3.4 %copy-start.27 = (f32[256,2048]{1,0:T(8,128)S(1)}, f32[256,2048]{1,0:T(8,128)}, u32[]{:S(2)}) copy-start(f32[256,2048]{1,0:T(8,128)} %get-tuple-element.160) | copy-start | bytes 6291460
  273.4 1.4 copy-start.42
  273.4 2.0 copy-start.45
  273.4 2.6 copy-start.28
  273.4 3.4 %copy-start.29 = (f32[128,1024]{1,0:T(8,128)S(1)}, f32[128,1024]{1,0:T(8,128)}, u32[]{:S(2)}) copy-start(f32[128,1024]{1,0:T(8,128)} %get-tuple-element.164) | copy-start | bytes 1572868
  273.4 5.4 %copy-start.1 = (bf16[160,1024]{1,0:T(8,128)(2,1)S(1)}, bf16[160,1024]{1,0:T(8,128)(2,1)}, u32[]{:S(2)}) copy-start(bf16[160,1024]{1,0:T(8,128)(2,1)} %param.18) | copy-start | bytes 983044
  274.8 2.8 %copy-start.44 = (f32[1,1024]{1,0:T(1,128)S(1)}, f32[1,1024]{1,0:T(1,128)}, u32[]{:S(2)}) copy-start(f32[1,1024]{1,0:T(1,128)} %get-tuple-element.111) | copy-start | bytes 12292
  274.8 3.4 %copy-start.43 = (f32[1,1024]{1,0:T(1,128)S(1)}, f32[1,1024]{1,0:T(1,128)}, u32[]{:S(2)}) copy-start(f32[1,1024]{1,0:T(1,128)} %get-tuple-element.112) | copy-start | bytes 12292
